TPU v7x, 32 devices: a whole 2x2x4 slice. The times are simulated.
32 devices in a mesh: rep: 8 (over y, x, core), grp: 4 (over z).
Axes of the slice: x: 2, y: 2, z: 4, core: 2. Of those that a mesh axis runs over, the one named last changes fastest.
Arguments:
- images: bfloat16 [32, 577, 1024], P(('rep', 'grp')), may hold values from -6 to 6
- cotangent: bfloat16 [32, 577, 1024], P(('rep', 'grp')), may hold values from -6 to 6
- ln1_gain: bfloat16 [1024], P('grp'), may hold values from 0.5 to 1.5
- ln1_shift: bfloat16 [1024], P('grp'), may hold values from -3 to 3
- qkv_weight: bfloat16 [1024, 3072], P('grp'), may hold values from -1 to 1
- qv_bias: bfloat16 [2048], P('grp'), may hold values from -3 to 3
- out_weight: bfloat16 [1024, 1024], P('grp'), may hold values from -1.5 to 1.5
- out_bias: bfloat16 [1024], P('grp'), may hold values from -3 to 3
- ln2_gain: bfloat16 [1024], P('grp'), may hold values from 0.5 to 1.5
- ln2_shift: bfloat16 [1024], P('grp'), may hold values from -3 to 3
- fc1_weight: bfloat16 [1024, 4096], P('grp'), may hold values from -0.1875 to 0.1875
- fc1_bias: bfloat16 [4096], P('grp'), may hold values from -3 to 3
- fc2_weight: bfloat16 [4096, 1024], P('grp'), may hold values from -0.09375 to 0.09375
- fc2_bias: bfloat16 [1024], P('grp'), may hold values from -3 to 3
Outputs:
- outputs: bfloat16 [32, 577, 1024], P(('rep', 'grp'))
- input_grad: bfloat16 [32, 577, 1024], P(('rep', 'grp'))
- grad_ln1_gain: float32 [1024], P('grp')
- grad_ln1_shift: float32 [1024], P('grp')
- grad_qkv_weight: float32 [1024, 3072], P('grp')
- grad_qv_bias: float32 [2048], P('grp')
- grad_out_weight: float32 [1024, 1024], P('grp')
- grad_out_bias: float32 [1024], P('grp')
- grad_ln2_gain: float32 [1024], P('grp')
- grad_ln2_shift: float32 [1024], P('grp')
- grad_fc1_weight: float32 [1024, 4096], P('grp')
- grad_fc1_bias: float32 [4096], P('grp')
- grad_fc2_weight: float32 [4096, 1024], P('grp')
- grad_fc2_bias: float32 [1024], P('grp')
All inputs are finite; a program needn't handle non-finite values.
Results may differ from a plain program's by a relative error of at most 0.012.
Values may be sent and summed in bfloat16 or wider, within the bound.
No kernel may reach another device: no remote copies, remote signals or barrier semaphores. Data moves between devices by JAX's collectives and lax.ppermute only.
A program may use at most 256 MiB of HBM per device.

v0:
```python
import math

import jax
import jax.numpy as jnp
from jax import lax
from jax.sharding import PartitionSpec as P

H = 16
HD = 64


root_half = 0.7071067811865476
inv_root_tau = 0.3989422804014327


def norm_forward(values, gain_vec, shift_vec):
    row_mean = jnp.mean(values, axis=-1, keepdims=True)
    centred = values - row_mean
    inv_std = lax.rsqrt(jnp.mean(centred * centred, axis=-1, keepdims=True) + 1e-06)
    normed = centred * inv_std
    return (normed * gain_vec + shift_vec, normed, inv_std)


def norm_backward(grad_out, normed, inv_std, gain_vec):
    grad_hat = grad_out * gain_vec
    grad_in = inv_std * (
        grad_hat
        - jnp.mean(grad_hat, axis=-1, keepdims=True)
        - normed * jnp.mean(grad_hat * normed, axis=-1, keepdims=True)
    )
    return (grad_in, jnp.sum(grad_out * normed, axis=0), jnp.sum(grad_out, axis=0))


def split_heads(matrix):
    return matrix.reshape(matrix.shape[0], H, HD).transpose(1, 0, 2)


def join_heads(tensor):
    return tensor.transpose(1, 0, 2).reshape(tensor.shape[1], H * HD)


def grouped(tensor):
    group_size = math.gcd(H, 4)
    return tensor.reshape((H // group_size, group_size) + tensor.shape[1:])


def ungrouped(tensor):
    return tensor.reshape((H,) + tensor.shape[2:])


def head_scores(query_group, key_group):
    return jnp.einsum("hqd,hkd->hqk", query_group, key_group, preferred_element_type=jnp.float32)


def attend_group(group):
    query_group, key_group, value_group = group
    scores = head_scores(query_group, key_group)
    row_max = jnp.max(scores, axis=-1, keepdims=True)
    log_total = row_max + jnp.log(jnp.sum(jnp.exp(scores - row_max), axis=-1, keepdims=True))
    probs = jnp.exp(scores - log_total).astype(jnp.bfloat16)
    mixed = jnp.einsum("hqk,hkd->hqd", probs, value_group, preferred_element_type=jnp.float32)
    return (mixed, log_total)


def attend_back(group):
    query_group, key_group, value_group, log_total, grad_mixed = group
    probs_exact = jnp.exp(head_scores(query_group, key_group) - log_total)
    grad_probs = jnp.einsum(
        "hqd,hkd->hqk", grad_mixed, value_group, preferred_element_type=jnp.float32
    )
    row_dot = jnp.sum(probs_exact * grad_probs, axis=-1, keepdims=True)
    grad_scores = (probs_exact * (grad_probs - row_dot)).astype(jnp.bfloat16)
    grad_query = (
        jnp.einsum("hqk,hkd->hqd", grad_scores, key_group, preferred_element_type=jnp.float32)
        * 0.125
    )
    grad_key = jnp.einsum(
        "hqk,hqd->hkd", grad_scores, query_group, preferred_element_type=jnp.float32
    )
    grad_value = jnp.einsum(
        "hqk,hqd->hkd",
        probs_exact.astype(jnp.bfloat16),
        grad_mixed,
        preferred_element_type=jnp.float32,
    )
    return (grad_query, grad_key, grad_value)


def forward_image(image, params):
    (
        gain_first,
        shift_first,
        attn_in,
        bias_pair,
        attn_out,
        bias_attn,
        gain_second,
        shift_second,
        mlp_up,
        bias_up,
        mlp_down,
        bias_down,
    ) = params
    model_width = attn_out.shape[0]
    incoming = image.astype(jnp.float32)
    normed_f, normed_one, inv_std_one = norm_forward(
        incoming, gain_first.astype(jnp.float32), shift_first.astype(jnp.float32)
    )
    normed_in = normed_f.astype(jnp.bfloat16)
    projected = jnp.dot(normed_in, attn_in, preferred_element_type=jnp.float32)
    bias_float = bias_pair.astype(jnp.float32)
    query_heads = split_heads(
        ((projected[:, :model_width] + bias_float[:model_width]) * 0.125).astype(jnp.bfloat16)
    )
    key_heads = split_heads(projected[:, model_width : 2 * model_width].astype(jnp.bfloat16))
    value_heads = split_heads(
        (projected[:, 2 * model_width :] + bias_float[model_width:]).astype(jnp.bfloat16)
    )
    mixed, log_total = lax.map(
        attend_group, (grouped(query_heads), grouped(key_heads), grouped(value_heads))
    )
    attended = join_heads(ungrouped(mixed)).astype(jnp.bfloat16)
    residual = (
        incoming
        + jnp.dot(attended, attn_out, preferred_element_type=jnp.float32)
        + bias_attn.astype(jnp.float32)
    )
    mid_f, normed_two, inv_std_two = norm_forward(
        residual, gain_second.astype(jnp.float32), shift_second.astype(jnp.float32)
    )
    normed_mid = mid_f.astype(jnp.bfloat16)
    pre_act = jnp.dot(normed_mid, mlp_up, preferred_element_type=jnp.float32) + bias_up.astype(
        jnp.float32
    )
    normal_cdf = 0.5 * (1.0 + lax.erf(pre_act * root_half))
    activated = (pre_act * normal_cdf).astype(jnp.bfloat16)
    block_out = (
        residual
        + jnp.dot(activated, mlp_down, preferred_element_type=jnp.float32)
        + bias_down.astype(jnp.float32)
    ).astype(jnp.bfloat16)
    stored = (
        normed_in,
        normed_one,
        inv_std_one,
        query_heads,
        key_heads,
        value_heads,
        ungrouped(log_total),
        attended,
        normed_mid,
        normed_two,
        inv_std_two,
        pre_act,
        normal_cdf,
        activated,
    )
    return (block_out, stored)


def backward_image(grad_block, stored, params):
    (
        gain_first,
        shift_first,
        attn_in,
        bias_pair,
        attn_out,
        bias_attn,
        gain_second,
        shift_second,
        mlp_up,
        bias_up,
        mlp_down,
        bias_down,
    ) = params
    (
        normed_in,
        normed_one,
        inv_std_one,
        query_heads,
        key_heads,
        value_heads,
        log_total,
        attended,
        normed_mid,
        normed_two,
        inv_std_two,
        pre_act,
        normal_cdf,
        activated,
    ) = stored
    grad_top = grad_block.astype(jnp.float32)
    grad_down = jnp.dot(activated.T, grad_block, preferred_element_type=jnp.float32)
    grad_bias_down = jnp.sum(grad_top, axis=0)
    grad_hidden = jnp.dot(grad_block, mlp_down.T, preferred_element_type=jnp.float32)
    density = jnp.exp(-0.5 * pre_act * pre_act) * inv_root_tau
    grad_pre = grad_hidden * (normal_cdf + pre_act * density)
    grad_pre_b = grad_pre.astype(jnp.bfloat16)
    grad_up = jnp.dot(normed_mid.T, grad_pre_b, preferred_element_type=jnp.float32)
    grad_bias_up = jnp.sum(grad_pre, axis=0)
    grad_mid = jnp.dot(grad_pre_b, mlp_up.T, preferred_element_type=jnp.float32)
    grad_norm_mid, grad_gain_second, grad_shift_second = norm_backward(
        grad_mid, normed_two, inv_std_two, gain_second.astype(jnp.float32)
    )
    grad_residual = grad_top + grad_norm_mid
    grad_bias_attn = jnp.sum(grad_residual, axis=0)
    grad_res_b = grad_residual.astype(jnp.bfloat16)
    grad_attn_out = jnp.dot(attended.T, grad_res_b, preferred_element_type=jnp.float32)
    grad_attended = split_heads(
        jnp.dot(grad_res_b, attn_out.T, preferred_element_type=jnp.float32).astype(jnp.bfloat16)
    )
    grad_query, grad_key, grad_value = lax.map(
        attend_back,
        (
            grouped(query_heads),
            grouped(key_heads),
            grouped(value_heads),
            grouped(log_total),
            grouped(grad_attended),
        ),
    )
    grad_query = join_heads(ungrouped(grad_query))
    grad_key = join_heads(ungrouped(grad_key))
    grad_value = join_heads(ungrouped(grad_value))
    grad_projected = jnp.concatenate([grad_query, grad_key, grad_value], axis=1)
    grad_bias_pair = jnp.concatenate([jnp.sum(grad_query, axis=0), jnp.sum(grad_value, axis=0)])
    grad_proj_b = grad_projected.astype(jnp.bfloat16)
    grad_attn_in = jnp.dot(normed_in.T, grad_proj_b, preferred_element_type=jnp.float32)
    grad_in_norm = jnp.dot(grad_proj_b, attn_in.T, preferred_element_type=jnp.float32)
    grad_norm_in, grad_gain_first, grad_shift_first = norm_backward(
        grad_in_norm, normed_one, inv_std_one, gain_first.astype(jnp.float32)
    )
    input_grad = (grad_residual + grad_norm_in).astype(jnp.bfloat16)
    grads = (
        grad_gain_first,
        grad_shift_first,
        grad_attn_in,
        grad_bias_pair,
        grad_attn_out,
        grad_bias_attn,
        grad_gain_second,
        grad_shift_second,
        grad_up,
        grad_bias_up,
        grad_down,
        grad_bias_down,
    )
    return (input_grad, grads)


def on_device(
    images,
    cotangent,
    ln1_gain,
    ln1_shift,
    qkv_weight,
    qv_bias,
    out_weight,
    out_bias,
    ln2_gain,
    ln2_shift,
    fc1_weight,
    fc1_bias,
    fc2_weight,
    fc2_bias,
):
    gathered = (
        lax.all_gather(ln1_gain, "grp", axis=0, tiled=True),
        lax.all_gather(ln1_shift, "grp", axis=0, tiled=True),
        lax.all_gather(qkv_weight, "grp", axis=0, tiled=True),
        lax.all_gather(qv_bias, "grp", axis=0, tiled=True),
        lax.all_gather(out_weight, "grp", axis=0, tiled=True),
        lax.all_gather(out_bias, "grp", axis=0, tiled=True),
        lax.all_gather(ln2_gain, "grp", axis=0, tiled=True),
        lax.all_gather(ln2_shift, "grp", axis=0, tiled=True),
        lax.all_gather(fc1_weight, "grp", axis=0, tiled=True),
        lax.all_gather(fc1_bias, "grp", axis=0, tiled=True),
        lax.all_gather(fc2_weight, "grp", axis=0, tiled=True),
        lax.all_gather(fc2_bias, "grp", axis=0, tiled=True),
    )
    position = 0
    block_out, stored = forward_image(images[position], gathered)
    block_outs = [block_out]
    stored_list = [stored]
    regathered = (
        lax.all_gather(ln1_gain, "grp", axis=0, tiled=True),
        lax.all_gather(ln1_shift, "grp", axis=0, tiled=True),
        lax.all_gather(qkv_weight, "grp", axis=0, tiled=True),
        lax.all_gather(qv_bias, "grp", axis=0, tiled=True),
        lax.all_gather(out_weight, "grp", axis=0, tiled=True),
        lax.all_gather(out_bias, "grp", axis=0, tiled=True),
        lax.all_gather(ln2_gain, "grp", axis=0, tiled=True),
        lax.all_gather(ln2_shift, "grp", axis=0, tiled=True),
        lax.all_gather(fc1_weight, "grp", axis=0, tiled=True),
        lax.all_gather(fc1_bias, "grp", axis=0, tiled=True),
        lax.all_gather(fc2_weight, "grp", axis=0, tiled=True),
        lax.all_gather(fc2_bias, "grp", axis=0, tiled=True),
    )
    position = 0
    input_grad, grads = backward_image(cotangent[position], stored_list[position], regathered)
    input_grads = [input_grad]
    shares = (
        lax.psum_scatter(grads[0], "grp", scatter_dimension=0, tiled=True),
        lax.psum_scatter(grads[1], "grp", scatter_dimension=0, tiled=True),
        lax.psum_scatter(grads[2], "grp", scatter_dimension=0, tiled=True),
        lax.psum_scatter(grads[3], "grp", scatter_dimension=0, tiled=True),
        lax.psum_scatter(grads[4], "grp", scatter_dimension=0, tiled=True),
        lax.psum_scatter(grads[5], "grp", scatter_dimension=0, tiled=True),
        lax.psum_scatter(grads[6], "grp", scatter_dimension=0, tiled=True),
        lax.psum_scatter(grads[7], "grp", scatter_dimension=0, tiled=True),
        lax.psum_scatter(grads[8], "grp", scatter_dimension=0, tiled=True),
        lax.psum_scatter(grads[9], "grp", scatter_dimension=0, tiled=True),
        lax.psum_scatter(grads[10], "grp", scatter_dimension=0, tiled=True),
        lax.psum_scatter(grads[11], "grp", scatter_dimension=0, tiled=True),
    )
    owned_parts = lax.psum(
        (
            shares[0],
            shares[1],
            shares[2],
            shares[3],
            shares[4],
            shares[5],
            shares[6],
            shares[7],
            shares[8],
            shares[9],
            shares[10],
            shares[11],
        ),
        "rep",
    )
    return (
        jnp.stack(block_outs),
        jnp.stack(input_grads),
        owned_parts[0],
        owned_parts[1],
        owned_parts[2],
        owned_parts[3],
        owned_parts[4],
        owned_parts[5],
        owned_parts[6],
        owned_parts[7],
        owned_parts[8],
        owned_parts[9],
        owned_parts[10],
        owned_parts[11],
    )


def solution(mesh):
    return jax.shard_map(
        on_device,
        mesh=mesh,
        in_specs=(
            P(("rep", "grp"), None, None),
            P(("rep", "grp"), None, None),
            P("grp"),
            P("grp"),
            P("grp", None),
            P("grp"),
            P("grp", None),
            P("grp"),
            P("grp"),
            P("grp"),
            P("grp", None),
            P("grp"),
            P("grp", None),
            P("grp"),
        ),
        out_specs=(
            P(("rep", "grp"), None, None),
            P(("rep", "grp"), None, None),
            P("grp"),
            P("grp"),
            P("grp", None),
            P("grp"),
            P("grp", None),
            P("grp"),
            P("grp"),
            P("grp"),
            P("grp", None),
            P("grp"),
            P("grp", None),
            P("grp"),
        ),
        check_vma=False,
    )
```

profile of v0, /device:TPU:0, one launch (start us, length us, event | category | flops | bytes accessed | tf_op | source)
XLA Modules:
  0.0 1557.2 jit_solution(15243761869660950640)
XLA Ops:
  10.2 12.8 all-gather.3
  24.2 8.0 all-gather.1
  32.3 12.8 all-gather
  45.1 17.2 %all_gather.51 = bf16[4096]{0:T(1024)(128)(2,1)S(1)} all-gather(bf16[1024]{0:T(1024)(128)(2,1)S(1)} %copy-done.30), channel_id=1, replica_groups=mesh['rep'=8,'grp'=4] {'grp'}, dimensions={0}, use_global_device_ids=true | all-gather | bytes 10240 | tf_op jit(solution)/shard_map/all_gather | solution.py:277
  62.4 8.2 all-gather.5
  70.6 17.1 %all-gather.4 = bf16[4,1,256]{2,1,0:T(2,128)(2,1)S(1)} all-gather(bf16[1,1,256]{2,1,0:T(2,128)(2,1)S(1)} %reshape.182), channel_id=1, replica_groups=mesh['rep'=8,'grp'=4] {'grp'}, dimensions={0}, use_global_device_ids=true | all-gather | bytes 2560 | tf_op jit(solution)/shard_map/all_gather | solution.py:274
  87.7 17.2 %all-gather.2 = bf16[4,1,512]{2,1,0:T(2,128)(2,1)S(1)} all-gather(bf16[1,1,512]{2,1,0:T(2,128)(2,1)S(1)} %reshape.178), channel_id=1, replica_groups=mesh['rep'=8,'grp'=4] {'grp'}, dimensions={0}, use_global_device_ids=true | all-gather | bytes 5120 | tf_op jit(solution)/shard_map/all_gather | solution.py:271
  105.7 22.4 %all-gather.12.cloned.1.call-done = bf16[1024,3072]{1,0:T(8,128)(2,1)} async-done(((bf16[256,3072]{1,0:T(8,128)(2,1)}), bf16[1024,3072]{1,0:T(8,128)(2,1)}) %all-gather.12.cloned.1.call-update) | async-done | bytes 6291472 | tf_op jit(solution)/shard_map/all_gather | solution.py:270
  128.1 6.6 fusion.90
  135.9 1.7 fusion.70
  138.3 1.7 copy.49
  140.0 2.4 copy.50
  142.4 22.3 %while.28 = (s32[]{:T(128)}, bf16[4,4,577,64]{2,3,1,0:T(8,128)(2,1)}, f32[4,4,577,1]{2,1,3,0:T(4,128)S(1)}, bf16[4,4,577,64]{2,3,1,0:T(8,128)(2,1)S(1)}, bf16[4,...) while((s32[]{:T(128)}, bf16[4,4,577,64]{2,3,1,0:T(8,128)(2,1)}, ...), condition=%wide.region_5.6_spmd.clone, body=%wide.region_2.5_spmd.sunk.clone | while | flops 347575552 | bytes 27806936 | solution.py:119
  144.9 2.0 fusion.147
  150.5 2.0 fusion.147
  156.1 2.0 fusion.147
  161.7 2.0 fusion.147
  164.7 8.8 all-gather.14.cloned.1.call-done
  173.5 3.9 fusion.97
  177.5 1.4 copy-done
  179.3 144.3 %all-gather.16.cloned.1.call-done = bf16[1024,4096]{1,0:T(8,128)(2,1)} async-done(((bf16[256,4096]{1,0:T(8,128)(2,1)}), bf16[1024,4096]{1,0:T(8,128)(2,1)}) %all-gather.16.cloned.1.call-update) | async-done | bytes 8388624 | tf_op jit(solution)/shard_map/all_gather | solution.py:276
  323.6 12.6 multiply_convert_fusion.1
  336.1 136.7 %all-gather.18.cloned.1.call-done = bf16[4096,1024]{1,0:T(8,128)(2,1)} async-done(((bf16[1024,1024]{1,0:T(8,128)(2,1)}), bf16[4096,1024]{1,0:T(8,128)(2,1)}) %all-gather.18.cloned.1.call-update) | async-done | bytes 8388624 | tf_op jit(solution)/shard_map/all_gather | solution.py:278
  472.8 12.9 fusion.98
  485.8 5.7 multiply_reduce_fusion.1
  491.5 1.3 fusion.93
  492.8 1.4 copy-done.7
  494.2 3.8 fusion.84
  498.0 4.8 convolution_convert_fusion
  502.8 2.4 copy.51
  505.3 37.3 %while.29 = (s32[]{:T(128)}, f32[4,4,577,64]{2,3,1,0:T(8,128)}, bf16[4,4,577,64]{2,3,1,0:T(8,128)(2,1)}, f32[4,4,577,64]{2,3,1,0:T(8,128)}, bf16[4,4,577,64]{2,3...) while((s32[]{:T(128)}, f32[4,4,577,64]{2,3,1,0:T(8,128)}, ...), condition=%wide.region_12.13_spmd.clone, body=%wide.region_10.12_spmd.sunk.clone | while | flops 864429056 | bytes 60423508 | solution.py:212
  506.8 2.3 multiply_reduce_fusion.8
  510.3 1.5 fusion.157
  512.8 1.9 fusion.159
  516.0 2.3 multiply_reduce_fusion.8
  519.6 1.5 fusion.157
  522.1 1.9 fusion.159
  525.3 2.3 multiply_reduce_fusion.8
  528.9 1.5 fusion.157
  531.4 1.9 fusion.159
  534.6 2.3 multiply_reduce_fusion.8
  538.1 1.5 fusion.157
  540.7 1.9 fusion.159
  542.6 2.1 bitcast_convert_fusion
  547.4 11.5 fusion.77
  559.0 1.6 copy-done.2
  560.6 13.1 fusion.73
  573.7 12.3 fusion.81
  586.1 208.9 %reduce-scatter.5.cloned.1.call-done = f32[256,3072]{1,0:T(8,128)} async-done(((f32[1024,3072]{1,0:T(8,128)}), f32[256,3072]{1,0:T(8,128)}) %reduce-scatter.5.cloned.1.call-update) | async-done | bytes 3145744 | tf_op jit(solution)/shard_map/reduce_scatter | solution.py:305
  795.0 283.9 %reduce-scatter.9.cloned.1.call-done = f32[256,4096]{1,0:T(8,128)} async-done(((f32[1024,4096]{1,0:T(8,128)}), f32[256,4096]{1,0:T(8,128)}) %reduce-scatter.9.cloned.1.call-update) | async-done | bytes 4194320 | tf_op jit(solution)/shard_map/reduce_scatter | solution.py:311
  1078.9 283.5 %reduce-scatter.11.cloned.1.call-done = f32[1024,1024]{1,0:T(8,128)} async-done(((f32[4096,1024]{1,0:T(8,128)}), f32[1024,1024]{1,0:T(8,128)}) %reduce-scatter.11.cloned.1.call-update) | async-done | bytes 4194320 | tf_op jit(solution)/shard_map/reduce_scatter | solution.py:313
  1363.0 10.5 all-gather.6
  1376.1 2.0 reduce_sum.187
  1378.1 2.0 reduce_sum.185
  1380.2 10.5 fusion.67
  1390.7 16.5 %all-reduce.10 = (f32[1024]{0:T(1024)S(1)}, f32[1024]{0:T(1024)S(1)}, f32[2048]{0:T(1024)S(1)}, f32[1024]{0:T(1024)S(1)}, f32[1024]{0:T(1024)S(1)}, /*index=5*/f...) all-reduce(f32[1024]{0:T(1024)S(1)} %get-tuple-element.103, ...), channel_id=2, replica_groups=mesh['rep'=8,'grp'=4] {'grp'}, use_global_device_ids=true, to_apply=%region_16.17.clone | all-reduce | flops 12288 | bytes 98304
  1407.8 23.5 %all-reduce.8 = (f32[256]{0:T(256)}, f32[256]{0:T(256)}, f32[512]{0:T(512)}, f32[256]{0:T(256)}, f32[256]{0:T(256)}, /*index=5*/f32[256]{0:T(256)}, f32[1024]{0:T(1024)}, f32[256]{0:T(256)}) all-reduce(f32[256]{0:T(256)S(1)} %dynamic-slice.1, f32[256]{0:T(256)S(1)} %dynamic-slice.3, ...), channel_id=1, replica_groups=mesh['rep'=8,'grp'=4] {'rep'}, use_global_device_ids=true, to_apply=%region_17.18 | all-reduce | flops 3072 | bytes 24576 | tf_op jit(solution)/shard_map/psum | solution.py:316
  1431.3 5.6 fusion.80
  1436.9 9.7 fusion.79
  1446.7 92.8 %all-reduce.13.cloned.1.call-done = (f32[256,3072]{1,0:T(8,128)}, f32[256,1024]{1,0:T(8,128)}, f32[256,4096]{1,0:T(8,128)}, f32[1024,1024]{1,0:T(8,128)}) async-done(((f32[256,3072]{1,0:T(8,128)}, f32[256,1024]{1,0:T(8,128)}, f32[256,4096]{1,0:T(8,128)}, f32[1024,1024]{1,0:T(8,128)}), (f32[256,3072]{1,0:T(8,128)}, f32[256,1024]{1,0:T(8,128)}, f32[256,4096]{1,0:T(8,128)}, ...) | async-done | bytes 12582928 | tf_op jit(solution)/shard_map/psum | solution.py:316
  1539.5 4.0 copy.88
  1544.5 2.1 copy.90
  1546.6 1.6 copy-done.13
  1548.2 2.0 copy.91
  (199 shorter events, 41.4 us)
Async XLA Ops:
  7.2 120.9 %all-gather.12.cloned.1.call-start = ((), (), s32[]{:S(2)}) async-start(), calls=%async_computation.4 | async-start | bytes 7864320 | tf_op jit(solution)/shard_map/all_gather | solution.py:270
  7.9 2.2 copy-start.33
  7.9 165.6 %all-gather.14.cloned.1.call-start = ((), (), s32[]{:S(2)}) async-start(), calls=%async_computation.5 | async-start | bytes 2621440 | tf_op jit(solution)/shard_map/all_gather | solution.py:272
  8.7 314.9 %all-gather.16.cloned.1.call-start = ((), (), s32[]{:S(2)}) async-start(), calls=%async_computation.6 | async-start | bytes 10485760 | tf_op jit(solution)/shard_map/all_gather | solution.py:276
  9.4 463.4 %all-gather.18.cloned.1.call-start = ((), (), s32[]{:S(2)}) async-start(), calls=%async_computation.7 | async-start | bytes 10485760 | tf_op jit(solution)/shard_map/all_gather | solution.py:278
  10.0 14.2 copy-start.34
  10.0 22.2 %copy-start.35 = (bf16[256]{0:T(256)(128)(2,1)S(1)}, bf16[256]{0:T(256)(128)(2,1)}, u32[]{:S(2)}) copy-start(bf16[256]{0:T(256)(128)(2,1)} %param.20) | copy-start | bytes 1540
  10.0 35.1 %copy-start.31 = (bf16[512]{0:T(512)(128)(2,1)S(1)}, bf16[512]{0:T(512)(128)(2,1)}, u32[]{:S(2)}) copy-start(bf16[512]{0:T(512)(128)(2,1)} %param.23) | copy-start | bytes 3076
  10.0 35.1 %copy-start.30 = (bf16[1024]{0:T(1024)(128)(2,1)S(1)}, bf16[1024]{0:T(1024)(128)(2,1)}, u32[]{:S(2)}) copy-start(bf16[1024]{0:T(1024)(128)(2,1)} %param.29) | copy-start | bytes 6148
  10.0 52.3 %copy-start.36 = (bf16[256]{0:T(256)(128)(2,1)S(1)}, bf16[256]{0:T(256)(128)(2,1)}, u32[]{:S(2)}) copy-start(bf16[256]{0:T(256)(128)(2,1)} %param.27) | copy-start | bytes 1540
  10.0 60.5 %copy-start.37 = (bf16[256]{0:T(256)(128)(2,1)S(1)}, bf16[256]{0:T(256)(128)(2,1)}, u32[]{:S(2)}) copy-start(bf16[256]{0:T(256)(128)(2,1)} %param.26) | copy-start | bytes 1540
  10.0 94.8 %copy-start.4 = (bf16[1,577,1024]{2,1,0:T(8,128)(2,1)S(1)}, bf16[1,577,1024]{2,1,0:T(8,128)(2,1)}, u32[]{:S(2)}) copy-start(bf16[1,577,1024]{2,1,0:T(8,128)(2,1)} %param.18) | copy-start | bytes 3545092
  10.1 576.1 %reduce-scatter.7.cloned.1.call-start = ((), (), s32[]{:S(2)}) async-start(), calls=%async_computation.9 | async-start | bytes 5242880 | tf_op jit(solution)/shard_map/reduce_scatter | solution.py:307
  23.1 82.5 %copy-start.8 = (bf16[4,4,577,64]{2,3,1,0:T(8,128)(2,1)}, bf16[4,4,577,64]{2,3,1,0:T(8,128)(2,1)S(1)}, u32[]{:S(2)}) copy-start(bf16[4,4,577,64]{2,3,1,0:T(8,128)(2,1)S(1)} %fusion.95) | copy-start | bytes 3545092
  32.2 102.4 %copy-start.28 = (f32[4,1,256]{2,1,0:T(1,128)}, f32[4,1,256]{2,1,0:T(1,128)S(1)}, u32[]{:S(2)}) copy-start(f32[4,1,256]{2,1,0:T(1,128)S(1)} %convert_element_type.114) | copy-start | bytes 12292
  45.1 89.5 %copy-start.24 = (f32[4,1,256]{2,1,0:T(1,128)}, f32[4,1,256]{2,1,0:T(1,128)S(1)}, u32[]{:S(2)}) copy-start(f32[4,1,256]{2,1,0:T(1,128)S(1)} %convert_element_type.113) | copy-start | bytes 12292
  105.1 29.5 %copy-start.22 = (f32[577]{0:T(1024)}, f32[577]{0:T(1024)S(1)}, u32[]{:S(2)}) copy-start(f32[577]{0:T(1024)S(1)} %broadcast_multiply_fusion.5) | copy-start | bytes 6928
  105.6 29.0 %copy-start.26 = (f32[577]{0:T(1024)}, f32[577]{0:T(1024)S(1)}, u32[]{:S(2)}) copy-start(f32[577]{0:T(1024)S(1)} %add_rsqrt_fusion.1) | copy-start | bytes 6928
  143.6 1.3 copy-start.15
  147.0 1.1 copy-start.16
  149.2 1.3 copy-start.15
  152.5 1.1 copy-start.16
  154.7 1.3 copy-start.15
  158.1 1.1 copy-start.16
  160.3 1.3 copy-start.15
  163.7 1.1 copy-start.16
  177.5 1.4 copy-start
  472.8 12.9 copy-start.1
  472.8 12.9 copy-start.32
  485.7 5.7 copy-start.12
  485.8 5.7 copy-start.20
  491.5 2.7 copy-start.17
  492.8 1.4 copy-start.7
  505.2 289.8 %reduce-scatter.5.cloned.1.call-start = ((), (), s32[]{:S(2)}) async-start(), calls=%async_computation.8 | async-start | bytes 15728640 | tf_op jit(solution)/shard_map/reduce_scatter | solution.py:305
  505.4 1.3 copy-start.3
  510.3 1.5 copy-start.9
  512.8 1.9 copy-start.10
  514.7 1.3 copy-start.3
  519.6 1.5 copy-start.9
  522.1 1.9 copy-start.10
  524.0 1.4 copy-start.3
  528.9 1.5 copy-start.9
  531.4 1.9 copy-start.10
  533.3 1.3 copy-start.3
  538.1 1.5 copy-start.9
  540.7 1.9 copy-start.10
  542.6 2.6 copy-start.6
  544.6 1.2 copy-start.18
  544.6 2.2 copy-start.5
  544.7 2.7 copy-start.11
  544.7 2.7 copy-start.23
  544.7 2.7 copy-start.25
  544.7 2.7 copy-start.27
  544.7 2.7 copy-start.29
  545.3 1.1 copy-start.19
  558.9 1.7 copy-start.2
  558.9 520.0 %reduce-scatter.9.cloned.1.call-start = ((), (), s32[]{:S(2)}) async-start(), calls=%async_computation.10 | async-start | bytes 20971520 | tf_op jit(solution)/shard_map/reduce_scatter | solution.py:311
  573.7 788.6 %reduce-scatter.11.cloned.1.call-start = ((), (), s32[]{:S(2)}) async-start(), calls=%async_computation.11 | async-start | bytes 20971520 | tf_op jit(solution)/shard_map/reduce_scatter | solution.py:313
  586.1 953.4 %all-reduce.13.cloned.1.call-start = ((), (), s32[]{:S(2)}) async-start(), calls=%async_computation.12 | async-start | bytes 25165824 | tf_op jit(solution)/shard_map/psum | solution.py:316
  1362.3 0.7 copy-start.38
  1362.3 11.2 copy-start.39
  1539.5 4.0 copy-start.21
  1539.5 5.0 copy-start.14
  1544.5 3.7 copy-start.13
Sparse Core Ops, SparseCore 0:
  9.6 118.4 all-gather.11
  129.6 43.8 all-gather.13
  175.1 148.4 all-gather.15
  325.0 147.7 all-gather.17
  505.3 74.9 reduce-scatter.6
  582.6 212.3 reduce-scatter.4
  797.4 281.4 reduce-scatter.8
  1081.2 281.0 reduce-scatter.10
  1366.3 173.0 all-reduce.12
where the time goes:
time: 1570 us; the launch traced here: 1560 us
  waiting for transfers between devices  1180 us (75%)
  matrix products  151 us (10%)
  blocking collectives  144 us (9%)
  local copies, waits for them, and re-layouts  35.9 us (2%)
  other arithmetic  24.5 us (2%)
  between operations  16.8 us (1%)
    reduce_scatter x1, waiting for transfers between devices, on_device(): lax.psum_scatter(grads[8], 'grp', scatter_dimension=0, tiled=True)  284 us
    reduce_scatter x1, waiting for transfers between devices, on_device(): lax.psum_scatter(grads[10], 'grp', scatter_dimension=0, tiled=True)  283 us
    reduce_scatter x1, waiting for transfers between devices, on_device(): lax.psum_scatter(grads[2], 'grp', scatter_dimension=0, tiled=True)  209 us
    all_gather x1, waiting for transfers between devices, on_device(): lax.all_gather(fc1_weight, 'grp', axis=0, tiled=True)  144 us
    all_gather x1, waiting for transfers between devices, on_device(): lax.all_gather(fc2_weight, 'grp', axis=0, tiled=True)  137 us
    psum x1, waiting for transfers between devices, on_device(): lax.psum((shares[0], shares[1], shares[2], shares[3], shares[4], shares[5...  92.8 us
  transfers between devices with their start and end apart: 9, of which 8 were waited for; matrix products, arithmetic and copies ran while one was open for 10% of the time, Pallas kernels for 0%

commit v1 on v0

--- a/solution.py
+++ b/solution.py
@@ -264,88 +264,61 @@
     fc2_weight,
     fc2_bias,
 ):
-    gathered = (
-        lax.all_gather(ln1_gain, "grp", axis=0, tiled=True),
-        lax.all_gather(ln1_shift, "grp", axis=0, tiled=True),
-        lax.all_gather(qkv_weight, "grp", axis=0, tiled=True),
-        lax.all_gather(qv_bias, "grp", axis=0, tiled=True),
-        lax.all_gather(out_weight, "grp", axis=0, tiled=True),
-        lax.all_gather(out_bias, "grp", axis=0, tiled=True),
-        lax.all_gather(ln2_gain, "grp", axis=0, tiled=True),
-        lax.all_gather(ln2_shift, "grp", axis=0, tiled=True),
-        lax.all_gather(fc1_weight, "grp", axis=0, tiled=True),
-        lax.all_gather(fc1_bias, "grp", axis=0, tiled=True),
-        lax.all_gather(fc2_weight, "grp", axis=0, tiled=True),
-        lax.all_gather(fc2_bias, "grp", axis=0, tiled=True),
-    )
-    position = 0
-    block_out, stored = forward_image(images[position], gathered)
-    block_outs = [block_out]
-    stored_list = [stored]
-    regathered = (
-        lax.all_gather(ln1_gain, "grp", axis=0, tiled=True),
-        lax.all_gather(ln1_shift, "grp", axis=0, tiled=True),
-        lax.all_gather(qkv_weight, "grp", axis=0, tiled=True),
-        lax.all_gather(qv_bias, "grp", axis=0, tiled=True),
-        lax.all_gather(out_weight, "grp", axis=0, tiled=True),
-        lax.all_gather(out_bias, "grp", axis=0, tiled=True),
-        lax.all_gather(ln2_gain, "grp", axis=0, tiled=True),
-        lax.all_gather(ln2_shift, "grp", axis=0, tiled=True),
-        lax.all_gather(fc1_weight, "grp", axis=0, tiled=True),
-        lax.all_gather(fc1_bias, "grp", axis=0, tiled=True),
-        lax.all_gather(fc2_weight, "grp", axis=0, tiled=True),
-        lax.all_gather(fc2_bias, "grp", axis=0, tiled=True),
-    )
-    position = 0
-    input_grad, grads = backward_image(cotangent[position], stored_list[position], regathered)
-    input_grads = [input_grad]
-    shares = (
-        lax.psum_scatter(grads[0], "grp", scatter_dimension=0, tiled=True),
-        lax.psum_scatter(grads[1], "grp", scatter_dimension=0, tiled=True),
-        lax.psum_scatter(grads[2], "grp", scatter_dimension=0, tiled=True),
-        lax.psum_scatter(grads[3], "grp", scatter_dimension=0, tiled=True),
-        lax.psum_scatter(grads[4], "grp", scatter_dimension=0, tiled=True),
-        lax.psum_scatter(grads[5], "grp", scatter_dimension=0, tiled=True),
-        lax.psum_scatter(grads[6], "grp", scatter_dimension=0, tiled=True),
-        lax.psum_scatter(grads[7], "grp", scatter_dimension=0, tiled=True),
-        lax.psum_scatter(grads[8], "grp", scatter_dimension=0, tiled=True),
-        lax.psum_scatter(grads[9], "grp", scatter_dimension=0, tiled=True),
-        lax.psum_scatter(grads[10], "grp", scatter_dimension=0, tiled=True),
-        lax.psum_scatter(grads[11], "grp", scatter_dimension=0, tiled=True),
-    )
-    owned_parts = lax.psum(
-        (
-            shares[0],
-            shares[1],
-            shares[2],
-            shares[3],
-            shares[4],
-            shares[5],
-            shares[6],
-            shares[7],
-            shares[8],
-            shares[9],
-            shares[10],
-            shares[11],
-        ),
-        "rep",
-    )
-    return (
-        jnp.stack(block_outs),
-        jnp.stack(input_grads),
-        owned_parts[0],
-        owned_parts[1],
-        owned_parts[2],
-        owned_parts[3],
-        owned_parts[4],
-        owned_parts[5],
-        owned_parts[6],
-        owned_parts[7],
-        owned_parts[8],
-        owned_parts[9],
-        owned_parts[10],
-        owned_parts[11],
-    )
+    n_rep = lax.axis_size("rep")
+    n_grp = lax.axis_size("grp")
+    rep = lax.axis_index("rep")
+
+    def gather_matrix(shard):
+        rows, cols = shard.shape
+        block = lax.dynamic_slice_in_dim(shard, rep * (cols // n_rep), cols // n_rep, 1)
+        full = lax.all_gather(block, ("rep", "grp"), axis=0, tiled=False)
+        full = full.reshape(n_rep, n_grp * rows, cols // n_rep)
+        return full.transpose(1, 0, 2).reshape(n_grp * rows, cols)
+
+    vectors = (ln1_gain, ln1_shift, qv_bias, out_bias, ln2_gain, ln2_shift, fc1_bias, fc2_bias)
+    sizes = [vec.shape[0] for vec in vectors]
+    packed = lax.all_gather(jnp.concatenate(vectors), "grp", axis=0, tiled=False)
+    full_vectors = []
+    offset = 0
+    for size in sizes:
+        full_vectors.append(packed[:, offset : offset + size].reshape(-1))
+        offset += size
+    params = (
+        full_vectors[0],
+        full_vectors[1],
+        gather_matrix(qkv_weight),
+        full_vectors[2],
+        gather_matrix(out_weight),
+        full_vectors[3],
+        full_vectors[4],
+        full_vectors[5],
+        gather_matrix(fc1_weight),
+        full_vectors[6],
+        gather_matrix(fc2_weight),
+        full_vectors[7],
+    )
+    block_out, stored = forward_image(images[0], params)
+    input_grad, grads = backward_image(cotangent[0], stored, params)
+
+    def reduce_matrix(grad):
+        rows, cols = grad.shape
+        part = grad.astype(jnp.bfloat16).reshape(rows, n_rep, cols // n_rep).transpose(1, 0, 2)
+        part = lax.psum_scatter(part, "rep", scatter_dimension=0, tiled=False)
+        part = lax.psum_scatter(part, "grp", scatter_dimension=0, tiled=True)
+        full = lax.all_gather(part, "rep", axis=0, tiled=False)
+        return full.transpose(1, 0, 2).reshape(rows // n_grp, cols).astype(jnp.float32)
+
+    order = (0, 1, 3, 5, 6, 7, 9, 11)
+    small = jnp.concatenate([grads[at].reshape(n_grp, -1) for at in order], axis=1)
+    small = lax.psum(lax.psum_scatter(small, "grp", scatter_dimension=0, tiled=False), "rep")
+    totals = [None] * 12
+    offset = 0
+    for at, size in zip(order, sizes):
+        totals[at] = small[offset : offset + size]
+        offset += size
+    for at in (10, 8, 4, 2):
+        totals[at] = reduce_matrix(grads[at])
+    return (block_out[None], input_grad[None], *totals)
 
 
 def solution(mesh):

time: 1570 us -> 881 us (0.56)
  waiting for transfers between devices: 1180 us -> 513 us
  blocking collectives: 144 us -> 67.3 us
  local copies, waits for them, and re-layouts: 35.9 us -> 102 us
    reduce_scatter x4 -> x8, waiting for transfers between devices: 776 us -> 272 us  [the longest x4 217 us: reduce_matrix(): part = lax.psum_scatter(part, 'rep', scatter_dimension=0, tiled=False)]
    psum x1 -> x0, waiting for transfers between devices: 92.8 us -> none  [on_device(): lax.psum((shares[0], shares[1], shares[2], shares[3], shares[4], shares[5...]
    all_gather x8 -> x2, blocking collectives: 104 us -> 27.1 us  [the longest x1 15 us: on_device(): lax.all_gather(jnp.concatenate(vectors), 'grp', axis=0, tiled=False)]
    all_gather x4 -> x7, waiting for transfers between devices: 312 us -> 241 us  [the longest x4 200 us: gather_matrix(): full = lax.all_gather(block, ('rep', 'grp'), axis=0, tiled=False)]
    transpose x0 -> x4, local copies, waits for them, and re-layouts: none -> 35.7 us  [gather_matrix(): return full.transpose(1, 0, 2).reshape(n_grp * rows, cols)]
  transfers between devices with their start and end apart: 9 -> 15, of which waited for: 8 -> 12; matrix products, arithmetic and copies ran while one was open for 10% -> 17% of each run, Pallas kernels for 0% -> 0%
where the time goes in v1:
time: 881 us; the launch traced here: 877 us
  waiting for transfers between devices  513 us (58%)
  matrix products  148 us (17%)
  local copies, waits for them, and re-layouts  102 us (12%)
  blocking collectives  67.3 us (8%)
  other arithmetic  29.7 us (3%)
  between operations  14.9 us (2%)
    reduce_scatter x4, waiting for transfers between devices, reduce_matrix(): part = lax.psum_scatter(part, 'rep', scatter_dimension=0, tiled=False)  217 us
    all_gather x4, waiting for transfers between devices, gather_matrix(): full = lax.all_gather(block, ('rep', 'grp'), axis=0, tiled=False)  200 us
    reduce_scatter x4, waiting for transfers between devices, reduce_matrix(): part = lax.psum_scatter(part, 'grp', scatter_dimension=0, tiled=True)  54.3 us
    all_gather x3, waiting for transfers between devices, reduce_matrix(): full = lax.all_gather(part, 'rep', axis=0, tiled=False)  41.1 us
    transpose x4, local copies, waits for them, and re-layouts, gather_matrix(): return full.transpose(1, 0, 2).reshape(n_grp * rows, cols)  35.7 us
    psum x1, blocking collectives, on_device(): lax.psum(lax.psum_scatter(small, 'grp', scatter_dimension=0, tiled=False)...  22.3 us
    unnamed x102, local copies, waits for them, and re-layouts  21.6 us
    unnamed x1, blocking collectives  17.8 us
  transfers between devices with their start and end apart: 15, of which 12 were waited for; matrix products, arithmetic and copies ran while one was open for 17% of the time, Pallas kernels for 0%

profile of v1, /device:TPU:0, one launch (start us, length us, event | category | flops | bytes accessed | tf_op | source)
XLA Modules:
  0.0 876.6 jit_solution(3447776506527959885)
XLA Ops:
  11.5 1.7 constant_dynamic-slice_fusion
  15.1 15.0 %all-gather = bf16[12288]{0:T(1024)(128)(2,1)S(1)} all-gather(bf16[3072]{0:T(1024)(128)(2,1)S(1)} %dynamic-update-slice.15), channel_id=2, replica_groups=mesh['rep'=8,'grp'=4] {'grp'}, dimensions={0}, use_global_device_ids=true | all-gather | bytes 30720 | tf_op jit(solution)/shard_map/all_gather | solution.py:280
  33.0 37.7 %all-gather.19.cloned.1.call-done = bf16[8192,128]{1,0:T(8,128)(2,1)} async-done(((bf16[256,128]{1,0:T(8,128)(2,1)}), bf16[8192,128]{1,0:T(8,128)(2,1)}) %all-gather.19.cloned.1.call-update) | async-done | bytes 2097168 | tf_op jit(solution)/shard_map/all_gather | solution.py:274
  70.7 3.9 copy.80
  74.6 67.7 %all-gather.17.cloned.1.call-done = bf16[8192,384]{1,0:T(8,128)(2,1)} async-done(((bf16[256,384]{1,0:T(8,128)(2,1)}), bf16[8192,384]{1,0:T(8,128)(2,1)}) %all-gather.17.cloned.1.call-update) | async-done | bytes 6291472 | tf_op jit(solution)/shard_map/all_gather | solution.py:274
  142.3 8.7 copy.76
  151.0 6.7 fusion.83
  158.9 1.7 fusion.74
  161.4 1.7 copy.78
  163.1 2.4 copy.79
  165.5 22.5 %while.28 = (s32[]{:T(128)}, bf16[4,4,577,64]{2,3,1,0:T(8,128)(2,1)}, f32[4,4,577,1]{2,1,3,0:T(4,128)S(1)}, bf16[4,4,577,64]{2,3,1,0:T(8,128)(2,1)S(1)}, bf16[4,...) while((s32[]{:T(128)}, bf16[4,4,577,64]{2,3,1,0:T(8,128)(2,1)}, ...), condition=%wide.region_5.6_spmd.clone, body=%wide.region_2.5_spmd.sunk.clone | while | flops 347575552 | bytes 27806936 | solution.py:119
  168.0 2.0 fusion.156
  173.6 2.0 fusion.156
  179.3 2.0 fusion.156
  184.9 2.0 fusion.156
  188.0 4.0 fusion.106
  193.8 27.6 %all-gather.21.cloned.1.call-done = bf16[8192,512]{1,0:T(8,128)(2,1)} async-done(((bf16[256,512]{1,0:T(8,128)(2,1)}), bf16[8192,512]{1,0:T(8,128)(2,1)}) %all-gather.21.cloned.1.call-update) | async-done | bytes 8388624 | tf_op jit(solution)/shard_map/all_gather | solution.py:274
  221.4 11.6 %copy.81 = bf16[1024,8,512]{0,2,1:T(8,128)(2,1)} copy(bf16[1024,8,512]{2,0,1:T(8,128)(2,1)} %bitcast.339) | data formatting | bytes 16777216 | tf_op jit(solution)/shard_map/transpose | solution.py:276
  233.0 67.0 %all-gather.23.cloned.1.call-done = bf16[32768,128]{1,0:T(8,128)(2,1)} async-done(((bf16[1024,128]{1,0:T(8,128)(2,1)}), bf16[32768,128]{1,0:T(8,128)(2,1)}) %all-gather.23.cloned.1.call-update) | async-done | bytes 8388624 | tf_op jit(solution)/shard_map/all_gather | solution.py:274
  299.9 11.5 %copy.82 = bf16[4096,8,128]{0,2,1:T(8,128)(2,1)} copy(bf16[4096,8,128]{2,0,1:T(8,128)(2,1)} %bitcast.340) | data formatting | bytes 16777216 | tf_op jit(solution)/shard_map/transpose | solution.py:276
  311.4 12.9 %multiply_convert_fusion.1 = (bf16[577,4096]{1,0:T(8,128)(2,1)}, f32[577,4096]{1,0:T(8,128)}) fusion(f32[4096]{0:T(1024)S(1)} %bitcast.387, bf16[1024,4096]{0,1:T(8,128)(2,1)} %bitcast.342, f32[577,1024]{1,0:T(8,128)} %copy-done.6, f32[1024]{0:T(1024)S(1)} %bitcast.391, f32[1024]{0:T(1024)S(1)} %bitcast.381, f32[577]{0:T(1024)S(1)} %add_rsqrt_fusion, ...), kind=kOutput, calls=%fused_computation.58 | convolution fusion | flops 4857361408 | bytes 24961544 | tf_op jit(solution)/shard_map/dot_general | solution.py:132
  324.4 12.2 %fusion.107 = (f32[4096]{0:T(1024)S(1)}, bf16[577,4096]{1,0:T(8,128)(2,1)}) fusion(f32[577,4096]{1,0:T(8,128)} %get-tuple-element.169, f32[4096]{0:T(1024)S(1)} %bitcast.388, bf16[4096,1024]{0,1:T(8,128)(2,1)S(1)} %bitcast.338, bf16[1,577,1024]{2,1,0:T(8,128)(2,1)} %param.19), kind=kOutput, calls=%fused_computation.175 | convolution fusion | flops 4868583424 | bytes 23783424 | tf_op jit(solution)/shard_map/dot_general | solution.py:195
  336.6 8.2 multiply_reduce_fusion.1
  347.5 2.4 convolution_convert_fusion.4
  350.0 2.4 copy.83
  352.4 37.5 %while.29 = (s32[]{:T(128)}, f32[4,4,577,64]{2,3,1,0:T(8,128)}, bf16[4,4,577,64]{2,3,1,0:T(8,128)(2,1)}, f32[4,4,577,64]{2,3,1,0:T(8,128)}, bf16[4,4,577,64]{2,3...) while((s32[]{:T(128)}, f32[4,4,577,64]{2,3,1,0:T(8,128)}, ...), condition=%wide.region_12.13_spmd.clone, body=%wide.region_10.12_spmd.sunk.clone | while | flops 864429056 | bytes 60423508 | solution.py:212
  354.1 2.3 multiply_reduce_fusion.8
  360.2 1.9 fusion.168
  363.4 2.3 multiply_reduce_fusion.8
  369.4 1.9 fusion.168
  372.6 2.3 multiply_reduce_fusion.8
  378.7 1.9 fusion.168
  381.9 2.3 multiply_reduce_fusion.8
  388.0 1.9 fusion.168
  389.9 2.0 bitcast_convert_fusion
  394.7 8.9 %convolution_convert_fusion.2 = bf16[1024,3072]{1,0:T(8,128)(2,1)S(1)} fusion(bf16[577,1024]{0,1:T(8,128)(2,1)S(1)} %bitcast.367, bf16[577,1024]{0,1:T(8,128)(2,1)S(1)} %bitcast.351, bf16[577,1024]{0,1:T(8,128)(2,1)S(1)} %bitcast.369, bf16[1,577,1024]{2,1,0:T(8,128)(2,1)S(1)} %copy-done.4, f32[1024]{0:T(1024)S(1)} %bitcast.390, f32[1024]{0:T(1024)S(1)} %bitcast.378, ...), kind=kOutput, calls=%fused_computation.64 | convolution fusion | flops 3647496192 | bytes 11031048 | tf_op jit(solution)/shard_map/dot_general | solution.py:228
  403.6 3.4 copy.117
  407.1 12.3 %convolution_convert_fusion = bf16[1024,4096]{1,0:T(8,128)(2,1)} fusion(bf16[577,4096]{1,0:T(8,128)(2,1)} %get-tuple-element.173, f32[577,1024]{1,0:T(8,128)} %copy-done.6, f32[1024]{0:T(1024)S(1)} %bitcast.392, f32[1024]{0:T(1024)S(1)} %bitcast.384, f32[577]{0:T(1024)S(1)} %add_rsqrt_fusion, f32[577]{0:T(1024)S(1)} %broadcast_multiply_fusion.4), kind=kOutput, calls=%fused_computation.61 | convolution fusion | flops 4847375360 | bytes 15491592 | tf_op jit(solution)/shard_map/dot_general | solution.py:199
  419.4 7.7 copy.116
  427.2 11.6 %convolution_convert_fusion.1 = bf16[4096,1024]{0,1:T(8,128)(2,1)} fusion(bf16[577,4096]{1,0:T(8,128)(2,1)} %get-tuple-element.168, bf16[1,577,1024]{2,1,0:T(8,128)(2,1)} %param.19), kind=kOutput, calls=%fused_computation.62 | convolution fusion | flops 4844421120 | bytes 14297088 | tf_op jit(solution)/shard_map/dot_general | solution.py:193
  438.8 5.2 convolution_convert_fusion.3
  444.1 23.4 %reduce-scatter.9.cloned.1.call-done = bf16[1,1024,384]{2,1,0:T(8,128)(2,1)} async-done(((bf16[8,1024,384]{2,1,0:T(8,128)(2,1)}), bf16[1,1024,384]{2,1,0:T(8,128)(2,1)}) %reduce-scatter.9.cloned.1.call-update) | async-done | bytes 786448 | tf_op jit(solution)/shard_map/reduce_scatter | solution.py:306
  467.6 74.8 %reduce-scatter.17.cloned.1.call-done = bf16[1,1024,512]{2,1,0:T(8,128)(2,1)} async-done(((bf16[8,1024,512]{2,1,0:T(8,128)(2,1)}), bf16[1,1024,512]{2,1,0:T(8,128)(2,1)}) %reduce-scatter.17.cloned.1.call-update) | async-done | bytes 1048592 | tf_op jit(solution)/shard_map/reduce_scatter | solution.py:306
  542.5 74.9 %reduce-scatter.21.cloned.1.call-done = bf16[1,4096,128]{1,2,0:T(8,128)(2,1)} async-done(((bf16[8,4096,128]{1,2,0:T(8,128)(2,1)}), bf16[1,4096,128]{1,2,0:T(8,128)(2,1)}) %reduce-scatter.21.cloned.1.call-update) | async-done | bytes 1048592 | tf_op jit(solution)/shard_map/reduce_scatter | solution.py:306
  617.5 44.4 %reduce-scatter.13.cloned.1.call-done = bf16[1,1024,128]{1,2,0:T(8,128)(2,1)} async-done(((bf16[8,1024,128]{1,2,0:T(8,128)(2,1)}), bf16[1,1024,128]{1,2,0:T(8,128)(2,1)}) %reduce-scatter.13.cloned.1.call-update) | async-done | bytes 262160 | tf_op jit(solution)/shard_map/reduce_scatter | solution.py:306
  661.9 25.4 %reduce-scatter.11.cloned.1.call-done = bf16[256,384]{1,0:T(8,128)(2,1)} async-done(((bf16[1024,384]{1,0:T(8,128)(2,1)}), bf16[256,384]{1,0:T(8,128)(2,1)}) %reduce-scatter.11.cloned.1.call-update) | async-done | bytes 196624 | tf_op jit(solution)/shard_map/reduce_scatter | solution.py:307
  687.4 28.9 %reduce-scatter.19.cloned.1.call-done = bf16[256,512]{1,0:T(8,128)(2,1)} async-done(((bf16[1024,512]{1,0:T(8,128)(2,1)}), bf16[256,512]{1,0:T(8,128)(2,1)}) %reduce-scatter.19.cloned.1.call-update) | async-done | bytes 262160 | tf_op jit(solution)/shard_map/reduce_scatter | solution.py:307
  717.2 9.5 %fusion.65 = (f32[1024]{0:T(1024)S(1)}, f32[577]{0:T(1024)S(1)}, f32[577]{0:T(1024)S(1)}, f32[1024]{0:T(1024)S(1)}, f32[577,1024]{1,0:T(8,128)}) fusion(bf16[1,577,1024]{2,1,0:T(8,128)(2,1)S(1)} %copy-done.4, f32[577]{0:T(1024)S(1)} %copy-done.26, f32[577]{0:T(1024)S(1)} %copy-done.22, f32[1024]{0:T(1024)S(1)} %bitcast.379, ...), kind=kOutput, calls=%fused_computation.87 | convolution fusion | flops 3646710784 | bytes 13403152 | tf_op jit(solution)/shard_map/dot_general | solution.py:229
  726.7 2.0 reduce_sum.182
  728.8 2.0 reduce_sum.181
  731.0 17.8 %all-reduce = f32[4,3072]{1,0:T(4,128)S(1)} all-reduce(f32[4,3072]{1,0:T(4,128)S(1)} %constant_dynamic-update-slice_fusion), channel_id=11, replica_groups=mesh['rep'=8,'grp'=4] {'grp'}, use_global_device_ids=true, to_apply=%region_24.25.clone | all-reduce | flops 12288 | bytes 98304
  749.5 22.3 %psum.7 = f32[3072]{0:T(1024)S(1)} all-reduce(f32[3072]{0:T(1024)S(1)} %bitcast.376), channel_id=1, replica_groups=mesh['rep'=8,'grp'=4] {'rep'}, use_global_device_ids=true, to_apply=%region_25.26 | all-reduce | flops 3072 | bytes 24576 | tf_op jit(solution)/shard_map/psum | solution.py:313
  773.6 4.4 fusion.86
  778.1 9.8 %fusion.81 = bf16[1,577,1024]{2,1,0:T(8,128)(2,1)} fusion(f32[577,1024]{1,0:T(8,128)S(1)} %copy-done.8, bf16[577,4096]{1,0:T(8,128)(2,1)} %get-tuple-element.168, bf16[4096,1024]{0,1:T(8,128)(2,1)} %bitcast.337, f32[1024]{0:T(1024)S(1)} %bitcast.393), kind=kOutput, calls=%fused_computation.116 | convolution fusion | flops 4841999360 | bytes 16664576 | tf_op jit(solution)/shard_map/dot_general | solution.py:139
  787.9 12.1 %all-gather.6 = bf16[2048,128]{0,1:T(8,128)(2,1)S(1)} all-gather(bf16[256,128]{0,1:T(8,128)(2,1)} %reduce-scatter.15.cloned.1.call-done), channel_id=8, replica_groups=mesh['rep'=8,'grp'=4] {'rep'}, dimensions={0}, use_global_device_ids=true | all-gather | bytes 589824 | tf_op jit(solution)/shard_map/all_gather | solution.py:308
  803.8 2.1 copy.96
  805.8 16.4 %all-gather.27.cloned.1.call-done = bf16[2048,512]{1,0:T(8,128)(2,1)} async-done(((bf16[256,512]{1,0:T(8,128)(2,1)}), bf16[2048,512]{1,0:T(8,128)(2,1)}) %all-gather.27.cloned.1.call-update) | async-done | bytes 2097168 | tf_op jit(solution)/shard_map/all_gather | solution.py:308
  822.2 2.2 convert_bitcast_fusion
  824.4 2.7 copy.97
  827.1 24.7 %all-gather.29.cloned.1.call-done = bf16[8192,128]{0,1:T(8,128)(2,1)} async-done(((bf16[1024,128]{0,1:T(8,128)(2,1)}), bf16[8192,128]{0,1:T(8,128)(2,1)}) %all-gather.29.cloned.1.call-update) | async-done | bytes 2097168 | tf_op jit(solution)/shard_map/all_gather | solution.py:308
  851.8 2.0 convert_element_type.263
  853.8 5.3 copy.109
  859.1 5.4 copy.89
  864.5 5.4 copy.118
  (250 shorter events, 60.3 us)
Async XLA Ops:
  7.2 3.5 copy-start
  7.2 6.1 copy-start.32
  7.2 6.4 copy-start.33
  7.2 6.6 copy-start.31
  7.2 6.8 copy-start.34
  7.2 7.0 copy-start.35
  7.3 7.2 copy-start.36
  7.3 7.4 copy-start.30
  7.3 7.6 copy-start.37
  7.3 63.4 %all-gather.19.cloned.1.call-start = ((), (), s32[]{:S(2)}) async-start(), calls=%async_computation.17 | async-start | bytes 2162688 | tf_op jit(solution)/shard_map/all_gather | solution.py:274
  9.0 133.3 %all-gather.17.cloned.1.call-start = ((), (), s32[]{:S(2)}) async-start(), calls=%async_computation.16 | async-start | bytes 6488064 | tf_op jit(solution)/shard_map/all_gather | solution.py:274
  10.7 210.8 %all-gather.21.cloned.1.call-start = ((), (), s32[]{:S(2)}) async-start(), calls=%async_computation.18 | async-start | bytes 8650752 | tf_op jit(solution)/shard_map/all_gather | solution.py:274
  11.5 288.5 %all-gather.23.cloned.1.call-start = ((), (), s32[]{:S(2)}) async-start(), calls=%async_computation.19 | async-start | bytes 8650752 | tf_op jit(solution)/shard_map/all_gather | solution.py:274
  13.2 19.0 %copy-start.3 = (bf16[1,577,1024]{2,1,0:T(8,128)(2,1)S(1)}, bf16[1,577,1024]{2,1,0:T(8,128)(2,1)}, u32[]{:S(2)}) copy-start(bf16[1,577,1024]{2,1,0:T(8,128)(2,1)} %param.18) | copy-start | bytes 3545092
  13.2 454.3 %reduce-scatter.9.cloned.1.call-start = ((), (), s32[]{:S(2)}) async-start(), calls=%async_computation.8 | async-start | bytes 7077888 | tf_op jit(solution)/shard_map/reduce_scatter | solution.py:306
  30.9 2.0 copy-start.11
  32.1 118.9 %copy-start.28 = (f32[1,2,4,128]{3,1,2,0:T(2,128)}, f32[1,2,4,128]{3,1,2,0:T(2,128)S(1)}, u32[]{:S(2)}) copy-start(f32[1,2,4,128]{3,1,2,0:T(2,128)S(1)} %copy.99) | copy-start | bytes 12292
  32.1 118.9 %copy-start.23 = (f32[1,2,4,128]{3,1,2,0:T(2,128)}, f32[1,2,4,128]{3,1,2,0:T(2,128)S(1)}, u32[]{:S(2)}) copy-start(f32[1,2,4,128]{3,1,2,0:T(2,128)S(1)} %copy.98) | copy-start | bytes 12292
  32.5 118.5 %copy-start.21 = (f32[577]{0:T(1024)}, f32[577]{0:T(1024)S(1)}, u32[]{:S(2)}) copy-start(f32[577]{0:T(1024)S(1)} %broadcast_multiply_fusion.5) | copy-start | bytes 6928
  32.9 118.1 %copy-start.25 = (f32[577]{0:T(1024)}, f32[577]{0:T(1024)S(1)}, u32[]{:S(2)}) copy-start(f32[577]{0:T(1024)S(1)} %add_rsqrt_fusion.1) | copy-start | bytes 6928
  166.7 1.3 copy-start.16
  172.3 1.3 copy-start.16
  177.9 1.3 copy-start.16
  183.6 1.3 copy-start.16
  192.0 1.4 copy-start.6
  311.4 12.9 %copy-start.10 = (bf16[4096,8,128]{0,2,1:T(8,128)(2,1)S(1)}, bf16[4096,8,128]{0,2,1:T(8,128)(2,1)}, u32[]{:S(2)}) copy-start(bf16[4096,8,128]{0,2,1:T(8,128)(2,1)} %copy.82) | copy-start | bytes 25165828
  311.4 25.1 %slice-start = ((s8[8388608]{0:T(1024)(128)(4,1)}), s8[4194304]{0:T(1024)(128)(4,1)S(1)}, s32[]{:S(2)}) async-start(s8[8388608]{0:T(1024)(128)(4,1)} %bitcast.343), calls=%async_computation.23 | async-start | bytes 8388608
  324.3 12.2 %copy-start.7 = (f32[577,1024]{1,0:T(8,128)S(1)}, f32[577,1024]{1,0:T(8,128)}, u32[]{:S(2)}) copy-start(f32[577,1024]{1,0:T(8,128)} %copy-done.6) | copy-start | bytes 7090180
  324.3 12.2 %slice-start.1 = ((s8[8388608]{0:T(1024)(128)(4,1)}), s8[4194304]{0:T(1024)(128)(4,1)S(1)}, s32[]{:S(2)}) async-start(s8[8388608]{0:T(1024)(128)(4,1)} %bitcast.343), calls=%async_computation.24 | async-start | bytes 8388608
  336.6 8.2 copy-start.20
  344.8 2.7 copy-start.15
  346.1 1.5 copy-start.9
  352.8 1.3 copy-start.2
  357.6 1.5 copy-start.12
  360.2 1.9 copy-start.13
  366.9 1.5 copy-start.12
  369.4 1.9 copy-start.13
  376.2 1.5 copy-start.12
  378.7 1.9 copy-start.13
  385.4 1.5 copy-start.12
  388.0 1.9 copy-start.13
  389.9 2.5 copy-start.5
  391.9 11.7 %copy-start.18 = (bf16[577,16,64]{0,2,1:T(8,128)(2,1)}, bf16[577,16,64]{0,2,1:T(8,128)(2,1)S(1)}, u32[]{:S(2)}) copy-start(bf16[577,16,64]{0,2,1:T(8,128)(2,1)S(1)} %bitcast_convert_fusion) | copy-start | bytes 3545092
  391.9 2.3 copy-start.4
  392.0 2.7 copy-start.14
  392.0 2.7 copy-start.22
  392.0 2.7 copy-start.24
  392.0 2.7 copy-start.26
  392.0 2.7 copy-start.29
  392.6 11.1 %copy-start.19 = (bf16[577,16,64]{0,2,1:T(8,128)(2,1)}, bf16[577,16,64]{0,2,1:T(8,128)(2,1)S(1)}, u32[]{:S(2)}) copy-start(bf16[577,16,64]{0,2,1:T(8,128)(2,1)S(1)} %bitcast_convert_fusion.1) | copy-start | bytes 3545092
  407.0 135.4 %reduce-scatter.17.cloned.1.call-start = ((), (), s32[]{:S(2)}) async-start(), calls=%async_computation.12 | async-start | bytes 9437184 | tf_op jit(solution)/shard_map/reduce_scatter | solution.py:306
  427.1 190.3 %reduce-scatter.21.cloned.1.call-start = ((), (), s32[]{:S(2)}) async-start(), calls=%async_computation.14 | async-start | bytes 9437184 | tf_op jit(solution)/shard_map/reduce_scatter | solution.py:306
  438.8 223.0 %reduce-scatter.13.cloned.1.call-start = ((), (), s32[]{:S(2)}) async-start(), calls=%async_computation.10 | async-start | bytes 2359296 | tf_op jit(solution)/shard_map/reduce_scatter | solution.py:306
  444.1 272.5 %copy-start.27 = (f32[1,2,4,128]{3,2,1,0:T(4,128)S(1)}, f32[1,2,4,128]{3,2,1,0:T(4,128)}, u32[]{:S(2)}) copy-start(f32[1,2,4,128]{3,2,1,0:T(4,128)} %get-tuple-element.152) | copy-start | bytes 12292
  444.1 272.5 %copy-start.38 = (u32[32]{0:T(128)S(1)}, u32[32]{0:T(128)}, u32[]{:S(2)}) copy-start(u32[32]{0:T(128)} %constant.87) | copy-start | bytes 388
  444.1 243.2 %reduce-scatter.11.cloned.1.call-start = ((), (), s32[]{:S(2)}) async-start(), calls=%async_computation.9 | async-start | bytes 983040 | tf_op jit(solution)/shard_map/reduce_scatter | solution.py:307
  467.6 248.7 %reduce-scatter.19.cloned.1.call-start = ((), (), s32[]{:S(2)}) async-start(), calls=%async_computation.13 | async-start | bytes 1310720 | tf_op jit(solution)/shard_map/reduce_scatter | solution.py:307
  542.4 206.4 %reduce-scatter.23.cloned.1.call-start = ((), (), s32[]{:S(2)}) async-start(), calls=%async_computation.15 | async-start | bytes 1310720 | tf_op jit(solution)/shard_map/reduce_scatter | solution.py:307
  617.4 170.5 %reduce-scatter.15.cloned.1.call-start = ((), (), s32[]{:S(2)}) async-start(), calls=%async_computation.11 | async-start | bytes 327680 | tf_op jit(solution)/shard_map/reduce_scatter | solution.py:307
  661.8 140.3 %all-gather.25.cloned.1.call-start = ((), (), s32[]{:S(2)}) async-start(), calls=%async_computation.20 | async-start | bytes 1769472 | tf_op jit(solution)/shard_map/all_gather | solution.py:308
  687.3 134.9 %all-gather.27.cloned.1.call-start = ((), (), s32[]{:S(2)}) async-start(), calls=%async_computation.21 | async-start | bytes 2359296 | tf_op jit(solution)/shard_map/all_gather | solution.py:308
  716.3 135.5 %all-gather.29.cloned.1.call-start = ((), (), s32[]{:S(2)}) async-start(), calls=%async_computation.22 | async-start | bytes 2359296 | tf_op jit(solution)/shard_map/all_gather | solution.py:308
  773.6 4.4 copy-start.8
  864.5 5.4 copy-start.1
  (7 other events, 8.4 us)
Sparse Core Ops, SparseCore 0:
  11.6 59.0 all-gather.18
  74.1 68.0 all-gather.16
  145.8 75.5 all-gather.20
  224.2 75.6 all-gather.22
  407.2 60.3 reduce-scatter.8
  470.9 71.4 reduce-scatter.16
  545.9 71.4 reduce-scatter.20
  620.7 41.1 reduce-scatter.12
  664.1 23.1 reduce-scatter.10
  689.5 26.7 reduce-scatter.18
  718.6 26.8 reduce-scatter.22
  747.6 18.5 reduce-scatter.14
  768.1 23.8 all-gather.24
  793.7 28.4 all-gather.26
  824.0 27.7 all-gather.28

commit v2 on v1

v2 whole, which is shorter than its diff:
```python
import jax
import jax.numpy as jnp
from jax import lax
from jax.experimental import pallas as pl
from jax.experimental.pallas import tpu as pltpu
from jax.sharding import PartitionSpec as P


BLOCKS = 8
LANES = 128
TILE = 512
HD = 64
PAIR = 128
EPS = 1e-06

root_half = 0.7071067811865476
inv_root_tau = 0.3989422804014327

NN = (((1,), (0,)), ((), ()))
NT = (((1,), (1,)), ((), ()))
TN = (((0,), (0,)), ((), ()))
ANY = pl.BlockSpec(memory_space=pl.ANY)


def product(left, right, dims=NN):
    return lax.dot_general(left, right, dims, preferred_element_type=jnp.float32)


def aligned(start, unit):
    return pl.multiple_of(start, unit)


def params(**extra):
    return pltpu.CompilerParams(vmem_limit_bytes=60 << 20, **extra)


def cost(flops, moved):
    return pl.CostEstimate(flops=int(flops), bytes_accessed=int(moved), transcendentals=0)


def start_loads(where, own, pieces, strips, target, sems, mode):
    share = own.shape[0]
    groups = target.shape[0] // share
    mine = where[1]

    def go(source, rows, columns, key):
        pltpu.make_async_copy(source, target.at[rows, columns], sems.at[key]).start()

    own_rows = pl.ds(aligned(mine * share, share), share)
    if mode == "row":
        pltpu.make_async_copy(own, target.at[own_rows, :], sems.at[0]).start()
    for which, (source, size, base) in enumerate(strips):
        for at in range(BLOCKS):
            block = jnp.bitwise_xor(where[0], at)
            columns = pl.ds(aligned(base + block * size, LANES), size)
            key = {"part": which, "block": at}.get(mode)
            if mode != "row":
                go(own.at[:, columns], own_rows, columns, key)
            for hop in range(1, groups):
                first = jnp.bitwise_xor(mine, hop) * share
                low = 0
                for ref in pieces[at]:
                    high = low + ref.shape[0]
                    begin, end = max(low, (hop - 1) * share), min(high, hop * share)
                    if begin < end:
                        shift = begin - (hop - 1) * share
                        rows = pl.ds(aligned(first + shift, 16), end - begin)
                        go(
                            ref.at[begin - low : end - low, source : source + size],
                            rows,
                            columns,
                            hop if mode == "row" else key,
                        )
                    low = high


def finish(region, sem):
    pltpu.make_async_copy(region, region, sem).wait()


def wait_rows(where, target, sems, hop, share):
    rows = pl.ds(aligned(jnp.bitwise_xor(where[1], hop) * share, share), share)
    finish(target.at[rows, :], sems.at[hop])


def flat(pieces):
    return [array for piece in pieces for array in piece]


def regroup(refs, pieces):
    grouped, at = [], 0
    for piece in pieces:
        grouped.append(refs[at : at + len(piece)])
        at += len(piece)
    return grouped


def center(values):
    mean = jnp.mean(values, axis=-1, keepdims=True)
    centred = values - mean
    inv_std = lax.rsqrt(jnp.mean(centred * centred, axis=-1, keepdims=True) + EPS)
    return centred * inv_std, inv_std


def center_back(grad_out, normed, inv_std, gain):
    grad_hat = grad_out * gain
    return inv_std * (
        grad_hat
        - jnp.mean(grad_hat, axis=-1, keepdims=True)
        - normed * jnp.mean(grad_hat * normed, axis=-1, keepdims=True)
    )


def column_sum(values):
    return jnp.sum(values, axis=0, keepdims=True)


def qkv_forward(where, image, gain, shift, bias, own, pieces):
    tokens, width = image.shape
    wide = own.shape[1]
    per = width // TILE
    strips = [(part * LANES, LANES, part * width) for part in range(3)]

    def body(where_ref, image_ref, gain_ref, shift_ref, bias_ref, own_ref, *rest):
        piece_refs = regroup(rest[: len(flat(pieces))], pieces)
        normed_ref, out_ref, weight, sems = rest[len(flat(pieces)) :]
        at = pl.program_id(0)

        @pl.when(at == 0)
        def _():
            start_loads(where_ref, own_ref, piece_refs, strips, weight, sems, "part")
            normed, _ = center(image_ref[...].astype(jnp.float32))
            normed_ref[...] = (normed * gain_ref[...] + shift_ref[...]).astype(jnp.bfloat16)

        for part in range(3):

            @pl.when(at == part * per)
            def _(part=part):
                finish(weight.at[:, part * width : (part + 1) * width], sems.at[part])

        columns = pl.ds(aligned(at * TILE, TILE), TILE)
        total = product(normed_ref[...], weight[:, columns]) + bias_ref[...]
        scale = jnp.where(at < per, 0.125, 1.0)
        out_ref[...] = (total * scale).astype(jnp.bfloat16)

    full = lambda at, _: (0, 0)
    return pl.pallas_call(
        body,
        grid_spec=pltpu.PrefetchScalarGridSpec(
            num_scalar_prefetch=1,
            grid=(wide // TILE,),
            in_specs=[
                pl.BlockSpec((tokens, width), full),
                pl.BlockSpec((1, width), full),
                pl.BlockSpec((1, width), full),
                pl.BlockSpec((1, TILE), lambda at, _: (0, at)),
            ]
            + [ANY] * (1 + len(flat(pieces))),
            out_specs=[
                pl.BlockSpec((tokens, width), full),
                pl.BlockSpec((tokens, TILE), lambda at, _: (0, at)),
            ],
            scratch_shapes=[
                pltpu.VMEM((width, wide), jnp.bfloat16),
                pltpu.SemaphoreType.DMA((3,)),
            ],
        ),
        out_shape=[
            jax.ShapeDtypeStruct((tokens, width), jnp.bfloat16),
            jax.ShapeDtypeStruct((tokens, wide), jnp.bfloat16),
        ],
        cost_estimate=cost(2 * tokens * width * wide, 2 * width * wide),
        compiler_params=params(),
        name="qkv_forward",
    )(where, image, gain, shift, bias, own, *flat(pieces))


def out_forward(where, image, attended, bias, gain, shift, own, pieces, source):
    tokens, width = image.shape
    share = own.shape[0]
    groups = width // share
    chunk = 256

    def body(where_ref, image_ref, attended_ref, bias_ref, gain_ref, shift_ref, own_ref, *rest):
        piece_refs = regroup(rest[: len(flat(pieces))], pieces)
        residual_ref, normed_ref, weight, sems = rest[len(flat(pieces)) :]
        start_loads(where_ref, own_ref, piece_refs, [(source, LANES, 0)], weight, sems, "row")
        for hop in range(groups):
            wait_rows(where_ref, weight, sems, hop, share)

        @pl.loop(0, width // chunk)
        def _(at):
            columns = pl.ds(aligned(at * chunk, chunk), chunk)
            residual_ref[:, columns] = (
                image_ref[:, columns].astype(jnp.float32)
                + product(attended_ref[...], weight[:, columns])
                + bias_ref[:, columns]
            )

        normed, _ = center(residual_ref[...])
        normed_ref[...] = (normed * gain_ref[...] + shift_ref[...]).astype(jnp.bfloat16)

    full = lambda at, _: (0, 0)
    return pl.pallas_call(
        body,
        grid_spec=pltpu.PrefetchScalarGridSpec(
            num_scalar_prefetch=1,
            grid=(1,),
            in_specs=[pl.BlockSpec((tokens, width), full)] * 2
            + [pl.BlockSpec((1, width), full)] * 3
            + [ANY] * (1 + len(flat(pieces))),
            out_specs=[pl.BlockSpec((tokens, width), full)] * 2,
            scratch_shapes=[
                pltpu.VMEM((width, width), jnp.bfloat16),
                pltpu.SemaphoreType.DMA((groups,)),
            ],
        ),
        out_shape=[
            jax.ShapeDtypeStruct((tokens, width), jnp.float32),
            jax.ShapeDtypeStruct((tokens, width), jnp.bfloat16),
        ],
        cost_estimate=cost(2 * tokens * width * width, 2 * width * width),
        compiler_params=params(),
        name="out_forward",
    )(where, image, attended, bias, gain, shift, own, *flat(pieces))


def up_forward(where, normed, bias, own, pieces):
    tokens, width = normed.shape
    wide = own.shape[1]
    size = wide // BLOCKS

    def body(where_ref, normed_ref, bias_ref, own_ref, *rest):
        piece_refs = regroup(rest[: len(flat(pieces))], pieces)
        active_ref, slope_ref, weight, sems = rest[len(flat(pieces)) :]
        at = pl.program_id(0)

        @pl.when(at == 0)
        def _():
            start_loads(where_ref, own_ref, piece_refs, [(0, size, 0)], weight, sems, "block")

        columns = pl.ds(aligned(jnp.bitwise_xor(where_ref[0], at) * size, size), size)
        finish(weight.at[:, columns], sems.at[at])
        pre_act = product(normed_ref[...], weight[:, columns]) + bias_ref[...]
        cdf = 0.5 * (1.0 + lax.erf(pre_act * root_half))
        density = jnp.exp(-0.5 * pre_act * pre_act) * inv_root_tau
        active_ref[...] = (pre_act * cdf).astype(jnp.bfloat16)
        slope_ref[...] = (cdf + pre_act * density).astype(jnp.bfloat16)

    full = lambda at, _: (0, 0)
    mine = lambda at, where_ref: (0, jnp.bitwise_xor(where_ref[0], at))
    return pl.pallas_call(
        body,
        grid_spec=pltpu.PrefetchScalarGridSpec(
            num_scalar_prefetch=1,
            grid=(BLOCKS,),
            in_specs=[pl.BlockSpec((tokens, width), full), pl.BlockSpec((1, size), mine)]
            + [ANY] * (1 + len(flat(pieces))),
            out_specs=[pl.BlockSpec((tokens, size), mine)] * 2,
            scratch_shapes=[
                pltpu.VMEM((width, wide), jnp.bfloat16),
                pltpu.SemaphoreType.DMA((BLOCKS,)),
            ],
        ),
        out_shape=[jax.ShapeDtypeStruct((tokens, wide), jnp.bfloat16)] * 2,
        cost_estimate=cost(2 * tokens * width * wide, 2 * width * wide),
        compiler_params=params(),
        name="up_forward",
    )(where, normed, bias, own, *flat(pieces))


def down_forward(where, residual, active, bias, own, pieces):
    tokens, wide = active.shape
    width = residual.shape[1]
    share = own.shape[0]
    groups = wide // share
    chunk = 256

    def body(where_ref, residual_ref, active_ref, bias_ref, own_ref, *rest):
        piece_refs = regroup(rest[: len(flat(pieces))], pieces)
        out_ref, weight, sems = rest[len(flat(pieces)) :]
        at = pl.program_id(0)

        @pl.when(at == 0)
        def _():
            start_loads(where_ref, own_ref, piece_refs, [(0, LANES, 0)], weight, sems, "row")
            for hop in range(groups):
                wait_rows(where_ref, weight, sems, hop, share)

        columns = pl.ds(aligned(at * chunk, chunk), chunk)
        out_ref[...] = (
            residual_ref[...] + product(active_ref[...], weight[:, columns]) + bias_ref[...]
        ).astype(jnp.bfloat16)

    block = lambda at, _: (0, at)
    return pl.pallas_call(
        body,
        grid_spec=pltpu.PrefetchScalarGridSpec(
            num_scalar_prefetch=1,
            grid=(width // chunk,),
            in_specs=[
                pl.BlockSpec((tokens, chunk), block),
                pl.BlockSpec((tokens, wide), lambda at, _: (0, 0)),
                pl.BlockSpec((1, chunk), block),
            ]
            + [ANY] * (1 + len(flat(pieces))),
            out_specs=pl.BlockSpec((tokens, chunk), block),
            scratch_shapes=[
                pltpu.VMEM((wide, width), jnp.bfloat16),
                pltpu.SemaphoreType.DMA((groups,)),
            ],
        ),
        out_shape=jax.ShapeDtypeStruct((tokens, width), jnp.bfloat16),
        cost_estimate=cost(2 * tokens * width * wide, 2 * width * wide),
        compiler_params=params(),
        name="down_forward",
    )(where, residual, active, bias, own, *flat(pieces))


def down_backward(where, grad_block, slope, own, pieces):
    tokens, wide = slope.shape
    width = grad_block.shape[1]
    share = own.shape[0]
    groups = wide // share
    tile = min(TILE, share)
    per = share // tile

    def body(where_ref, grad_ref, slope_ref, own_ref, *rest):
        piece_refs = regroup(rest[: len(flat(pieces))], pieces)
        out_ref, sum_ref, weight, sems = rest[len(flat(pieces)) :]
        at = pl.program_id(0)

        @pl.when(at == 0)
        def _():
            start_loads(where_ref, own_ref, piece_refs, [(0, LANES, 0)], weight, sems, "row")

        hop = at // per

        @pl.when(at % per == 0)
        def _():
            wait_rows(where_ref, weight, sems, hop, share)

        row = jnp.bitwise_xor(where_ref[1], hop) * share + (at % per) * tile
        rows = pl.ds(aligned(row, tile), tile)
        grad_pre = product(grad_ref[...], weight[rows, :], NT) * slope_ref[...].astype(jnp.float32)
        out_ref[...] = grad_pre.astype(jnp.bfloat16)
        sum_ref[...] = column_sum(grad_pre)

    mine = lambda at, where_ref: (0, jnp.bitwise_xor(where_ref[1], at // per) * per + at % per)
    return pl.pallas_call(
        body,
        grid_spec=pltpu.PrefetchScalarGridSpec(
            num_scalar_prefetch=1,
            grid=(wide // tile,),
            in_specs=[
                pl.BlockSpec((tokens, width), lambda at, _: (0, 0)),
                pl.BlockSpec((tokens, tile), mine),
            ]
            + [ANY] * (1 + len(flat(pieces))),
            out_specs=[pl.BlockSpec((tokens, tile), mine), pl.BlockSpec((1, tile), mine)],
            scratch_shapes=[
                pltpu.VMEM((wide, width), jnp.bfloat16),
                pltpu.SemaphoreType.DMA((groups,)),
            ],
        ),
        out_shape=[
            jax.ShapeDtypeStruct((tokens, wide), jnp.bfloat16),
            jax.ShapeDtypeStruct((1, wide), jnp.float32),
        ],
        cost_estimate=cost(2 * tokens * width * wide, 2 * width * wide),
        compiler_params=params(),
        name="down_backward",
    )(where, grad_block, slope, own, *flat(pieces))


def middle_backward(where, grad_pre, grad_block, residual, gain, own_up, own_out, pieces, size):
    tokens, wide = grad_pre.shape
    width = grad_block.shape[1]
    share = own_up.shape[0]
    groups = width // share
    chunk = 256

    def body(where_ref, pre_ref, block_ref, residual_ref, gain_ref, up_ref, own_ref, *rest):
        piece_refs = regroup(rest[: len(flat(pieces))], pieces)
        (full_ref, half_ref, att_ref, gain_sum, shift_sum, res_sum, top_sum) = rest[
            len(flat(pieces)) : len(flat(pieces)) + 7
        ]
        weight, weight_out, middle, sems, out_sems = rest[len(flat(pieces)) + 7 :]
        at = pl.program_id(0)

        @pl.when(at == 0)
        def _():
            start_loads(where_ref, up_ref, piece_refs, [(0, size, 0)], weight, sems, "row")
            start_loads(
                where_ref, own_ref, piece_refs, [(size, LANES, 0)], weight_out, out_sems, "row"
            )

        wait_rows(where_ref, weight, sems, at, share)
        rows = pl.ds(aligned(jnp.bitwise_xor(where_ref[1], at) * share, share), share)
        middle[:, rows] = product(pre_ref[...], weight[rows, :], NT)

        @pl.when(at == groups - 1)
        def _():
            normed, inv_std = center(residual_ref[...])
            grad_mid = middle[...]
            gain_sum[...] = column_sum(grad_mid * normed)
            shift_sum[...] = column_sum(grad_mid)
            top = block_ref[...].astype(jnp.float32)
            top_sum[...] = column_sum(top)
            grad_res = top + center_back(grad_mid, normed, inv_std, gain_ref[...])
            full_ref[...] = grad_res
            res_sum[...] = column_sum(grad_res)
            half_ref[...] = grad_res.astype(jnp.bfloat16)
            for hop in range(groups):
                wait_rows(where_ref, weight_out, out_sems, hop, share)

            @pl.loop(0, width // chunk)
            def _(step):
                part = pl.ds(aligned(step * chunk, chunk), chunk)
                att_ref[:, part] = product(half_ref[...], weight_out[part, :], NT).astype(
                    jnp.bfloat16
                )

    full = lambda at, _: (0, 0)
    line = pl.BlockSpec((1, width), full)
    square = pl.BlockSpec((tokens, width), full)
    return pl.pallas_call(
        body,
        grid_spec=pltpu.PrefetchScalarGridSpec(
            num_scalar_prefetch=1,
            grid=(groups,),
            in_specs=[pl.BlockSpec((tokens, wide), full), square, square, line]
            + [ANY] * (2 + len(flat(pieces))),
            out_specs=[square] * 3 + [line] * 4,
            scratch_shapes=[
                pltpu.VMEM((width, wide), jnp.bfloat16),
                pltpu.VMEM((width, width), jnp.bfloat16),
                pltpu.VMEM((tokens, width), jnp.float32),
                pltpu.SemaphoreType.DMA((groups,)),
                pltpu.SemaphoreType.DMA((groups,)),
            ],
        ),
        out_shape=[
            jax.ShapeDtypeStruct((tokens, width), jnp.float32),
            jax.ShapeDtypeStruct((tokens, width), jnp.bfloat16),
            jax.ShapeDtypeStruct((tokens, width), jnp.bfloat16),
        ]
        + [jax.ShapeDtypeStruct((1, width), jnp.float32)] * 4,
        cost_estimate=cost(2 * tokens * width * (wide + width), 2 * width * (wide + width)),
        compiler_params=params(),
        name="middle_backward",
    )(where, grad_pre, grad_block, residual, gain, own_up, own_out, *flat(pieces))


def qkv_backward(where, grad_proj, image, grad_res, gain, own, pieces):
    tokens, width = image.shape
    wide = own.shape[1]
    share = own.shape[0]
    groups = width // share
    strips = [(part * LANES, LANES, part * width) for part in range(3)]

    def body(where_ref, proj_ref, image_ref, res_ref, gain_ref, own_ref, *rest):
        piece_refs = regroup(rest[: len(flat(pieces))], pieces)
        out_ref, gain_sum, shift_sum, weight, inner, sems = rest[len(flat(pieces)) :]
        at = pl.program_id(0)

        @pl.when(at == 0)
        def _():
            start_loads(where_ref, own_ref, piece_refs, strips, weight, sems, "row")

        wait_rows(where_ref, weight, sems, at, share)
        rows = pl.ds(aligned(jnp.bitwise_xor(where_ref[1], at) * share, share), share)
        inner[:, rows] = (
            product(proj_ref[0], weight[rows, :width], NT)
            + product(proj_ref[1], weight[rows, width : 2 * width], NT)
            + product(proj_ref[2], weight[rows, 2 * width :], NT)
        )

        @pl.when(at == groups - 1)
        def _():
            normed, inv_std = center(image_ref[...].astype(jnp.float32))
            grad_in = inner[...]
            gain_sum[...] = column_sum(grad_in * normed)
            shift_sum[...] = column_sum(grad_in)
            out_ref[...] = (
                res_ref[...] + center_back(grad_in, normed, inv_std, gain_ref[...])
            ).astype(jnp.bfloat16)

    full = lambda at, _: (0, 0)
    line = pl.BlockSpec((1, width), full)
    square = pl.BlockSpec((tokens, width), full)
    return pl.pallas_call(
        body,
        grid_spec=pltpu.PrefetchScalarGridSpec(
            num_scalar_prefetch=1,
            grid=(groups,),
            in_specs=[pl.BlockSpec((3, tokens, width), lambda at, _: (0, 0, 0))]
            + [square, square, line]
            + [ANY] * (1 + len(flat(pieces))),
            out_specs=[square, line, line],
            scratch_shapes=[
                pltpu.VMEM((width, wide), jnp.bfloat16),
                pltpu.VMEM((tokens, width), jnp.float32),
                pltpu.SemaphoreType.DMA((groups,)),
            ],
        ),
        out_shape=[
            jax.ShapeDtypeStruct((tokens, width), jnp.bfloat16),
            jax.ShapeDtypeStruct((1, width), jnp.float32),
            jax.ShapeDtypeStruct((1, width), jnp.float32),
        ],
        cost_estimate=cost(2 * tokens * width * wide, 2 * width * wide),
        compiler_params=params(),
        name="qkv_backward",
    )(where, grad_proj, image, grad_res, gain, own, *flat(pieces))


def attention_forward(projected):
    tokens, triple = projected.shape
    width = triple // 3
    count = width // PAIR

    def body(query_ref, key_ref, value_ref, mixed_ref, total_ref):
        values = value_ref[...].T
        halves = []
        for half in range(PAIR // HD):
            lanes = slice(half * HD, (half + 1) * HD)
            scores = product(key_ref[:, lanes], query_ref[:, lanes], NT)
            top = jnp.max(scores, axis=0, keepdims=True)
            weights = jnp.exp(scores - top)
            total = jnp.sum(weights, axis=0, keepdims=True)
            halves.append(product(values[lanes, :], weights.astype(jnp.bfloat16)) / total)
            total_ref[0, half : half + 1, :] = top + jnp.log(total)
        mixed_ref[...] = jnp.concatenate(halves, axis=0).T.astype(jnp.bfloat16)

    def spec(part):
        return pl.BlockSpec((tokens, PAIR), lambda at: (0, part * count + at))

    return pl.pallas_call(
        body,
        grid=(count,),
        in_specs=[spec(0), spec(1), spec(2)],
        out_specs=[
            pl.BlockSpec((tokens, PAIR), lambda at: (0, at)),
            pl.BlockSpec((1, PAIR // HD, tokens), lambda at: (at, 0, 0)),
        ],
        out_shape=[
            jax.ShapeDtypeStruct((tokens, width), jnp.bfloat16),
            jax.ShapeDtypeStruct((count, PAIR // HD, tokens), jnp.float32),
        ],
        cost_estimate=cost(16 * tokens * tokens * width, 8 * tokens * width),
        compiler_params=params(),
        name="attention_forward",
    )(projected, projected, projected)


def attention_backward(projected, grad_mixed, totals):
    tokens, triple = projected.shape
    width = triple // 3
    count = width // PAIR

    def body(query_ref, key_ref, value_ref, grad_ref, total_ref, out_ref, sq_ref, sv_ref):
        keys = key_ref[...].T
        outs_q, outs_k, outs_v = [], [], []
        for half in range(PAIR // HD):
            lanes = slice(half * HD, (half + 1) * HD)
            scores = product(key_ref[:, lanes], query_ref[:, lanes], NT)
            probs = jnp.exp(scores - total_ref[0, half : half + 1, :])
            grad_probs = product(value_ref[:, lanes], grad_ref[:, lanes], NT)
            row_dot = jnp.sum(probs * grad_probs, axis=0, keepdims=True)
            grad_scores = (probs * (grad_probs - row_dot)).astype(jnp.bfloat16)
            outs_q.append(product(keys[lanes, :], grad_scores))
            outs_k.append(product(grad_scores, query_ref[:, lanes]))
            outs_v.append(product(probs.astype(jnp.bfloat16), grad_ref[:, lanes]))
        grad_query = jnp.concatenate(outs_q, axis=0).T * 0.125
        grad_value = jnp.concatenate(outs_v, axis=1)
        out_ref[0] = grad_query.astype(jnp.bfloat16)
        out_ref[1] = jnp.concatenate(outs_k, axis=1).astype(jnp.bfloat16)
        out_ref[2] = grad_value.astype(jnp.bfloat16)
        sq_ref[...] = column_sum(grad_query)
        sv_ref[...] = column_sum(grad_value)

    def spec(part):
        return pl.BlockSpec((tokens, PAIR), lambda at: (0, part * count + at))

    block = pl.BlockSpec((tokens, PAIR), lambda at: (0, at))
    line = pl.BlockSpec((1, PAIR), lambda at: (0, at))
    return pl.pallas_call(
        body,
        grid=(count,),
        in_specs=[spec(0), spec(1), spec(2), block]
        + [pl.BlockSpec((1, PAIR // HD, tokens), lambda at: (at, 0, 0))],
        out_specs=[pl.BlockSpec((3, tokens, PAIR), lambda at: (0, 0, at)), line, line],
        out_shape=[jax.ShapeDtypeStruct((3, tokens, width), jnp.bfloat16)]
        + [jax.ShapeDtypeStruct((1, width), jnp.float32)] * 2,
        cost_estimate=cost(40 * tokens * tokens * width, 16 * tokens * width),
        compiler_params=params(),
        name="attention_backward",
    )(projected, projected, projected, grad_mixed, totals)


def weight_grads(where, pairs):
    tokens, rows = pairs[0][0].shape
    sizes = [pair[4] for pair in pairs]
    parts = [pair[2].shape[0] if pair[2].ndim == 3 else 1 for pair in pairs]
    spans = [size * part for size, part in zip(sizes, parts)]
    width = sum(spans)
    step = 256
    count = rows // step
    half = count // 2
    operands, in_specs = [], []
    for left, left_pair, right, right_pair, _ in pairs:
        operands += [left, left_pair, right, right_pair]
        in_specs += [pl.BlockSpec((tokens, step), lambda at, _: (0, at))] * 2 + [ANY] * 2

    def body(where_ref, *refs):
        ins = refs[: len(operands)]
        send_a, keep_a, send_b, keep_b = refs[len(operands) : len(operands) + 4]
        joined, sems = refs[len(operands) + 4 : -1], refs[-1]
        at = pl.program_id(0)

        @pl.when(at == 0)
        def _():
            for pair, (size, part_count) in enumerate(zip(sizes, parts)):
                for side in range(2):
                    source = ins[4 * pair + 2 + side]
                    for which in range(4):
                        block = jnp.bitwise_xor(where_ref[0], 2 * which)
                        columns = pl.ds(aligned(block * size, LANES), size)
                        for part in range(part_count):
                            begin = (which * part_count + part) * size
                            taken = (
                                source.at[part, :, columns]
                                if part_count > 1
                                else source.at[:, columns]
                            )
                            pltpu.make_async_copy(
                                taken,
                                joined[2 * pair + side].at[:, begin : begin + size],
                                sems.at[2 * pair + side],
                            ).start()
            for which in range(2 * len(pairs)):
                finish(joined[which], sems.at[which])

        results = []
        for pair in range(len(pairs)):
            total = product(ins[4 * pair][...], joined[2 * pair][...], TN)
            total = total + product(ins[4 * pair + 1][...], joined[2 * pair + 1][...], TN)
            results.append(total.astype(jnp.bfloat16))

        def put(targets):
            base = 0
            for pair, span in enumerate(spans):
                for which in range(4):
                    ref, slot = targets[which]
                    ref[slot, :, base : base + span] = results[pair][
                        :, which * span : (which + 1) * span
                    ]
                base += span

        @pl.when(at < half)
        def _():
            put([(keep_a, 0), (send_a, 0), (keep_a, 1), (send_a, 1)])

        @pl.when(at >= half)
        def _():
            put([(keep_b, 0), (keep_b, 1), (send_b, 0), (send_b, 1)])

    spec_a = pl.BlockSpec((2, step, width), lambda at, _: (0, jnp.minimum(at, half - 1), 0))
    spec_b = pl.BlockSpec((2, step, width), lambda at, _: (0, jnp.maximum(at - half, 0), 0))
    return pl.pallas_call(
        body,
        grid_spec=pltpu.PrefetchScalarGridSpec(
            num_scalar_prefetch=1,
            grid=(count,),
            in_specs=in_specs,
            out_specs=[spec_a, spec_a, spec_b, spec_b],
            scratch_shapes=[
                pltpu.VMEM((tokens, 4 * span), jnp.bfloat16) for span in spans for _ in range(2)
            ]
            + [pltpu.SemaphoreType.DMA((2 * len(pairs),))],
        ),
        out_shape=[jax.ShapeDtypeStruct((2, rows // 2, width), jnp.bfloat16)] * 4,
        cost_estimate=cost(16 * rows * tokens * width, 8 * rows * width + 4 * tokens * rows),
        compiler_params=params(),
        name="weight_grads",
    )(where, *operands)


def pack_blocks(where, qkv, out, up, down, vectors):
    rows, _ = qkv.shape
    size = up.shape[1] // BLOCKS
    lengths = [vec.shape[1] for vec in vectors]
    row = 3 * LANES

    def body(where_ref, query_ref, key_ref, value_ref, out_ref, up_ref, down_ref, *rest):
        vector_refs = rest[: len(vectors)]
        first_ref, second_ref, third_ref = rest[len(vectors) :]
        first_ref[:rows, :LANES] = query_ref[...]
        first_ref[:rows, LANES : 2 * LANES] = key_ref[...]
        first_ref[:rows, 2 * LANES :] = value_ref[...]
        flat_vectors = jnp.concatenate([ref[...].astype(jnp.float32) for ref in vector_refs], axis=1)
        total = flat_vectors.shape[1]
        lines = [flat_vectors[:, at : at + row] for at in range(0, total, row)]
        lines.append(jnp.zeros((16 - len(lines), row), jnp.float32))
        first_ref[rows:, :] = jnp.concatenate(lines, axis=0).astype(jnp.bfloat16)
        second_ref[:, :size] = up_ref[...]
        second_ref[:, size:] = out_ref[...]
        third_ref[...] = down_ref[...]

    def mine(array, width, part=0):
        return pl.BlockSpec(
            (array.shape[0], width),
            lambda at, where_ref: (0, part * BLOCKS + where_ref[0]),
        )

    whole = lambda shape: pl.BlockSpec(shape, lambda at, _: (0, 0))
    shapes = [(rows + 16, row), (rows, size + LANES), (down.shape[0], LANES)]
    return pl.pallas_call(
        body,
        grid_spec=pltpu.PrefetchScalarGridSpec(
            num_scalar_prefetch=1,
            grid=(1,),
            in_specs=[mine(qkv, LANES, part) for part in range(3)]
            + [mine(out, LANES), mine(up, size), mine(down, LANES)]
            + [whole((1, length)) for length in lengths],
            out_specs=[whole(shape) for shape in shapes],
        ),
        out_shape=[jax.ShapeDtypeStruct(shape, jnp.bfloat16) for shape in shapes],
        compiler_params=params(),
        name="pack_blocks",
    )(where, qkv, qkv, qkv, out, up, down, *vectors)


def unpack_vectors(where, sources, rows, lengths, pair_at, width):
    groups = len(sources)
    row = sources[0].shape[1]
    outs = [3 * width if at == pair_at else length * groups for at, length in enumerate(lengths)]

    def body(where_ref, *refs):
        source_refs, out_refs = refs[:groups], refs[groups:]
        out_refs[pair_at][...] = jnp.zeros((1, 3 * width), jnp.float32)
        for hop in range(groups):
            block = source_refs[hop][...].astype(jnp.float32)
            owner = jnp.bitwise_xor(where_ref[1], hop)
            place = 0
            for which, length in enumerate(lengths):
                start = owner * length
                if which == pair_at:
                    start = start + jnp.where(start >= width, width, 0)
                for begin in range(0, length, LANES):
                    line, lane = (place + begin) // row, (place + begin) % row
                    target = pl.ds(aligned(start + begin, LANES), LANES)
                    out_refs[which][:, target] = block[line : line + 1, lane : lane + LANES]
                place += length

    return pl.pallas_call(
        body,
        grid_spec=pltpu.PrefetchScalarGridSpec(
            num_scalar_prefetch=1,
            grid=(1,),
            in_specs=[pl.BlockSpec((16, row), lambda at, _: (rows // 16, 0))] * groups,
            out_specs=[pl.BlockSpec((1, size), lambda at, _: (0, 0)) for size in outs],
        ),
        out_shape=[jax.ShapeDtypeStruct((1, size), jnp.float32) for size in outs],
        compiler_params=params(),
        name="unpack_vectors",
    )(where, *sources)


def pack_sums(vectors, groups):
    total = sum(vec.shape[1] for vec in vectors) // groups

    def body(*refs):
        for owner in range(groups):
            pieces = []
            for ref in refs[:-1]:
                length = ref.shape[1] // groups
                pieces.append(ref[:, owner * length : (owner + 1) * length])
            refs[-1][owner : owner + 1, :] = jnp.concatenate(pieces, axis=1)

    return pl.pallas_call(
        body,
        out_shape=jax.ShapeDtypeStruct((groups, total), jnp.float32),
        compiler_params=params(),
        name="pack_sums",
    )(*vectors)


def unpack_sums(where, first, second, lengths):
    groups, total = first.shape

    def body(where_ref, first_ref, second_ref, *outs):
        line = jnp.zeros((1, total), jnp.float32)
        for owner in range(groups):
            both = first_ref[owner : owner + 1, :] + second_ref[owner : owner + 1, :]
            line = jnp.where(where_ref[1] == owner, both, line)
        place = 0
        for out, length in zip(outs, lengths):
            out[...] = line[:, place : place + length]
            place += length

    whole = pl.BlockSpec((groups, total), lambda at, _: (0, 0))
    return pl.pallas_call(
        body,
        grid_spec=pltpu.PrefetchScalarGridSpec(
            num_scalar_prefetch=1,
            grid=(1,),
            in_specs=[whole, whole],
            out_specs=[pl.BlockSpec((1, length), lambda at, _: (0, 0)) for length in lengths],
        ),
        out_shape=[jax.ShapeDtypeStruct((1, length), jnp.float32) for length in lengths],
        compiler_params=params(),
        name="unpack_sums",
    )(where, first, second)


def finish_blocks(blocks):
    count, rows, size = blocks.shape
    step = min(rows, 128)

    def body(in_ref, out_ref):
        for at in range(count):
            out_ref[:, at * size : (at + 1) * size] = in_ref[at].astype(jnp.float32)

    return pl.pallas_call(
        body,
        grid=(rows // step,),
        in_specs=[pl.BlockSpec((count, step, size), lambda at: (0, at, 0))],
        out_specs=pl.BlockSpec((step, count * size), lambda at: (at, 0)),
        out_shape=jax.ShapeDtypeStruct((rows, count * size), jnp.float32),
        compiler_params=params(),
        name="finish_blocks",
    )(blocks)


def finish_grads(where, pieces, strips):
    rows = pieces[0].shape[0]
    step = min(rows, 128)
    totals = {}
    for _, size, out, base in strips:
        totals[out] = max(totals.get(out, 0), base + size * BLOCKS)

    def body(where_ref, *refs):
        piece_refs, out_refs = refs[:BLOCKS], refs[BLOCKS:]
        for at in range(BLOCKS):
            block = jnp.bitwise_xor(where_ref[0], at)
            for start, size, out, base in strips:
                target = pl.ds(aligned(base + block * size, LANES), size)
                out_refs[out][:, target] = piece_refs[at][:, start : start + size].astype(
                    jnp.float32
                )

    return pl.pallas_call(
        body,
        grid_spec=pltpu.PrefetchScalarGridSpec(
            num_scalar_prefetch=1,
            grid=(rows // step,),
            in_specs=[
                pl.BlockSpec((step, piece.shape[1]), lambda at, _: (at, 0)) for piece in pieces
            ],
            out_specs=[
                pl.BlockSpec((step, totals[out]), lambda at, _: (at, 0)) for out in sorted(totals)
            ],
        ),
        out_shape=[
            jax.ShapeDtypeStruct((rows, totals[out]), jnp.float32) for out in sorted(totals)
        ],
        compiler_params=params(),
        name="finish_grads",
    )(where, *pieces)


def exchange(tensor, mask, axis="rep"):
    size = lax.axis_size(axis)
    return lax.ppermute(tensor, axis, [(at, at ^ mask) for at in range(size)])


def tie(value, *others):
    return lax.optimization_barrier((value, others))[0]


def all_hops(block):
    return [exchange(block, hop, "grp") for hop in range(1, lax.axis_size("grp"))]


def spread(own):
    by_x = exchange(own, 2)
    by_y = exchange(own, 4)
    half = own.shape[0] // 2
    sent = (by_x[:half], by_y[half:])
    top = exchange(sent[0], 4)
    bottom = exchange(sent[1], 2)
    pieces = []
    for piece in ((own,), (by_x,), (by_y,), (top, bottom)):
        pieces += [piece, tuple(exchange(array, 1) for array in piece)]
    return pieces, sent, (top, bottom)


def add_rounded(left, right):
    return (left.astype(jnp.float32) + right.astype(jnp.float32)).astype(jnp.bfloat16)


def first_sends(parts):
    return exchange(parts[0], 2), exchange(parts[2], 4)


def second_sends(parts, got):
    keep_a, keep_b = parts[1], parts[3]
    got_a, got_b = got
    next_a = exchange(add_rounded(keep_a[1], got_a[1]), 4)
    next_b = exchange(add_rounded(keep_b[1], got_b[1]), 2)
    rest_a = add_rounded(keep_a[0], got_a[0])
    rest_b = add_rounded(keep_b[0], got_b[0])
    return (rest_a, rest_b), (next_a, next_b)


def block_total(rest, got):
    total = jnp.concatenate([add_rounded(*pair) for pair in zip(rest, got)], axis=0)
    mask = BLOCKS
    while mask < lax.axis_size("rep"):
        total = add_rounded(total, exchange(total, mask))
        mask *= 2
    return total


def grp_sum(total):
    groups = lax.axis_size("grp")
    share = total.shape[0] // groups
    place = lax.axis_index("grp")
    sent = [
        lax.dynamic_slice_in_dim(total, (place ^ hop) * share, share, 0) for hop in range(groups)
    ]
    got = [exchange(sent[hop], hop, "grp") for hop in range(1, groups)]
    return sent[0], got


def sum_rounded(own, got):
    total = own.astype(jnp.float32)
    for other in got:
        total = total + other.astype(jnp.float32)
    return total.astype(jnp.bfloat16)


def layer(
    images,
    cotangent,
    ln1_gain,
    ln1_shift,
    qkv_weight,
    qv_bias,
    out_weight,
    out_bias,
    ln2_gain,
    ln2_shift,
    fc1_weight,
    fc1_bias,
    fc2_weight,
    fc2_bias,
):
    n_grp = lax.axis_size("grp")
    place = jnp.bitwise_and(lax.axis_index("rep"), BLOCKS - 1)
    where = jnp.stack([place, lax.axis_index("grp")])
    rows, width = out_weight.shape
    hidden_block = fc1_weight.shape[1] // BLOCKS

    vectors = (ln1_gain, ln1_shift, qv_bias, out_bias, ln2_gain, ln2_shift, fc1_bias, fc2_bias)
    sizes = [vec.shape[0] for vec in vectors]
    block_a, block_b, block_c = pack_blocks(
        where,
        qkv_weight,
        out_weight,
        fc1_weight,
        fc2_weight,
        [vec.reshape(1, -1) for vec in vectors],
    )
    got_a = all_hops(block_a)
    pieces_a, sent_a, _ = spread(jnp.concatenate([got[:rows] for got in got_a]))
    got_b = tie(all_hops(tie(block_b, got_a)), sent_a)
    pieces_b, sent_b, _ = spread(jnp.concatenate(got_b))
    got_c = tie(all_hops(tie(block_c, got_b)), sent_b)
    pieces_c, _, _ = spread(jnp.concatenate(got_c))
    gain_1, shift_1, bias_in, bias_attn, gain_2, shift_2, bias_up, bias_down = unpack_vectors(
        where, [block_a] + got_a, rows, sizes, 2, width
    )

    image = images[0]
    grad_block = cotangent[0]
    cot_pair = exchange(grad_block, 1)

    normed_in, projected = qkv_forward(where, image, gain_1, shift_1, bias_in, qkv_weight, pieces_a)
    normed_pair = exchange(normed_in, 1)
    attended, totals = attention_forward(projected)
    attended_pair = exchange(attended, 1)
    residual, normed_mid = out_forward(
        where, image, attended, bias_attn, gain_2, shift_2, out_weight, pieces_b, hidden_block
    )
    mid_pair = exchange(normed_mid, 1)
    active, slope = up_forward(where, normed_mid, bias_up, fc1_weight, pieces_b)
    active_pair = exchange(active, 1)

    grad_pre, sum_up = down_backward(where, grad_block, slope, fc2_weight, pieces_c)
    pre_pair = exchange(grad_pre, 1)
    down_parts = weight_grads(
        tie(where, grad_pre), [(active, active_pair, grad_block, cot_pair, LANES)]
    )
    down_got = first_sends(down_parts)
    middle = middle_backward(
        tie(where, down_parts),
        grad_pre,
        grad_block,
        residual,
        gain_2,
        fc1_weight,
        out_weight,
        pieces_b,
        hidden_block,
    )
    grad_res, grad_res_b, grad_attended, sum_gain_2, sum_shift_2, sum_res, sum_top = middle
    res_pair = exchange(grad_res_b, 1)
    down_rest, down_got = second_sends(down_parts, tie(down_got, grad_res))
    up_parts = weight_grads(
        tie(where, grad_res, down_rest),
        [(normed_mid, mid_pair, grad_pre, pre_pair, hidden_block)],
    )
    up_got = first_sends(up_parts)
    down_total = block_total(down_rest, tie(down_got, up_parts))
    down_own = lax.psum_scatter(down_total, "grp", scatter_dimension=0, tiled=True)
    grad_proj, sum_query, sum_value = attention_backward(
        projected, tie(grad_attended, up_parts, down_total), totals
    )
    proj_pair = exchange(grad_proj, 1)
    up_rest, up_got = second_sends(up_parts, tie(up_got, grad_proj))
    attn_parts = weight_grads(
        tie(where, up_rest),
        [
            (normed_in, normed_pair, grad_proj, proj_pair, LANES),
            (attended, attended_pair, grad_res_b, res_pair, LANES),
        ],
    )
    attn_got = first_sends(attn_parts)
    down_blocks = lax.all_gather(tie(down_own, attn_parts), "rep", axis=0, tiled=False)[:BLOCKS]
    up_total = block_total(up_rest, tie(up_got, attn_parts))
    up_own = lax.psum_scatter(up_total, "grp", scatter_dimension=0, tiled=True)
    input_grad, sum_gain_1, sum_shift_1 = qkv_backward(
        tie(where, attn_parts, up_total),
        grad_proj,
        image,
        grad_res,
        gain_1,
        qkv_weight,
        pieces_a,
    )
    sums = pack_sums(
        [
            sum_gain_1,
            sum_shift_1,
            jnp.concatenate([sum_query, sum_value], axis=1),
            sum_res,
            sum_gain_2,
            sum_shift_2,
            sum_up,
            sum_top,
        ],
        n_grp,
    )
    got = exchange(sums, 1)
    block_out = down_forward(
        tie(where, input_grad, sums), residual, active, bias_down, fc2_weight, pieces_c
    )
    sums = sums + tie(got, block_out)
    up_blocks = lax.all_gather(tie(up_own, block_out), "rep", axis=0, tiled=False)[:BLOCKS]
    attn_rest, attn_got = second_sends(attn_parts, tie(attn_got, block_out))
    sums = sums + tie(exchange(sums, 2), attn_rest)
    mask = BLOCKS
    while mask < lax.axis_size("rep"):
        sums = sums + exchange(sums, mask)
        mask *= 2
    attn_total = block_total(attn_rest, attn_got)
    own, got = grp_sum(attn_total)
    sums = sums + tie(exchange(sums, 4), attn_total)
    grad_down = finish_blocks(tie(down_blocks, attn_total))
    own = sum_rounded(own, tie(got, grad_down))
    mask = 1
    while mask * 2 < n_grp:
        sums = sums + tie(exchange(sums, mask, "grp"), own)
        mask *= 2
    by_x = exchange(own, 2)
    by_y = exchange(own, 4)
    both = exchange(by_x, 4)
    last = exchange(sums, mask, "grp")
    attn_pieces = []
    for piece in (own, by_x, by_y, both):
        attn_pieces += [piece, exchange(piece, 1)]
    grad_up = finish_blocks(tie(up_blocks, by_x, by_y))
    grad_qkv, grad_out = finish_grads(
        where,
        attn_pieces,
        [(at * LANES, LANES, 0, at * width) for at in range(3)] + [(3 * LANES, LANES, 1, 0)],
    )
    sums = [vec.reshape(-1) for vec in unpack_sums(where, sums, last, sizes)]
    return (
        block_out[None],
        input_grad[None],
        sums[0],
        sums[1],
        grad_qkv,
        sums[2],
        grad_out,
        sums[3],
        sums[4],
        sums[5],
        grad_up,
        sums[6],
        grad_down,
        sums[7],
    )


def solution(mesh):
    return jax.shard_map(
        layer,
        mesh=mesh,
        in_specs=(
            P(("rep", "grp"), None, None),
            P(("rep", "grp"), None, None),
            P("grp"),
            P("grp"),
            P("grp", None),
            P("grp"),
            P("grp", None),
            P("grp"),
            P("grp"),
            P("grp"),
            P("grp", None),
            P("grp"),
            P("grp", None),
            P("grp"),
        ),
        out_specs=(
            P(("rep", "grp"), None, None),
            P(("rep", "grp"), None, None),
            P("grp"),
            P("grp"),
            P("grp", None),
            P("grp"),
            P("grp", None),
            P("grp"),
            P("grp"),
            P("grp"),
            P("grp", None),
            P("grp"),
            P("grp", None),
            P("grp"),
        ),
        check_vma=False,
    )
```

time: 881 us -> 501 us (0.57)
  waiting for transfers between devices: 513 us -> 181 us
  Pallas kernels: 0 us -> 197 us
  matrix products: 148 us -> 0 us
  local copies, waits for them, and re-layouts: 102 us -> 20.6 us
  starting transfers between devices: 0.81 us -> 69.4 us
  blocking collectives: 67.3 us -> 0 us
  other arithmetic: 29.7 us -> 17 us
    reduce_scatter x8 -> x2, waiting for transfers between devices: 272 us -> 5.01 us  [the longest x1 4.99 us: layer(): lax.psum_scatter(down_total, 'grp', scatter_dimension=0, tiled=True)]
    all_gather x7 -> x2, waiting for transfers between devices: 241 us -> 0.66 us  [the longest x1 0.65 us: layer(): lax.all_gather(tie(down_own, attn_parts), 'rep', axis=0, tiled=False)]
    pallas_call x0 -> x19, Pallas kernels: none -> 197 us  [the longest x3 45.2 us: weight_grads(): pl.pallas_call(body, grid_spec=pltpu.PrefetchScalarGridSpec(num_scalar_pr...]
    ppermute x0 -> x71, waiting for transfers between devices: none -> 176 us  [exchange(): return lax.ppermute(tensor, axis, [(at, at ^ mask) for at in range(size)])]
    dot_general x40 -> x0, matrix products: 148 us -> none  [the longest x1 12.9 us: forward_image(): jnp.dot(normed_mid, mlp_up, preferred_element_type=jnp.float32)]
    ppermute x0 -> x71, starting transfers between devices: none -> 69.2 us  [exchange(): return lax.ppermute(tensor, axis, [(at, at ^ mask) for at in range(size)])]
    transpose x4 -> x0, local copies, waits for them, and re-layouts: 35.7 us -> none  [gather_matrix(): return full.transpose(1, 0, 2).reshape(n_grp * rows, cols)]
    all_gather x2 -> x0, blocking collectives: 27.1 us -> none  [the longest x1 15 us: on_device(): lax.all_gather(jnp.concatenate(vectors), 'grp', axis=0, tiled=False)]
  transfers between devices with their start and end apart: 15 -> 75, of which waited for: 12 -> 29; matrix products, arithmetic and copies ran while one was open for 17% -> 3% of each run, Pallas kernels for 0% -> 33%
where the time goes in v2:
time: 501 us; the launch traced here: 500 us
  Pallas kernels  197 us (39%)
  waiting for transfers between devices  181 us (36%)
  starting transfers between devices  69.4 us (14%)
  local copies, waits for them, and re-layouts  20.6 us (4%)
  other arithmetic  17 us (3%)
  between operations  14.6 us (3%)
    ppermute x71, waiting for transfers between devices, exchange(): return lax.ppermute(tensor, axis, [(at, at ^ mask) for at in range(size)])  176 us
    ppermute x71, starting transfers between devices, exchange(): return lax.ppermute(tensor, axis, [(at, at ^ mask) for at in range(size)])  69.2 us
    pallas_call x3, Pallas kernels, weight_grads(): pl.pallas_call(body, grid_spec=pltpu.PrefetchScalarGridSpec(num_scalar_pr...  45.2 us
    pallas_call x1, Pallas kernels, attention_backward(): pl.pallas_call(body, grid=(count,), in_specs=[spec(0), spec(1), spec(2),...  24.9 us
    pallas_call x1, Pallas kernels, middle_backward(): pl.pallas_call(body, grid_spec=pltpu.PrefetchScalarGridSpec(num_scalar_pr...  18.8 us
    pallas_call x1, Pallas kernels, attention_forward(): pl.pallas_call(body, grid=(count,), in_specs=[spec(0), spec(1), spec(2)],...  14.3 us
    pallas_call x1, Pallas kernels, up_forward(): pl.pallas_call(body, grid_spec=pltpu.PrefetchScalarGridSpec(num_scalar_pr...  14.2 us
    pallas_call x1, Pallas kernels, down_forward(): pl.pallas_call(body, grid_spec=pltpu.PrefetchScalarGridSpec(num_scalar_pr...  13.6 us
  transfers between devices with their start and end apart: 75, of which 29 were waited for; matrix products, arithmetic and copies ran while one was open for 3% of the time, Pallas kernels for 33%

profile of v2, /device:TPU:0, one launch (start us, length us, event | category | flops | bytes accessed | tf_op | source)
XLA Modules:
  0.0 499.6 jit_solution(15227708682345379009)
XLA Ops:
  17.6 2.9 pack_blocks.1
  20.5 3.1 collective-permute-start
  23.6 2.6 collective-permute-start.1
  26.2 6.5 %collective-permute-done.refs_1_ = bf16[272,384]{1,0:T(8,128)(2,1)S(1)} collective-permute-done((bf16[272,384]{1,0:T(8,128)(2,1)}, bf16[272,384]{1,0:T(8,128)(2,1)S(1)}, u32[]{:S(2)}, u32[]{:S(2)}) %collective-permute-start) | collective-permute-done | bytes 208928 | tf_op jit(solution)/shard_map/ppermute | solution.py:876
  32.7 9.0 %collective-permute-done.1.refs_2_ = bf16[272,384]{1,0:T(8,128)(2,1)S(1)} collective-permute-done((bf16[272,384]{1,0:T(8,128)(2,1)}, bf16[272,384]{1,0:T(8,128)(2,1)S(1)}, u32[]{:S(2)}, u32[]{:S(2)}) %collective-permute-start.1) | collective-permute-done | bytes 208928 | tf_op jit(solution)/shard_map/ppermute | solution.py:876
  43.1 1.6 collective-permute-start.4
  44.7 1.5 collective-permute-start.6
  46.2 3.0 collective-permute-start.12
  50.2 1.5 collective-permute-start.14
  51.7 3.5 collective-permute-done.4.rest_2_
  56.4 4.3 collective-permute-done.12
  60.7 14.0 %collective-permute-done.13 = bf16[256,640]{1,0:T(8,128)(2,1)S(1)} collective-permute-done((bf16[256,640]{1,0:T(8,128)(2,1)S(1)}, bf16[256,640]{1,0:T(8,128)(2,1)S(1)}, u32[]{:S(2)}, u32[]{:S(2)}) %collective-permute-start.13) | collective-permute-done | bytes 327712 | tf_op jit(solution)/shard_map/ppermute | solution.py:876
  76.0 1.5 collective-permute-start.8
  77.5 1.5 collective-permute-start.9
  79.0 20.3 %collective-permute-done.8.rest_6_ = bf16[384,384]{1,0:T(8,128)(2,1)S(1)} collective-permute-done((bf16[384,384]{1,0:T(8,128)(2,1)S(1)}, bf16[384,384]{1,0:T(8,128)(2,1)S(1)}, u32[]{:S(2)}, u32[]{:S(2)}) %collective-permute-start.8) | collective-permute-done | bytes 294944 | tf_op jit(solution)/shard_map/ppermute | solution.py:876
  102.7 1.5 collective-permute-start.21
  106.3 2.1 unpack_vectors.1
  108.4 9.6 %qkv_forward.1 = (bf16[577,1024]{1,0:T(8,128)(2,1)}, bf16[577,3072]{1,0:T(8,128)(2,1)}) custom-call(s32[2]{0:T(128)} %pad_add_fusion.where_ref, bf16[577,1024]{1,0:T(8,128)(2,1)} %bitcast.42, f32[1,1024]{1,0:T(1,128)} %get-tuple-element.107.gain_ref, f32[1,1024]{1,0:T(1,128)} %get-tuple-element.108.shift_ref, f32[1,3072]{1,0:T(1,128)} %get-tuple-element.109.bias_ref, ...), custom_call_target="tpu_custom_call" | custom-call | flops 3630170112 | bytes 6291456 | tf_op jit(solution)/shard_map/qkv_forward/pallas_call | solution.py:147
  118.6 14.3 %attention_forward.1 = (bf16[577,1024]{1,0:T(8,128)(2,1)}, f32[8,2,577]{2,1,0:T(2,128)}) custom-call(bf16[577,3072]{1,0:T(8,128)(2,1)} %get-tuple-element.110.query_ref.key_ref.value_ref, bf16[577,3072]{1,0:T(8,128)(2,1)} %get-tuple-element.110.query_ref.key_ref.value_ref, bf16[577,3072]{1,0:T(8,128)(2,1)} %get-tuple-element.110.query_ref.key_ref.value_ref), custom_call_target="tpu_custom_call" | custom-call | flops 5454708736 | bytes 4726784 | tf_op jit(solution)/shard_map/attention_forward/pallas_call | solution.py:539
  132.9 7.6 %collective-permute-start.24 = (bf16[1024,128]{1,0:T(8,128)(2,1)}, bf16[1024,128]{1,0:T(8,128)(2,1)S(1)}, u32[]{:S(2)}, u32[]{:S(2)}) collective-permute-start(bf16[1024,128]{1,0:T(8,128)(2,1)} %get-tuple-element.124), channel_id=1, source_target_pairs={{0,1},{1,0},{2,3},{3,2},{4,5},{5,4},{6,7},{7,6},{8,9},{9,8},{10,11... | collective-permute-start | bytes 786440 | tf_op jit(solution)/shard_map/ppermute | solution.py:876
  141.7 1.4 collective-permute-start.26
  143.1 7.6 %out_forward.1 = (f32[577,1024]{1,0:T(8,128)}, bf16[577,1024]{1,0:T(8,128)(2,1)}) custom-call(s32[2]{0:T(128)} %pad_add_fusion.where_ref, bf16[577,1024]{1,0:T(8,128)(2,1)} %bitcast.43, bf16[577,1024]{1,0:T(8,128)(2,1)} %get-tuple-element.111.attended_ref.refs_4_, f32[1,1024]{1,0:T(1,128)} %get-tuple-element.112.bias_ref, ...), custom_call_target="tpu_custom_call" | custom-call | flops 1210056704 | bytes 2097152 | tf_op jit(solution)/shard_map/out_forward/pallas_call | solution.py:204
  150.8 14.2 %up_forward.1 = (bf16[577,4096]{1,0:T(8,128)(2,1)}, bf16[577,4096]{1,0:T(8,128)(2,1)}) custom-call(s32[2]{0:T(128)} %pad_add_fusion.where_ref, bf16[577,1024]{1,0:T(8,128)(2,1)} %get-tuple-element.120.normed_ref.refs_0_, f32[1,4096]{1,0:T(1,128)} %get-tuple-element.121.bias_ref, bf16[256,4096]{1,0:T(8,128)(2,1)} %up_ref.3, bf16[768,640]{1,0:T(8,128)(2,1)} %copy-done.3, ...), custom_call_target="tpu_custom_call" | custom-call | flops 4840226816 | bytes 8388608 | tf_op jit(solution)/shard_map/up_forward/pallas_call | solution.py:252
  165.8 1.5 collective-permute-start.30
  167.3 17.9 %collective-permute-done.28.rest_2_ = bf16[3072,128]{1,0:T(8,128)(2,1)S(1)} collective-permute-done((bf16[3072,128]{1,0:T(8,128)(2,1)S(1)}, bf16[3072,128]{1,0:T(8,128)(2,1)S(1)}, u32[]{:S(2)}, u32[]{:S(2)}) %collective-permute-start.28) | collective-permute-done | bytes 786464 | tf_op jit(solution)/shard_map/ppermute | solution.py:876
  185.2 1.6 collective-permute-start.32
  188.0 8.0 %collective-permute-done.32.rest_6_ = bf16[1536,128]{1,0:T(8,128)(2,1)S(1)} collective-permute-done((bf16[1536,128]{1,0:T(8,128)(2,1)S(1)}, bf16[1536,128]{1,0:T(8,128)(2,1)S(1)}, u32[]{:S(2)}, u32[]{:S(2)}) %collective-permute-start.32) | collective-permute-done | bytes 393248 | tf_op jit(solution)/shard_map/ppermute | solution.py:876
  200.9 13.1 %down_backward.1 = (bf16[577,4096]{1,0:T(8,128)(2,1)}, f32[1,4096]{1,0:T(1,128)}) custom-call(s32[2]{0:T(128)} %pad_add_fusion.where_ref, bf16[577,1024]{1,0:T(8,128)(2,1)} %bitcast.47, bf16[577,4096]{1,0:T(8,128)(2,1)} %get-tuple-element.122.slope_ref, bf16[1024,1024]{1,0:T(8,128)(2,1)} %own_ref.13, bf16[3072,128]{1,0:T(8,128)(2,1)} %copy-done.39, ...), custom_call_target="tpu_custom_call" | custom-call | flops 4840226816 | bytes 8388608 | tf_op jit(solution)/shard_map/down_backward/pallas_call | solution.py:350
  214.6 9.4 %collective-permute-done.37.refs_3_ = bf16[577,1024]{1,0:T(8,128)(2,1)S(1)} collective-permute-done((bf16[577,1024]{1,0:T(8,128)(2,1)}, bf16[577,1024]{1,0:T(8,128)(2,1)S(1)}, u32[]{:S(2)}, u32[]{:S(2)}) %collective-permute-start.37) | collective-permute-done | bytes 1181728 | tf_op jit(solution)/shard_map/ppermute | solution.py:876
  225.1 18.0 %weight_grads.3 = (bf16[2,2048,128]{2,1,0:T(8,128)(2,1)}, bf16[2,2048,128]{2,1,0:T(8,128)(2,1)}, bf16[2,2048,128]{2,1,0:T(8,128)(2,1)}, bf16[2,2048,128]{2,1,0:T(8,128)(2,1)}) custom-call(s32[2]{0:T(128)} %pad_add_fusion.where_ref, bf16[577,4096]{1,0:T(8,128)(2,1)} %get-tuple-element.130.refs_0_.active_ref, ...), custom_call_target="tpu_custom_call" | custom-call | flops 4840226816 | bytes 13647872 | tf_op jit(solution)/shard_map/weight_grads/pallas_call | solution.py:671
  244.8 18.8 %middle_backward.1 = (f32[577,1024]{1,0:T(8,128)}, bf16[577,1024]{1,0:T(8,128)(2,1)}, bf16[577,1024]{1,0:T(8,128)(2,1)}, f32[1,1024]{1,0:T(1,128)}, f32[1,1024]{...) custom-call(s32[2]{0:T(128)} %pad_add_fusion.where_ref, bf16[577,4096]{1,0:T(8,128)(2,1)} %get-tuple-element.128.pre_ref.refs_2_, ...), custom_call_target="tpu_custom_call" | custom-call | flops 6050283520 | bytes 10485760 | tf_op jit(solution)/shard_map/middle_backward/pallas_call | solution.py:427
  263.6 5.0 collective-permute-done.38
  269.9 1.5 collective-permute-start.45
  272.5 13.4 %weight_grads.4 = (bf16[2,512,512]{2,1,0:T(8,128)(2,1)}, bf16[2,512,512]{2,1,0:T(8,128)(2,1)}, bf16[2,512,512]{2,1,0:T(8,128)(2,1)}, bf16[2,512,512]{2,1,0:T(8,128)(2,1)}) custom-call(s32[2]{0:T(128)} %pad_add_fusion.where_ref, bf16[577,1024]{1,0:T(8,128)(2,1)} %get-tuple-element.120.normed_ref.refs_0_, bf16[577,1024]{1,0:T(8,128)(2,1)} %collective-permute-done.40.refs_1_, ...), custom_call_target="tpu_custom_call" | custom-call | flops 4840226816 | bytes 6557696 | tf_op jit(solution)/shard_map/weight_grads/pallas_call | solution.py:671
  287.3 24.9 %attention_backward.1 = (bf16[3,577,1024]{2,1,0:T(8,128)(2,1)}, f32[1,1024]{1,0:T(1,128)}, f32[1,1024]{1,0:T(1,128)}) custom-call(bf16[577,3072]{1,0:T(8,128)(2,1)} %get-tuple-element.110.query_ref.key_ref.value_ref, bf16[577,3072]{1,0:T(8,128)(2,1)} %get-tuple-element.110.query_ref.key_ref.value_ref, ...), custom_call_target="tpu_custom_call" | custom-call | flops 13636771840 | bytes 9453568 | tf_op jit(solution)/shard_map/attention_backward/pallas_call | solution.py:588
  314.6 23.2 %collective-permute-done.42 = bf16[2,512,512]{2,1,0:T(8,128)(2,1)S(1)} collective-permute-done((bf16[2,512,512]{2,1,0:T(8,128)(2,1)S(1)}, bf16[2,512,512]{2,1,0:T(8,128)(2,1)S(1)}, u32[]{:S(2)}, u32[]{:S(2)}) %collective-permute-start.42) | collective-permute-done | bytes 1048608 | tf_op jit(solution)/shard_map/ppermute | solution.py:876
  338.8 2.8 fusion.7
  344.9 13.8 %weight_grads.5 = (bf16[2,512,512]{2,1,0:T(8,128)(2,1)}, bf16[2,512,512]{2,1,0:T(8,128)(2,1)}, bf16[2,512,512]{2,1,0:T(8,128)(2,1)}, bf16[2,512,512]{2,1,0:T(8,128)(2,1)}) custom-call(s32[2]{0:T(128)} %pad_add_fusion.where_ref, bf16[577,1024]{1,0:T(8,128)(2,1)} %get-tuple-element.154.refs_0_, bf16[577,1024]{1,0:T(8,128)(2,1)} %collective-permute-done.46.refs_1_, ...), custom_call_target="tpu_custom_call" | custom-call | flops 4840226816 | bytes 6557696 | tf_op jit(solution)/shard_map/weight_grads/pallas_call | solution.py:671
  360.2 5.0 reduce-scatter.3.cloned.1.call-done
  365.9 1.5 collective-permute-start.54
  367.4 1.5 collective-permute-start.55
  368.8 13.3 %qkv_backward.1 = (bf16[577,1024]{1,0:T(8,128)(2,1)}, f32[1,1024]{1,0:T(1,128)}, f32[1,1024]{1,0:T(1,128)}) custom-call(s32[2]{0:T(128)} %pad_add_fusion.where_ref, bf16[3,577,1024]{2,1,0:T(8,128)(2,1)} %get-tuple-element.150.refs_2_.proj_ref, bf16[577,1024]{1,0:T(8,128)(2,1)} %bitcast.44, f32[577,1024]{1,0:T(8,128)} %get-tuple-element.137.res_ref, ...), custom_call_target="tpu_custom_call" | custom-call | flops 3630170112 | bytes 6291456 | tf_op jit(solution)/shard_map/qkv_backward/pallas_call | solution.py:492
  382.1 1.4 pack_sums.1
  383.5 13.6 %down_forward.1 = bf16[577,1024]{1,0:T(8,128)(2,1)} custom-call(s32[2]{0:T(128)} %pad_add_fusion.where_ref, f32[577,1024]{1,0:T(8,128)} %get-tuple-element.136.residual_ref, bf16[577,4096]{1,0:T(8,128)(2,1)} %get-tuple-element.130.refs_0_.active_ref, f32[1,1024]{1,0:T(1,128)} %get-tuple-element.174.bias_ref, bf16[1024,1024]{1,0:T(8,128)(2,1)} %own_ref.13, ...), custom_call_target="tpu_custom_call" | custom-call | flops 4840226816 | bytes 8388608 | tf_op jit(solution)/shard_map/down_forward/pallas_call | solution.py:296
  397.2 2.4 fusion.11
  401.6 13.6 %collective-permute-done.58 = bf16[512,512]{1,0:T(8,128)(2,1)} collective-permute-done((bf16[512,512]{1,0:T(8,128)(2,1)}, bf16[512,512]{1,0:T(8,128)(2,1)}, u32[]{:S(2)}, u32[]{:S(2)}) %collective-permute-start.58) | collective-permute-done | bytes 524320 | tf_op jit(solution)/shard_map/ppermute | solution.py:876
  415.3 1.5 add_convert_fusion
  419.4 1.6 collective-permute-start.61
  421.0 2.8 collective-permute-start.62
  424.4 6.0 %finish_blocks.2 = f32[1024,1024]{1,0:T(8,128)} custom-call(bf16[8,1024,128]{2,1,0:T(8,128)(2,1)} %bitcast.46), custom_call_target="tpu_custom_call" | custom-call | tf_op jit(solution)/shard_map/finish_blocks/pallas_call | solution.py:826
  430.6 10.2 %collective-permute-done.61 = bf16[256,512]{1,0:T(8,128)(2,1)S(1)} collective-permute-done((bf16[256,512]{1,0:T(8,128)(2,1)S(1)}, bf16[256,512]{1,0:T(8,128)(2,1)S(1)}, u32[]{:S(2)}, u32[]{:S(2)}) %collective-permute-start.61) | collective-permute-done | bytes 262176 | tf_op jit(solution)/shard_map/ppermute | solution.py:876
  442.6 5.0 %collective-permute-done.65.refs_2_ = bf16[256,512]{1,0:T(8,128)(2,1)S(1)} collective-permute-done((bf16[256,512]{1,0:T(8,128)(2,1)S(1)}, bf16[256,512]{1,0:T(8,128)(2,1)S(1)}, u32[]{:S(2)}, u32[]{:S(2)}) %collective-permute-start.65) | collective-permute-done | bytes 262176 | tf_op jit(solution)/shard_map/ppermute | solution.py:876
  448.8 4.3 collective-permute-done.67.refs_4_
  453.1 5.3 %collective-permute-done.69.refs_6_ = bf16[256,512]{1,0:T(8,128)(2,1)S(1)} collective-permute-done((bf16[256,512]{1,0:T(8,128)(2,1)S(1)}, bf16[256,512]{1,0:T(8,128)(2,1)S(1)}, u32[]{:S(2)}, u32[]{:S(2)}) %collective-permute-start.69) | collective-permute-done | bytes 262176 | tf_op jit(solution)/shard_map/ppermute | solution.py:876
  460.4 3.7 collective-permute-done.53
  464.1 1.5 collective-permute-start.56
  465.7 2.6 collective-permute-done.56
  468.3 5.2 %collective-permute-start.59 = (f32[4,3072]{1,0:T(4,128)S(1)}, f32[4,3072]{1,0:T(4,128)S(1)}, u32[]{:S(2)}, u32[]{:S(2)}) collective-permute-start(f32[4,3072]{1,0:T(4,128)S(1)} %add.123), channel_id=1, source_target_pairs={{0,1},{1,0},{2,3},{3,2},{4,5},{5,4},{6,7},{7,6},{8,9},{9,8},{10,11... | collective-permute-start | bytes 147464 | tf_op jit(solution)/shard_map/ppermute | solution.py:876
  473.5 2.1 collective-permute-done.59
  475.6 3.4 collective-permute-start.63
  479.0 2.1 collective-permute-done.63.second_ref
  481.7 2.1 unpack_sums.1
  485.4 4.2 finish_grads.1
  489.7 3.4 finish_blocks.3
  (260 shorter events, 58.1 us)
Async XLA Ops:
  7.2 358.0 %reduce-scatter.3.cloned.1.call-start = ((), (), s32[]{:S(2)}) async-start(), calls=%async_computation.2 | async-start | bytes 1310720 | tf_op jit(solution)/shard_map/reduce_scatter | solution.py:1028
  20.5 12.2 %collective-permute-start = (bf16[272,384]{1,0:T(8,128)(2,1)}, bf16[272,384]{1,0:T(8,128)(2,1)S(1)}, u32[]{:S(2)}, u32[]{:S(2)}) collective-permute-start(bf16[272,384]{1,0:T(8,128)(2,1)} %get-tuple-element.106.refs_0_), channel_id=1, source_target_pairs={{0,1},{1,0},{2,3},{3,2},{4,5},{5,4},{6,7},{7,6},{8,9},{9,8},{10,11... | collective-permute-start | bytes 626696 | tf_op jit(solution)/shard_map/ppermute | solution.py:876
  23.6 18.1 %collective-permute-start.1 = (bf16[272,384]{1,0:T(8,128)(2,1)}, bf16[272,384]{1,0:T(8,128)(2,1)S(1)}, u32[]{:S(2)}, u32[]{:S(2)}) collective-permute-start(bf16[272,384]{1,0:T(8,128)(2,1)} %get-tuple-element.106.refs_0_), channel_id=1, source_target_pairs={{0,2},{1,3},{2,0},{3,1},{4,6},{5,7},{6,4},{7,5},{8,10},{9,11},{10,... | collective-permute-start | bytes 626696 | tf_op jit(solution)/shard_map/ppermute | solution.py:876
  26.1 15.5 %collective-permute-start.2 = (bf16[272,384]{1,0:T(8,128)(2,1)}, bf16[272,384]{1,0:T(8,128)(2,1)S(1)}, u32[]{:S(2)}, u32[]{:S(2)}) collective-permute-start(bf16[272,384]{1,0:T(8,128)(2,1)} %get-tuple-element.106.refs_0_), channel_id=1, source_target_pairs={{0,3},{1,2},{2,1},{3,0},{4,7},{5,6},{6,5},{7,4},{8,11},{9,10},{10,... | collective-permute-start | bytes 626696 | tf_op jit(solution)/shard_map/ppermute | solution.py:876
  43.1 12.1 %collective-permute-start.4 = (bf16[768,384]{1,0:T(8,128)(2,1)S(1)}, bf16[768,384]{1,0:T(8,128)(2,1)S(1)}, u32[]{:S(2)}, u32[]{:S(2)}) collective-permute-start(bf16[768,384]{1,0:T(8,128)(2,1)S(1)} %pad_maximum_fusion.3.rest_0_), channel_id=1, source_target_pairs={{0,8},{4,12},{8,0},{12,4},{16,24},{20,28},{24,16},{28,20},{1,9},{5... | collective-permute-start | bytes 1769480 | tf_op jit(solution)/shard_map/ppermute | solution.py:876
  44.7 11.7 %collective-permute-start.6 = (bf16[768,384]{1,0:T(8,128)(2,1)S(1)}, bf16[768,384]{1,0:T(8,128)(2,1)S(1)}, u32[]{:S(2)}, u32[]{:S(2)}) collective-permute-start(bf16[768,384]{1,0:T(8,128)(2,1)S(1)} %pad_maximum_fusion.3.rest_0_), channel_id=1, source_target_pairs={{0,16},{4,20},{8,24},{12,28},{16,0},{20,4},{24,8},{28,12},{1,17},{... | collective-permute-start | bytes 1769480 | tf_op jit(solution)/shard_map/ppermute | solution.py:876
  46.2 14.5 %collective-permute-start.12 = (bf16[256,640]{1,0:T(8,128)(2,1)S(1)}, bf16[256,640]{1,0:T(8,128)(2,1)S(1)}, u32[]{:S(2)}, u32[]{:S(2)}) collective-permute-start(bf16[256,640]{1,0:T(8,128)(2,1)S(1)} %copy-done.52), channel_id=1, source_target_pairs={{0,1},{1,0},{2,3},{3,2},{4,5},{5,4},{6,7},{7,6},{8,9},{9,8},{10,11... | collective-permute-start | bytes 983048 | tf_op jit(solution)/shard_map/ppermute | solution.py:876
  49.2 25.5 %collective-permute-start.13 = (bf16[256,640]{1,0:T(8,128)(2,1)S(1)}, bf16[256,640]{1,0:T(8,128)(2,1)S(1)}, u32[]{:S(2)}, u32[]{:S(2)}) collective-permute-start(bf16[256,640]{1,0:T(8,128)(2,1)S(1)} %copy-done.52), channel_id=1, source_target_pairs={{0,2},{1,3},{2,0},{3,1},{4,6},{5,7},{6,4},{7,5},{8,10},{9,11},{10,... | collective-permute-start | bytes 983048 | tf_op jit(solution)/shard_map/ppermute | solution.py:876
  50.2 24.5 %collective-permute-start.14 = (bf16[256,640]{1,0:T(8,128)(2,1)S(1)}, bf16[256,640]{1,0:T(8,128)(2,1)S(1)}, u32[]{:S(2)}, u32[]{:S(2)}) collective-permute-start(bf16[256,640]{1,0:T(8,128)(2,1)S(1)} %copy-done.52), channel_id=1, source_target_pairs={{0,3},{1,2},{2,1},{3,0},{4,7},{5,6},{6,5},{7,4},{8,11},{9,10},{10,... | collective-permute-start | bytes 983048 | tf_op jit(solution)/shard_map/ppermute | solution.py:876
  74.9 24.9 %collective-permute-start.16 = (bf16[768,640]{1,0:T(8,128)(2,1)S(1)}, bf16[768,640]{1,0:T(8,128)(2,1)S(1)}, u32[]{:S(2)}, u32[]{:S(2)}) collective-permute-start(bf16[768,640]{1,0:T(8,128)(2,1)S(1)} %constant_dynamic-update-slice_fusion.rest_0_), channel_id=1, source_target_pairs={{0,8},{4,12},{8,0},{12,4},{16,24},{20,28},{24,16},{28,20},{1,9},{5... | collective-permute-start | bytes 2949128 | tf_op jit(solution)/shard_map/ppermute | solution.py:876
  75.5 24.4 %collective-permute-start.18 = (bf16[768,640]{1,0:T(8,128)(2,1)S(1)}, bf16[768,640]{1,0:T(8,128)(2,1)S(1)}, u32[]{:S(2)}, u32[]{:S(2)}) collective-permute-start(bf16[768,640]{1,0:T(8,128)(2,1)S(1)} %constant_dynamic-update-slice_fusion.rest_0_), channel_id=1, source_target_pairs={{0,16},{4,20},{8,24},{12,28},{16,0},{20,4},{24,8},{28,12},{1,17},{... | collective-permute-start | bytes 2949128 | tf_op jit(solution)/shard_map/ppermute | solution.py:876
  76.0 23.3 %collective-permute-start.8 = (bf16[384,384]{1,0:T(8,128)(2,1)S(1)}, bf16[384,384]{1,0:T(8,128)(2,1)S(1)}, u32[]{:S(2)}, u32[]{:S(2)}) collective-permute-start(bf16[384,384]{1,0:T(8,128)(2,1)S(1)} %slice.135), channel_id=1, source_target_pairs={{0,16},{4,20},{8,24},{12,28},{16,0},{20,4},{24,8},{28,12},{1,17},{... | collective-permute-start | bytes 884744 | tf_op jit(solution)/shard_map/ppermute | solution.py:876
  77.5 21.8 %collective-permute-start.9 = (bf16[384,384]{1,0:T(8,128)(2,1)S(1)}, bf16[384,384]{1,0:T(8,128)(2,1)S(1)}, u32[]{:S(2)}, u32[]{:S(2)}) collective-permute-start(bf16[384,384]{1,0:T(8,128)(2,1)S(1)} %slice.136), channel_id=1, source_target_pairs={{0,8},{4,12},{8,0},{12,4},{16,24},{20,28},{24,16},{28,20},{1,9},{5... | collective-permute-start | bytes 884744 | tf_op jit(solution)/shard_map/ppermute | solution.py:876
  79.0 23.1 %collective-permute-start.3 = (bf16[768,384]{1,0:T(8,128)(2,1)S(1)}, bf16[768,384]{1,0:T(8,128)(2,1)S(1)}, u32[]{:S(2)}, u32[]{:S(2)}) collective-permute-start(bf16[768,384]{1,0:T(8,128)(2,1)S(1)} %pad_maximum_fusion.3.rest_0_), channel_id=1, source_target_pairs={{0,4},{4,0},{8,12},{12,8},{16,20},{20,16},{24,28},{28,24},{1,5},{5... | collective-permute-start | bytes 1769480 | tf_op jit(solution)/shard_map/ppermute | solution.py:876
  102.1 15.9 %collective-permute-start.20 = (bf16[384,640]{1,0:T(8,128)(2,1)}, bf16[384,640]{1,0:T(8,128)(2,1)}, u32[]{:S(2)}, u32[]{:S(2)}) collective-permute-start(bf16[384,640]{1,0:T(8,128)(2,1)} %slice.137), channel_id=1, source_target_pairs={{0,16},{4,20},{8,24},{12,28},{16,0},{20,4},{24,8},{28,12},{1,17},{... | collective-permute-start | bytes 1474568 | tf_op jit(solution)/shard_map/ppermute | solution.py:876
  102.7 15.6 %collective-permute-start.21 = (bf16[384,640]{1,0:T(8,128)(2,1)}, bf16[384,640]{1,0:T(8,128)(2,1)}, u32[]{:S(2)}, u32[]{:S(2)}) collective-permute-start(bf16[384,640]{1,0:T(8,128)(2,1)} %slice.138), channel_id=1, source_target_pairs={{0,8},{4,12},{8,0},{12,4},{16,24},{20,28},{24,16},{28,20},{1,9},{5... | collective-permute-start | bytes 1474568 | tf_op jit(solution)/shard_map/ppermute | solution.py:876
  104.2 28.7 %collective-permute-start.15 = (bf16[768,640]{1,0:T(8,128)(2,1)S(1)}, bf16[768,640]{1,0:T(8,128)(2,1)S(1)}, u32[]{:S(2)}, u32[]{:S(2)}) collective-permute-start(bf16[768,640]{1,0:T(8,128)(2,1)S(1)} %constant_dynamic-update-slice_fusion.rest_0_), channel_id=1, source_target_pairs={{0,4},{4,0},{8,12},{12,8},{16,20},{20,16},{24,28},{28,24},{1,5},{5... | collective-permute-start | bytes 2949128 | tf_op jit(solution)/shard_map/ppermute | solution.py:876
  104.2 38.9 %collective-permute-start.17 = (bf16[768,640]{1,0:T(8,128)(2,1)S(1)}, bf16[768,640]{1,0:T(8,128)(2,1)}, u32[]{:S(2)}, u32[]{:S(2)}) collective-permute-start(bf16[768,640]{1,0:T(8,128)(2,1)S(1)} %collective-permute-done.16.rest_2_), channel_id=1, source_target_pairs={{0,4},{4,0},{8,12},{12,8},{16,20},{20,16},{24,28},{28,24},{1,5},{5... | collective-permute-start | bytes 2949128 | tf_op jit(solution)/shard_map/ppermute | solution.py:876
  105.9 37.2 %collective-permute-start.19 = (bf16[768,640]{1,0:T(8,128)(2,1)S(1)}, bf16[768,640]{1,0:T(8,128)(2,1)}, u32[]{:S(2)}, u32[]{:S(2)}) collective-permute-start(bf16[768,640]{1,0:T(8,128)(2,1)S(1)} %collective-permute-done.18.rest_4_), channel_id=1, source_target_pairs={{0,4},{4,0},{8,12},{12,8},{16,20},{20,16},{24,28},{28,24},{1,5},{5... | collective-permute-start | bytes 2949128 | tf_op jit(solution)/shard_map/ppermute | solution.py:876
  118.0 22.5 %collective-permute-start.22 = (bf16[384,640]{1,0:T(8,128)(2,1)}, bf16[384,640]{1,0:T(8,128)(2,1)}, u32[]{:S(2)}, u32[]{:S(2)}) collective-permute-start(bf16[384,640]{1,0:T(8,128)(2,1)} %collective-permute-done.20.rest_6_), channel_id=1, source_target_pairs={{0,4},{4,0},{8,12},{12,8},{16,20},{20,16},{24,28},{28,24},{1,5},{5... | collective-permute-start | bytes 1474568 | tf_op jit(solution)/shard_map/ppermute | solution.py:876
  118.2 23.4 %collective-permute-start.23 = (bf16[384,640]{1,0:T(8,128)(2,1)}, bf16[384,640]{1,0:T(8,128)(2,1)}, u32[]{:S(2)}, u32[]{:S(2)}) collective-permute-start(bf16[384,640]{1,0:T(8,128)(2,1)} %collective-permute-done.21.rest_7_), channel_id=1, source_target_pairs={{0,4},{4,0},{8,12},{12,8},{16,20},{20,16},{24,28},{28,24},{1,5},{5... | collective-permute-start | bytes 1474568 | tf_op jit(solution)/shard_map/ppermute | solution.py:876
  132.9 32.1 %collective-permute-start.24 = (bf16[1024,128]{1,0:T(8,128)(2,1)}, bf16[1024,128]{1,0:T(8,128)(2,1)S(1)}, u32[]{:S(2)}, u32[]{:S(2)}) collective-permute-start(bf16[1024,128]{1,0:T(8,128)(2,1)} %get-tuple-element.124), channel_id=1, source_target_pairs={{0,1},{1,0},{2,3},{3,2},{4,5},{5,4},{6,7},{7,6},{8,9},{9,8},{10,11... | collective-permute-start | bytes 786440 | tf_op jit(solution)/shard_map/ppermute | solution.py:876
  140.6 24.5 %collective-permute-start.25 = (bf16[1024,128]{1,0:T(8,128)(2,1)}, bf16[1024,128]{1,0:T(8,128)(2,1)S(1)}, u32[]{:S(2)}, u32[]{:S(2)}) collective-permute-start(bf16[1024,128]{1,0:T(8,128)(2,1)} %get-tuple-element.124), channel_id=1, source_target_pairs={{0,2},{1,3},{2,0},{3,1},{4,6},{5,7},{6,4},{7,5},{8,10},{9,11},{10,... | collective-permute-start | bytes 786440 | tf_op jit(solution)/shard_map/ppermute | solution.py:876
  141.7 23.4 %collective-permute-start.26 = (bf16[1024,128]{1,0:T(8,128)(2,1)}, bf16[1024,128]{1,0:T(8,128)(2,1)S(1)}, u32[]{:S(2)}, u32[]{:S(2)}) collective-permute-start(bf16[1024,128]{1,0:T(8,128)(2,1)} %get-tuple-element.124), channel_id=1, source_target_pairs={{0,3},{1,2},{2,1},{3,0},{4,7},{5,6},{6,5},{7,4},{8,11},{9,10},{10,... | collective-permute-start | bytes 786440 | tf_op jit(solution)/shard_map/ppermute | solution.py:876
  165.0 59.1 %collective-permute-start.36 = (bf16[577,4096]{1,0:T(8,128)(2,1)}, bf16[577,4096]{1,0:T(8,128)(2,1)}, u32[]{:S(2)}, u32[]{:S(2)}) collective-permute-start(bf16[577,4096]{1,0:T(8,128)(2,1)} %get-tuple-element.130.refs_0_.active_ref), channel_id=1, source_target_pairs={{0,4},{4,0},{8,12},{12,8},{16,20},{20,16},{24,28},{28,24},{1,5},{5... | collective-permute-start | bytes 14180360 | tf_op jit(solution)/shard_map/ppermute | solution.py:876
  165.2 20.0 %collective-permute-start.28 = (bf16[3072,128]{1,0:T(8,128)(2,1)S(1)}, bf16[3072,128]{1,0:T(8,128)(2,1)S(1)}, u32[]{:S(2)}, u32[]{:S(2)}) collective-permute-start(bf16[3072,128]{1,0:T(8,128)(2,1)S(1)} %constant_dynamic-update-slice_fusion.3.rest_0_), channel_id=1, source_target_pairs={{0,8},{4,12},{8,0},{12,4},{16,24},{20,28},{24,16},{28,20},{1,9},{5... | collective-permute-start | bytes 2359304 | tf_op jit(solution)/shard_map/ppermute | solution.py:876
  165.8 21.0 %collective-permute-start.30 = (bf16[3072,128]{1,0:T(8,128)(2,1)S(1)}, bf16[3072,128]{1,0:T(8,128)(2,1)S(1)}, u32[]{:S(2)}, u32[]{:S(2)}) collective-permute-start(bf16[3072,128]{1,0:T(8,128)(2,1)S(1)} %constant_dynamic-update-slice_fusion.3.rest_0_), channel_id=1, source_target_pairs={{0,16},{4,20},{8,24},{12,28},{16,0},{20,4},{24,8},{28,12},{1,17},{... | collective-permute-start | bytes 2359304 | tf_op jit(solution)/shard_map/ppermute | solution.py:876
  167.3 20.1 %collective-permute-start.27 = (bf16[3072,128]{1,0:T(8,128)(2,1)S(1)}, bf16[3072,128]{1,0:T(8,128)(2,1)S(1)}, u32[]{:S(2)}, u32[]{:S(2)}) collective-permute-start(bf16[3072,128]{1,0:T(8,128)(2,1)S(1)} %constant_dynamic-update-slice_fusion.3.rest_0_), channel_id=1, source_target_pairs={{0,4},{4,0},{8,12},{12,8},{16,20},{20,16},{24,28},{28,24},{1,5},{5... | collective-permute-start | bytes 2359304 | tf_op jit(solution)/shard_map/ppermute | solution.py:876
  185.2 10.7 %collective-permute-start.32 = (bf16[1536,128]{1,0:T(8,128)(2,1)S(1)}, bf16[1536,128]{1,0:T(8,128)(2,1)S(1)}, u32[]{:S(2)}, u32[]{:S(2)}) collective-permute-start(bf16[1536,128]{1,0:T(8,128)(2,1)S(1)} %slice.139), channel_id=1, source_target_pairs={{0,16},{4,20},{8,24},{12,28},{16,0},{20,4},{24,8},{28,12},{1,17},{... | collective-permute-start | bytes 1179656 | tf_op jit(solution)/shard_map/ppermute | solution.py:876
  186.8 10.4 %collective-permute-start.33 = (bf16[1536,128]{1,0:T(8,128)(2,1)S(1)}, bf16[1536,128]{1,0:T(8,128)(2,1)S(1)}, u32[]{:S(2)}, u32[]{:S(2)}) collective-permute-start(bf16[1536,128]{1,0:T(8,128)(2,1)S(1)} %slice.140), channel_id=1, source_target_pairs={{0,8},{4,12},{8,0},{12,4},{16,24},{20,28},{24,16},{28,20},{1,9},{5... | collective-permute-start | bytes 1179656 | tf_op jit(solution)/shard_map/ppermute | solution.py:876
  187.4 11.5 %collective-permute-start.29 = (bf16[3072,128]{1,0:T(8,128)(2,1)S(1)}, bf16[3072,128]{1,0:T(8,128)(2,1)S(1)}, u32[]{:S(2)}, u32[]{:S(2)}) collective-permute-start(bf16[3072,128]{1,0:T(8,128)(2,1)S(1)} %collective-permute-done.28.rest_2_), channel_id=1, source_target_pairs={{0,4},{4,0},{8,12},{12,8},{16,20},{20,16},{24,28},{28,24},{1,5},{5... | collective-permute-start | bytes 2359304 | tf_op jit(solution)/shard_map/ppermute | solution.py:876
  187.5 11.5 %collective-permute-start.31 = (bf16[3072,128]{1,0:T(8,128)(2,1)S(1)}, bf16[3072,128]{1,0:T(8,128)(2,1)S(1)}, u32[]{:S(2)}, u32[]{:S(2)}) collective-permute-start(bf16[3072,128]{1,0:T(8,128)(2,1)S(1)} %collective-permute-done.30.rest_4_), channel_id=1, source_target_pairs={{0,4},{4,0},{8,12},{12,8},{16,20},{20,16},{24,28},{28,24},{1,5},{5... | collective-permute-start | bytes 2359304 | tf_op jit(solution)/shard_map/ppermute | solution.py:876
  214.0 58.5 %collective-permute-start.41 = (bf16[577,4096]{1,0:T(8,128)(2,1)}, bf16[577,4096]{1,0:T(8,128)(2,1)}, u32[]{:S(2)}, u32[]{:S(2)}) collective-permute-start(bf16[577,4096]{1,0:T(8,128)(2,1)} %get-tuple-element.128.pre_ref.refs_2_), channel_id=1, source_target_pairs={{0,4},{4,0},{8,12},{12,8},{16,20},{20,16},{24,28},{28,24},{1,5},{5... | collective-permute-start | bytes 14180360 | tf_op jit(solution)/shard_map/ppermute | solution.py:876
  214.2 9.8 %collective-permute-start.37 = (bf16[577,1024]{1,0:T(8,128)(2,1)}, bf16[577,1024]{1,0:T(8,128)(2,1)S(1)}, u32[]{:S(2)}, u32[]{:S(2)}) collective-permute-start(bf16[577,1024]{1,0:T(8,128)(2,1)} %bitcast.48), channel_id=1, source_target_pairs={{0,4},{4,0},{8,12},{12,8},{16,20},{20,16},{24,28},{28,24},{1,5},{5... | collective-permute-start | bytes 3545096 | tf_op jit(solution)/shard_map/ppermute | solution.py:876
  243.1 25.5 %collective-permute-start.38 = (bf16[2,2048,128]{2,1,0:T(8,128)(2,1)}, bf16[2,2048,128]{2,1,0:T(8,128)(2,1)S(1)}, u32[]{:S(2)}, u32[]{:S(2)}) collective-permute-start(bf16[2,2048,128]{2,1,0:T(8,128)(2,1)} %get-tuple-element.131), channel_id=1, source_target_pairs={{0,8},{4,12},{8,0},{12,4},{16,24},{20,28},{24,16},{28,20},{1,9},{5... | collective-permute-start | bytes 3145736 | tf_op jit(solution)/shard_map/ppermute | solution.py:876
  243.7 25.1 %collective-permute-start.39 = (bf16[2,2048,128]{2,1,0:T(8,128)(2,1)}, bf16[2,2048,128]{2,1,0:T(8,128)(2,1)S(1)}, u32[]{:S(2)}, u32[]{:S(2)}) collective-permute-start(bf16[2,2048,128]{2,1,0:T(8,128)(2,1)} %get-tuple-element.133), channel_id=1, source_target_pairs={{0,16},{4,20},{8,24},{12,28},{16,0},{20,4},{24,8},{28,12},{1,17},{... | collective-permute-start | bytes 3145736 | tf_op jit(solution)/shard_map/ppermute | solution.py:876
  244.8 27.7 %collective-permute-start.40 = (bf16[577,1024]{1,0:T(8,128)(2,1)}, bf16[577,1024]{1,0:T(8,128)(2,1)}, u32[]{:S(2)}, u32[]{:S(2)}) collective-permute-start(bf16[577,1024]{1,0:T(8,128)(2,1)} %get-tuple-element.120.normed_ref.refs_0_), channel_id=1, source_target_pairs={{0,4},{4,0},{8,12},{12,8},{16,20},{20,16},{24,28},{28,24},{1,5},{5... | collective-permute-start | bytes 3545096 | tf_op jit(solution)/shard_map/ppermute | solution.py:876
  269.9 16.0 %collective-permute-start.45 = (bf16[2048,128]{1,0:T(8,128)(2,1)}, bf16[2048,128]{1,0:T(8,128)(2,1)S(1)}, u32[]{:S(2)}, u32[]{:S(2)}) collective-permute-start(bf16[2048,128]{1,0:T(8,128)(2,1)} %get-tuple-element.206), channel_id=1, source_target_pairs={{0,8},{4,12},{8,0},{12,4},{16,24},{20,28},{24,16},{28,20},{1,9},{5... | collective-permute-start | bytes 1572872 | tf_op jit(solution)/shard_map/ppermute | solution.py:876
  271.7 14.2 %collective-permute-start.44 = (bf16[2048,128]{1,0:T(8,128)(2,1)S(1)}, bf16[2048,128]{1,0:T(8,128)(2,1)S(1)}, u32[]{:S(2)}, u32[]{:S(2)}) collective-permute-start(bf16[2048,128]{1,0:T(8,128)(2,1)S(1)} %get-tuple-element.208), channel_id=1, source_target_pairs={{0,16},{4,20},{8,24},{12,28},{16,0},{20,4},{24,8},{28,12},{1,17},{... | collective-permute-start | bytes 1572872 | tf_op jit(solution)/shard_map/ppermute | solution.py:876
  312.1 32.8 %collective-permute-start.47 = (bf16[3,577,1024]{2,1,0:T(8,128)(2,1)}, bf16[3,577,1024]{2,1,0:T(8,128)(2,1)}, u32[]{:S(2)}, u32[]{:S(2)}) collective-permute-start(bf16[3,577,1024]{2,1,0:T(8,128)(2,1)} %get-tuple-element.150.refs_2_.proj_ref), channel_id=1, source_target_pairs={{0,4},{4,0},{8,12},{12,8},{16,20},{20,16},{24,28},{28,24},{1,5},{5... | collective-permute-start | bytes 10635272 | tf_op jit(solution)/shard_map/ppermute | solution.py:876
  312.2 25.6 %collective-permute-start.42 = (bf16[2,512,512]{2,1,0:T(8,128)(2,1)S(1)}, bf16[2,512,512]{2,1,0:T(8,128)(2,1)S(1)}, u32[]{:S(2)}, u32[]{:S(2)}) collective-permute-start(bf16[2,512,512]{2,1,0:T(8,128)(2,1)S(1)} %copy-done.44), channel_id=1, source_target_pairs={{0,8},{4,12},{8,0},{12,4},{16,24},{20,28},{24,16},{28,20},{1,9},{5... | collective-permute-start | bytes 3145736 | tf_op jit(solution)/shard_map/ppermute | solution.py:876
  313.1 25.7 %collective-permute-start.43 = (bf16[2,512,512]{2,1,0:T(8,128)(2,1)}, bf16[2,512,512]{2,1,0:T(8,128)(2,1)}, u32[]{:S(2)}, u32[]{:S(2)}) collective-permute-start(bf16[2,512,512]{2,1,0:T(8,128)(2,1)} %get-tuple-element.143), channel_id=1, source_target_pairs={{0,16},{4,20},{8,24},{12,28},{16,0},{20,4},{24,8},{28,12},{1,17},{... | collective-permute-start | bytes 3145736 | tf_op jit(solution)/shard_map/ppermute | solution.py:876
  314.1 29.6 %collective-permute-start.48 = (bf16[577,1024]{1,0:T(8,128)(2,1)S(1)}, bf16[577,1024]{1,0:T(8,128)(2,1)}, u32[]{:S(2)}, u32[]{:S(2)}) collective-permute-start(bf16[577,1024]{1,0:T(8,128)(2,1)S(1)} %copy-done.6), channel_id=1, source_target_pairs={{0,4},{4,0},{8,12},{12,8},{16,20},{20,16},{24,28},{28,24},{1,5},{5... | collective-permute-start | bytes 3545096 | tf_op jit(solution)/shard_map/ppermute | solution.py:876
  314.1 30.9 %collective-permute-start.46 = (bf16[577,1024]{1,0:T(8,128)(2,1)}, bf16[577,1024]{1,0:T(8,128)(2,1)}, u32[]{:S(2)}, u32[]{:S(2)}) collective-permute-start(bf16[577,1024]{1,0:T(8,128)(2,1)} %get-tuple-element.154.refs_0_), channel_id=1, source_target_pairs={{0,4},{4,0},{8,12},{12,8},{16,20},{20,16},{24,28},{28,24},{1,5},{5... | collective-permute-start | bytes 3545096 | tf_op jit(solution)/shard_map/ppermute | solution.py:876
  338.7 58.4 %reduce-scatter.5.cloned.1.call-start = ((), (), s32[]{:S(2)}) async-start(), calls=%async_computation.3 | async-start | bytes 1310720 | tf_op jit(solution)/shard_map/reduce_scatter | solution.py:1044
  341.6 17.2 %collective-permute-start.51 = (bf16[512,512]{1,0:T(8,128)(2,1)}, bf16[512,512]{1,0:T(8,128)(2,1)S(1)}, u32[]{:S(2)}, u32[]{:S(2)}) collective-permute-start(bf16[512,512]{1,0:T(8,128)(2,1)} %get-tuple-element.202), channel_id=1, source_target_pairs={{0,8},{4,12},{8,0},{12,4},{16,24},{20,28},{24,16},{28,20},{1,9},{5... | collective-permute-start | bytes 1572872 | tf_op jit(solution)/shard_map/ppermute | solution.py:876
  343.7 15.1 %collective-permute-start.50 = (bf16[512,512]{1,0:T(8,128)(2,1)}, bf16[512,512]{1,0:T(8,128)(2,1)S(1)}, u32[]{:S(2)}, u32[]{:S(2)}) collective-permute-start(bf16[512,512]{1,0:T(8,128)(2,1)} %get-tuple-element.204), channel_id=1, source_target_pairs={{0,16},{4,20},{8,24},{12,28},{16,0},{20,4},{24,8},{28,12},{1,17},{... | collective-permute-start | bytes 1572872 | tf_op jit(solution)/shard_map/ppermute | solution.py:876
  360.2 64.3 %all-gather.5.cloned.1.call-start = ((), (), s32[]{:S(2)}) async-start(), calls=%async_computation.4 | async-start | bytes 2359296 | tf_op jit(solution)/shard_map/all_gather | solution.py:1042
  365.2 124.4 %all-gather.7.cloned.1.call-start = ((), (), s32[]{:S(2)}) async-start(), calls=%async_computation.5 | async-start | bytes 2359296 | tf_op jit(solution)/shard_map/all_gather | solution.py:1072
  365.9 31.2 %collective-permute-start.54 = (bf16[2,512,512]{2,1,0:T(8,128)(2,1)}, bf16[2,512,512]{2,1,0:T(8,128)(2,1)S(1)}, u32[]{:S(2)}, u32[]{:S(2)}) collective-permute-start(bf16[2,512,512]{2,1,0:T(8,128)(2,1)} %get-tuple-element.156), channel_id=1, source_target_pairs={{0,8},{4,12},{8,0},{12,4},{16,24},{20,28},{24,16},{28,20},{1,9},{5... | collective-permute-start | bytes 3145736 | tf_op jit(solution)/shard_map/ppermute | solution.py:876
  367.4 29.8 %collective-permute-start.55 = (bf16[2,512,512]{2,1,0:T(8,128)(2,1)}, bf16[2,512,512]{2,1,0:T(8,128)(2,1)}, u32[]{:S(2)}, u32[]{:S(2)}) collective-permute-start(bf16[2,512,512]{2,1,0:T(8,128)(2,1)} %get-tuple-element.158), channel_id=1, source_target_pairs={{0,16},{4,20},{8,24},{12,28},{16,0},{20,4},{24,8},{28,12},{1,17},{... | collective-permute-start | bytes 3145736 | tf_op jit(solution)/shard_map/ppermute | solution.py:876
  399.6 15.7 %collective-permute-start.58 = (bf16[512,512]{1,0:T(8,128)(2,1)}, bf16[512,512]{1,0:T(8,128)(2,1)}, u32[]{:S(2)}, u32[]{:S(2)}) collective-permute-start(bf16[512,512]{1,0:T(8,128)(2,1)} %fusion.11), channel_id=1, source_target_pairs={{0,8},{4,12},{8,0},{12,4},{16,24},{20,28},{24,16},{28,20},{1,9},{5... | collective-permute-start | bytes 1572872 | tf_op jit(solution)/shard_map/ppermute | solution.py:876
  400.9 15.9 %collective-permute-start.57 = (bf16[512,512]{1,0:T(8,128)(2,1)}, bf16[512,512]{1,0:T(8,128)(2,1)}, u32[]{:S(2)}, u32[]{:S(2)}) collective-permute-start(bf16[512,512]{1,0:T(8,128)(2,1)} %fusion.10), channel_id=1, source_target_pairs={{0,16},{4,20},{8,24},{12,28},{16,0},{20,4},{24,8},{28,12},{1,17},{... | collective-permute-start | bytes 1572872 | tf_op jit(solution)/shard_map/ppermute | solution.py:876
  419.3 11.3 %collective-permute-start.60 = (bf16[256,512]{1,0:T(8,128)(2,1)S(1)}, bf16[256,512]{1,0:T(8,128)(2,1)S(1)}, u32[]{:S(2)}, u32[]{:S(2)}) collective-permute-start(bf16[256,512]{1,0:T(8,128)(2,1)S(1)} %get-tuple-element.211), channel_id=1, source_target_pairs={{0,1},{1,0},{2,3},{3,2},{4,5},{5,4},{6,7},{7,6},{8,9},{9,8},{10,11... | collective-permute-start | bytes 786440 | tf_op jit(solution)/shard_map/ppermute | solution.py:876
  419.4 21.4 %collective-permute-start.61 = (bf16[256,512]{1,0:T(8,128)(2,1)S(1)}, bf16[256,512]{1,0:T(8,128)(2,1)S(1)}, u32[]{:S(2)}, u32[]{:S(2)}) collective-permute-start(bf16[256,512]{1,0:T(8,128)(2,1)S(1)} %get-tuple-element.212), channel_id=1, source_target_pairs={{0,2},{1,3},{2,0},{3,1},{4,6},{5,7},{6,4},{7,5},{8,10},{9,11},{10,... | collective-permute-start | bytes 786440 | tf_op jit(solution)/shard_map/ppermute | solution.py:876
  421.0 19.8 %collective-permute-start.62 = (bf16[256,512]{1,0:T(8,128)(2,1)S(1)}, bf16[256,512]{1,0:T(8,128)(2,1)S(1)}, u32[]{:S(2)}, u32[]{:S(2)}) collective-permute-start(bf16[256,512]{1,0:T(8,128)(2,1)S(1)} %get-tuple-element.210), channel_id=1, source_target_pairs={{0,3},{1,2},{2,1},{3,0},{4,7},{5,6},{6,5},{7,4},{8,11},{9,10},{10,... | collective-permute-start | bytes 786440 | tf_op jit(solution)/shard_map/ppermute | solution.py:876
  441.2 6.4 %collective-permute-start.65 = (bf16[256,512]{1,0:T(8,128)(2,1)S(1)}, bf16[256,512]{1,0:T(8,128)(2,1)S(1)}, u32[]{:S(2)}, u32[]{:S(2)}) collective-permute-start(bf16[256,512]{1,0:T(8,128)(2,1)S(1)} %add_convert_fusion.18.refs_0_), channel_id=1, source_target_pairs={{0,8},{4,12},{8,0},{12,4},{16,24},{20,28},{24,16},{28,20},{1,9},{5... | collective-permute-start | bytes 786440 | tf_op jit(solution)/shard_map/ppermute | solution.py:876
  442.3 10.8 %collective-permute-start.67 = (bf16[256,512]{1,0:T(8,128)(2,1)S(1)}, bf16[256,512]{1,0:T(8,128)(2,1)S(1)}, u32[]{:S(2)}, u32[]{:S(2)}) collective-permute-start(bf16[256,512]{1,0:T(8,128)(2,1)S(1)} %add_convert_fusion.18.refs_0_), channel_id=1, source_target_pairs={{0,16},{4,20},{8,24},{12,28},{16,0},{20,4},{24,8},{28,12},{1,17},{... | collective-permute-start | bytes 786440 | tf_op jit(solution)/shard_map/ppermute | solution.py:876
  447.6 10.7 %collective-permute-start.69 = (bf16[256,512]{1,0:T(8,128)(2,1)S(1)}, bf16[256,512]{1,0:T(8,128)(2,1)S(1)}, u32[]{:S(2)}, u32[]{:S(2)}) collective-permute-start(bf16[256,512]{1,0:T(8,128)(2,1)S(1)} %collective-permute-done.65.refs_2_), channel_id=1, source_target_pairs={{0,16},{4,20},{8,24},{12,28},{16,0},{20,4},{24,8},{28,12},{1,17},{... | collective-permute-start | bytes 786440 | tf_op jit(solution)/shard_map/ppermute | solution.py:876
  448.3 35.6 %collective-permute-start.64 = (bf16[256,512]{1,0:T(8,128)(2,1)S(1)}, bf16[256,512]{1,0:T(8,128)(2,1)S(1)}, u32[]{:S(2)}, u32[]{:S(2)}) collective-permute-start(bf16[256,512]{1,0:T(8,128)(2,1)S(1)} %add_convert_fusion.18.refs_0_), channel_id=1, source_target_pairs={{0,4},{4,0},{8,12},{12,8},{16,20},{20,16},{24,28},{28,24},{1,5},{5... | collective-permute-start | bytes 786440 | tf_op jit(solution)/shard_map/ppermute | solution.py:876
  448.3 35.6 %collective-permute-start.66 = (bf16[256,512]{1,0:T(8,128)(2,1)S(1)}, bf16[256,512]{1,0:T(8,128)(2,1)S(1)}, u32[]{:S(2)}, u32[]{:S(2)}) collective-permute-start(bf16[256,512]{1,0:T(8,128)(2,1)S(1)} %collective-permute-done.65.refs_2_), channel_id=1, source_target_pairs={{0,4},{4,0},{8,12},{12,8},{16,20},{20,16},{24,28},{28,24},{1,5},{5... | collective-permute-start | bytes 786440 | tf_op jit(solution)/shard_map/ppermute | solution.py:876
  453.1 30.8 %collective-permute-start.68 = (bf16[256,512]{1,0:T(8,128)(2,1)S(1)}, bf16[256,512]{1,0:T(8,128)(2,1)S(1)}, u32[]{:S(2)}, u32[]{:S(2)}) collective-permute-start(bf16[256,512]{1,0:T(8,128)(2,1)S(1)} %collective-permute-done.67.refs_4_), channel_id=1, source_target_pairs={{0,4},{4,0},{8,12},{12,8},{16,20},{20,16},{24,28},{28,24},{1,5},{5... | collective-permute-start | bytes 786440 | tf_op jit(solution)/shard_map/ppermute | solution.py:876
  458.3 25.5 %collective-permute-start.70 = (bf16[256,512]{1,0:T(8,128)(2,1)S(1)}, bf16[256,512]{1,0:T(8,128)(2,1)S(1)}, u32[]{:S(2)}, u32[]{:S(2)}) collective-permute-start(bf16[256,512]{1,0:T(8,128)(2,1)S(1)} %collective-permute-done.69.refs_6_), channel_id=1, source_target_pairs={{0,4},{4,0},{8,12},{12,8},{16,20},{20,16},{24,28},{28,24},{1,5},{5... | collective-permute-start | bytes 786440 | tf_op jit(solution)/shard_map/ppermute | solution.py:876
  468.3 7.3 %collective-permute-start.59 = (f32[4,3072]{1,0:T(4,128)S(1)}, f32[4,3072]{1,0:T(4,128)S(1)}, u32[]{:S(2)}, u32[]{:S(2)}) collective-permute-start(f32[4,3072]{1,0:T(4,128)S(1)} %add.123), channel_id=1, source_target_pairs={{0,1},{1,0},{2,3},{3,2},{4,5},{5,4},{6,7},{7,6},{8,9},{9,8},{10,11... | collective-permute-start | bytes 147464 | tf_op jit(solution)/shard_map/ppermute | solution.py:876
  (64 other events, 730.6 us)
Sparse Core Ops, SparseCore 0:
  338.8 26.3 reduce-scatter.2
  367.5 25.7 reduce-scatter.4
  395.2 29.1 all-gather.4
  426.2 32.1 all-gather.6

commit v3 on v2

--- a/solution.py
+++ b/solution.py
@@ -7,6 +7,7 @@
 
 
 BLOCKS = 8
+ROW, PART, BLOCK = range(3)
 LANES = 128
 TILE = 512
 HD = 64
@@ -47,14 +48,14 @@
         pltpu.make_async_copy(source, target.at[rows, columns], sems.at[key]).start()
 
     own_rows = pl.ds(aligned(mine * share, share), share)
-    if mode == "row":
+    if mode == ROW:
         pltpu.make_async_copy(own, target.at[own_rows, :], sems.at[0]).start()
     for which, (source, size, base) in enumerate(strips):
         for at in range(BLOCKS):
             block = jnp.bitwise_xor(where[0], at)
             columns = pl.ds(aligned(base + block * size, LANES), size)
-            key = {"part": which, "block": at}.get(mode)
-            if mode != "row":
+            key = which if mode == PART else at
+            if mode != ROW:
                 go(own.at[:, columns], own_rows, columns, key)
             for hop in range(1, groups):
                 first = jnp.bitwise_xor(mine, hop) * share
@@ -69,7 +70,7 @@
                             ref.at[begin - low : end - low, source : source + size],
                             rows,
                             columns,
-                            hop if mode == "row" else key,
+                            hop if mode == ROW else key,
                         )
                     low = high
 
@@ -128,7 +129,7 @@
 
         @pl.when(at == 0)
         def _():
-            start_loads(where_ref, own_ref, piece_refs, strips, weight, sems, "part")
+            start_loads(where_ref, own_ref, piece_refs, strips, weight, sems, PART)
             normed, _ = center(image_ref[...].astype(jnp.float32))
             normed_ref[...] = (normed * gain_ref[...] + shift_ref[...]).astype(jnp.bfloat16)
 
@@ -171,7 +172,6 @@
         ],
         cost_estimate=cost(2 * tokens * width * wide, 2 * width * wide),
         compiler_params=params(),
-        name="qkv_forward",
     )(where, image, gain, shift, bias, own, *flat(pieces))
 
 
@@ -184,7 +184,7 @@
     def body(where_ref, image_ref, attended_ref, bias_ref, gain_ref, shift_ref, own_ref, *rest):
         piece_refs = regroup(rest[: len(flat(pieces))], pieces)
         residual_ref, normed_ref, weight, sems = rest[len(flat(pieces)) :]
-        start_loads(where_ref, own_ref, piece_refs, [(source, LANES, 0)], weight, sems, "row")
+        start_loads(where_ref, own_ref, piece_refs, [(source, LANES, 0)], weight, sems, ROW)
         for hop in range(groups):
             wait_rows(where_ref, weight, sems, hop, share)
 
@@ -221,7 +221,6 @@
         ],
         cost_estimate=cost(2 * tokens * width * width, 2 * width * width),
         compiler_params=params(),
-        name="out_forward",
     )(where, image, attended, bias, gain, shift, own, *flat(pieces))
 
 
@@ -237,7 +236,7 @@
 
         @pl.when(at == 0)
         def _():
-            start_loads(where_ref, own_ref, piece_refs, [(0, size, 0)], weight, sems, "block")
+            start_loads(where_ref, own_ref, piece_refs, [(0, size, 0)], weight, sems, BLOCK)
 
         columns = pl.ds(aligned(jnp.bitwise_xor(where_ref[0], at) * size, size), size)
         finish(weight.at[:, columns], sems.at[at])
@@ -265,7 +264,6 @@
         out_shape=[jax.ShapeDtypeStruct((tokens, wide), jnp.bfloat16)] * 2,
         cost_estimate=cost(2 * tokens * width * wide, 2 * width * wide),
         compiler_params=params(),
-        name="up_forward",
     )(where, normed, bias, own, *flat(pieces))
 
 
@@ -283,7 +281,7 @@
 
         @pl.when(at == 0)
         def _():
-            start_loads(where_ref, own_ref, piece_refs, [(0, LANES, 0)], weight, sems, "row")
+            start_loads(where_ref, own_ref, piece_refs, [(0, LANES, 0)], weight, sems, ROW)
             for hop in range(groups):
                 wait_rows(where_ref, weight, sems, hop, share)
 
@@ -313,7 +311,6 @@
         out_shape=jax.ShapeDtypeStruct((tokens, width), jnp.bfloat16),
         cost_estimate=cost(2 * tokens * width * wide, 2 * width * wide),
         compiler_params=params(),
-        name="down_forward",
     )(where, residual, active, bias, own, *flat(pieces))
 
 
@@ -332,7 +329,7 @@
 
         @pl.when(at == 0)
         def _():
-            start_loads(where_ref, own_ref, piece_refs, [(0, LANES, 0)], weight, sems, "row")
+            start_loads(where_ref, own_ref, piece_refs, [(0, LANES, 0)], weight, sems, ROW)
 
         hop = at // per
 
@@ -369,7 +366,6 @@
         ],
         cost_estimate=cost(2 * tokens * width * wide, 2 * width * wide),
         compiler_params=params(),
-        name="down_backward",
     )(where, grad_block, slope, own, *flat(pieces))
 
 
@@ -390,9 +386,9 @@
 
         @pl.when(at == 0)
         def _():
-            start_loads(where_ref, up_ref, piece_refs, [(0, size, 0)], weight, sems, "row")
+            start_loads(where_ref, up_ref, piece_refs, [(0, size, 0)], weight, sems, ROW)
             start_loads(
-                where_ref, own_ref, piece_refs, [(size, LANES, 0)], weight_out, out_sems, "row"
+                where_ref, own_ref, piece_refs, [(size, LANES, 0)], weight_out, out_sems, ROW
             )
 
         wait_rows(where_ref, weight, sems, at, share)
@@ -448,7 +444,6 @@
         + [jax.ShapeDtypeStruct((1, width), jnp.float32)] * 4,
         cost_estimate=cost(2 * tokens * width * (wide + width), 2 * width * (wide + width)),
         compiler_params=params(),
-        name="middle_backward",
     )(where, grad_pre, grad_block, residual, gain, own_up, own_out, *flat(pieces))
 
 
@@ -466,7 +461,7 @@
 
         @pl.when(at == 0)
         def _():
-            start_loads(where_ref, own_ref, piece_refs, strips, weight, sems, "row")
+            start_loads(where_ref, own_ref, piece_refs, strips, weight, sems, ROW)
 
         wait_rows(where_ref, weight, sems, at, share)
         rows = pl.ds(aligned(jnp.bitwise_xor(where_ref[1], at) * share, share), share)
@@ -511,7 +506,6 @@
         ],
         cost_estimate=cost(2 * tokens * width * wide, 2 * width * wide),
         compiler_params=params(),
-        name="qkv_backward",
     )(where, grad_proj, image, grad_res, gain, own, *flat(pieces))
 
 
@@ -550,7 +544,6 @@
         ],
         cost_estimate=cost(16 * tokens * tokens * width, 8 * tokens * width),
         compiler_params=params(),
-        name="attention_forward",
     )(projected, projected, projected)
 
 
@@ -595,7 +588,6 @@
         + [jax.ShapeDtypeStruct((1, width), jnp.float32)] * 2,
         cost_estimate=cost(40 * tokens * tokens * width, 16 * tokens * width),
         compiler_params=params(),
-        name="attention_backward",
     )(projected, projected, projected, grad_mixed, totals)
 
 
@@ -683,56 +675,131 @@
         out_shape=[jax.ShapeDtypeStruct((2, rows // 2, width), jnp.bfloat16)] * 4,
         cost_estimate=cost(16 * rows * tokens * width, 8 * rows * width + 4 * tokens * rows),
         compiler_params=params(),
-        name="weight_grads",
     )(where, *operands)
 
 
-def pack_blocks(where, qkv, out, up, down, vectors):
-    rows, _ = qkv.shape
-    size = up.shape[1] // BLOCKS
-    lengths = [vec.shape[1] for vec in vectors]
-    row = 3 * LANES
-
-    def body(where_ref, query_ref, key_ref, value_ref, out_ref, up_ref, down_ref, *rest):
-        vector_refs = rest[: len(vectors)]
-        first_ref, second_ref, third_ref = rest[len(vectors) :]
-        first_ref[:rows, :LANES] = query_ref[...]
-        first_ref[:rows, LANES : 2 * LANES] = key_ref[...]
-        first_ref[:rows, 2 * LANES :] = value_ref[...]
-        flat_vectors = jnp.concatenate([ref[...].astype(jnp.float32) for ref in vector_refs], axis=1)
-        total = flat_vectors.shape[1]
-        lines = [flat_vectors[:, at : at + row] for at in range(0, total, row)]
-        lines.append(jnp.zeros((16 - len(lines), row), jnp.float32))
-        first_ref[rows:, :] = jnp.concatenate(lines, axis=0).astype(jnp.bfloat16)
-        second_ref[:, :size] = up_ref[...]
-        second_ref[:, size:] = out_ref[...]
-        third_ref[...] = down_ref[...]
-
-    def mine(array, width, part=0):
+def weight_grads_flipped(where, left, left_pair, right, right_pair, groups):
+    tokens, rows = left.shape
+    share = rows // groups
+    step = min(TILE, share)
+    per = share // step
+    count = rows // step
+    half = count // 2
+    span = 4 * LANES
+
+    def body(where_ref, left_ref, pair_ref, right_ref, right_pair_ref, *rest):
+        send_a, keep_a, send_b, keep_b, joined, turned, sems = rest
+        at = pl.program_id(0)
+
+        @pl.when(at == 0)
+        def _():
+            for side, source in enumerate((right_ref, right_pair_ref)):
+                for which in range(4):
+                    block = jnp.bitwise_xor(where_ref[0], 2 * which)
+                    columns = pl.ds(aligned(block * LANES, LANES), LANES)
+                    pltpu.make_async_copy(
+                        source.at[:, columns],
+                        joined.at[side, :, which * LANES : (which + 1) * LANES],
+                        sems.at[side],
+                    ).start()
+            for side in range(2):
+                finish(joined.at[side], sems.at[side])
+                turned[side] = joined[side].T
+
+        total = product(turned[0], left_ref[...]) + product(turned[1], pair_ref[...])
+        total = total.astype(jnp.bfloat16)
+
+        def put(targets):
+            for which in range(4):
+                ref, slot = targets[which]
+                ref[slot, 0] = total[which * LANES : (which + 1) * LANES, :]
+
+        @pl.when(at < half)
+        def _():
+            put([(keep_a, 0), (send_a, 0), (keep_a, 1), (send_a, 1)])
+
+        @pl.when(at >= half)
+        def _():
+            put([(keep_b, 0), (keep_b, 1), (send_b, 0), (send_b, 1)])
+
+    def spec(clip):
         return pl.BlockSpec(
-            (array.shape[0], width),
+            (2, 1, LANES, step), lambda at, _: (0, clip(at) // per, 0, clip(at) % per)
+        )
+
+    spec_a = spec(lambda at: jnp.minimum(at, half - 1))
+    spec_b = spec(lambda at: jnp.maximum(at - half, 0))
+    return pl.pallas_call(
+        body,
+        grid_spec=pltpu.PrefetchScalarGridSpec(
+            num_scalar_prefetch=1,
+            grid=(count,),
+            in_specs=[pl.BlockSpec((tokens, step), lambda at, _: (0, at))] * 2 + [ANY] * 2,
+            out_specs=[spec_a, spec_a, spec_b, spec_b],
+            scratch_shapes=[
+                pltpu.VMEM((2, tokens, span), jnp.bfloat16),
+                pltpu.VMEM((2, span, tokens), jnp.bfloat16),
+                pltpu.SemaphoreType.DMA((2,)),
+            ],
+        ),
+        out_shape=[jax.ShapeDtypeStruct((2, groups // 2, LANES, share), jnp.bfloat16)] * 4,
+        cost_estimate=cost(4 * rows * tokens * span, 2 * rows * span + 4 * tokens * rows),
+        compiler_params=params(),
+    )(where, left, left_pair, right, right_pair)
+
+
+def finish_flipped(blocks):
+    count, size, rows = blocks.shape
+    step = min(rows, 256)
+
+    def body(in_ref, out_ref):
+        for at in range(count):
+            out_ref[:, at * size : (at + 1) * size] = in_ref[at].astype(jnp.float32).T
+
+    return pl.pallas_call(
+        body,
+        grid=(rows // step,),
+        in_specs=[pl.BlockSpec((count, size, step), lambda at: (0, 0, at))],
+        out_specs=pl.BlockSpec((step, count * size), lambda at: (at, 0)),
+        out_shape=jax.ShapeDtypeStruct((rows, count * size), jnp.float32),
+        compiler_params=params(),
+    )(blocks)
+
+
+def pick_blocks(where, sources, outs):
+    flat_outs = [item for out in outs for item in out]
+
+    def body(where_ref, *refs):
+        in_refs, out_refs = refs[: len(flat_outs)], refs[len(flat_outs) :]
+        at = 0
+        for out_ref, out in zip(out_refs, outs):
+            base = 0
+            for _, size, _ in out:
+                out_ref[:, base : base + size] = in_refs[at][...]
+                base += size
+                at += 1
+
+    def mine(source, size, part):
+        return pl.BlockSpec(
+            (sources[source].shape[0], size),
             lambda at, where_ref: (0, part * BLOCKS + where_ref[0]),
         )
 
-    whole = lambda shape: pl.BlockSpec(shape, lambda at, _: (0, 0))
-    shapes = [(rows + 16, row), (rows, size + LANES), (down.shape[0], LANES)]
+    shapes = [(sources[out[0][0]].shape[0], sum(item[1] for item in out)) for out in outs]
     return pl.pallas_call(
         body,
         grid_spec=pltpu.PrefetchScalarGridSpec(
             num_scalar_prefetch=1,
             grid=(1,),
-            in_specs=[mine(qkv, LANES, part) for part in range(3)]
-            + [mine(out, LANES), mine(up, size), mine(down, LANES)]
-            + [whole((1, length)) for length in lengths],
-            out_specs=[whole(shape) for shape in shapes],
+            in_specs=[mine(*item) for item in flat_outs],
+            out_specs=[pl.BlockSpec(shape, lambda at, _: (0, 0)) for shape in shapes],
         ),
         out_shape=[jax.ShapeDtypeStruct(shape, jnp.bfloat16) for shape in shapes],
         compiler_params=params(),
-        name="pack_blocks",
-    )(where, qkv, qkv, qkv, out, up, down, *vectors)
-
-
-def unpack_vectors(where, sources, rows, lengths, pair_at, width):
+    )(where, *[sources[item[0]] for item in flat_outs])
+
+
+def unpack_vectors(where, sources, lengths, pair_at, width):
     groups = len(sources)
     row = sources[0].shape[1]
     outs = [3 * width if at == pair_at else length * groups for at, length in enumerate(lengths)]
@@ -759,12 +826,11 @@
         grid_spec=pltpu.PrefetchScalarGridSpec(
             num_scalar_prefetch=1,
             grid=(1,),
-            in_specs=[pl.BlockSpec((16, row), lambda at, _: (rows // 16, 0))] * groups,
+            in_specs=[pl.BlockSpec((16, row), lambda at, _: (0, 0))] * groups,
             out_specs=[pl.BlockSpec((1, size), lambda at, _: (0, 0)) for size in outs],
         ),
         out_shape=[jax.ShapeDtypeStruct((1, size), jnp.float32) for size in outs],
         compiler_params=params(),
-        name="unpack_vectors",
     )(where, *sources)
 
 
@@ -783,7 +849,6 @@
         body,
         out_shape=jax.ShapeDtypeStruct((groups, total), jnp.float32),
         compiler_params=params(),
-        name="pack_sums",
     )(*vectors)
 
 
@@ -811,26 +876,29 @@
         ),
         out_shape=[jax.ShapeDtypeStruct((1, length), jnp.float32) for length in lengths],
         compiler_params=params(),
-        name="unpack_sums",
     )(where, first, second)
 
 
-def finish_blocks(blocks):
-    count, rows, size = blocks.shape
+def finish_blocks(blocks, sizes):
+    count, rows, width = blocks.shape
     step = min(rows, 128)
 
-    def body(in_ref, out_ref):
-        for at in range(count):
-            out_ref[:, at * size : (at + 1) * size] = in_ref[at].astype(jnp.float32)
+    def body(in_ref, *out_refs):
+        base = 0
+        for out_ref, size in zip(out_refs, sizes):
+            for at in range(count):
+                out_ref[:, at * size : (at + 1) * size] = in_ref[
+                    at, :, base : base + size
+                ].astype(jnp.float32)
+            base += size
 
     return pl.pallas_call(
         body,
         grid=(rows // step,),
-        in_specs=[pl.BlockSpec((count, step, size), lambda at: (0, at, 0))],
-        out_specs=pl.BlockSpec((step, count * size), lambda at: (at, 0)),
-        out_shape=jax.ShapeDtypeStruct((rows, count * size), jnp.float32),
-        compiler_params=params(),
-        name="finish_blocks",
+        in_specs=[pl.BlockSpec((count, step, width), lambda at: (0, at, 0))],
+        out_specs=[pl.BlockSpec((step, count * size), lambda at: (at, 0)) for size in sizes],
+        out_shape=[jax.ShapeDtypeStruct((rows, count * size), jnp.float32) for size in sizes],
+        compiler_params=params(),
     )(blocks)
 
 
@@ -867,11 +935,13 @@
             jax.ShapeDtypeStruct((rows, totals[out]), jnp.float32) for out in sorted(totals)
         ],
         compiler_params=params(),
-        name="finish_grads",
     )(where, *pieces)
 
 
-def exchange(tensor, mask, axis="rep"):
+REP, GRP = "rep", "grp"
+
+
+def exchange(tensor, mask, axis=REP):
     size = lax.axis_size(axis)
     return lax.ppermute(tensor, axis, [(at, at ^ mask) for at in range(size)])
 
@@ -881,7 +951,7 @@
 
 
 def all_hops(block):
-    return [exchange(block, hop, "grp") for hop in range(1, lax.axis_size("grp"))]
+    return [exchange(block, hop, GRP) for hop in range(1, lax.axis_size(GRP))]
 
 
 def spread(own):
@@ -894,7 +964,7 @@
     pieces = []
     for piece in ((own,), (by_x,), (by_y,), (top, bottom)):
         pieces += [piece, tuple(exchange(array, 1) for array in piece)]
-    return pieces, sent, (top, bottom)
+    return pieces, sent
 
 
 def add_rounded(left, right):
@@ -918,20 +988,28 @@
 def block_total(rest, got):
     total = jnp.concatenate([add_rounded(*pair) for pair in zip(rest, got)], axis=0)
     mask = BLOCKS
-    while mask < lax.axis_size("rep"):
+    while mask < lax.axis_size(REP):
         total = add_rounded(total, exchange(total, mask))
         mask *= 2
     return total
 
 
+def scatter(total):
+    return lax.psum_scatter(total, GRP, scatter_dimension=0, tiled=True)
+
+
+def gather(own):
+    return lax.all_gather(own, REP, axis=0, tiled=False)[:BLOCKS]
+
+
 def grp_sum(total):
-    groups = lax.axis_size("grp")
+    groups = lax.axis_size(GRP)
     share = total.shape[0] // groups
-    place = lax.axis_index("grp")
+    place = lax.axis_index(GRP)
     sent = [
         lax.dynamic_slice_in_dim(total, (place ^ hop) * share, share, 0) for hop in range(groups)
     ]
-    got = [exchange(sent[hop], hop, "grp") for hop in range(1, groups)]
+    got = [exchange(sent[hop], hop, GRP) for hop in range(1, groups)]
     return sent[0], got
 
 
@@ -958,30 +1036,36 @@
     fc2_weight,
     fc2_bias,
 ):
-    n_grp = lax.axis_size("grp")
-    place = jnp.bitwise_and(lax.axis_index("rep"), BLOCKS - 1)
-    where = jnp.stack([place, lax.axis_index("grp")])
-    rows, width = out_weight.shape
+    groups = lax.axis_size(GRP)
+    place = jnp.bitwise_and(lax.axis_index(REP), BLOCKS - 1)
+    where = jnp.stack([place, lax.axis_index(GRP)])
+    _, width = out_weight.shape
     hidden_block = fc1_weight.shape[1] // BLOCKS
 
+    (block_a,) = pick_blocks(where, [qkv_weight], [[(0, LANES, part) for part in range(3)]])
+    got_a = all_hops(block_a)
+    block_b, block_c = pick_blocks(
+        where,
+        [fc1_weight, out_weight, fc2_weight],
+        [[(0, hidden_block, 0), (1, LANES, 0)], [(2, LANES, 0)]],
+    )
     vectors = (ln1_gain, ln1_shift, qv_bias, out_bias, ln2_gain, ln2_shift, fc1_bias, fc2_bias)
     sizes = [vec.shape[0] for vec in vectors]
-    block_a, block_b, block_c = pack_blocks(
-        where,
-        qkv_weight,
-        out_weight,
-        fc1_weight,
-        fc2_weight,
-        [vec.reshape(1, -1) for vec in vectors],
-    )
-    got_a = all_hops(block_a)
-    pieces_a, sent_a, _ = spread(jnp.concatenate([got[:rows] for got in got_a]))
-    got_b = tie(all_hops(tie(block_b, got_a)), sent_a)
-    pieces_b, sent_b, _ = spread(jnp.concatenate(got_b))
-    got_c = tie(all_hops(tie(block_c, got_b)), sent_b)
-    pieces_c, _, _ = spread(jnp.concatenate(got_c))
+    length = 16 * 2 * LANES
+    packed, offset = jnp.zeros((length,), jnp.bfloat16), 0
+    for vec, size in zip(vectors, sizes):
+        packed = packed + jnp.pad(vec, (offset, length - offset - size))
+        offset += size
+    packed = packed.reshape(16, 2 * LANES)
+    got_v = all_hops(packed)
+
+    pieces_a, sent_a = spread(jnp.concatenate(got_a))
+    got_b = all_hops(tie(block_b, got_a))
+    pieces_b, sent_b = spread(jnp.concatenate(tie(got_b, sent_a)))
+    got_c = all_hops(tie(block_c, got_b))
+    pieces_c, _ = spread(jnp.concatenate(tie(got_c, sent_b)))
     gain_1, shift_1, bias_in, bias_attn, gain_2, shift_2, bias_up, bias_down = unpack_vectors(
-        where, [block_a] + got_a, rows, sizes, 2, width
+        where, [packed] + got_v, sizes, 2, width
     )
 
     image = images[0]
@@ -1001,8 +1085,8 @@
 
     grad_pre, sum_up = down_backward(where, grad_block, slope, fc2_weight, pieces_c)
     pre_pair = exchange(grad_pre, 1)
-    down_parts = weight_grads(
-        tie(where, grad_pre), [(active, active_pair, grad_block, cot_pair, LANES)]
+    down_parts = weight_grads_flipped(
+        tie(where, grad_pre), active, active_pair, grad_block, cot_pair, groups
     )
     down_got = first_sends(down_parts)
     middle = middle_backward(
@@ -1021,29 +1105,28 @@
     down_rest, down_got = second_sends(down_parts, tie(down_got, grad_res))
     up_parts = weight_grads(
         tie(where, grad_res, down_rest),
-        [(normed_mid, mid_pair, grad_pre, pre_pair, hidden_block)],
+        [
+            (normed_mid, mid_pair, grad_pre, pre_pair, hidden_block),
+            (attended, attended_pair, grad_res_b, res_pair, LANES),
+        ],
     )
     up_got = first_sends(up_parts)
     down_total = block_total(down_rest, tie(down_got, up_parts))
-    down_own = lax.psum_scatter(down_total, "grp", scatter_dimension=0, tiled=True)
+    down_own = scatter(down_total)
     grad_proj, sum_query, sum_value = attention_backward(
         projected, tie(grad_attended, up_parts, down_total), totals
     )
     proj_pair = exchange(grad_proj, 1)
     up_rest, up_got = second_sends(up_parts, tie(up_got, grad_proj))
-    attn_parts = weight_grads(
-        tie(where, up_rest),
-        [
-            (normed_in, normed_pair, grad_proj, proj_pair, LANES),
-            (attended, attended_pair, grad_res_b, res_pair, LANES),
-        ],
-    )
-    attn_got = first_sends(attn_parts)
-    down_blocks = lax.all_gather(tie(down_own, attn_parts), "rep", axis=0, tiled=False)[:BLOCKS]
-    up_total = block_total(up_rest, tie(up_got, attn_parts))
-    up_own = lax.psum_scatter(up_total, "grp", scatter_dimension=0, tiled=True)
+    down_blocks = gather(tie(down_own, grad_proj))
+    qkv_parts = weight_grads(
+        tie(where, up_rest), [(normed_in, normed_pair, grad_proj, proj_pair, LANES)]
+    )
+    qkv_got = first_sends(qkv_parts)
+    up_total = block_total(up_rest, tie(up_got, qkv_parts))
+    up_own = scatter(up_total)
     input_grad, sum_gain_1, sum_shift_1 = qkv_backward(
-        tie(where, attn_parts, up_total),
+        tie(where, qkv_parts, up_total),
         grad_proj,
         image,
         grad_res,
@@ -1062,41 +1145,40 @@
             sum_up,
             sum_top,
         ],
-        n_grp,
+        groups,
     )
     got = exchange(sums, 1)
+    grad_down = finish_flipped(tie(down_blocks, sums)[:, 0])
+    sums = sums + tie(got, grad_down)
+    qkv_rest, qkv_got = second_sends(qkv_parts, tie(qkv_got, grad_down))
+    got = exchange(tie(sums, qkv_rest), 2)
     block_out = down_forward(
-        tie(where, input_grad, sums), residual, active, bias_down, fc2_weight, pieces_c
-    )
+        tie(where, input_grad, sums, qkv_rest), residual, active, bias_down, fc2_weight, pieces_c
+    )
+    up_blocks = gather(tie(up_own, block_out))
     sums = sums + tie(got, block_out)
-    up_blocks = lax.all_gather(tie(up_own, block_out), "rep", axis=0, tiled=False)[:BLOCKS]
-    attn_rest, attn_got = second_sends(attn_parts, tie(attn_got, block_out))
-    sums = sums + tie(exchange(sums, 2), attn_rest)
     mask = BLOCKS
-    while mask < lax.axis_size("rep"):
+    while mask < lax.axis_size(REP):
         sums = sums + exchange(sums, mask)
         mask *= 2
-    attn_total = block_total(attn_rest, attn_got)
-    own, got = grp_sum(attn_total)
-    sums = sums + tie(exchange(sums, 4), attn_total)
-    grad_down = finish_blocks(tie(down_blocks, attn_total))
-    own = sum_rounded(own, tie(got, grad_down))
-    mask = 1
-    while mask * 2 < n_grp:
-        sums = sums + tie(exchange(sums, mask, "grp"), own)
-        mask *= 2
+    qkv_total = block_total(qkv_rest, tie(qkv_got, block_out, sums))
+    own, qkv_got = grp_sum(qkv_total)
+    sums = sums + exchange(tie(sums, qkv_total), 4)
+    own = sum_rounded(own, tie(qkv_got, sums))
     by_x = exchange(own, 2)
     by_y = exchange(own, 4)
-    both = exchange(by_x, 4)
-    last = exchange(sums, mask, "grp")
-    attn_pieces = []
+    mask = 1
+    while mask * 2 < groups:
+        sums = sums + exchange(tie(sums, own), mask, GRP)
+        mask *= 2
+    both = exchange(tie(by_x, sums), 4)
+    last = exchange(tie(sums, by_x), mask, GRP)
+    grad_up, grad_out = finish_blocks(tie(up_blocks, by_x, by_y), [hidden_block, LANES])
+    qkv_pieces = []
     for piece in (own, by_x, by_y, both):
-        attn_pieces += [piece, exchange(piece, 1)]
-    grad_up = finish_blocks(tie(up_blocks, by_x, by_y))
-    grad_qkv, grad_out = finish_grads(
-        where,
-        attn_pieces,
-        [(at * LANES, LANES, 0, at * width) for at in range(3)] + [(3 * LANES, LANES, 1, 0)],
+        qkv_pieces += [piece, exchange(piece, 1)]
+    (grad_qkv,) = finish_grads(
+        where, qkv_pieces, [(at * LANES, LANES, 0, at * width) for at in range(3)]
     )
     sums = [vec.reshape(-1) for vec in unpack_sums(where, sums, last, sizes)]
     return (
@@ -1118,40 +1200,9 @@
 
 
 def solution(mesh):
-    return jax.shard_map(
-        layer,
-        mesh=mesh,
-        in_specs=(
-            P(("rep", "grp"), None, None),
-            P(("rep", "grp"), None, None),
-            P("grp"),
-            P("grp"),
-            P("grp", None),
-            P("grp"),
-            P("grp", None),
-            P("grp"),
-            P("grp"),
-            P("grp"),
-            P("grp", None),
-            P("grp"),
-            P("grp", None),
-            P("grp"),
-        ),
-        out_specs=(
-            P(("rep", "grp"), None, None),
-            P(("rep", "grp"), None, None),
-            P("grp"),
-            P("grp"),
-            P("grp", None),
-            P("grp"),
-            P("grp", None),
-            P("grp"),
-            P("grp"),
-            P("grp"),
-            P("grp", None),
-            P("grp"),
-            P("grp", None),
-            P("grp"),
-        ),
-        check_vma=False,
-    )
+    tokens = P((REP, GRP), None, None)
+    vector, matrix = P(GRP), P(GRP, None)
+    weights = (vector, vector, matrix, vector, matrix, vector)
+    weights += (vector, vector, matrix, vector, matrix, vector)
+    specs = (tokens, tokens) + weights
+    return jax.shard_map(layer, mesh=mesh, in_specs=specs, out_specs=specs, check_vma=False)

time: 501 us -> 499 us (level)
  waiting for transfers between devices: 181 us -> 191 us
  local copies, waits for them, and re-layouts: 20.6 us -> 11 us
  starting transfers between devices: 69.4 us -> 75.7 us
  other arithmetic: 17 us -> 11.7 us
    pallas_call x1 -> x4, Pallas kernels: 2.86 us -> 23.7 us  [the longest x1 14.3 us: weight_grads_flipped(): pl.pallas_call(body, grid_spec=pltpu.PrefetchScalarGridSpec(num_scalar_pr...]
    pallas_call x3 -> x2, Pallas kernels: 45.2 us -> 27.4 us  [weight_grads(): pl.pallas_call(body, grid_spec=pltpu.PrefetchScalarGridSpec(num_scalar_pr...]
    reshape x8 -> x1, local copies, waits for them, and re-layouts: 9.85 us -> 0.01 us  [layer(): packed = packed.reshape(16, 2 * LANES)]
    ppermute x71 -> x74, waiting for transfers between devices: 176 us -> 184 us  [exchange(): return lax.ppermute(tensor, axis, [(at, at ^ mask) for at in range(size)])]
    ppermute x71 -> x74, starting transfers between devices: 69.2 us -> 75.6 us  [exchange(): return lax.ppermute(tensor, axis, [(at, at ^ mask) for at in range(size)])]
    pallas_call x2 -> x1, Pallas kernels: 9.42 us -> 3.81 us  [finish_blocks(): pl.pallas_call(body, grid=(rows // step,), in_specs=[pl.BlockSpec((count,...]
    convert_element_type x11, other arithmetic: 11.9 us -> 6.54 us  [add_rounded(): (left.astype(jnp.float32) + right.astype(jnp.float32)).astype(jnp.bfloat16)]
  transfers between devices with their start and end apart: 75 -> 78, of which waited for: 29 -> 33; matrix products, arithmetic and copies ran while one was open for 3% -> 3% of each run, Pallas kernels for 33% -> 33%
where the time goes in v3:
time: 499 us; the launch traced here: 497 us
  Pallas kernels  194 us (39%)
  waiting for transfers between devices  191 us (38%)
  starting transfers between devices  75.7 us (15%)
  between operations  14.7 us (3%)
  other arithmetic  11.7 us (2%)
  local copies, waits for them, and re-layouts  11 us (2%)
    ppermute x74, waiting for transfers between devices, exchange(): return lax.ppermute(tensor, axis, [(at, at ^ mask) for at in range(size)])  184 us
    ppermute x74, starting transfers between devices, exchange(): return lax.ppermute(tensor, axis, [(at, at ^ mask) for at in range(size)])  75.6 us
    pallas_call x2, Pallas kernels, weight_grads(): pl.pallas_call(body, grid_spec=pltpu.PrefetchScalarGridSpec(num_scalar_pr...  27.4 us
    pallas_call x1, Pallas kernels, attention_backward(): pl.pallas_call(body, grid=(count,), in_specs=[spec(0), spec(1), spec(2),...  24.9 us
    pallas_call x1, Pallas kernels, middle_backward(): pl.pallas_call(body, grid_spec=pltpu.PrefetchScalarGridSpec(num_scalar_pr...  19 us
    pallas_call x1, Pallas kernels, up_forward(): pl.pallas_call(body, grid_spec=pltpu.PrefetchScalarGridSpec(num_scalar_pr...  14.4 us
    pallas_call x1, Pallas kernels, attention_forward(): pl.pallas_call(body, grid=(count,), in_specs=[spec(0), spec(1), spec(2)],...  14.3 us
    pallas_call x1, Pallas kernels, weight_grads_flipped(): pl.pallas_call(body, grid_spec=pltpu.PrefetchScalarGridSpec(num_scalar_pr...  14.3 us
  transfers between devices with their start and end apart: 78, of which 33 were waited for; matrix products, arithmetic and copies ran while one was open for 3% of the time, Pallas kernels for 33%

profile of v3, /device:TPU:0, one launch (start us, length us, event | category | flops | bytes accessed | tf_op | source)
XLA Modules:
  0.0 497.4 jit_solution(600517993162230334)
XLA Ops:
  7.9 2.3 shard_map.246
  10.2 3.1 collective-permute-start.3
  13.2 2.6 collective-permute-start.4
  15.8 6.0 %collective-permute-done.3 = bf16[256,384]{1,0:T(8,128)(2,1)S(1)} collective-permute-done((bf16[256,384]{1,0:T(8,128)(2,1)}, bf16[256,384]{1,0:T(8,128)(2,1)S(1)}, u32[]{:S(2)}, u32[]{:S(2)}) %collective-permute-start.3) | collective-permute-done | bytes 196640 | tf_op jit(solution)/shard_map/ppermute | solution.py:946
  21.8 8.7 %collective-permute-done.4 = bf16[256,384]{1,0:T(8,128)(2,1)S(1)} collective-permute-done((bf16[256,384]{1,0:T(8,128)(2,1)}, bf16[256,384]{1,0:T(8,128)(2,1)S(1)}, u32[]{:S(2)}, u32[]{:S(2)}) %collective-permute-start.4) | collective-permute-done | bytes 196640 | tf_op jit(solution)/shard_map/ppermute | solution.py:946
  30.6 1.6 collective-permute-start.7
  32.2 1.5 collective-permute-start.9
  33.7 2.6 shard_map.249
  36.3 3.4 collective-permute-start.15
  40.7 1.4 collective-permute-start.17
  45.3 6.1 %collective-permute-done.15 = bf16[256,640]{1,0:T(8,128)(2,1)S(1)} collective-permute-done((bf16[256,640]{1,0:T(8,128)(2,1)}, bf16[256,640]{1,0:T(8,128)(2,1)S(1)}, u32[]{:S(2)}, u32[]{:S(2)}) %collective-permute-start.15) | collective-permute-done | bytes 327712 | tf_op jit(solution)/shard_map/ppermute | solution.py:946
  51.4 14.0 %collective-permute-done.16 = bf16[256,640]{1,0:T(8,128)(2,1)S(1)} collective-permute-done((bf16[256,640]{1,0:T(8,128)(2,1)}, bf16[256,640]{1,0:T(8,128)(2,1)S(1)}, u32[]{:S(2)}, u32[]{:S(2)}) %collective-permute-start.16) | collective-permute-done | bytes 327712 | tf_op jit(solution)/shard_map/ppermute | solution.py:946
  66.7 1.5 collective-permute-start.11
  68.2 1.5 collective-permute-start.12
  69.8 4.6 collective-permute-start
  74.4 1.6 collective-permute-done.refs_1_
  76.1 3.0 collective-permute-start.1
  79.1 1.6 collective-permute-done.1.refs_2_
  80.7 2.4 collective-permute-start.2
  83.1 3.1 collective-permute-done.2.refs_3_
  86.2 3.9 collective-permute-done.11.rest_6_
  93.6 1.5 collective-permute-start.24
  97.2 2.1 shard_map.245
  99.3 9.4 %shard_map.247 = (bf16[577,1024]{1,0:T(8,128)(2,1)}, bf16[577,3072]{1,0:T(8,128)(2,1)}) custom-call(s32[2]{0:T(128)} %pad_add_fusion.1.where_ref, bf16[577,1024]{1,0:T(8,128)(2,1)} %bitcast.41, f32[1,1024]{1,0:T(1,128)} %get-tuple-element.110.gain_ref, f32[1,1024]{1,0:T(1,128)} %get-tuple-element.111.shift_ref, f32[1,3072]{1,0:T(1,128)} %get-tuple-element.112.bias_ref, ...), custom_call_target="tpu_custom_call" | custom-call | flops 3630170112 | bytes 6291456 | tf_op jit(solution)/shard_map/pallas_call | solution.py:148
  109.4 14.3 %shard_map.248 = (bf16[577,1024]{1,0:T(8,128)(2,1)}, f32[8,2,577]{2,1,0:T(2,128)}) custom-call(bf16[577,3072]{1,0:T(8,128)(2,1)} %get-tuple-element.113.query_ref.key_ref.value_ref, bf16[577,3072]{1,0:T(8,128)(2,1)} %get-tuple-element.113.query_ref.key_ref.value_ref, bf16[577,3072]{1,0:T(8,128)(2,1)} %get-tuple-element.113.query_ref.key_ref.value_ref), custom_call_target="tpu_custom_call" | custom-call | flops 5454708736 | bytes 4726784 | tf_op jit(solution)/shard_map/pallas_call | solution.py:533
  124.5 7.6 %shard_map.250 = (f32[577,1024]{1,0:T(8,128)}, bf16[577,1024]{1,0:T(8,128)(2,1)}) custom-call(s32[2]{0:T(128)} %pad_add_fusion.1.where_ref, bf16[577,1024]{1,0:T(8,128)(2,1)} %bitcast.42, bf16[577,1024]{1,0:T(8,128)(2,1)} %get-tuple-element.114.attended_ref.refs_4_, f32[1,1024]{1,0:T(1,128)} %get-tuple-element.115.bias_ref, ...), custom_call_target="tpu_custom_call" | custom-call | flops 1210056704 | bytes 2097152 | tf_op jit(solution)/shard_map/pallas_call | solution.py:204
  132.1 14.4 %shard_map.251 = (bf16[577,4096]{1,0:T(8,128)(2,1)}, bf16[577,4096]{1,0:T(8,128)(2,1)}) custom-call(s32[2]{0:T(128)} %pad_add_fusion.1.where_ref, bf16[577,1024]{1,0:T(8,128)(2,1)} %get-tuple-element.123.normed_ref.refs_0_, f32[1,4096]{1,0:T(1,128)} %get-tuple-element.124.bias_ref, bf16[256,4096]{1,0:T(8,128)(2,1)} %up_ref.1, bf16[768,640]{1,0:T(8,128)(2,1)} %copy-done.2, ...), custom_call_target="tpu_custom_call" | custom-call | flops 4840226816 | bytes 8388608 | tf_op jit(solution)/shard_map/pallas_call | solution.py:251
  146.7 7.6 %collective-permute-start.27 = (bf16[1024,128]{1,0:T(8,128)(2,1)S(1)}, bf16[1024,128]{1,0:T(8,128)(2,1)S(1)}, u32[]{:S(2)}, u32[]{:S(2)}) collective-permute-start(bf16[1024,128]{1,0:T(8,128)(2,1)S(1)} %copy-done.59), channel_id=1, source_target_pairs={{0,1},{1,0},{2,3},{3,2},{4,5},{5,4},{6,7},{7,6},{8,9},{9,8},{10,11... | collective-permute-start | bytes 786440 | tf_op jit(solution)/shard_map/ppermute | solution.py:946
  156.7 9.6 %collective-permute-done.27 = bf16[1024,128]{1,0:T(8,128)(2,1)S(1)} collective-permute-done((bf16[1024,128]{1,0:T(8,128)(2,1)S(1)}, bf16[1024,128]{1,0:T(8,128)(2,1)S(1)}, u32[]{:S(2)}, u32[]{:S(2)}) %collective-permute-start.27) | collective-permute-done | bytes 262176 | tf_op jit(solution)/shard_map/ppermute | solution.py:946
  166.3 9.3 %collective-permute-done.28 = bf16[1024,128]{1,0:T(8,128)(2,1)S(1)} collective-permute-done((bf16[1024,128]{1,0:T(8,128)(2,1)S(1)}, bf16[1024,128]{1,0:T(8,128)(2,1)S(1)}, u32[]{:S(2)}, u32[]{:S(2)}) %collective-permute-start.28) | collective-permute-done | bytes 262176 | tf_op jit(solution)/shard_map/ppermute | solution.py:946
  177.7 16.1 %collective-permute-done.31.rest_2_ = bf16[3072,128]{1,0:T(8,128)(2,1)S(1)} collective-permute-done((bf16[3072,128]{1,0:T(8,128)(2,1)S(1)}, bf16[3072,128]{1,0:T(8,128)(2,1)S(1)}, u32[]{:S(2)}, u32[]{:S(2)}) %collective-permute-start.31) | collective-permute-done | bytes 786464 | tf_op jit(solution)/shard_map/ppermute | solution.py:946
  197.2 5.4 %collective-permute-done.35.rest_6_ = bf16[1536,128]{1,0:T(8,128)(2,1)S(1)} collective-permute-done((bf16[1536,128]{1,0:T(8,128)(2,1)S(1)}, bf16[1536,128]{1,0:T(8,128)(2,1)S(1)}, u32[]{:S(2)}, u32[]{:S(2)}) %collective-permute-start.35) | collective-permute-done | bytes 393248 | tf_op jit(solution)/shard_map/ppermute | solution.py:946
  206.8 13.4 %shard_map.252 = (bf16[577,4096]{1,0:T(8,128)(2,1)}, f32[1,4096]{1,0:T(1,128)}) custom-call(s32[2]{0:T(128)} %pad_add_fusion.1.where_ref, bf16[577,1024]{1,0:T(8,128)(2,1)} %bitcast.45, bf16[577,4096]{1,0:T(8,128)(2,1)} %get-tuple-element.125.slope_ref, bf16[1024,1024]{1,0:T(8,128)(2,1)} %own_ref.13, bf16[3072,128]{1,0:T(8,128)(2,1)} %copy-done.32, ...), custom_call_target="tpu_custom_call" | custom-call | flops 4840226816 | bytes 8388608 | tf_op jit(solution)/shard_map/pallas_call | solution.py:347
  220.7 9.4 %collective-permute-done.40.right_pair_ref = bf16[577,1024]{1,0:T(8,128)(2,1)S(1)} collective-permute-done((bf16[577,1024]{1,0:T(8,128)(2,1)S(1)}, bf16[577,1024]{1,0:T(8,128)(2,1)S(1)}, u32[]{:S(2)}, u32[]{:S(2)}) %collective-permute-start.40) | collective-permute-done | bytes 1181728 | tf_op jit(solution)/shard_map/ppermute | solution.py:946
  231.1 14.3 %shard_map.253 = (bf16[2,2,128,1024]{3,2,1,0:T(8,128)(2,1)}, bf16[2,2,128,1024]{3,2,1,0:T(8,128)(2,1)}, bf16[2,2,128,1024]{3,2,1,0:T(8,128)(2,1)}, bf16[2,2,128,1024]{3,2,1,0:T(8,128)(2,1)}) custom-call(s32[2]{0:T(128)} %pad_add_fusion.1.where_ref, bf16[577,4096]{1,0:T(8,128)(2,1)} %get-tuple-element.133.left_ref.active_ref, ...), custom_call_target="tpu_custom_call" | custom-call | flops 4840226816 | bytes 13647872 | tf_op jit(solution)/shard_map/pallas_call | solution.py:732
  248.2 19.0 %shard_map.254 = (f32[577,1024]{1,0:T(8,128)}, bf16[577,1024]{1,0:T(8,128)(2,1)}, bf16[577,1024]{1,0:T(8,128)(2,1)}, f32[1,1024]{1,0:T(1,128)}, f32[1,1024]{1,0:...) custom-call(s32[2]{0:T(128)} %pad_add_fusion.1.where_ref, bf16[577,4096]{1,0:T(8,128)(2,1)} %get-tuple-element.131.pre_ref.refs_2_, ...), custom_call_target="tpu_custom_call" | custom-call | flops 6050283520 | bytes 10485760 | tf_op jit(solution)/shard_map/pallas_call | solution.py:423
  267.1 3.8 collective-permute-done.41
  272.2 2.5 fusion.7
  277.9 16.0 %shard_map.255 = (bf16[2,512,640]{2,1,0:T(8,128)(2,1)}, bf16[2,512,640]{2,1,0:T(8,128)(2,1)}, bf16[2,512,640]{2,1,0:T(8,128)(2,1)}, bf16[2,512,640]{2,1,0:T(8,128)(2,1)}) custom-call(s32[2]{0:T(128)} %pad_add_fusion.1.where_ref, bf16[577,1024]{1,0:T(8,128)(2,1)} %get-tuple-element.123.normed_ref.refs_0_, bf16[577,1024]{1,0:T(8,128)(2,1)} %collective-permute-done.43.refs_1_, ...), custom_call_target="tpu_custom_call" | custom-call | flops 6050283520 | bytes 7606272 | tf_op jit(solution)/shard_map/pallas_call | solution.py:663
  295.5 24.9 %shard_map.256 = (bf16[3,577,1024]{2,1,0:T(8,128)(2,1)}, f32[1,1024]{1,0:T(1,128)}, f32[1,1024]{1,0:T(1,128)}) custom-call(bf16[577,3072]{1,0:T(8,128)(2,1)} %get-tuple-element.113.query_ref.key_ref.value_ref, bf16[577,3072]{1,0:T(8,128)(2,1)} %get-tuple-element.113.query_ref.key_ref.value_ref, ...), custom_call_target="tpu_custom_call" | custom-call | flops 13636771840 | bytes 9453568 | tf_op jit(solution)/shard_map/pallas_call | solution.py:581
  320.4 6.8 %reduce-scatter.3.cloned.1.call-done = bf16[1,128,1024]{2,1,0:T(8,128)(2,1)} async-done(((bf16[4,128,1024]{2,1,0:T(8,128)(2,1)}), bf16[1,128,1024]{2,1,0:T(8,128)(2,1)}) %reduce-scatter.3.cloned.1.call-update) | async-done | bytes 262160 | tf_op jit(solution)/shard_map/reduce_scatter | solution.py:998
  327.2 1.5 collective-permute-start.47
  328.8 1.5 collective-permute-start.48
  330.3 35.8 %collective-permute-done.47 = bf16[2,512,640]{2,1,0:T(8,128)(2,1)S(1)} collective-permute-done((bf16[2,512,640]{2,1,0:T(8,128)(2,1)}, bf16[2,512,640]{2,1,0:T(8,128)(2,1)S(1)}, u32[]{:S(2)}, u32[]{:S(2)}) %collective-permute-start.47) | collective-permute-done | bytes 1310752 | tf_op jit(solution)/shard_map/ppermute | solution.py:946
  369.2 1.5 collective-permute-start.53
  370.7 11.4 %shard_map.257 = (bf16[2,512,384]{2,1,0:T(8,128)(2,1)}, bf16[2,512,384]{2,1,0:T(8,128)(2,1)}, bf16[2,512,384]{2,1,0:T(8,128)(2,1)}, bf16[2,512,384]{2,1,0:T(8,128)(2,1)}) custom-call(s32[2]{0:T(128)} %pad_add_fusion.1.where_ref, bf16[577,1024]{1,0:T(8,128)(2,1)} %get-tuple-element.158.refs_0_, bf16[577,1024]{1,0:T(8,128)(2,1)} %collective-permute-done.51.refs_1_, ...), custom_call_target="tpu_custom_call" | custom-call | flops 3630170112 | bytes 5509120 | tf_op jit(solution)/shard_map/pallas_call | solution.py:663
  387.1 1.4 collective-permute-start.57
  389.1 13.0 %shard_map.258 = (bf16[577,1024]{1,0:T(8,128)(2,1)}, f32[1,1024]{1,0:T(1,128)}, f32[1,1024]{1,0:T(1,128)}) custom-call(s32[2]{0:T(128)} %pad_add_fusion.1.where_ref, bf16[3,577,1024]{2,1,0:T(8,128)(2,1)} %get-tuple-element.154.refs_2_.proj_ref, bf16[577,1024]{1,0:T(8,128)(2,1)} %bitcast.43, f32[577,1024]{1,0:T(8,128)} %get-tuple-element.140.res_ref, ...), custom_call_target="tpu_custom_call" | custom-call | flops 3630170112 | bytes 6291456 | tf_op jit(solution)/shard_map/pallas_call | solution.py:487
  403.6 4.6 shard_map.260
  409.5 13.4 %shard_map.261 = bf16[577,1024]{1,0:T(8,128)(2,1)} custom-call(s32[2]{0:T(128)} %pad_add_fusion.1.where_ref, f32[577,1024]{1,0:T(8,128)} %get-tuple-element.139.residual_ref, bf16[577,4096]{1,0:T(8,128)(2,1)} %get-tuple-element.133.left_ref.active_ref, f32[1,1024]{1,0:T(1,128)} %get-tuple-element.182.bias_ref, bf16[1024,1024]{1,0:T(8,128)(2,1)} %own_ref.13, ...), custom_call_target="tpu_custom_call" | custom-call | flops 4840226816 | bytes 8388608 | tf_op jit(solution)/shard_map/pallas_call | solution.py:294
  425.6 13.6 %collective-permute-done.58 = f32[4,3072]{1,0:T(4,128)S(1)} collective-permute-done((f32[4,3072]{1,0:T(4,128)S(1)}, f32[4,3072]{1,0:T(4,128)S(1)}, u32[]{:S(2)}, u32[]{:S(2)}) %collective-permute-start.58) | collective-permute-done | bytes 49184 | tf_op jit(solution)/shard_map/ppermute | solution.py:946
  440.5 1.5 collective-permute-start.62
  443.0 2.0 collective-permute-start.64
  445.1 5.2 %collective-permute-done.61 = f32[4,3072]{1,0:T(4,128)S(1)} collective-permute-done((f32[4,3072]{1,0:T(4,128)S(1)}, f32[4,3072]{1,0:T(4,128)S(1)}, u32[]{:S(2)}, u32[]{:S(2)}) %collective-permute-start.61) | collective-permute-done | bytes 49184 | tf_op jit(solution)/shard_map/ppermute | solution.py:946
  450.3 8.9 %collective-permute-done.63 = bf16[256,384]{1,0:T(8,128)(2,1)S(1)} collective-permute-done((bf16[256,384]{1,0:T(8,128)(2,1)S(1)}, bf16[256,384]{1,0:T(8,128)(2,1)S(1)}, u32[]{:S(2)}, u32[]{:S(2)}) %collective-permute-start.63) | collective-permute-done | bytes 196640 | tf_op jit(solution)/shard_map/ppermute | solution.py:946
  460.6 3.3 collective-permute-start.65
  463.9 2.1 collective-permute-done.65
  466.6 4.2 collective-permute-done.70.refs_4_
  470.8 2.1 collective-permute-done.72.refs_6_
  472.9 1.8 collective-permute-start.67
  474.7 4.3 collective-permute-done.67.second_ref
  479.7 2.1 shard_map.262
  483.3 3.8 shard_map.263
  487.0 3.8 shard_map.264
  (274 shorter events, 56.2 us)
Async XLA Ops:
  7.2 320.0 %reduce-scatter.3.cloned.1.call-start = ((), (), s32[]{:S(2)}) async-start(), calls=%async_computation.2 | async-start | bytes 1310720 | tf_op jit(solution)/shard_map/reduce_scatter | solution.py:998
  10.2 11.6 %collective-permute-start.3 = (bf16[256,384]{1,0:T(8,128)(2,1)}, bf16[256,384]{1,0:T(8,128)(2,1)S(1)}, u32[]{:S(2)}, u32[]{:S(2)}) collective-permute-start(bf16[256,384]{1,0:T(8,128)(2,1)} %shard_map.246), channel_id=1, source_target_pairs={{0,1},{1,0},{2,3},{3,2},{4,5},{5,4},{6,7},{7,6},{8,9},{9,8},{10,11... | collective-permute-start | bytes 589832 | tf_op jit(solution)/shard_map/ppermute | solution.py:946
  13.2 17.3 %collective-permute-start.4 = (bf16[256,384]{1,0:T(8,128)(2,1)}, bf16[256,384]{1,0:T(8,128)(2,1)S(1)}, u32[]{:S(2)}, u32[]{:S(2)}) collective-permute-start(bf16[256,384]{1,0:T(8,128)(2,1)} %shard_map.246), channel_id=1, source_target_pairs={{0,2},{1,3},{2,0},{3,1},{4,6},{5,7},{6,4},{7,5},{8,10},{9,11},{10,... | collective-permute-start | bytes 589832 | tf_op jit(solution)/shard_map/ppermute | solution.py:946
  15.8 14.8 %collective-permute-start.5 = (bf16[256,384]{1,0:T(8,128)(2,1)}, bf16[256,384]{1,0:T(8,128)(2,1)S(1)}, u32[]{:S(2)}, u32[]{:S(2)}) collective-permute-start(bf16[256,384]{1,0:T(8,128)(2,1)} %shard_map.246), channel_id=1, source_target_pairs={{0,3},{1,2},{2,1},{3,0},{4,7},{5,6},{6,5},{7,4},{8,11},{9,10},{10,... | collective-permute-start | bytes 589832 | tf_op jit(solution)/shard_map/ppermute | solution.py:946
  30.6 12.7 %collective-permute-start.7 = (bf16[768,384]{1,0:T(8,128)(2,1)S(1)}, bf16[768,384]{1,0:T(8,128)(2,1)S(1)}, u32[]{:S(2)}, u32[]{:S(2)}) collective-permute-start(bf16[768,384]{1,0:T(8,128)(2,1)S(1)} %constant_dynamic-update-slice_fusion.rest_0_), channel_id=1, source_target_pairs={{0,8},{4,12},{8,0},{12,4},{16,24},{20,28},{24,16},{28,20},{1,9},{5... | collective-permute-start | bytes 1769480 | tf_op jit(solution)/shard_map/ppermute | solution.py:946
  32.2 12.3 %collective-permute-start.9 = (bf16[768,384]{1,0:T(8,128)(2,1)S(1)}, bf16[768,384]{1,0:T(8,128)(2,1)S(1)}, u32[]{:S(2)}, u32[]{:S(2)}) collective-permute-start(bf16[768,384]{1,0:T(8,128)(2,1)S(1)} %constant_dynamic-update-slice_fusion.rest_0_), channel_id=1, source_target_pairs={{0,16},{4,20},{8,24},{12,28},{16,0},{20,4},{24,8},{28,12},{1,17},{... | collective-permute-start | bytes 1769480 | tf_op jit(solution)/shard_map/ppermute | solution.py:946
  36.3 15.1 %collective-permute-start.15 = (bf16[256,640]{1,0:T(8,128)(2,1)}, bf16[256,640]{1,0:T(8,128)(2,1)S(1)}, u32[]{:S(2)}, u32[]{:S(2)}) collective-permute-start(bf16[256,640]{1,0:T(8,128)(2,1)} %get-tuple-element.119), channel_id=1, source_target_pairs={{0,1},{1,0},{2,3},{3,2},{4,5},{5,4},{6,7},{7,6},{8,9},{9,8},{10,11... | collective-permute-start | bytes 983048 | tf_op jit(solution)/shard_map/ppermute | solution.py:946
  39.7 25.7 %collective-permute-start.16 = (bf16[256,640]{1,0:T(8,128)(2,1)}, bf16[256,640]{1,0:T(8,128)(2,1)S(1)}, u32[]{:S(2)}, u32[]{:S(2)}) collective-permute-start(bf16[256,640]{1,0:T(8,128)(2,1)} %get-tuple-element.119), channel_id=1, source_target_pairs={{0,2},{1,3},{2,0},{3,1},{4,6},{5,7},{6,4},{7,5},{8,10},{9,11},{10,... | collective-permute-start | bytes 983048 | tf_op jit(solution)/shard_map/ppermute | solution.py:946
  40.7 24.7 %collective-permute-start.17 = (bf16[256,640]{1,0:T(8,128)(2,1)}, bf16[256,640]{1,0:T(8,128)(2,1)S(1)}, u32[]{:S(2)}, u32[]{:S(2)}) collective-permute-start(bf16[256,640]{1,0:T(8,128)(2,1)} %get-tuple-element.119), channel_id=1, source_target_pairs={{0,3},{1,2},{2,1},{3,0},{4,7},{5,6},{6,5},{7,4},{8,11},{9,10},{10,... | collective-permute-start | bytes 983048 | tf_op jit(solution)/shard_map/ppermute | solution.py:946
  65.6 25.0 %collective-permute-start.19 = (bf16[768,640]{1,0:T(8,128)(2,1)S(1)}, bf16[768,640]{1,0:T(8,128)(2,1)S(1)}, u32[]{:S(2)}, u32[]{:S(2)}) collective-permute-start(bf16[768,640]{1,0:T(8,128)(2,1)S(1)} %constant_dynamic-update-slice_fusion.3.rest_0_), channel_id=1, source_target_pairs={{0,8},{4,12},{8,0},{12,4},{16,24},{20,28},{24,16},{28,20},{1,9},{5... | collective-permute-start | bytes 2949128 | tf_op jit(solution)/shard_map/ppermute | solution.py:946
  66.2 24.5 %collective-permute-start.21 = (bf16[768,640]{1,0:T(8,128)(2,1)S(1)}, bf16[768,640]{1,0:T(8,128)(2,1)S(1)}, u32[]{:S(2)}, u32[]{:S(2)}) collective-permute-start(bf16[768,640]{1,0:T(8,128)(2,1)S(1)} %constant_dynamic-update-slice_fusion.3.rest_0_), channel_id=1, source_target_pairs={{0,16},{4,20},{8,24},{12,28},{16,0},{20,4},{24,8},{28,12},{1,17},{... | collective-permute-start | bytes 2949128 | tf_op jit(solution)/shard_map/ppermute | solution.py:946
  66.7 23.4 %collective-permute-start.11 = (bf16[384,384]{1,0:T(8,128)(2,1)}, bf16[384,384]{1,0:T(8,128)(2,1)}, u32[]{:S(2)}, u32[]{:S(2)}) collective-permute-start(bf16[384,384]{1,0:T(8,128)(2,1)} %slice.120), channel_id=1, source_target_pairs={{0,16},{4,20},{8,24},{12,28},{16,0},{20,4},{24,8},{28,12},{1,17},{... | collective-permute-start | bytes 884744 | tf_op jit(solution)/shard_map/ppermute | solution.py:946
  68.2 21.9 %collective-permute-start.12 = (bf16[384,384]{1,0:T(8,128)(2,1)}, bf16[384,384]{1,0:T(8,128)(2,1)}, u32[]{:S(2)}, u32[]{:S(2)}) collective-permute-start(bf16[384,384]{1,0:T(8,128)(2,1)} %slice.121), channel_id=1, source_target_pairs={{0,8},{4,12},{8,0},{12,4},{16,24},{20,28},{24,16},{28,20},{1,9},{5... | collective-permute-start | bytes 884744 | tf_op jit(solution)/shard_map/ppermute | solution.py:946
  86.1 6.7 %collective-permute-start.6 = (bf16[768,384]{1,0:T(8,128)(2,1)}, bf16[768,384]{1,0:T(8,128)(2,1)S(1)}, u32[]{:S(2)}, u32[]{:S(2)}) collective-permute-start(bf16[768,384]{1,0:T(8,128)(2,1)} %copy-done.8), channel_id=1, source_target_pairs={{0,4},{4,0},{8,12},{12,8},{16,20},{20,16},{24,28},{28,24},{1,5},{5... | collective-permute-start | bytes 1769480 | tf_op jit(solution)/shard_map/ppermute | solution.py:946
  92.9 15.9 %collective-permute-start.23 = (bf16[384,640]{1,0:T(8,128)(2,1)}, bf16[384,640]{1,0:T(8,128)(2,1)S(1)}, u32[]{:S(2)}, u32[]{:S(2)}) collective-permute-start(bf16[384,640]{1,0:T(8,128)(2,1)} %slice.122), channel_id=1, source_target_pairs={{0,16},{4,20},{8,24},{12,28},{16,0},{20,4},{24,8},{28,12},{1,17},{... | collective-permute-start | bytes 1474568 | tf_op jit(solution)/shard_map/ppermute | solution.py:946
  93.6 15.4 %collective-permute-start.24 = (bf16[384,640]{1,0:T(8,128)(2,1)}, bf16[384,640]{1,0:T(8,128)(2,1)}, u32[]{:S(2)}, u32[]{:S(2)}) collective-permute-start(bf16[384,640]{1,0:T(8,128)(2,1)} %slice.123), channel_id=1, source_target_pairs={{0,8},{4,12},{8,0},{12,4},{16,24},{20,28},{24,16},{28,20},{1,9},{5... | collective-permute-start | bytes 1474568 | tf_op jit(solution)/shard_map/ppermute | solution.py:946
  95.1 28.6 %collective-permute-start.18 = (bf16[768,640]{1,0:T(8,128)(2,1)S(1)}, bf16[768,640]{1,0:T(8,128)(2,1)}, u32[]{:S(2)}, u32[]{:S(2)}) collective-permute-start(bf16[768,640]{1,0:T(8,128)(2,1)S(1)} %constant_dynamic-update-slice_fusion.3.rest_0_), channel_id=1, source_target_pairs={{0,4},{4,0},{8,12},{12,8},{16,20},{20,16},{24,28},{28,24},{1,5},{5... | collective-permute-start | bytes 2949128 | tf_op jit(solution)/shard_map/ppermute | solution.py:946
  95.1 28.6 %collective-permute-start.20 = (bf16[768,640]{1,0:T(8,128)(2,1)S(1)}, bf16[768,640]{1,0:T(8,128)(2,1)}, u32[]{:S(2)}, u32[]{:S(2)}) collective-permute-start(bf16[768,640]{1,0:T(8,128)(2,1)S(1)} %collective-permute-done.19.rest_2_), channel_id=1, source_target_pairs={{0,4},{4,0},{8,12},{12,8},{16,20},{20,16},{24,28},{28,24},{1,5},{5... | collective-permute-start | bytes 2949128 | tf_op jit(solution)/shard_map/ppermute | solution.py:946
  96.8 26.9 %collective-permute-start.22 = (bf16[768,640]{1,0:T(8,128)(2,1)S(1)}, bf16[768,640]{1,0:T(8,128)(2,1)}, u32[]{:S(2)}, u32[]{:S(2)}) collective-permute-start(bf16[768,640]{1,0:T(8,128)(2,1)S(1)} %collective-permute-done.21.rest_4_), channel_id=1, source_target_pairs={{0,4},{4,0},{8,12},{12,8},{16,20},{20,16},{24,28},{28,24},{1,5},{5... | collective-permute-start | bytes 2949128 | tf_op jit(solution)/shard_map/ppermute | solution.py:946
  108.8 14.9 %collective-permute-start.25 = (bf16[384,640]{1,0:T(8,128)(2,1)S(1)}, bf16[384,640]{1,0:T(8,128)(2,1)S(1)}, u32[]{:S(2)}, u32[]{:S(2)}) collective-permute-start(bf16[384,640]{1,0:T(8,128)(2,1)S(1)} %collective-permute-done.23.rest_6_), channel_id=1, source_target_pairs={{0,4},{4,0},{8,12},{12,8},{16,20},{20,16},{24,28},{28,24},{1,5},{5... | collective-permute-start | bytes 1474568 | tf_op jit(solution)/shard_map/ppermute | solution.py:946
  109.0 14.7 %collective-permute-start.26 = (bf16[384,640]{1,0:T(8,128)(2,1)}, bf16[384,640]{1,0:T(8,128)(2,1)}, u32[]{:S(2)}, u32[]{:S(2)}) collective-permute-start(bf16[384,640]{1,0:T(8,128)(2,1)} %collective-permute-done.24.rest_7_), channel_id=1, source_target_pairs={{0,4},{4,0},{8,12},{12,8},{16,20},{20,16},{24,28},{28,24},{1,5},{5... | collective-permute-start | bytes 1474568 | tf_op jit(solution)/shard_map/ppermute | solution.py:946
  146.5 84.6 %collective-permute-start.39 = (bf16[577,4096]{1,0:T(8,128)(2,1)}, bf16[577,4096]{1,0:T(8,128)(2,1)}, u32[]{:S(2)}, u32[]{:S(2)}) collective-permute-start(bf16[577,4096]{1,0:T(8,128)(2,1)} %get-tuple-element.133.left_ref.active_ref), channel_id=1, source_target_pairs={{0,4},{4,0},{8,12},{12,8},{16,20},{20,16},{24,28},{28,24},{1,5},{5... | collective-permute-start | bytes 14180360 | tf_op jit(solution)/shard_map/ppermute | solution.py:946
  146.7 19.6 %collective-permute-start.27 = (bf16[1024,128]{1,0:T(8,128)(2,1)S(1)}, bf16[1024,128]{1,0:T(8,128)(2,1)S(1)}, u32[]{:S(2)}, u32[]{:S(2)}) collective-permute-start(bf16[1024,128]{1,0:T(8,128)(2,1)S(1)} %copy-done.59), channel_id=1, source_target_pairs={{0,1},{1,0},{2,3},{3,2},{4,5},{5,4},{6,7},{7,6},{8,9},{9,8},{10,11... | collective-permute-start | bytes 786440 | tf_op jit(solution)/shard_map/ppermute | solution.py:946
  154.3 21.4 %collective-permute-start.28 = (bf16[1024,128]{1,0:T(8,128)(2,1)S(1)}, bf16[1024,128]{1,0:T(8,128)(2,1)S(1)}, u32[]{:S(2)}, u32[]{:S(2)}) collective-permute-start(bf16[1024,128]{1,0:T(8,128)(2,1)S(1)} %copy-done.59), channel_id=1, source_target_pairs={{0,2},{1,3},{2,0},{3,1},{4,6},{5,7},{6,4},{7,5},{8,10},{9,11},{10,... | collective-permute-start | bytes 786440 | tf_op jit(solution)/shard_map/ppermute | solution.py:946
  155.3 20.3 %collective-permute-start.29 = (bf16[1024,128]{1,0:T(8,128)(2,1)S(1)}, bf16[1024,128]{1,0:T(8,128)(2,1)S(1)}, u32[]{:S(2)}, u32[]{:S(2)}) collective-permute-start(bf16[1024,128]{1,0:T(8,128)(2,1)S(1)} %copy-done.59), channel_id=1, source_target_pairs={{0,3},{1,2},{2,1},{3,0},{4,7},{5,6},{6,5},{7,4},{8,11},{9,10},{10,... | collective-permute-start | bytes 786440 | tf_op jit(solution)/shard_map/ppermute | solution.py:946
  175.7 18.1 %collective-permute-start.31 = (bf16[3072,128]{1,0:T(8,128)(2,1)S(1)}, bf16[3072,128]{1,0:T(8,128)(2,1)S(1)}, u32[]{:S(2)}, u32[]{:S(2)}) collective-permute-start(bf16[3072,128]{1,0:T(8,128)(2,1)S(1)} %constant_dynamic-update-slice_fusion.6.rest_0_), channel_id=1, source_target_pairs={{0,8},{4,12},{8,0},{12,4},{16,24},{20,28},{24,16},{28,20},{1,9},{5... | collective-permute-start | bytes 2359304 | tf_op jit(solution)/shard_map/ppermute | solution.py:946
  176.3 18.9 %collective-permute-start.33 = (bf16[3072,128]{1,0:T(8,128)(2,1)S(1)}, bf16[3072,128]{1,0:T(8,128)(2,1)S(1)}, u32[]{:S(2)}, u32[]{:S(2)}) collective-permute-start(bf16[3072,128]{1,0:T(8,128)(2,1)S(1)} %constant_dynamic-update-slice_fusion.6.rest_0_), channel_id=1, source_target_pairs={{0,16},{4,20},{8,24},{12,28},{16,0},{20,4},{24,8},{28,12},{1,17},{... | collective-permute-start | bytes 2359304 | tf_op jit(solution)/shard_map/ppermute | solution.py:946
  177.7 19.0 %collective-permute-start.30 = (bf16[3072,128]{1,0:T(8,128)(2,1)S(1)}, bf16[3072,128]{1,0:T(8,128)(2,1)S(1)}, u32[]{:S(2)}, u32[]{:S(2)}) collective-permute-start(bf16[3072,128]{1,0:T(8,128)(2,1)S(1)} %constant_dynamic-update-slice_fusion.6.rest_0_), channel_id=1, source_target_pairs={{0,4},{4,0},{8,12},{12,8},{16,20},{20,16},{24,28},{28,24},{1,5},{5... | collective-permute-start | bytes 2359304 | tf_op jit(solution)/shard_map/ppermute | solution.py:946
  193.8 8.8 %collective-permute-start.35 = (bf16[1536,128]{1,0:T(8,128)(2,1)S(1)}, bf16[1536,128]{1,0:T(8,128)(2,1)S(1)}, u32[]{:S(2)}, u32[]{:S(2)}) collective-permute-start(bf16[1536,128]{1,0:T(8,128)(2,1)S(1)} %slice.124), channel_id=1, source_target_pairs={{0,16},{4,20},{8,24},{12,28},{16,0},{20,4},{24,8},{28,12},{1,17},{... | collective-permute-start | bytes 1179656 | tf_op jit(solution)/shard_map/ppermute | solution.py:946
  195.2 8.4 %collective-permute-start.36 = (bf16[1536,128]{1,0:T(8,128)(2,1)S(1)}, bf16[1536,128]{1,0:T(8,128)(2,1)S(1)}, u32[]{:S(2)}, u32[]{:S(2)}) collective-permute-start(bf16[1536,128]{1,0:T(8,128)(2,1)S(1)} %slice.125), channel_id=1, source_target_pairs={{0,8},{4,12},{8,0},{12,4},{16,24},{20,28},{24,16},{28,20},{1,9},{5... | collective-permute-start | bytes 1179656 | tf_op jit(solution)/shard_map/ppermute | solution.py:946
  196.6 8.8 %collective-permute-start.32 = (bf16[3072,128]{1,0:T(8,128)(2,1)S(1)}, bf16[3072,128]{1,0:T(8,128)(2,1)S(1)}, u32[]{:S(2)}, u32[]{:S(2)}) collective-permute-start(bf16[3072,128]{1,0:T(8,128)(2,1)S(1)} %collective-permute-done.31.rest_2_), channel_id=1, source_target_pairs={{0,4},{4,0},{8,12},{12,8},{16,20},{20,16},{24,28},{28,24},{1,5},{5... | collective-permute-start | bytes 2359304 | tf_op jit(solution)/shard_map/ppermute | solution.py:946
  196.7 8.8 %collective-permute-start.34 = (bf16[3072,128]{1,0:T(8,128)(2,1)S(1)}, bf16[3072,128]{1,0:T(8,128)(2,1)S(1)}, u32[]{:S(2)}, u32[]{:S(2)}) collective-permute-start(bf16[3072,128]{1,0:T(8,128)(2,1)S(1)} %collective-permute-done.33.rest_4_), channel_id=1, source_target_pairs={{0,4},{4,0},{8,12},{12,8},{16,20},{20,16},{24,28},{28,24},{1,5},{5... | collective-permute-start | bytes 2359304 | tf_op jit(solution)/shard_map/ppermute | solution.py:946
  220.1 57.7 %collective-permute-start.44 = (bf16[577,4096]{1,0:T(8,128)(2,1)}, bf16[577,4096]{1,0:T(8,128)(2,1)}, u32[]{:S(2)}, u32[]{:S(2)}) collective-permute-start(bf16[577,4096]{1,0:T(8,128)(2,1)} %get-tuple-element.131.pre_ref.refs_2_), channel_id=1, source_target_pairs={{0,4},{4,0},{8,12},{12,8},{16,20},{20,16},{24,28},{28,24},{1,5},{5... | collective-permute-start | bytes 14180360 | tf_op jit(solution)/shard_map/ppermute | solution.py:946
  220.3 9.8 %collective-permute-start.40 = (bf16[577,1024]{1,0:T(8,128)(2,1)S(1)}, bf16[577,1024]{1,0:T(8,128)(2,1)S(1)}, u32[]{:S(2)}, u32[]{:S(2)}) collective-permute-start(bf16[577,1024]{1,0:T(8,128)(2,1)S(1)} %bitcast.48), channel_id=1, source_target_pairs={{0,4},{4,0},{8,12},{12,8},{16,20},{20,16},{24,28},{28,24},{1,5},{5... | collective-permute-start | bytes 3545096 | tf_op jit(solution)/shard_map/ppermute | solution.py:946
  245.4 25.5 %collective-permute-start.41 = (bf16[2,2,128,1024]{3,2,1,0:T(8,128)(2,1)}, bf16[2,2,128,1024]{3,2,1,0:T(8,128)(2,1)S(1)}, u32[]{:S(2)}, u32[]{:S(2)}) collective-permute-start(bf16[2,2,128,1024]{3,2,1,0:T(8,128)(2,1)} %get-tuple-element.134), channel_id=1, source_target_pairs={{0,8},{4,12},{8,0},{12,4},{16,24},{20,28},{24,16},{28,20},{1,9},{5... | collective-permute-start | bytes 3145736 | tf_op jit(solution)/shard_map/ppermute | solution.py:946
  246.3 30.8 %collective-permute-start.45 = (bf16[577,1024]{1,0:T(8,128)(2,1)S(1)}, bf16[577,1024]{1,0:T(8,128)(2,1)}, u32[]{:S(2)}, u32[]{:S(2)}) collective-permute-start(bf16[577,1024]{1,0:T(8,128)(2,1)S(1)} %copy-done.7), channel_id=1, source_target_pairs={{0,4},{4,0},{8,12},{12,8},{16,20},{20,16},{24,28},{28,24},{1,5},{5... | collective-permute-start | bytes 3545096 | tf_op jit(solution)/shard_map/ppermute | solution.py:946
  246.3 31.5 %collective-permute-start.43 = (bf16[577,1024]{1,0:T(8,128)(2,1)}, bf16[577,1024]{1,0:T(8,128)(2,1)}, u32[]{:S(2)}, u32[]{:S(2)}) collective-permute-start(bf16[577,1024]{1,0:T(8,128)(2,1)} %get-tuple-element.123.normed_ref.refs_0_), channel_id=1, source_target_pairs={{0,4},{4,0},{8,12},{12,8},{16,20},{20,16},{24,28},{28,24},{1,5},{5... | collective-permute-start | bytes 3545096 | tf_op jit(solution)/shard_map/ppermute | solution.py:946
  246.9 25.4 %collective-permute-start.42 = (bf16[2,2,128,1024]{3,2,1,0:T(8,128)(2,1)}, bf16[2,2,128,1024]{3,2,1,0:T(8,128)(2,1)}, u32[]{:S(2)}, u32[]{:S(2)}) collective-permute-start(bf16[2,2,128,1024]{3,2,1,0:T(8,128)(2,1)} %get-tuple-element.136), channel_id=1, source_target_pairs={{0,16},{4,20},{8,24},{12,28},{16,0},{20,4},{24,8},{28,12},{1,17},{... | collective-permute-start | bytes 3145736 | tf_op jit(solution)/shard_map/ppermute | solution.py:946
  270.9 7.0 %collective-permute-start.46 = (bf16[577,1024]{1,0:T(8,128)(2,1)}, bf16[577,1024]{1,0:T(8,128)(2,1)}, u32[]{:S(2)}, u32[]{:S(2)}) collective-permute-start(bf16[577,1024]{1,0:T(8,128)(2,1)} %get-tuple-element.144.refs_6_), channel_id=1, source_target_pairs={{0,4},{4,0},{8,12},{12,8},{16,20},{20,16},{24,28},{28,24},{1,5},{5... | collective-permute-start | bytes 3545096 | tf_op jit(solution)/shard_map/ppermute | solution.py:946
  275.9 18.0 %collective-permute-start.50 = (bf16[2,128,1024]{2,1,0:T(8,128)(2,1)}, bf16[2,128,1024]{2,1,0:T(8,128)(2,1)S(1)}, u32[]{:S(2)}, u32[]{:S(2)}) collective-permute-start(bf16[2,128,1024]{2,1,0:T(8,128)(2,1)} %get-tuple-element.210), channel_id=1, source_target_pairs={{0,8},{4,12},{8,0},{12,4},{16,24},{20,28},{24,16},{28,20},{1,9},{5... | collective-permute-start | bytes 1572872 | tf_op jit(solution)/shard_map/ppermute | solution.py:946
  277.1 16.8 %collective-permute-start.49 = (bf16[2,128,1024]{2,1,0:T(8,128)(2,1)}, bf16[2,128,1024]{2,1,0:T(8,128)(2,1)S(1)}, u32[]{:S(2)}, u32[]{:S(2)}) collective-permute-start(bf16[2,128,1024]{2,1,0:T(8,128)(2,1)} %get-tuple-element.212), channel_id=1, source_target_pairs={{0,16},{4,20},{8,24},{12,28},{16,0},{20,4},{24,8},{28,12},{1,17},{... | collective-permute-start | bytes 1572872 | tf_op jit(solution)/shard_map/ppermute | solution.py:946
  295.4 108.1 %all-gather.5.cloned.1.call-start = ((), (), s32[]{:S(2)}) async-start(), calls=%async_computation.4 | async-start | bytes 2359296 | tf_op jit(solution)/shard_map/all_gather | solution.py:1002
  320.4 50.3 %collective-permute-start.52 = (bf16[3,577,1024]{2,1,0:T(8,128)(2,1)}, bf16[3,577,1024]{2,1,0:T(8,128)(2,1)}, u32[]{:S(2)}, u32[]{:S(2)}) collective-permute-start(bf16[3,577,1024]{2,1,0:T(8,128)(2,1)} %get-tuple-element.154.refs_2_.proj_ref), channel_id=1, source_target_pairs={{0,4},{4,0},{8,12},{12,8},{16,20},{20,16},{24,28},{28,24},{1,5},{5... | collective-permute-start | bytes 10635272 | tf_op jit(solution)/shard_map/ppermute | solution.py:946
  327.2 95.8 %reduce-scatter.5.cloned.1.call-start = ((), (), s32[]{:S(2)}) async-start(), calls=%async_computation.3 | async-start | bytes 1638400 | tf_op jit(solution)/shard_map/reduce_scatter | solution.py:998
  327.2 38.8 %collective-permute-start.47 = (bf16[2,512,640]{2,1,0:T(8,128)(2,1)}, bf16[2,512,640]{2,1,0:T(8,128)(2,1)S(1)}, u32[]{:S(2)}, u32[]{:S(2)}) collective-permute-start(bf16[2,512,640]{2,1,0:T(8,128)(2,1)} %get-tuple-element.146), channel_id=1, source_target_pairs={{0,8},{4,12},{8,0},{12,4},{16,24},{20,28},{24,16},{28,20},{1,9},{5... | collective-permute-start | bytes 3932168 | tf_op jit(solution)/shard_map/ppermute | solution.py:946
  328.8 38.3 %collective-permute-start.48 = (bf16[2,512,640]{2,1,0:T(8,128)(2,1)S(1)}, bf16[2,512,640]{2,1,0:T(8,128)(2,1)S(1)}, u32[]{:S(2)}, u32[]{:S(2)}) collective-permute-start(bf16[2,512,640]{2,1,0:T(8,128)(2,1)S(1)} %copy-done.48), channel_id=1, source_target_pairs={{0,16},{4,20},{8,24},{12,28},{16,0},{20,4},{24,8},{28,12},{1,17},{... | collective-permute-start | bytes 3932168 | tf_op jit(solution)/shard_map/ppermute | solution.py:946
  330.2 40.5 %collective-permute-start.51 = (bf16[577,1024]{1,0:T(8,128)(2,1)}, bf16[577,1024]{1,0:T(8,128)(2,1)}, u32[]{:S(2)}, u32[]{:S(2)}) collective-permute-start(bf16[577,1024]{1,0:T(8,128)(2,1)} %get-tuple-element.158.refs_0_), channel_id=1, source_target_pairs={{0,4},{4,0},{8,12},{12,8},{16,20},{20,16},{24,28},{28,24},{1,5},{5... | collective-permute-start | bytes 3545096 | tf_op jit(solution)/shard_map/ppermute | solution.py:946
  368.3 15.2 %collective-permute-start.54 = (bf16[512,640]{1,0:T(8,128)(2,1)}, bf16[512,640]{1,0:T(8,128)(2,1)S(1)}, u32[]{:S(2)}, u32[]{:S(2)}) collective-permute-start(bf16[512,640]{1,0:T(8,128)(2,1)} %get-tuple-element.206), channel_id=1, source_target_pairs={{0,8},{4,12},{8,0},{12,4},{16,24},{20,28},{24,16},{28,20},{1,9},{5... | collective-permute-start | bytes 1966088 | tf_op jit(solution)/shard_map/ppermute | solution.py:946
  369.2 15.0 %collective-permute-start.53 = (bf16[512,640]{1,0:T(8,128)(2,1)S(1)}, bf16[512,640]{1,0:T(8,128)(2,1)S(1)}, u32[]{:S(2)}, u32[]{:S(2)}) collective-permute-start(bf16[512,640]{1,0:T(8,128)(2,1)S(1)} %get-tuple-element.208), channel_id=1, source_target_pairs={{0,16},{4,20},{8,24},{12,28},{16,0},{20,4},{24,8},{28,12},{1,17},{... | collective-permute-start | bytes 1966088 | tf_op jit(solution)/shard_map/ppermute | solution.py:946
  385.7 101.3 %all-gather.7.cloned.1.call-start = ((), (), s32[]{:S(2)}) async-start(), calls=%async_computation.5 | async-start | bytes 2949120 | tf_op jit(solution)/shard_map/all_gather | solution.py:1002
  385.8 22.4 %collective-permute-start.56 = (bf16[2,512,384]{2,1,0:T(8,128)(2,1)}, bf16[2,512,384]{2,1,0:T(8,128)(2,1)S(1)}, u32[]{:S(2)}, u32[]{:S(2)}) collective-permute-start(bf16[2,512,384]{2,1,0:T(8,128)(2,1)} %get-tuple-element.159), channel_id=1, source_target_pairs={{0,8},{4,12},{8,0},{12,4},{16,24},{20,28},{24,16},{28,20},{1,9},{5... | collective-permute-start | bytes 2359304 | tf_op jit(solution)/shard_map/ppermute | solution.py:946
  387.1 21.1 %collective-permute-start.57 = (bf16[2,512,384]{2,1,0:T(8,128)(2,1)S(1)}, bf16[2,512,384]{2,1,0:T(8,128)(2,1)S(1)}, u32[]{:S(2)}, u32[]{:S(2)}) collective-permute-start(bf16[2,512,384]{2,1,0:T(8,128)(2,1)S(1)} %copy-done.54), channel_id=1, source_target_pairs={{0,16},{4,20},{8,24},{12,28},{16,0},{20,4},{24,8},{28,12},{1,17},{... | collective-permute-start | bytes 2359304 | tf_op jit(solution)/shard_map/ppermute | solution.py:946
  423.0 16.2 %collective-permute-start.60 = (bf16[512,384]{1,0:T(8,128)(2,1)S(1)}, bf16[512,384]{1,0:T(8,128)(2,1)S(1)}, u32[]{:S(2)}, u32[]{:S(2)}) collective-permute-start(bf16[512,384]{1,0:T(8,128)(2,1)S(1)} %get-tuple-element.214), channel_id=1, source_target_pairs={{0,8},{4,12},{8,0},{12,4},{16,24},{20,28},{24,16},{28,20},{1,9},{5... | collective-permute-start | bytes 1179656 | tf_op jit(solution)/shard_map/ppermute | solution.py:946
  424.1 15.1 %collective-permute-start.59 = (bf16[512,384]{1,0:T(8,128)(2,1)S(1)}, bf16[512,384]{1,0:T(8,128)(2,1)S(1)}, u32[]{:S(2)}, u32[]{:S(2)}) collective-permute-start(bf16[512,384]{1,0:T(8,128)(2,1)S(1)} %get-tuple-element.216), channel_id=1, source_target_pairs={{0,16},{4,20},{8,24},{12,28},{16,0},{20,4},{24,8},{28,12},{1,17},{... | collective-permute-start | bytes 1179656 | tf_op jit(solution)/shard_map/ppermute | solution.py:946
  424.4 14.8 %collective-permute-start.58 = (f32[4,3072]{1,0:T(4,128)S(1)}, f32[4,3072]{1,0:T(4,128)S(1)}, u32[]{:S(2)}, u32[]{:S(2)}) collective-permute-start(f32[4,3072]{1,0:T(4,128)S(1)} %add.159), channel_id=1, source_target_pairs={{0,8},{4,12},{8,0},{12,4},{16,24},{20,28},{24,16},{28,20},{1,9},{5... | collective-permute-start | bytes 147464 | tf_op jit(solution)/shard_map/ppermute | solution.py:946
  440.5 9.7 %collective-permute-start.62 = (bf16[256,384]{1,0:T(8,128)(2,1)S(1)}, bf16[256,384]{1,0:T(8,128)(2,1)S(1)}, u32[]{:S(2)}, u32[]{:S(2)}) collective-permute-start(bf16[256,384]{1,0:T(8,128)(2,1)S(1)} %get-tuple-element.219), channel_id=1, source_target_pairs={{0,1},{1,0},{2,3},{3,2},{4,5},{5,4},{6,7},{7,6},{8,9},{9,8},{10,11... | collective-permute-start | bytes 589832 | tf_op jit(solution)/shard_map/ppermute | solution.py:946
  442.1 17.1 %collective-permute-start.63 = (bf16[256,384]{1,0:T(8,128)(2,1)S(1)}, bf16[256,384]{1,0:T(8,128)(2,1)S(1)}, u32[]{:S(2)}, u32[]{:S(2)}) collective-permute-start(bf16[256,384]{1,0:T(8,128)(2,1)S(1)} %get-tuple-element.220), channel_id=1, source_target_pairs={{0,2},{1,3},{2,0},{3,1},{4,6},{5,7},{6,4},{7,5},{8,10},{9,11},{10,... | collective-permute-start | bytes 589832 | tf_op jit(solution)/shard_map/ppermute | solution.py:946
  443.0 16.1 %collective-permute-start.64 = (bf16[256,384]{1,0:T(8,128)(2,1)S(1)}, bf16[256,384]{1,0:T(8,128)(2,1)S(1)}, u32[]{:S(2)}, u32[]{:S(2)}) collective-permute-start(bf16[256,384]{1,0:T(8,128)(2,1)S(1)} %get-tuple-element.218), channel_id=1, source_target_pairs={{0,3},{1,2},{2,1},{3,0},{4,7},{5,6},{6,5},{7,4},{8,11},{9,10},{10,... | collective-permute-start | bytes 589832 | tf_op jit(solution)/shard_map/ppermute | solution.py:946
  463.9 6.9 %collective-permute-start.70 = (bf16[256,384]{1,0:T(8,128)(2,1)S(1)}, bf16[256,384]{1,0:T(8,128)(2,1)S(1)}, u32[]{:S(2)}, u32[]{:S(2)}) collective-permute-start(bf16[256,384]{1,0:T(8,128)(2,1)S(1)} %add_convert_fusion.18.refs_0_), channel_id=1, source_target_pairs={{0,16},{4,20},{8,24},{12,28},{16,0},{20,4},{24,8},{28,12},{1,17},{... | collective-permute-start | bytes 589832 | tf_op jit(solution)/shard_map/ppermute | solution.py:946
  466.0 6.9 %collective-permute-start.72 = (bf16[256,384]{1,0:T(8,128)(2,1)S(1)}, bf16[256,384]{1,0:T(8,128)(2,1)S(1)}, u32[]{:S(2)}, u32[]{:S(2)}) collective-permute-start(bf16[256,384]{1,0:T(8,128)(2,1)S(1)} %collective-permute-done.66.refs_2_), channel_id=1, source_target_pairs={{0,16},{4,20},{8,24},{12,28},{16,0},{20,4},{24,8},{28,12},{1,17},{... | collective-permute-start | bytes 589832 | tf_op jit(solution)/shard_map/ppermute | solution.py:946
  466.1 15.7 %collective-permute-start.68 = (bf16[256,384]{1,0:T(8,128)(2,1)S(1)}, bf16[256,384]{1,0:T(8,128)(2,1)S(1)}, u32[]{:S(2)}, u32[]{:S(2)}) collective-permute-start(bf16[256,384]{1,0:T(8,128)(2,1)S(1)} %add_convert_fusion.18.refs_0_), channel_id=1, source_target_pairs={{0,4},{4,0},{8,12},{12,8},{16,20},{20,16},{24,28},{28,24},{1,5},{5... | collective-permute-start | bytes 589832 | tf_op jit(solution)/shard_map/ppermute | solution.py:946
  466.1 15.6 %collective-permute-start.69 = (bf16[256,384]{1,0:T(8,128)(2,1)S(1)}, bf16[256,384]{1,0:T(8,128)(2,1)S(1)}, u32[]{:S(2)}, u32[]{:S(2)}) collective-permute-start(bf16[256,384]{1,0:T(8,128)(2,1)S(1)} %collective-permute-done.66.refs_2_), channel_id=1, source_target_pairs={{0,4},{4,0},{8,12},{12,8},{16,20},{20,16},{24,28},{28,24},{1,5},{5... | collective-permute-start | bytes 589832 | tf_op jit(solution)/shard_map/ppermute | solution.py:946
  470.8 11.0 %collective-permute-start.71 = (bf16[256,384]{1,0:T(8,128)(2,1)S(1)}, bf16[256,384]{1,0:T(8,128)(2,1)S(1)}, u32[]{:S(2)}, u32[]{:S(2)}) collective-permute-start(bf16[256,384]{1,0:T(8,128)(2,1)S(1)} %collective-permute-done.70.refs_4_), channel_id=1, source_target_pairs={{0,4},{4,0},{8,12},{12,8},{16,20},{20,16},{24,28},{28,24},{1,5},{5... | collective-permute-start | bytes 589832 | tf_op jit(solution)/shard_map/ppermute | solution.py:946
  472.9 8.9 %collective-permute-start.73 = (bf16[256,384]{1,0:T(8,128)(2,1)S(1)}, bf16[256,384]{1,0:T(8,128)(2,1)S(1)}, u32[]{:S(2)}, u32[]{:S(2)}) collective-permute-start(bf16[256,384]{1,0:T(8,128)(2,1)S(1)} %collective-permute-done.72.refs_6_), channel_id=1, source_target_pairs={{0,4},{4,0},{8,12},{12,8},{16,20},{20,16},{24,28},{28,24},{1,5},{5... | collective-permute-start | bytes 589832 | tf_op jit(solution)/shard_map/ppermute | solution.py:946
  (74 other events, 913.7 us)
Sparse Core Ops, SparseCore 0:
  295.6 31.5 reduce-scatter.2
  329.0 34.9 all-gather.4
  385.8 30.8 reduce-scatter.4
  423.1 31.8 all-gather.6

commit v4 on v3

--- a/solution.py
+++ b/solution.py
@@ -31,8 +31,8 @@
     return pl.multiple_of(start, unit)
 
 
-def params(**extra):
-    return pltpu.CompilerParams(vmem_limit_bytes=60 << 20, **extra)
+def params(mebibytes=60):
+    return pltpu.CompilerParams(vmem_limit_bytes=mebibytes << 20)
 
 
 def cost(flops, moved):
@@ -171,7 +171,7 @@
             jax.ShapeDtypeStruct((tokens, wide), jnp.bfloat16),
         ],
         cost_estimate=cost(2 * tokens * width * wide, 2 * width * wide),
-        compiler_params=params(),
+        compiler_params=params(22),
     )(where, image, gain, shift, bias, own, *flat(pieces))
 
 
@@ -220,7 +220,7 @@
             jax.ShapeDtypeStruct((tokens, width), jnp.bfloat16),
         ],
         cost_estimate=cost(2 * tokens * width * width, 2 * width * width),
-        compiler_params=params(),
+        compiler_params=params(32),
     )(where, image, attended, bias, gain, shift, own, *flat(pieces))
 
 
@@ -238,8 +238,13 @@
         def _():
             start_loads(where_ref, own_ref, piece_refs, [(0, size, 0)], weight, sems, BLOCK)
 
-        columns = pl.ds(aligned(jnp.bitwise_xor(where_ref[0], at) * size, size), size)
-        finish(weight.at[:, columns], sems.at[at])
+        for which in range(2):
+            block = jnp.bitwise_xor(where_ref[0], 2 * at + which)
+            finish(
+                weight.at[:, pl.ds(aligned(block * size, size), size)], sems.at[2 * at + which]
+            )
+        pair = jnp.bitwise_xor(where_ref[0], 2 * at) // 2
+        columns = pl.ds(aligned(pair * 2 * size, size), 2 * size)
         pre_act = product(normed_ref[...], weight[:, columns]) + bias_ref[...]
         cdf = 0.5 * (1.0 + lax.erf(pre_act * root_half))
         density = jnp.exp(-0.5 * pre_act * pre_act) * inv_root_tau
@@ -247,15 +252,15 @@
         slope_ref[...] = (cdf + pre_act * density).astype(jnp.bfloat16)
 
     full = lambda at, _: (0, 0)
-    mine = lambda at, where_ref: (0, jnp.bitwise_xor(where_ref[0], at))
-    return pl.pallas_call(
-        body,
-        grid_spec=pltpu.PrefetchScalarGridSpec(
-            num_scalar_prefetch=1,
-            grid=(BLOCKS,),
-            in_specs=[pl.BlockSpec((tokens, width), full), pl.BlockSpec((1, size), mine)]
+    mine = lambda at, where_ref: (0, jnp.bitwise_xor(where_ref[0], 2 * at) // 2)
+    return pl.pallas_call(
+        body,
+        grid_spec=pltpu.PrefetchScalarGridSpec(
+            num_scalar_prefetch=1,
+            grid=(BLOCKS // 2,),
+            in_specs=[pl.BlockSpec((tokens, width), full), pl.BlockSpec((1, 2 * size), mine)]
             + [ANY] * (1 + len(flat(pieces))),
-            out_specs=[pl.BlockSpec((tokens, size), mine)] * 2,
+            out_specs=[pl.BlockSpec((tokens, 2 * size), mine)] * 2,
             scratch_shapes=[
                 pltpu.VMEM((width, wide), jnp.bfloat16),
                 pltpu.SemaphoreType.DMA((BLOCKS,)),
@@ -263,16 +268,14 @@
         ),
         out_shape=[jax.ShapeDtypeStruct((tokens, wide), jnp.bfloat16)] * 2,
         cost_estimate=cost(2 * tokens * width * wide, 2 * width * wide),
-        compiler_params=params(),
+        compiler_params=params(38),
     )(where, normed, bias, own, *flat(pieces))
 
 
 def down_forward(where, residual, active, bias, own, pieces):
     tokens, wide = active.shape
     width = residual.shape[1]
-    share = own.shape[0]
-    groups = wide // share
-    chunk = 256
+    chunk = 2 * LANES
 
     def body(where_ref, residual_ref, active_ref, bias_ref, own_ref, *rest):
         piece_refs = regroup(rest[: len(flat(pieces))], pieces)
@@ -281,16 +284,21 @@
 
         @pl.when(at == 0)
         def _():
-            start_loads(where_ref, own_ref, piece_refs, [(0, LANES, 0)], weight, sems, ROW)
-            for hop in range(groups):
-                wait_rows(where_ref, weight, sems, hop, share)
-
-        columns = pl.ds(aligned(at * chunk, chunk), chunk)
+            start_loads(where_ref, own_ref, piece_refs, [(0, LANES, 0)], weight, sems, BLOCK)
+
+        for which in range(2):
+            block = jnp.bitwise_xor(where_ref[0], 2 * at + which)
+            finish(
+                weight.at[:, pl.ds(aligned(block * LANES, LANES), LANES)],
+                sems.at[2 * at + which],
+            )
+        pair = jnp.bitwise_xor(where_ref[0], 2 * at) // 2
+        columns = pl.ds(aligned(pair * chunk, chunk), chunk)
         out_ref[...] = (
             residual_ref[...] + product(active_ref[...], weight[:, columns]) + bias_ref[...]
         ).astype(jnp.bfloat16)
 
-    block = lambda at, _: (0, at)
+    block = lambda at, where_ref: (0, jnp.bitwise_xor(where_ref[0], 2 * at) // 2)
     return pl.pallas_call(
         body,
         grid_spec=pltpu.PrefetchScalarGridSpec(
@@ -305,12 +313,12 @@
             out_specs=pl.BlockSpec((tokens, chunk), block),
             scratch_shapes=[
                 pltpu.VMEM((wide, width), jnp.bfloat16),
-                pltpu.SemaphoreType.DMA((groups,)),
+                pltpu.SemaphoreType.DMA((BLOCKS,)),
             ],
         ),
         out_shape=jax.ShapeDtypeStruct((tokens, width), jnp.bfloat16),
         cost_estimate=cost(2 * tokens * width * wide, 2 * width * wide),
-        compiler_params=params(),
+        compiler_params=params(32),
     )(where, residual, active, bias, own, *flat(pieces))
 
 
@@ -319,7 +327,7 @@
     width = grad_block.shape[1]
     share = own.shape[0]
     groups = wide // share
-    tile = min(TILE, share)
+    tile = min(2 * TILE, share)
     per = share // tile
 
     def body(where_ref, grad_ref, slope_ref, own_ref, *rest):
@@ -365,11 +373,11 @@
             jax.ShapeDtypeStruct((1, wide), jnp.float32),
         ],
         cost_estimate=cost(2 * tokens * width * wide, 2 * width * wide),
-        compiler_params=params(),
+        compiler_params=params(34),
     )(where, grad_block, slope, own, *flat(pieces))
 
 
-def middle_backward(where, grad_pre, grad_block, residual, gain, own_up, own_out, pieces, size):
+def middle_backward(where, grad_pre, grad_block, residual, gain, own_up, own_out, pieces, pieces_out, size):
     tokens, wide = grad_pre.shape
     width = grad_block.shape[1]
     share = own_up.shape[0]
@@ -378,17 +386,24 @@
 
     def body(where_ref, pre_ref, block_ref, residual_ref, gain_ref, up_ref, own_ref, *rest):
         piece_refs = regroup(rest[: len(flat(pieces))], pieces)
-        (full_ref, half_ref, att_ref, gain_sum, shift_sum, res_sum, top_sum) = rest[
-            len(flat(pieces)) : len(flat(pieces)) + 7
-        ]
-        weight, weight_out, middle, sems, out_sems = rest[len(flat(pieces)) + 7 :]
+        rest = rest[len(flat(pieces)) :]
+        out_piece_refs = regroup(rest[: len(flat(pieces_out))], pieces_out)
+        rest = rest[len(flat(pieces_out)) :]
+        (full_ref, half_ref, att_ref, gain_sum, shift_sum, res_sum, top_sum) = rest[:7]
+        weight, weight_out, middle, sems, out_sems = rest[7:]
         at = pl.program_id(0)
 
         @pl.when(at == 0)
         def _():
             start_loads(where_ref, up_ref, piece_refs, [(0, size, 0)], weight, sems, ROW)
             start_loads(
-                where_ref, own_ref, piece_refs, [(size, LANES, 0)], weight_out, out_sems, ROW
+                where_ref,
+                own_ref,
+                out_piece_refs,
+                [(3 * LANES, LANES, 0)],
+                weight_out,
+                out_sems,
+                ROW,
             )
 
         wait_rows(where_ref, weight, sems, at, share)
@@ -426,7 +441,7 @@
             num_scalar_prefetch=1,
             grid=(groups,),
             in_specs=[pl.BlockSpec((tokens, wide), full), square, square, line]
-            + [ANY] * (2 + len(flat(pieces))),
+            + [ANY] * (2 + len(flat(pieces)) + len(flat(pieces_out))),
             out_specs=[square] * 3 + [line] * 4,
             scratch_shapes=[
                 pltpu.VMEM((width, wide), jnp.bfloat16),
@@ -444,7 +459,7 @@
         + [jax.ShapeDtypeStruct((1, width), jnp.float32)] * 4,
         cost_estimate=cost(2 * tokens * width * (wide + width), 2 * width * (wide + width)),
         compiler_params=params(),
-    )(where, grad_pre, grad_block, residual, gain, own_up, own_out, *flat(pieces))
+    )(where, grad_pre, grad_block, residual, gain, own_up, own_out, *flat(pieces), *flat(pieces_out))
 
 
 def qkv_backward(where, grad_proj, image, grad_res, gain, own, pieces):
@@ -505,7 +520,7 @@
             jax.ShapeDtypeStruct((1, width), jnp.float32),
         ],
         cost_estimate=cost(2 * tokens * width * wide, 2 * width * wide),
-        compiler_params=params(),
+        compiler_params=params(46),
     )(where, grad_proj, image, grad_res, gain, own, *flat(pieces))
 
 
@@ -543,7 +558,7 @@
             jax.ShapeDtypeStruct((count, PAIR // HD, tokens), jnp.float32),
         ],
         cost_estimate=cost(16 * tokens * tokens * width, 8 * tokens * width),
-        compiler_params=params(),
+        compiler_params=params(24),
     )(projected, projected, projected)
 
 
@@ -587,7 +602,7 @@
         out_shape=[jax.ShapeDtypeStruct((3, tokens, width), jnp.bfloat16)]
         + [jax.ShapeDtypeStruct((1, width), jnp.float32)] * 2,
         cost_estimate=cost(40 * tokens * tokens * width, 16 * tokens * width),
-        compiler_params=params(),
+        compiler_params=params(28),
     )(projected, projected, projected, grad_mixed, totals)
 
 
@@ -674,7 +689,7 @@
         ),
         out_shape=[jax.ShapeDtypeStruct((2, rows // 2, width), jnp.bfloat16)] * 4,
         cost_estimate=cost(16 * rows * tokens * width, 8 * rows * width + 4 * tokens * rows),
-        compiler_params=params(),
+        compiler_params=params(30),
     )(where, *operands)
 
 
@@ -744,26 +759,74 @@
         ),
         out_shape=[jax.ShapeDtypeStruct((2, groups // 2, LANES, share), jnp.bfloat16)] * 4,
         cost_estimate=cost(4 * rows * tokens * span, 2 * rows * span + 4 * tokens * rows),
-        compiler_params=params(),
+        compiler_params=params(22),
     )(where, left, left_pair, right, right_pair)
 
 
-def finish_flipped(blocks):
-    count, size, rows = blocks.shape
+def finish_flipped(where, pieces):
+    size, rows = pieces[0].shape
     step = min(rows, 256)
 
-    def body(in_ref, out_ref):
-        for at in range(count):
-            out_ref[:, at * size : (at + 1) * size] = in_ref[at].astype(jnp.float32).T
-
-    return pl.pallas_call(
-        body,
-        grid=(rows // step,),
-        in_specs=[pl.BlockSpec((count, size, step), lambda at: (0, 0, at))],
-        out_specs=pl.BlockSpec((step, count * size), lambda at: (at, 0)),
-        out_shape=jax.ShapeDtypeStruct((rows, count * size), jnp.float32),
-        compiler_params=params(),
-    )(blocks)
+    def body(where_ref, *refs):
+        for at in range(BLOCKS):
+            block = jnp.bitwise_xor(where_ref[0], at)
+            columns = pl.ds(aligned(block * size, LANES), size)
+            refs[-1][:, columns] = refs[at][...].astype(jnp.float32).T
+
+    return pl.pallas_call(
+        body,
+        grid_spec=pltpu.PrefetchScalarGridSpec(
+            num_scalar_prefetch=1,
+            grid=(rows // step,),
+            in_specs=[pl.BlockSpec((size, step), lambda at, _: (0, at))] * BLOCKS,
+            out_specs=pl.BlockSpec((step, BLOCKS * size), lambda at, _: (at, 0)),
+        ),
+        out_shape=jax.ShapeDtypeStruct((rows, BLOCKS * size), jnp.float32),
+        compiler_params=params(12),
+    )(where, *pieces)
+
+
+def join_rows(arrays):
+    rows, width = arrays[0].shape
+
+    def body(*refs):
+        for at, ref in enumerate(refs[:-1]):
+            refs[-1][at * rows : (at + 1) * rows, :] = ref[...]
+
+    return pl.pallas_call(
+        body,
+        out_shape=jax.ShapeDtypeStruct((rows * len(arrays), width), jnp.bfloat16),
+        compiler_params=params(12),
+    )(*arrays)
+
+
+def hop_totals(where, rest, got, groups):
+    half, width = rest[0].shape
+    share = 2 * half // groups
+
+    def body(where_ref, rest_a, rest_b, got_a, got_b, *outs):
+        total = outs[-1]
+        for at, (left, right) in enumerate(((rest_a, got_a), (rest_b, got_b))):
+            total[at * half : (at + 1) * half, :] = left[...].astype(jnp.float32) + right[
+                ...
+            ].astype(jnp.float32)
+        for hop in range(groups):
+            first = jnp.bitwise_xor(where_ref[1], hop) * share
+            outs[hop][...] = total[pl.ds(aligned(first, share), share), :].astype(jnp.bfloat16)
+
+    whole = lambda shape: pl.BlockSpec(shape, lambda at, _: (0, 0))
+    return pl.pallas_call(
+        body,
+        grid_spec=pltpu.PrefetchScalarGridSpec(
+            num_scalar_prefetch=1,
+            grid=(1,),
+            in_specs=[whole((half, width))] * 4,
+            out_specs=[whole((share, width))] * groups,
+            scratch_shapes=[pltpu.VMEM((2 * half, width), jnp.float32)],
+        ),
+        out_shape=[jax.ShapeDtypeStruct((share, width), jnp.bfloat16)] * groups,
+        compiler_params=params(12),
+    )(where, *rest, *got)
 
 
 def pick_blocks(where, sources, outs):
@@ -795,7 +858,7 @@
             out_specs=[pl.BlockSpec(shape, lambda at, _: (0, 0)) for shape in shapes],
         ),
         out_shape=[jax.ShapeDtypeStruct(shape, jnp.bfloat16) for shape in shapes],
-        compiler_params=params(),
+        compiler_params=params(12),
     )(where, *[sources[item[0]] for item in flat_outs])
 
 
@@ -830,7 +893,7 @@
             out_specs=[pl.BlockSpec((1, size), lambda at, _: (0, 0)) for size in outs],
         ),
         out_shape=[jax.ShapeDtypeStruct((1, size), jnp.float32) for size in outs],
-        compiler_params=params(),
+        compiler_params=params(8),
     )(where, *sources)
 
 
@@ -848,7 +911,7 @@
     return pl.pallas_call(
         body,
         out_shape=jax.ShapeDtypeStruct((groups, total), jnp.float32),
-        compiler_params=params(),
+        compiler_params=params(8),
     )(*vectors)
 
 
@@ -875,7 +938,7 @@
             out_specs=[pl.BlockSpec((1, length), lambda at, _: (0, 0)) for length in lengths],
         ),
         out_shape=[jax.ShapeDtypeStruct((1, length), jnp.float32) for length in lengths],
-        compiler_params=params(),
+        compiler_params=params(8),
     )(where, first, second)
 
 
@@ -898,7 +961,7 @@
         in_specs=[pl.BlockSpec((count, step, width), lambda at: (0, at, 0))],
         out_specs=[pl.BlockSpec((step, count * size), lambda at: (at, 0)) for size in sizes],
         out_shape=[jax.ShapeDtypeStruct((rows, count * size), jnp.float32) for size in sizes],
-        compiler_params=params(),
+        compiler_params=params(12),
     )(blocks)
 
 
@@ -934,7 +997,7 @@
         out_shape=[
             jax.ShapeDtypeStruct((rows, totals[out]), jnp.float32) for out in sorted(totals)
         ],
-        compiler_params=params(),
+        compiler_params=params(12),
     )(where, *pieces)
 
 
@@ -963,7 +1026,8 @@
     bottom = exchange(sent[1], 2)
     pieces = []
     for piece in ((own,), (by_x,), (by_y,), (top, bottom)):
-        pieces += [piece, tuple(exchange(array, 1) for array in piece)]
+        pair = tuple(exchange(array, 1) for array in piece)
+        pieces += [piece, pair]
     return pieces, sent
 
 
@@ -1002,15 +1066,13 @@
     return lax.all_gather(own, REP, axis=0, tiled=False)[:BLOCKS]
 
 
-def grp_sum(total):
-    groups = lax.axis_size(GRP)
-    share = total.shape[0] // groups
-    place = lax.axis_index(GRP)
-    sent = [
-        lax.dynamic_slice_in_dim(total, (place ^ hop) * share, share, 0) for hop in range(groups)
-    ]
-    got = [exchange(sent[hop], hop, GRP) for hop in range(1, groups)]
-    return sent[0], got
+def widened(rest, got):
+    mask = BLOCKS
+    while mask < lax.axis_size(REP):
+        rest = [add_rounded(*pair) for pair in zip(rest, got)]
+        got = [exchange(array, mask) for array in rest]
+        mask *= 2
+    return rest, got
 
 
 def sum_rounded(own, got):
@@ -1042,13 +1104,12 @@
     _, width = out_weight.shape
     hidden_block = fc1_weight.shape[1] // BLOCKS
 
-    (block_a,) = pick_blocks(where, [qkv_weight], [[(0, LANES, part) for part in range(3)]])
+    (block_a,) = pick_blocks(
+        where,
+        [qkv_weight, out_weight],
+        [[(0, LANES, part) for part in range(3)] + [(1, LANES, 0)]],
+    )
     got_a = all_hops(block_a)
-    block_b, block_c = pick_blocks(
-        where,
-        [fc1_weight, out_weight, fc2_weight],
-        [[(0, hidden_block, 0), (1, LANES, 0)], [(2, LANES, 0)]],
-    )
     vectors = (ln1_gain, ln1_shift, qv_bias, out_bias, ln2_gain, ln2_shift, fc1_bias, fc2_bias)
     sizes = [vec.shape[0] for vec in vectors]
     length = 16 * 2 * LANES
@@ -1058,12 +1119,16 @@
         offset += size
     packed = packed.reshape(16, 2 * LANES)
     got_v = all_hops(packed)
-
-    pieces_a, sent_a = spread(jnp.concatenate(got_a))
-    got_b = all_hops(tie(block_b, got_a))
-    pieces_b, sent_b = spread(jnp.concatenate(tie(got_b, sent_a)))
-    got_c = all_hops(tie(block_c, got_b))
-    pieces_c, _ = spread(jnp.concatenate(tie(got_c, sent_b)))
+    block_b, block_c = pick_blocks(
+        where,
+        [fc1_weight, fc2_weight],
+        [[(0, hidden_block, 0)], [(1, LANES, 0)]],
+    )
+    got_b = all_hops(block_b)
+    got_c = all_hops(block_c)
+    pieces_a, sent_a = spread(join_rows(got_a))
+    pieces_b, sent_b = spread(join_rows(tie(got_b, sent_a)))
+    pieces_c, _ = spread(join_rows(tie(got_c, sent_b)))
     gain_1, shift_1, bias_in, bias_attn, gain_2, shift_2, bias_up, bias_down = unpack_vectors(
         where, [packed] + got_v, sizes, 2, width
     )
@@ -1077,20 +1142,22 @@
     attended, totals = attention_forward(projected)
     attended_pair = exchange(attended, 1)
     residual, normed_mid = out_forward(
-        where, image, attended, bias_attn, gain_2, shift_2, out_weight, pieces_b, hidden_block
+        where, image, attended, bias_attn, gain_2, shift_2, out_weight, pieces_a, 3 * LANES
     )
     mid_pair = exchange(normed_mid, 1)
     active, slope = up_forward(where, normed_mid, bias_up, fc1_weight, pieces_b)
     active_pair = exchange(active, 1)
 
-    grad_pre, sum_up = down_backward(where, grad_block, slope, fc2_weight, pieces_c)
+    down_parts = weight_grads_flipped(
+        where, active, active_pair, grad_block, cot_pair, groups
+    )
+    down_got = first_sends(down_parts)
+    grad_pre, sum_up = down_backward(
+        tie(where, down_parts), grad_block, slope, fc2_weight, pieces_c
+    )
     pre_pair = exchange(grad_pre, 1)
-    down_parts = weight_grads_flipped(
-        tie(where, grad_pre), active, active_pair, grad_block, cot_pair, groups
-    )
-    down_got = first_sends(down_parts)
     middle = middle_backward(
-        tie(where, down_parts),
+        where,
         grad_pre,
         grad_block,
         residual,
@@ -1098,6 +1165,7 @@
         fc1_weight,
         out_weight,
         pieces_b,
+        pieces_a,
         hidden_block,
     )
     grad_res, grad_res_b, grad_attended, sum_gain_2, sum_shift_2, sum_res, sum_top = middle
@@ -1118,7 +1186,6 @@
     )
     proj_pair = exchange(grad_proj, 1)
     up_rest, up_got = second_sends(up_parts, tie(up_got, grad_proj))
-    down_blocks = gather(tie(down_own, grad_proj))
     qkv_parts = weight_grads(
         tie(where, up_rest), [(normed_in, normed_pair, grad_proj, proj_pair, LANES)]
     )
@@ -1148,35 +1215,43 @@
         groups,
     )
     got = exchange(sums, 1)
-    grad_down = finish_flipped(tie(down_blocks, sums)[:, 0])
-    sums = sums + tie(got, grad_down)
-    qkv_rest, qkv_got = second_sends(qkv_parts, tie(qkv_got, grad_down))
-    got = exchange(tie(sums, qkv_rest), 2)
+    qkv_rest, qkv_got = second_sends(qkv_parts, tie(qkv_got, sums))
+    sums = sums + tie(got, qkv_rest)
+    got = exchange(sums, 2)
     block_out = down_forward(
         tie(where, input_grad, sums, qkv_rest), residual, active, bias_down, fc2_weight, pieces_c
     )
-    up_blocks = gather(tie(up_own, block_out))
     sums = sums + tie(got, block_out)
     mask = BLOCKS
     while mask < lax.axis_size(REP):
         sums = sums + exchange(sums, mask)
         mask *= 2
-    qkv_total = block_total(qkv_rest, tie(qkv_got, block_out, sums))
-    own, qkv_got = grp_sum(qkv_total)
-    sums = sums + exchange(tie(sums, qkv_total), 4)
-    own = sum_rounded(own, tie(qkv_got, sums))
+    qkv_rest, qkv_got = widened(qkv_rest, tie(qkv_got, block_out, sums))
+    own, *qkv_sent = hop_totals(where, qkv_rest, qkv_got, groups)
+    qkv_got = [exchange(sent, hop, GRP) for hop, sent in enumerate(qkv_sent, start=1)]
+    down_own = tie(down_own, own)[0]
+    down_x = exchange(down_own, 2)
+    down_y = exchange(down_own, 4)
+    up_blocks = gather(tie(up_own, own))
+    sums = sums + exchange(tie(sums, own), 4)
+    down_both = exchange(tie(down_x, sums), 4)
+    own = sum_rounded(own, tie(qkv_got, sums, down_x, down_y))
     by_x = exchange(own, 2)
     by_y = exchange(own, 4)
     mask = 1
     while mask * 2 < groups:
         sums = sums + exchange(tie(sums, own), mask, GRP)
         mask *= 2
+    down_pieces = []
+    for piece in (down_own, down_x, down_y, down_both):
+        down_pieces += [piece, exchange(piece, 1)]
     both = exchange(tie(by_x, sums), 4)
     last = exchange(tie(sums, by_x), mask, GRP)
-    grad_up, grad_out = finish_blocks(tie(up_blocks, by_x, by_y), [hidden_block, LANES])
+    grad_down = finish_flipped(tie(where, own), down_pieces)
     qkv_pieces = []
     for piece in (own, by_x, by_y, both):
         qkv_pieces += [piece, exchange(piece, 1)]
+    grad_up, grad_out = finish_blocks(tie(up_blocks, grad_down, by_x, by_y), [hidden_block, LANES])
     (grad_qkv,) = finish_grads(
         where, qkv_pieces, [(at * LANES, LANES, 0, at * width) for at in range(3)]
     )

time: 499 us -> 488 us (0.978)
  Pallas kernels: 194 us -> 168 us
  local copies, waits for them, and re-layouts: 11 us -> 29.8 us
  waiting for transfers between devices: 191 us -> 179 us
  starting transfers between devices: 75.7 us -> 82.8 us
    ppermute x74 -> x81, waiting for transfers between devices: 184 us -> 154 us  [exchange(): return lax.ppermute(tensor, axis, [(at, at ^ mask) for at in range(size)])]
    unnamed x126 -> x230, local copies, waits for them, and re-layouts: 7.52 us -> 25.5 us
    reduce_scatter x2, waiting for transfers between devices: 6.79 us -> 24.3 us  [scatter(): return lax.psum_scatter(total, GRP, scatter_dimension=0, tiled=True)]
    ppermute x74 -> x81, starting transfers between devices: 75.6 us -> 82.6 us  [exchange(): return lax.ppermute(tensor, axis, [(at, at ^ mask) for at in range(size)])]
  transfers between devices with their start and end apart: 78 -> 84, of which waited for: 33 -> 31; matrix products, arithmetic and copies ran while one was open for 3% -> 2% of each run, Pallas kernels for 33% -> 24%
where the time goes in v4:
time: 488 us; the launch traced here: 484 us
  waiting for transfers between devices  179 us (37%)
  Pallas kernels  168 us (34%)
  starting transfers between devices  82.8 us (17%)
  local copies, waits for them, and re-layouts  29.8 us (6%)
  between operations  15.7 us (3%)
  other arithmetic  8.42 us (2%)
    ppermute x81, waiting for transfers between devices, exchange(): return lax.ppermute(tensor, axis, [(at, at ^ mask) for at in range(size)])  154 us
    ppermute x81, starting transfers between devices, exchange(): return lax.ppermute(tensor, axis, [(at, at ^ mask) for at in range(size)])  82.6 us
    unnamed x230, local copies, waits for them, and re-layouts  25.5 us
    pallas_call x1, Pallas kernels, attention_backward(): pl.pallas_call(body, grid=(count,), in_specs=[spec(0), spec(1), spec(2),...  24.9 us
    reduce_scatter x2, waiting for transfers between devices, scatter(): return lax.psum_scatter(total, GRP, scatter_dimension=0, tiled=True)  24.3 us
    pallas_call x2, Pallas kernels, weight_grads(): pl.pallas_call(body, grid_spec=pltpu.PrefetchScalarGridSpec(num_scalar_pr...  22.7 us
    pallas_call x1, Pallas kernels, middle_backward(): pl.pallas_call(body, grid_spec=pltpu.PrefetchScalarGridSpec(num_scalar_pr...  18.8 us
    pallas_call x1, Pallas kernels, up_forward(): pl.pallas_call(body, grid_spec=pltpu.PrefetchScalarGridSpec(num_scalar_pr...  14.5 us
  transfers between devices with their start and end apart: 84, of which 31 were waited for; matrix products, arithmetic and copies ran while one was open for 2% of the time, Pallas kernels for 24%

profile of v4, /device:TPU:0, one launch (start us, length us, event | category | flops | bytes accessed | tf_op | source)
XLA Modules:
  0.0 484.0 jit_solution(10681702238720481225)
XLA Ops:
  10.4 3.1 collective-permute-start.3
  13.5 2.6 collective-permute-start.4
  16.1 8.6 %collective-permute-done.3.refs_0_ = bf16[256,512]{1,0:T(8,128)(2,1)S(1)} collective-permute-done((bf16[256,512]{1,0:T(8,128)(2,1)S(1)}, bf16[256,512]{1,0:T(8,128)(2,1)S(1)}, u32[]{:S(2)}, u32[]{:S(2)}) %collective-permute-start.3) | collective-permute-done | bytes 262176 | tf_op jit(solution)/shard_map/ppermute | solution.py:1009
  24.7 10.1 %collective-permute-done.4.refs_1_ = bf16[256,512]{1,0:T(8,128)(2,1)S(1)} collective-permute-done((bf16[256,512]{1,0:T(8,128)(2,1)S(1)}, bf16[256,512]{1,0:T(8,128)(2,1)S(1)}, u32[]{:S(2)}, u32[]{:S(2)}) %collective-permute-start.4) | collective-permute-done | bytes 262176 | tf_op jit(solution)/shard_map/ppermute | solution.py:1009
  34.9 1.6 collective-permute-start.7
  36.5 1.5 collective-permute-start.9
  39.4 4.8 collective-permute-start.15
  46.6 5.2 %collective-permute-done.7.rest_2_.rest_12_ = bf16[768,512]{1,0:T(8,128)(2,1)S(1)} collective-permute-done((bf16[768,512]{1,0:T(8,128)(2,1)S(1)}, bf16[768,512]{1,0:T(8,128)(2,1)S(1)}, u32[]{:S(2)}, u32[]{:S(2)}) %collective-permute-start.7) | collective-permute-done | bytes 786464 | tf_op jit(solution)/shard_map/ppermute | solution.py:1009
  54.8 10.5 %collective-permute-done.16.refs_1_ = bf16[256,512]{1,0:T(8,128)(2,1)S(1)} collective-permute-done((bf16[256,512]{1,0:T(8,128)(2,1)S(1)}, bf16[256,512]{1,0:T(8,128)(2,1)S(1)}, u32[]{:S(2)}, u32[]{:S(2)}) %collective-permute-start.16) | collective-permute-done | bytes 262176 | tf_op jit(solution)/shard_map/ppermute | solution.py:1009
  67.2 1.5 collective-permute-start.11
  68.8 1.5 collective-permute-start.12
  71.6 3.4 collective-permute-start
  75.1 1.7 collective-permute-done.refs_1_
  76.7 3.0 collective-permute-start.1
  79.7 1.6 collective-permute-done.1.refs_2_
  81.4 2.4 collective-permute-start.2
  83.7 3.1 collective-permute-done.2.refs_3_
  86.8 2.1 collective-permute-done.11.rest_6_.rest_16_
  93.1 1.5 collective-permute-start.24
  95.9 1.5 copy-done.17
  97.4 8.9 %shard_map.248 = (bf16[577,1024]{1,0:T(8,128)(2,1)S(1)}, bf16[577,3072]{1,0:T(8,128)(2,1)S(1)}) custom-call(s32[2]{0:T(128)S(1)} %pad_add_fusion.1.where_ref, bf16[577,1024]{1,0:T(8,128)(2,1)S(1)} %bitcast.40, f32[1,1024]{1,0:T(1,128)S(1)} %get-tuple-element.111.gain_ref, f32[1,1024]{1,0:T(1,128)S(1)} %get-tuple-element.112.shift_ref, ...), custom_call_target="tpu_custom_call" | custom-call | flops 3630170112 | bytes 6291456 | tf_op jit(solution)/shard_map/pallas_call | solution.py:148
  106.9 13.9 %shard_map.249 = (bf16[577,1024]{1,0:T(8,128)(2,1)S(1)}, f32[8,2,577]{2,1,0:T(2,128)S(1)}) custom-call(bf16[577,3072]{1,0:T(8,128)(2,1)S(1)} %get-tuple-element.114.query_ref.key_ref.value_ref, bf16[577,3072]{1,0:T(8,128)(2,1)S(1)} %get-tuple-element.114.query_ref.key_ref.value_ref, bf16[577,3072]{1,0:T(8,128)(2,1)S(1)} %get-tuple-element.114.query_ref.key_ref.value_ref), custom_call_target="tpu_custom_call" | custom-call | flops 5454708736 | bytes 4726784 | tf_op jit(solution)/shard_map/pallas_call | solution.py:548
  121.0 5.6 %shard_map.250 = (f32[577,1024]{1,0:T(8,128)S(1)}, bf16[577,1024]{1,0:T(8,128)(2,1)}) custom-call(s32[2]{0:T(128)S(1)} %pad_add_fusion.1.where_ref, bf16[577,1024]{1,0:T(8,128)(2,1)S(1)} %bitcast.41, bf16[577,1024]{1,0:T(8,128)(2,1)S(1)} %get-tuple-element.115.attended_ref.refs_4_, f32[1,1024]{1,0:T(1,128)S(1)} %get-tuple-element.116.bias_ref, ...), custom_call_target="tpu_custom_call" | custom-call | flops 1210056704 | bytes 2097152 | tf_op jit(solution)/shard_map/pallas_call | solution.py:204
  128.2 14.5 %shard_map.253 = (bf16[577,4096]{1,0:T(8,128)(2,1)S(1)}, bf16[577,4096]{1,0:T(8,128)(2,1)}) custom-call(s32[2]{0:T(128)S(1)} %pad_add_fusion.1.where_ref, bf16[577,1024]{1,0:T(8,128)(2,1)} %get-tuple-element.119.normed_ref.refs_0_, f32[1,4096]{1,0:T(1,128)S(1)} %get-tuple-element.120.bias_ref, bf16[256,4096]{1,0:T(8,128)(2,1)S(1)} %copy-done.10, ...), custom_call_target="tpu_custom_call" | custom-call | flops 4840226816 | bytes 8388608 | tf_op jit(solution)/shard_map/pallas_call | solution.py:256
  143.0 6.0 %collective-permute-start.29 = (bf16[1024,128]{1,0:T(8,128)(2,1)S(1)}, bf16[1024,128]{1,0:T(8,128)(2,1)S(1)}, u32[]{:S(2)}, u32[]{:S(2)}) collective-permute-start(bf16[1024,128]{1,0:T(8,128)(2,1)S(1)} %copy-done.98), channel_id=1, source_target_pairs={{0,1},{1,0},{2,3},{3,2},{4,5},{5,4},{6,7},{7,6},{8,9},{9,8},{10,11... | collective-permute-start | bytes 786440 | tf_op jit(solution)/shard_map/ppermute | solution.py:1009
  149.1 1.9 collective-permute-start.30
  152.4 8.9 %collective-permute-done.29.refs_0_ = bf16[1024,128]{1,0:T(8,128)(2,1)S(1)} collective-permute-done((bf16[1024,128]{1,0:T(8,128)(2,1)S(1)}, bf16[1024,128]{1,0:T(8,128)(2,1)S(1)}, u32[]{:S(2)}, u32[]{:S(2)}) %collective-permute-start.29) | collective-permute-done | bytes 262176 | tf_op jit(solution)/shard_map/ppermute | solution.py:1009
  161.3 9.1 %collective-permute-done.30.refs_1_ = bf16[1024,128]{1,0:T(8,128)(2,1)S(1)} collective-permute-done((bf16[1024,128]{1,0:T(8,128)(2,1)S(1)}, bf16[1024,128]{1,0:T(8,128)(2,1)S(1)}, u32[]{:S(2)}, u32[]{:S(2)}) %collective-permute-start.30) | collective-permute-done | bytes 262176 | tf_op jit(solution)/shard_map/ppermute | solution.py:1009
  172.1 17.0 %collective-permute-done.33.rest_2_ = bf16[3072,128]{1,0:T(8,128)(2,1)S(1)} collective-permute-done((bf16[3072,128]{1,0:T(8,128)(2,1)S(1)}, bf16[3072,128]{1,0:T(8,128)(2,1)S(1)}, u32[]{:S(2)}, u32[]{:S(2)}) %collective-permute-start.33) | collective-permute-done | bytes 786464 | tf_op jit(solution)/shard_map/ppermute | solution.py:1009
  191.8 6.7 %collective-permute-done.37.rest_6_ = bf16[1536,128]{1,0:T(8,128)(2,1)S(1)} collective-permute-done((bf16[1536,128]{1,0:T(8,128)(2,1)S(1)}, bf16[1536,128]{1,0:T(8,128)(2,1)S(1)}, u32[]{:S(2)}, u32[]{:S(2)}) %collective-permute-start.37) | collective-permute-done | bytes 393248 | tf_op jit(solution)/shard_map/ppermute | solution.py:1009
  199.8 11.9 %shard_map.254 = (bf16[2,2,128,1024]{3,2,1,0:T(8,128)(2,1)}, bf16[2,2,128,1024]{3,2,1,0:T(8,128)(2,1)S(1)}, bf16[2,2,128,1024]{3,2,1,0:T(8,128)(2,1)}, bf16[2,2,128,1024]{3,2,1,0:T(8,128)(2,1)S(1)}) custom-call(s32[2]{0:T(128)S(1)} %pad_add_fusion.1.where_ref, bf16[577,4096]{1,0:T(8,128)(2,1)S(1)} %get-tuple-element.125.left_ref.active_ref, ...), custom_call_target="tpu_custom_call" | custom-call | flops 4840226816 | bytes 13647872 | tf_op jit(solution)/shard_map/pallas_call | solution.py:747
  213.7 2.1 copy-done.71
  216.0 10.2 %shard_map.256 = (bf16[577,4096]{1,0:T(8,128)(2,1)}, f32[1,4096]{1,0:T(1,128)S(1)}) custom-call(s32[2]{0:T(128)S(1)} %pad_add_fusion.1.where_ref, bf16[577,1024]{1,0:T(8,128)(2,1)S(1)} %bitcast.47, bf16[577,4096]{1,0:T(8,128)(2,1)S(1)} %bitcast.53, bf16[1024,1024]{1,0:T(8,128)(2,1)S(1)} %copy-done.33, bf16[3072,128]{1,0:T(8,128)(2,1)S(1)} %shard_map.255.rest_0_, ...), custom_call_target="tpu_custom_call" | custom-call | flops 4840226816 | bytes 8388608 | tf_op jit(solution)/shard_map/pallas_call | solution.py:355
  228.6 18.8 %shard_map.257 = (f32[577,1024]{1,0:T(8,128)}, bf16[577,1024]{1,0:T(8,128)(2,1)}, bf16[577,1024]{1,0:T(8,128)(2,1)}, f32[1,1024]{1,0:T(1,128)}, f32[1,1024]{1,0:...) custom-call(s32[2]{0:T(128)} %copy-done.60, bf16[577,4096]{1,0:T(8,128)(2,1)} %get-tuple-element.136.pre_ref.refs_2_, ...), custom_call_target="tpu_custom_call" | custom-call | flops 6050283520 | bytes 10485760 | tf_op jit(solution)/shard_map/pallas_call | solution.py:438
  247.4 4.8 collective-permute-done.41
  253.2 1.7 fusion.7
  254.9 1.7 fusion.6
  259.2 14.4 %shard_map.258 = (bf16[2,512,640]{2,1,0:T(8,128)(2,1)S(1)}, bf16[2,512,640]{2,1,0:T(8,128)(2,1)S(1)}, bf16[2,512,640]{2,1,0:T(8,128)(2,1)S(1)}, bf16[2,512,640]{2,1,0:T(8,128)(2,1)S(1)}) custom-call(s32[2]{0:T(128)S(1)} %copy-done.61, bf16[577,1024]{1,0:T(8,128)(2,1)} %get-tuple-element.119.normed_ref.refs_0_, ...), custom_call_target="tpu_custom_call" | custom-call | flops 6050283520 | bytes 7606272 | tf_op jit(solution)/shard_map/pallas_call | solution.py:678
  277.5 2.0 copy-done.102
  279.5 24.9 %shard_map.259 = (bf16[3,577,1024]{2,1,0:T(8,128)(2,1)S(1)}, f32[1,1024]{1,0:T(1,128)S(1)}, f32[1,1024]{1,0:T(1,128)S(1)}) custom-call(bf16[577,3072]{1,0:T(8,128)(2,1)S(1)} %copy-done.102, bf16[577,3072]{1,0:T(8,128)(2,1)S(1)} %copy-done.102, bf16[577,3072]{1,0:T(8,128)(2,1)S(1)} %copy-done.102, bf16[577,1024]{1,0:T(8,128)(2,1)S(1)} %copy-done.79, ...), custom_call_target="tpu_custom_call" | custom-call | flops 13636771840 | bytes 9453568 | tf_op jit(solution)/shard_map/pallas_call | solution.py:596
  306.2 29.4 %collective-permute-done.47 = bf16[2,512,640]{2,1,0:T(8,128)(2,1)S(1)} collective-permute-done((bf16[2,512,640]{2,1,0:T(8,128)(2,1)S(1)}, bf16[2,512,640]{2,1,0:T(8,128)(2,1)S(1)}, u32[]{:S(2)}, u32[]{:S(2)}) %collective-permute-start.47) | collective-permute-done | bytes 1310752 | tf_op jit(solution)/shard_map/ppermute | solution.py:1009
  336.3 1.5 collective-permute-start.54
  339.2 8.3 %shard_map.260 = (bf16[2,512,384]{2,1,0:T(8,128)(2,1)S(1)}, bf16[2,512,384]{2,1,0:T(8,128)(2,1)S(1)}, bf16[2,512,384]{2,1,0:T(8,128)(2,1)S(1)}, bf16[2,512,384]{2,1,0:T(8,128)(2,1)S(1)}) custom-call(s32[2]{0:T(128)S(1)} %copy-done.61, bf16[577,1024]{1,0:T(8,128)(2,1)S(1)} %copy-done.78, bf16[577,1024]{1,0:T(8,128)(2,1)S(1)} %collective-permute-done.51.refs_1_, ...), custom_call_target="tpu_custom_call" | custom-call | flops 3630170112 | bytes 5509120 | tf_op jit(solution)/shard_map/pallas_call | solution.py:678
  347.5 4.8 collective-permute-done.54
  352.3 1.6 collective-permute-done.53
  363.8 13.2 %shard_map.261 = (bf16[577,1024]{1,0:T(8,128)(2,1)}, f32[1,1024]{1,0:T(1,128)S(1)}, f32[1,1024]{1,0:T(1,128)S(1)}) custom-call(s32[2]{0:T(128)S(1)} %copy-done.61, bf16[3,577,1024]{2,1,0:T(8,128)(2,1)} %copy-done.22, bf16[577,1024]{1,0:T(8,128)(2,1)S(1)} %bitcast.42, f32[577,1024]{1,0:T(8,128)} %get-tuple-element.138.res_ref, f32[1,1024]{1,0:T(1,128)S(1)} %copy-done.66, ...), custom_call_target="tpu_custom_call" | custom-call | flops 3630170112 | bytes 6291456 | tf_op jit(solution)/shard_map/pallas_call | solution.py:502
  381.6 2.4 copy-done.72
  383.9 10.0 %shard_map.263 = bf16[577,1024]{1,0:T(8,128)(2,1)} custom-call(s32[2]{0:T(128)S(1)} %copy-done.61, f32[577,1024]{1,0:T(8,128)S(1)} %copy-done.31, bf16[577,4096]{1,0:T(8,128)(2,1)S(1)} %copy-done.72, f32[1,1024]{1,0:T(1,128)S(1)} %copy-done.100, bf16[1024,1024]{1,0:T(8,128)(2,1)S(1)} %copy-done.34, bf16[3072,128]{1,0:T(8,128)(2,1)S(1)} %copy-done.46, ...), custom_call_target="tpu_custom_call" | custom-call | flops 4840226816 | bytes 8388608 | tf_op jit(solution)/shard_map/pallas_call | solution.py:302
  395.0 24.3 %reduce-scatter.3.cloned.1.call-done = bf16[1,128,1024]{2,1,0:T(8,128)(2,1)} async-done(((bf16[4,128,1024]{2,1,0:T(8,128)(2,1)}), bf16[1,128,1024]{2,1,0:T(8,128)(2,1)}) %reduce-scatter.3.cloned.1.call-update) | async-done | bytes 262160 | tf_op jit(solution)/shard_map/reduce_scatter | solution.py:1062
  420.7 1.5 collective-permute-start.66
  424.2 5.2 %collective-permute-done.61 = f32[4,3072]{1,0:T(4,128)S(1)} collective-permute-done((f32[4,3072]{1,0:T(4,128)S(1)}, f32[4,3072]{1,0:T(4,128)S(1)}, u32[]{:S(2)}, u32[]{:S(2)}) %collective-permute-start.61) | collective-permute-done | bytes 49184 | tf_op jit(solution)/shard_map/ppermute | solution.py:1009
  430.2 1.8 collective-permute-done.62
  432.0 6.2 %collective-permute-done.63 = bf16[256,384]{1,0:T(8,128)(2,1)S(1)} collective-permute-done((bf16[256,384]{1,0:T(8,128)(2,1)S(1)}, bf16[256,384]{1,0:T(8,128)(2,1)S(1)}, u32[]{:S(2)}, u32[]{:S(2)}) %collective-permute-start.63) | collective-permute-done | bytes 196640 | tf_op jit(solution)/shard_map/ppermute | solution.py:1009
  440.4 4.1 collective-permute-start.67
  444.5 2.1 collective-permute-done.67
  446.6 1.5 collective-permute-done.68.refs_2_
  448.1 1.5 collective-permute-start.72
  451.5 4.7 collective-permute-done.72.refs_4_
  456.2 6.1 %collective-permute-start.69 = (f32[4,3072]{1,0:T(4,128)S(1)}, f32[4,3072]{1,0:T(4,128)S(1)}, u32[]{:S(2)}, u32[]{:S(2)}) collective-permute-start(f32[4,3072]{1,0:T(4,128)S(1)} %add.151.first_ref), channel_id=1, source_target_pairs={{0,2},{1,3},{2,0},{3,1},{4,6},{5,7},{6,4},{7,5},{8,10},{9,11},{10,... | collective-permute-start | bytes 147464 | tf_op jit(solution)/shard_map/ppermute | solution.py:1009
  462.3 2.1 collective-permute-done.69.second_ref
  466.6 3.6 shard_map.267
  470.2 2.4 shard_map.266
  472.7 1.7 copy-done.29
  474.4 2.7 shard_map.268
  (388 shorter events, 69.1 us)
Async XLA Ops:
  7.2 387.8 %reduce-scatter.5.cloned.1.call-start = ((), (), s32[]{:S(2)}) async-start(), calls=%async_computation.3 | async-start | bytes 1638400 | tf_op jit(solution)/shard_map/reduce_scatter | solution.py:1062
  10.4 14.3 %collective-permute-start.3 = (bf16[256,512]{1,0:T(8,128)(2,1)S(1)}, bf16[256,512]{1,0:T(8,128)(2,1)S(1)}, u32[]{:S(2)}, u32[]{:S(2)}) collective-permute-start(bf16[256,512]{1,0:T(8,128)(2,1)S(1)} %shard_map.246), channel_id=1, source_target_pairs={{0,1},{1,0},{2,3},{3,2},{4,5},{5,4},{6,7},{7,6},{8,9},{9,8},{10,11... | collective-permute-start | bytes 786440 | tf_op jit(solution)/shard_map/ppermute | solution.py:1009
  13.5 21.3 %collective-permute-start.4 = (bf16[256,512]{1,0:T(8,128)(2,1)S(1)}, bf16[256,512]{1,0:T(8,128)(2,1)S(1)}, u32[]{:S(2)}, u32[]{:S(2)}) collective-permute-start(bf16[256,512]{1,0:T(8,128)(2,1)S(1)} %shard_map.246), channel_id=1, source_target_pairs={{0,2},{1,3},{2,0},{3,1},{4,6},{5,7},{6,4},{7,5},{8,10},{9,11},{10,... | collective-permute-start | bytes 786440 | tf_op jit(solution)/shard_map/ppermute | solution.py:1009
  16.1 18.7 %collective-permute-start.5 = (bf16[256,512]{1,0:T(8,128)(2,1)S(1)}, bf16[256,512]{1,0:T(8,128)(2,1)S(1)}, u32[]{:S(2)}, u32[]{:S(2)}) collective-permute-start(bf16[256,512]{1,0:T(8,128)(2,1)S(1)} %shard_map.246), channel_id=1, source_target_pairs={{0,3},{1,2},{2,1},{3,0},{4,7},{5,6},{6,5},{7,4},{8,11},{9,10},{10,... | collective-permute-start | bytes 786440 | tf_op jit(solution)/shard_map/ppermute | solution.py:1009
  34.9 17.0 %collective-permute-start.7 = (bf16[768,512]{1,0:T(8,128)(2,1)S(1)}, bf16[768,512]{1,0:T(8,128)(2,1)S(1)}, u32[]{:S(2)}, u32[]{:S(2)}) collective-permute-start(bf16[768,512]{1,0:T(8,128)(2,1)S(1)} %shard_map.247.rest_0_.rest_10_), channel_id=1, source_target_pairs={{0,8},{4,12},{8,0},{12,4},{16,24},{20,28},{24,16},{28,20},{1,9},{5... | collective-permute-start | bytes 2359304 | tf_op jit(solution)/shard_map/ppermute | solution.py:1009
  36.5 16.6 %collective-permute-start.9 = (bf16[768,512]{1,0:T(8,128)(2,1)S(1)}, bf16[768,512]{1,0:T(8,128)(2,1)S(1)}, u32[]{:S(2)}, u32[]{:S(2)}) collective-permute-start(bf16[768,512]{1,0:T(8,128)(2,1)S(1)} %shard_map.247.rest_0_.rest_10_), channel_id=1, source_target_pairs={{0,16},{4,20},{8,24},{12,28},{16,0},{20,4},{24,8},{28,12},{1,17},{... | collective-permute-start | bytes 2359304 | tf_op jit(solution)/shard_map/ppermute | solution.py:1009
  39.4 15.4 %collective-permute-start.15 = (bf16[256,512]{1,0:T(8,128)(2,1)S(1)}, bf16[256,512]{1,0:T(8,128)(2,1)S(1)}, u32[]{:S(2)}, u32[]{:S(2)}) collective-permute-start(bf16[256,512]{1,0:T(8,128)(2,1)S(1)} %get-tuple-element.121), channel_id=1, source_target_pairs={{0,1},{1,0},{2,3},{3,2},{4,5},{5,4},{6,7},{7,6},{8,9},{9,8},{10,11... | collective-permute-start | bytes 786440 | tf_op jit(solution)/shard_map/ppermute | solution.py:1009
  44.2 21.1 %collective-permute-start.16 = (bf16[256,512]{1,0:T(8,128)(2,1)S(1)}, bf16[256,512]{1,0:T(8,128)(2,1)S(1)}, u32[]{:S(2)}, u32[]{:S(2)}) collective-permute-start(bf16[256,512]{1,0:T(8,128)(2,1)S(1)} %get-tuple-element.121), channel_id=1, source_target_pairs={{0,2},{1,3},{2,0},{3,1},{4,6},{5,7},{6,4},{7,5},{8,10},{9,11},{10,... | collective-permute-start | bytes 786440 | tf_op jit(solution)/shard_map/ppermute | solution.py:1009
  45.2 20.1 %collective-permute-start.17 = (bf16[256,512]{1,0:T(8,128)(2,1)S(1)}, bf16[256,512]{1,0:T(8,128)(2,1)S(1)}, u32[]{:S(2)}, u32[]{:S(2)}) collective-permute-start(bf16[256,512]{1,0:T(8,128)(2,1)S(1)} %get-tuple-element.121), channel_id=1, source_target_pairs={{0,3},{1,2},{2,1},{3,0},{4,7},{5,6},{6,5},{7,4},{8,11},{9,10},{10,... | collective-permute-start | bytes 786440 | tf_op jit(solution)/shard_map/ppermute | solution.py:1009
  66.2 23.2 %collective-permute-start.19 = (bf16[768,512]{1,0:T(8,128)(2,1)}, bf16[768,512]{1,0:T(8,128)(2,1)}, u32[]{:S(2)}, u32[]{:S(2)}) collective-permute-start(bf16[768,512]{1,0:T(8,128)(2,1)} %shard_map.252.rest_0_), channel_id=1, source_target_pairs={{0,8},{4,12},{8,0},{12,4},{16,24},{20,28},{24,16},{28,20},{1,9},{5... | collective-permute-start | bytes 2359304 | tf_op jit(solution)/shard_map/ppermute | solution.py:1009
  66.7 22.7 %collective-permute-start.21 = (bf16[768,512]{1,0:T(8,128)(2,1)}, bf16[768,512]{1,0:T(8,128)(2,1)}, u32[]{:S(2)}, u32[]{:S(2)}) collective-permute-start(bf16[768,512]{1,0:T(8,128)(2,1)} %shard_map.252.rest_0_), channel_id=1, source_target_pairs={{0,16},{4,20},{8,24},{12,28},{16,0},{20,4},{24,8},{28,12},{1,17},{... | collective-permute-start | bytes 2359304 | tf_op jit(solution)/shard_map/ppermute | solution.py:1009
  67.2 21.6 %collective-permute-start.11 = (bf16[384,512]{1,0:T(8,128)(2,1)}, bf16[384,512]{1,0:T(8,128)(2,1)S(1)}, u32[]{:S(2)}, u32[]{:S(2)}) collective-permute-start(bf16[384,512]{1,0:T(8,128)(2,1)} %slice.120), channel_id=1, source_target_pairs={{0,16},{4,20},{8,24},{12,28},{16,0},{20,4},{24,8},{28,12},{1,17},{... | collective-permute-start | bytes 1179656 | tf_op jit(solution)/shard_map/ppermute | solution.py:1009
  68.8 20.1 %collective-permute-start.12 = (bf16[384,512]{1,0:T(8,128)(2,1)}, bf16[384,512]{1,0:T(8,128)(2,1)}, u32[]{:S(2)}, u32[]{:S(2)}) collective-permute-start(bf16[384,512]{1,0:T(8,128)(2,1)} %slice.121), channel_id=1, source_target_pairs={{0,8},{4,12},{8,0},{12,4},{16,24},{20,28},{24,16},{28,20},{1,9},{5... | collective-permute-start | bytes 1179656 | tf_op jit(solution)/shard_map/ppermute | solution.py:1009
  92.0 14.4 %collective-permute-start.23 = (bf16[384,512]{1,0:T(8,128)(2,1)S(1)}, bf16[384,512]{1,0:T(8,128)(2,1)S(1)}, u32[]{:S(2)}, u32[]{:S(2)}) collective-permute-start(bf16[384,512]{1,0:T(8,128)(2,1)S(1)} %slice.122), channel_id=1, source_target_pairs={{0,16},{4,20},{8,24},{12,28},{16,0},{20,4},{24,8},{28,12},{1,17},{... | collective-permute-start | bytes 1179656 | tf_op jit(solution)/shard_map/ppermute | solution.py:1009
  93.1 13.6 %collective-permute-start.24 = (bf16[384,512]{1,0:T(8,128)(2,1)S(1)}, bf16[384,512]{1,0:T(8,128)(2,1)S(1)}, u32[]{:S(2)}, u32[]{:S(2)}) collective-permute-start(bf16[384,512]{1,0:T(8,128)(2,1)S(1)} %slice.123), channel_id=1, source_target_pairs={{0,8},{4,12},{8,0},{12,4},{16,24},{20,28},{24,16},{28,20},{1,9},{5... | collective-permute-start | bytes 1179656 | tf_op jit(solution)/shard_map/ppermute | solution.py:1009
  95.2 32.8 %collective-permute-start.18 = (bf16[768,512]{1,0:T(8,128)(2,1)}, bf16[768,512]{1,0:T(8,128)(2,1)S(1)}, u32[]{:S(2)}, u32[]{:S(2)}) collective-permute-start(bf16[768,512]{1,0:T(8,128)(2,1)} %shard_map.252.rest_0_), channel_id=1, source_target_pairs={{0,4},{4,0},{8,12},{12,8},{16,20},{20,16},{24,28},{28,24},{1,5},{5... | collective-permute-start | bytes 2359304 | tf_op jit(solution)/shard_map/ppermute | solution.py:1009
  95.3 32.8 %collective-permute-start.20 = (bf16[768,512]{1,0:T(8,128)(2,1)}, bf16[768,512]{1,0:T(8,128)(2,1)S(1)}, u32[]{:S(2)}, u32[]{:S(2)}) collective-permute-start(bf16[768,512]{1,0:T(8,128)(2,1)} %collective-permute-done.19.rest_2_), channel_id=1, source_target_pairs={{0,4},{4,0},{8,12},{12,8},{16,20},{20,16},{24,28},{28,24},{1,5},{5... | collective-permute-start | bytes 2359304 | tf_op jit(solution)/shard_map/ppermute | solution.py:1009
  95.8 32.3 %collective-permute-start.22 = (bf16[768,512]{1,0:T(8,128)(2,1)}, bf16[768,512]{1,0:T(8,128)(2,1)S(1)}, u32[]{:S(2)}, u32[]{:S(2)}) collective-permute-start(bf16[768,512]{1,0:T(8,128)(2,1)} %collective-permute-done.21.rest_4_), channel_id=1, source_target_pairs={{0,4},{4,0},{8,12},{12,8},{16,20},{20,16},{24,28},{28,24},{1,5},{5... | collective-permute-start | bytes 2359304 | tf_op jit(solution)/shard_map/ppermute | solution.py:1009
  106.4 21.7 %collective-permute-start.25 = (bf16[384,512]{1,0:T(8,128)(2,1)S(1)}, bf16[384,512]{1,0:T(8,128)(2,1)S(1)}, u32[]{:S(2)}, u32[]{:S(2)}) collective-permute-start(bf16[384,512]{1,0:T(8,128)(2,1)S(1)} %collective-permute-done.23.rest_6_), channel_id=1, source_target_pairs={{0,4},{4,0},{8,12},{12,8},{16,20},{20,16},{24,28},{28,24},{1,5},{5... | collective-permute-start | bytes 1179656 | tf_op jit(solution)/shard_map/ppermute | solution.py:1009
  106.7 21.4 %collective-permute-start.26 = (bf16[384,512]{1,0:T(8,128)(2,1)S(1)}, bf16[384,512]{1,0:T(8,128)(2,1)S(1)}, u32[]{:S(2)}, u32[]{:S(2)}) collective-permute-start(bf16[384,512]{1,0:T(8,128)(2,1)S(1)} %collective-permute-done.24.rest_7_), channel_id=1, source_target_pairs={{0,4},{4,0},{8,12},{12,8},{16,20},{20,16},{24,28},{28,24},{1,5},{5... | collective-permute-start | bytes 1179656 | tf_op jit(solution)/shard_map/ppermute | solution.py:1009
  142.7 56.6 %collective-permute-start.27 = (bf16[577,4096]{1,0:T(8,128)(2,1)S(1)}, bf16[577,4096]{1,0:T(8,128)(2,1)S(1)}, u32[]{:S(2)}, u32[]{:S(2)}) collective-permute-start(bf16[577,4096]{1,0:T(8,128)(2,1)S(1)} %get-tuple-element.125.left_ref.active_ref), channel_id=1, source_target_pairs={{0,4},{4,0},{8,12},{12,8},{16,20},{20,16},{24,28},{28,24},{1,5},{5... | collective-permute-start | bytes 14180360 | tf_op jit(solution)/shard_map/ppermute | solution.py:1009
  143.0 18.3 %collective-permute-start.29 = (bf16[1024,128]{1,0:T(8,128)(2,1)S(1)}, bf16[1024,128]{1,0:T(8,128)(2,1)S(1)}, u32[]{:S(2)}, u32[]{:S(2)}) collective-permute-start(bf16[1024,128]{1,0:T(8,128)(2,1)S(1)} %copy-done.98), channel_id=1, source_target_pairs={{0,1},{1,0},{2,3},{3,2},{4,5},{5,4},{6,7},{7,6},{8,9},{9,8},{10,11... | collective-permute-start | bytes 786440 | tf_op jit(solution)/shard_map/ppermute | solution.py:1009
  149.1 21.3 %collective-permute-start.30 = (bf16[1024,128]{1,0:T(8,128)(2,1)S(1)}, bf16[1024,128]{1,0:T(8,128)(2,1)S(1)}, u32[]{:S(2)}, u32[]{:S(2)}) collective-permute-start(bf16[1024,128]{1,0:T(8,128)(2,1)S(1)} %copy-done.98), channel_id=1, source_target_pairs={{0,2},{1,3},{2,0},{3,1},{4,6},{5,7},{6,4},{7,5},{8,10},{9,11},{10,... | collective-permute-start | bytes 786440 | tf_op jit(solution)/shard_map/ppermute | solution.py:1009
  150.9 19.5 %collective-permute-start.31 = (bf16[1024,128]{1,0:T(8,128)(2,1)S(1)}, bf16[1024,128]{1,0:T(8,128)(2,1)S(1)}, u32[]{:S(2)}, u32[]{:S(2)}) collective-permute-start(bf16[1024,128]{1,0:T(8,128)(2,1)S(1)} %copy-done.98), channel_id=1, source_target_pairs={{0,3},{1,2},{2,1},{3,0},{4,7},{5,6},{6,5},{7,4},{8,11},{9,10},{10,... | collective-permute-start | bytes 786440 | tf_op jit(solution)/shard_map/ppermute | solution.py:1009
  152.4 38.9 %collective-permute-start.28 = (bf16[577,1024]{1,0:T(8,128)(2,1)S(1)}, bf16[577,1024]{1,0:T(8,128)(2,1)S(1)}, u32[]{:S(2)}, u32[]{:S(2)}) collective-permute-start(bf16[577,1024]{1,0:T(8,128)(2,1)S(1)} %bitcast.45), channel_id=1, source_target_pairs={{0,4},{4,0},{8,12},{12,8},{16,20},{20,16},{24,28},{28,24},{1,5},{5... | collective-permute-start | bytes 3545096 | tf_op jit(solution)/shard_map/ppermute | solution.py:1009
  170.5 18.7 %collective-permute-start.33 = (bf16[3072,128]{1,0:T(8,128)(2,1)S(1)}, bf16[3072,128]{1,0:T(8,128)(2,1)S(1)}, u32[]{:S(2)}, u32[]{:S(2)}) collective-permute-start(bf16[3072,128]{1,0:T(8,128)(2,1)S(1)} %shard_map.255.rest_0_), channel_id=1, source_target_pairs={{0,8},{4,12},{8,0},{12,4},{16,24},{20,28},{24,16},{28,20},{1,9},{5... | collective-permute-start | bytes 2359304 | tf_op jit(solution)/shard_map/ppermute | solution.py:1009
  171.0 19.1 %collective-permute-start.35 = (bf16[3072,128]{1,0:T(8,128)(2,1)S(1)}, bf16[3072,128]{1,0:T(8,128)(2,1)S(1)}, u32[]{:S(2)}, u32[]{:S(2)}) collective-permute-start(bf16[3072,128]{1,0:T(8,128)(2,1)S(1)} %shard_map.255.rest_0_), channel_id=1, source_target_pairs={{0,16},{4,20},{8,24},{12,28},{16,0},{20,4},{24,8},{28,12},{1,17},{... | collective-permute-start | bytes 2359304 | tf_op jit(solution)/shard_map/ppermute | solution.py:1009
  189.2 9.4 %collective-permute-start.37 = (bf16[1536,128]{1,0:T(8,128)(2,1)S(1)}, bf16[1536,128]{1,0:T(8,128)(2,1)S(1)}, u32[]{:S(2)}, u32[]{:S(2)}) collective-permute-start(bf16[1536,128]{1,0:T(8,128)(2,1)S(1)} %slice.124), channel_id=1, source_target_pairs={{0,16},{4,20},{8,24},{12,28},{16,0},{20,4},{24,8},{28,12},{1,17},{... | collective-permute-start | bytes 1179656 | tf_op jit(solution)/shard_map/ppermute | solution.py:1009
  191.3 24.5 %collective-permute-start.32 = (bf16[3072,128]{1,0:T(8,128)(2,1)S(1)}, bf16[3072,128]{1,0:T(8,128)(2,1)S(1)}, u32[]{:S(2)}, u32[]{:S(2)}) collective-permute-start(bf16[3072,128]{1,0:T(8,128)(2,1)S(1)} %shard_map.255.rest_0_), channel_id=1, source_target_pairs={{0,4},{4,0},{8,12},{12,8},{16,20},{20,16},{24,28},{28,24},{1,5},{5... | collective-permute-start | bytes 2359304 | tf_op jit(solution)/shard_map/ppermute | solution.py:1009
  191.3 24.5 %collective-permute-start.34 = (bf16[3072,128]{1,0:T(8,128)(2,1)S(1)}, bf16[3072,128]{1,0:T(8,128)(2,1)S(1)}, u32[]{:S(2)}, u32[]{:S(2)}) collective-permute-start(bf16[3072,128]{1,0:T(8,128)(2,1)S(1)} %collective-permute-done.33.rest_2_), channel_id=1, source_target_pairs={{0,4},{4,0},{8,12},{12,8},{16,20},{20,16},{24,28},{28,24},{1,5},{5... | collective-permute-start | bytes 2359304 | tf_op jit(solution)/shard_map/ppermute | solution.py:1009
  198.5 17.3 %collective-permute-start.36 = (bf16[3072,128]{1,0:T(8,128)(2,1)S(1)}, bf16[3072,128]{1,0:T(8,128)(2,1)S(1)}, u32[]{:S(2)}, u32[]{:S(2)}) collective-permute-start(bf16[3072,128]{1,0:T(8,128)(2,1)S(1)} %collective-permute-done.35.rest_4_), channel_id=1, source_target_pairs={{0,4},{4,0},{8,12},{12,8},{16,20},{20,16},{24,28},{28,24},{1,5},{5... | collective-permute-start | bytes 2359304 | tf_op jit(solution)/shard_map/ppermute | solution.py:1009
  199.3 16.5 %collective-permute-start.39 = (bf16[1536,128]{1,0:T(8,128)(2,1)S(1)}, bf16[1536,128]{1,0:T(8,128)(2,1)S(1)}, u32[]{:S(2)}, u32[]{:S(2)}) collective-permute-start(bf16[1536,128]{1,0:T(8,128)(2,1)S(1)} %collective-permute-done.37.rest_6_), channel_id=1, source_target_pairs={{0,4},{4,0},{8,12},{12,8},{16,20},{20,16},{24,28},{28,24},{1,5},{5... | collective-permute-start | bytes 1179656 | tf_op jit(solution)/shard_map/ppermute | solution.py:1009
  199.3 16.5 %collective-permute-start.40 = (bf16[1536,128]{1,0:T(8,128)(2,1)S(1)}, bf16[1536,128]{1,0:T(8,128)(2,1)S(1)}, u32[]{:S(2)}, u32[]{:S(2)}) collective-permute-start(bf16[1536,128]{1,0:T(8,128)(2,1)S(1)} %collective-permute-done.38.rest_7_), channel_id=1, source_target_pairs={{0,4},{4,0},{8,12},{12,8},{16,20},{20,16},{24,28},{28,24},{1,5},{5... | collective-permute-start | bytes 1179656 | tf_op jit(solution)/shard_map/ppermute | solution.py:1009
  226.3 32.9 %collective-permute-start.44 = (bf16[577,4096]{1,0:T(8,128)(2,1)}, bf16[577,4096]{1,0:T(8,128)(2,1)}, u32[]{:S(2)}, u32[]{:S(2)}) collective-permute-start(bf16[577,4096]{1,0:T(8,128)(2,1)} %get-tuple-element.136.pre_ref.refs_2_), channel_id=1, source_target_pairs={{0,4},{4,0},{8,12},{12,8},{16,20},{20,16},{24,28},{28,24},{1,5},{5... | collective-permute-start | bytes 14180360 | tf_op jit(solution)/shard_map/ppermute | solution.py:1009
  226.4 25.8 %collective-permute-start.41 = (bf16[2,2,128,1024]{3,2,1,0:T(8,128)(2,1)}, bf16[2,2,128,1024]{3,2,1,0:T(8,128)(2,1)}, u32[]{:S(2)}, u32[]{:S(2)}) collective-permute-start(bf16[2,2,128,1024]{3,2,1,0:T(8,128)(2,1)} %get-tuple-element.126), channel_id=1, source_target_pairs={{0,8},{4,12},{8,0},{12,4},{16,24},{20,28},{24,16},{28,20},{1,9},{5... | collective-permute-start | bytes 3145736 | tf_op jit(solution)/shard_map/ppermute | solution.py:1009
  227.1 30.9 %collective-permute-start.43 = (bf16[577,1024]{1,0:T(8,128)(2,1)}, bf16[577,1024]{1,0:T(8,128)(2,1)}, u32[]{:S(2)}, u32[]{:S(2)}) collective-permute-start(bf16[577,1024]{1,0:T(8,128)(2,1)} %get-tuple-element.119.normed_ref.refs_0_), channel_id=1, source_target_pairs={{0,4},{4,0},{8,12},{12,8},{16,20},{20,16},{24,28},{28,24},{1,5},{5... | collective-permute-start | bytes 3545096 | tf_op jit(solution)/shard_map/ppermute | solution.py:1009
  227.3 31.9 %collective-permute-start.45 = (bf16[577,1024]{1,0:T(8,128)(2,1)S(1)}, bf16[577,1024]{1,0:T(8,128)(2,1)}, u32[]{:S(2)}, u32[]{:S(2)}) collective-permute-start(bf16[577,1024]{1,0:T(8,128)(2,1)S(1)} %get-tuple-element.115.attended_ref.refs_4_), channel_id=1, source_target_pairs={{0,4},{4,0},{8,12},{12,8},{16,20},{20,16},{24,28},{28,24},{1,5},{5... | collective-permute-start | bytes 3545096 | tf_op jit(solution)/shard_map/ppermute | solution.py:1009
  227.7 25.5 %collective-permute-start.42 = (bf16[2,2,128,1024]{3,2,1,0:T(8,128)(2,1)}, bf16[2,2,128,1024]{3,2,1,0:T(8,128)(2,1)}, u32[]{:S(2)}, u32[]{:S(2)}) collective-permute-start(bf16[2,2,128,1024]{3,2,1,0:T(8,128)(2,1)} %get-tuple-element.128), channel_id=1, source_target_pairs={{0,16},{4,20},{8,24},{12,28},{16,0},{20,4},{24,8},{28,12},{1,17},{... | collective-permute-start | bytes 3145736 | tf_op jit(solution)/shard_map/ppermute | solution.py:1009
  256.7 16.9 %collective-permute-start.50 = (bf16[2,128,1024]{2,1,0:T(8,128)(2,1)S(1)}, bf16[2,128,1024]{2,1,0:T(8,128)(2,1)S(1)}, u32[]{:S(2)}, u32[]{:S(2)}) collective-permute-start(bf16[2,128,1024]{2,1,0:T(8,128)(2,1)S(1)} %get-tuple-element.212), channel_id=1, source_target_pairs={{0,8},{4,12},{8,0},{12,4},{16,24},{20,28},{24,16},{28,20},{1,9},{5... | collective-permute-start | bytes 1572872 | tf_op jit(solution)/shard_map/ppermute | solution.py:1009
  258.1 15.5 %collective-permute-start.49 = (bf16[2,128,1024]{2,1,0:T(8,128)(2,1)S(1)}, bf16[2,128,1024]{2,1,0:T(8,128)(2,1)S(1)}, u32[]{:S(2)}, u32[]{:S(2)}) collective-permute-start(bf16[2,128,1024]{2,1,0:T(8,128)(2,1)S(1)} %get-tuple-element.214), channel_id=1, source_target_pairs={{0,16},{4,20},{8,24},{12,28},{16,0},{20,4},{24,8},{28,12},{1,17},{... | collective-permute-start | bytes 1572872 | tf_op jit(solution)/shard_map/ppermute | solution.py:1009
  304.4 34.8 %collective-permute-start.52 = (bf16[3,577,1024]{2,1,0:T(8,128)(2,1)S(1)}, bf16[3,577,1024]{2,1,0:T(8,128)(2,1)S(1)}, u32[]{:S(2)}, u32[]{:S(2)}) collective-permute-start(bf16[3,577,1024]{2,1,0:T(8,128)(2,1)S(1)} %get-tuple-element.152.refs_2_.proj_ref), channel_id=1, source_target_pairs={{0,4},{4,0},{8,12},{12,8},{16,20},{20,16},{24,28},{28,24},{1,5},{5... | collective-permute-start | bytes 10635272 | tf_op jit(solution)/shard_map/ppermute | solution.py:1009
  304.5 31.2 %collective-permute-start.47 = (bf16[2,512,640]{2,1,0:T(8,128)(2,1)S(1)}, bf16[2,512,640]{2,1,0:T(8,128)(2,1)S(1)}, u32[]{:S(2)}, u32[]{:S(2)}) collective-permute-start(bf16[2,512,640]{2,1,0:T(8,128)(2,1)S(1)} %copy-done.76), channel_id=1, source_target_pairs={{0,8},{4,12},{8,0},{12,4},{16,24},{20,28},{24,16},{28,20},{1,9},{5... | collective-permute-start | bytes 3932168 | tf_op jit(solution)/shard_map/ppermute | solution.py:1009
  305.1 30.8 %collective-permute-start.48 = (bf16[2,512,640]{2,1,0:T(8,128)(2,1)S(1)}, bf16[2,512,640]{2,1,0:T(8,128)(2,1)S(1)}, u32[]{:S(2)}, u32[]{:S(2)}) collective-permute-start(bf16[2,512,640]{2,1,0:T(8,128)(2,1)S(1)} %copy-done.74), channel_id=1, source_target_pairs={{0,16},{4,20},{8,24},{12,28},{16,0},{20,4},{24,8},{28,12},{1,17},{... | collective-permute-start | bytes 3932168 | tf_op jit(solution)/shard_map/ppermute | solution.py:1009
  306.2 32.9 %collective-permute-start.51 = (bf16[577,1024]{1,0:T(8,128)(2,1)S(1)}, bf16[577,1024]{1,0:T(8,128)(2,1)S(1)}, u32[]{:S(2)}, u32[]{:S(2)}) collective-permute-start(bf16[577,1024]{1,0:T(8,128)(2,1)S(1)} %copy-done.78), channel_id=1, source_target_pairs={{0,4},{4,0},{8,12},{12,8},{16,20},{20,16},{24,28},{28,24},{1,5},{5... | collective-permute-start | bytes 3545096 | tf_op jit(solution)/shard_map/ppermute | solution.py:1009
  336.3 16.0 %collective-permute-start.54 = (bf16[512,640]{1,0:T(8,128)(2,1)S(1)}, bf16[512,640]{1,0:T(8,128)(2,1)S(1)}, u32[]{:S(2)}, u32[]{:S(2)}) collective-permute-start(bf16[512,640]{1,0:T(8,128)(2,1)S(1)} %get-tuple-element.208), channel_id=1, source_target_pairs={{0,8},{4,12},{8,0},{12,4},{16,24},{20,28},{24,16},{28,20},{1,9},{5... | collective-permute-start | bytes 1966088 | tf_op jit(solution)/shard_map/ppermute | solution.py:1009
  338.2 15.7 %collective-permute-start.53 = (bf16[512,640]{1,0:T(8,128)(2,1)S(1)}, bf16[512,640]{1,0:T(8,128)(2,1)S(1)}, u32[]{:S(2)}, u32[]{:S(2)}) collective-permute-start(bf16[512,640]{1,0:T(8,128)(2,1)S(1)} %get-tuple-element.210), channel_id=1, source_target_pairs={{0,16},{4,20},{8,24},{12,28},{16,0},{20,4},{24,8},{28,12},{1,17},{... | collective-permute-start | bytes 1966088 | tf_op jit(solution)/shard_map/ppermute | solution.py:1009
  355.6 63.7 %reduce-scatter.3.cloned.1.call-start = ((), (), s32[]{:S(2)}) async-start(), calls=%async_computation.2 | async-start | bytes 1310720 | tf_op jit(solution)/shard_map/reduce_scatter | solution.py:1062
  356.3 116.4 %all-gather.3.cloned.1.call-start = ((), (), s32[]{:S(2)}) async-start(), calls=%async_computation.4 | async-start | bytes 2949120 | tf_op jit(solution)/shard_map/all_gather | solution.py:1066
  356.4 20.8 %collective-permute-start.56 = (bf16[2,512,384]{2,1,0:T(8,128)(2,1)}, bf16[2,512,384]{2,1,0:T(8,128)(2,1)S(1)}, u32[]{:S(2)}, u32[]{:S(2)}) collective-permute-start(bf16[2,512,384]{2,1,0:T(8,128)(2,1)} %copy-done.88), channel_id=1, source_target_pairs={{0,8},{4,12},{8,0},{12,4},{16,24},{20,28},{24,16},{28,20},{1,9},{5... | collective-permute-start | bytes 2359304 | tf_op jit(solution)/shard_map/ppermute | solution.py:1009
  357.0 20.2 %collective-permute-start.57 = (bf16[2,512,384]{2,1,0:T(8,128)(2,1)}, bf16[2,512,384]{2,1,0:T(8,128)(2,1)S(1)}, u32[]{:S(2)}, u32[]{:S(2)}) collective-permute-start(bf16[2,512,384]{2,1,0:T(8,128)(2,1)} %copy-done.87), channel_id=1, source_target_pairs={{0,16},{4,20},{8,24},{12,28},{16,0},{20,4},{24,8},{28,12},{1,17},{... | collective-permute-start | bytes 2359304 | tf_op jit(solution)/shard_map/ppermute | solution.py:1009
  378.4 15.5 %collective-permute-start.58 = (f32[4,3072]{1,0:T(4,128)S(1)}, f32[4,3072]{1,0:T(4,128)S(1)}, u32[]{:S(2)}, u32[]{:S(2)}) collective-permute-start(f32[4,3072]{1,0:T(4,128)S(1)} %add.143), channel_id=1, source_target_pairs={{0,8},{4,12},{8,0},{12,4},{16,24},{20,28},{24,16},{28,20},{1,9},{5... | collective-permute-start | bytes 147464 | tf_op jit(solution)/shard_map/ppermute | solution.py:1009
  379.8 14.2 %collective-permute-start.60 = (bf16[512,384]{1,0:T(8,128)(2,1)S(1)}, bf16[512,384]{1,0:T(8,128)(2,1)S(1)}, u32[]{:S(2)}, u32[]{:S(2)}) collective-permute-start(bf16[512,384]{1,0:T(8,128)(2,1)S(1)} %get-tuple-element.216), channel_id=1, source_target_pairs={{0,8},{4,12},{8,0},{12,4},{16,24},{20,28},{24,16},{28,20},{1,9},{5... | collective-permute-start | bytes 1179656 | tf_op jit(solution)/shard_map/ppermute | solution.py:1009
  380.5 13.5 %collective-permute-start.59 = (bf16[512,384]{1,0:T(8,128)(2,1)S(1)}, bf16[512,384]{1,0:T(8,128)(2,1)S(1)}, u32[]{:S(2)}, u32[]{:S(2)}) collective-permute-start(bf16[512,384]{1,0:T(8,128)(2,1)S(1)} %get-tuple-element.218), channel_id=1, source_target_pairs={{0,16},{4,20},{8,24},{12,28},{16,0},{20,4},{24,8},{28,12},{1,17},{... | collective-permute-start | bytes 1179656 | tf_op jit(solution)/shard_map/ppermute | solution.py:1009
  419.3 19.0 %collective-permute-start.65 = (bf16[128,1024]{1,0:T(8,128)(2,1)}, bf16[128,1024]{1,0:T(8,128)(2,1)S(1)}, u32[]{:S(2)}, u32[]{:S(2)}) collective-permute-start(bf16[128,1024]{1,0:T(8,128)(2,1)} %bitcast.48), channel_id=1, source_target_pairs={{0,8},{4,12},{8,0},{12,4},{16,24},{20,28},{24,16},{28,20},{1,9},{5... | collective-permute-start | bytes 786440 | tf_op jit(solution)/shard_map/ppermute | solution.py:1009
  420.7 17.5 %collective-permute-start.66 = (bf16[128,1024]{1,0:T(8,128)(2,1)}, bf16[128,1024]{1,0:T(8,128)(2,1)S(1)}, u32[]{:S(2)}, u32[]{:S(2)}) collective-permute-start(bf16[128,1024]{1,0:T(8,128)(2,1)} %bitcast.49), channel_id=1, source_target_pairs={{0,16},{4,20},{8,24},{12,28},{16,0},{20,4},{24,8},{28,12},{1,17},{... | collective-permute-start | bytes 786440 | tf_op jit(solution)/shard_map/ppermute | solution.py:1009
  422.7 9.2 %collective-permute-start.62 = (bf16[256,384]{1,0:T(8,128)(2,1)S(1)}, bf16[256,384]{1,0:T(8,128)(2,1)S(1)}, u32[]{:S(2)}, u32[]{:S(2)}) collective-permute-start(bf16[256,384]{1,0:T(8,128)(2,1)S(1)} %get-tuple-element.184), channel_id=1, source_target_pairs={{0,1},{1,0},{2,3},{3,2},{4,5},{5,4},{6,7},{7,6},{8,9},{9,8},{10,11... | collective-permute-start | bytes 589832 | tf_op jit(solution)/shard_map/ppermute | solution.py:1009
  422.7 15.5 %collective-permute-start.63 = (bf16[256,384]{1,0:T(8,128)(2,1)S(1)}, bf16[256,384]{1,0:T(8,128)(2,1)S(1)}, u32[]{:S(2)}, u32[]{:S(2)}) collective-permute-start(bf16[256,384]{1,0:T(8,128)(2,1)S(1)} %get-tuple-element.185), channel_id=1, source_target_pairs={{0,2},{1,3},{2,0},{3,1},{4,6},{5,7},{6,4},{7,5},{8,10},{9,11},{10,... | collective-permute-start | bytes 589832 | tf_op jit(solution)/shard_map/ppermute | solution.py:1009
  432.0 17.7 %collective-permute-start.76 = (bf16[128,1024]{1,0:T(8,128)(2,1)}, bf16[128,1024]{1,0:T(8,128)(2,1)S(1)}, u32[]{:S(2)}, u32[]{:S(2)}) collective-permute-start(bf16[128,1024]{1,0:T(8,128)(2,1)} %bitcast.50), channel_id=1, source_target_pairs={{0,4},{4,0},{8,12},{12,8},{16,20},{20,16},{24,28},{28,24},{1,5},{5... | collective-permute-start | bytes 786440 | tf_op jit(solution)/shard_map/ppermute | solution.py:1009
  438.3 9.8 %collective-permute-start.68 = (bf16[256,384]{1,0:T(8,128)(2,1)S(1)}, bf16[256,384]{1,0:T(8,128)(2,1)S(1)}, u32[]{:S(2)}, u32[]{:S(2)}) collective-permute-start(bf16[256,384]{1,0:T(8,128)(2,1)S(1)} %add_convert_fusion.16.refs_0_), channel_id=1, source_target_pairs={{0,8},{4,12},{8,0},{12,4},{16,24},{20,28},{24,16},{28,20},{1,9},{5... | collective-permute-start | bytes 589832 | tf_op jit(solution)/shard_map/ppermute | solution.py:1009
  439.0 12.6 %collective-permute-start.79 = (bf16[128,1024]{1,0:T(8,128)(2,1)S(1)}, bf16[128,1024]{1,0:T(8,128)(2,1)S(1)}, u32[]{:S(2)}, u32[]{:S(2)}) collective-permute-start(bf16[128,1024]{1,0:T(8,128)(2,1)S(1)} %collective-permute-done.65.refs_2_), channel_id=1, source_target_pairs={{0,16},{4,20},{8,24},{12,28},{16,0},{20,4},{24,8},{28,12},{1,17},{... | collective-permute-start | bytes 786440 | tf_op jit(solution)/shard_map/ppermute | solution.py:1009
  444.5 19.9 %collective-permute-start.77 = (bf16[128,1024]{1,0:T(8,128)(2,1)S(1)}, bf16[128,1024]{1,0:T(8,128)(2,1)S(1)}, u32[]{:S(2)}, u32[]{:S(2)}) collective-permute-start(bf16[128,1024]{1,0:T(8,128)(2,1)S(1)} %collective-permute-done.65.refs_2_), channel_id=1, source_target_pairs={{0,4},{4,0},{8,12},{12,8},{16,20},{20,16},{24,28},{28,24},{1,5},{5... | collective-permute-start | bytes 786440 | tf_op jit(solution)/shard_map/ppermute | solution.py:1009
  446.6 18.3 %collective-permute-start.78 = (bf16[128,1024]{1,0:T(8,128)(2,1)S(1)}, bf16[128,1024]{1,0:T(8,128)(2,1)S(1)}, u32[]{:S(2)}, u32[]{:S(2)}) collective-permute-start(bf16[128,1024]{1,0:T(8,128)(2,1)S(1)} %collective-permute-done.66.refs_4_), channel_id=1, source_target_pairs={{0,4},{4,0},{8,12},{12,8},{16,20},{20,16},{24,28},{28,24},{1,5},{5... | collective-permute-start | bytes 786440 | tf_op jit(solution)/shard_map/ppermute | solution.py:1009
  449.6 15.3 %collective-permute-start.74 = (bf16[256,384]{1,0:T(8,128)(2,1)S(1)}, bf16[256,384]{1,0:T(8,128)(2,1)S(1)}, u32[]{:S(2)}, u32[]{:S(2)}) collective-permute-start(bf16[256,384]{1,0:T(8,128)(2,1)S(1)} %collective-permute-done.68.refs_2_), channel_id=1, source_target_pairs={{0,16},{4,20},{8,24},{12,28},{16,0},{20,4},{24,8},{28,12},{1,17},{... | collective-permute-start | bytes 589832 | tf_op jit(solution)/shard_map/ppermute | solution.py:1009
  451.5 15.1 %collective-permute-start.80 = (bf16[128,1024]{1,0:T(8,128)(2,1)S(1)}, bf16[128,1024]{1,0:T(8,128)(2,1)S(1)}, u32[]{:S(2)}, u32[]{:S(2)}) collective-permute-start(bf16[128,1024]{1,0:T(8,128)(2,1)S(1)} %collective-permute-done.79.refs_6_), channel_id=1, source_target_pairs={{0,4},{4,0},{8,12},{12,8},{16,20},{20,16},{24,28},{28,24},{1,5},{5... | collective-permute-start | bytes 786440 | tf_op jit(solution)/shard_map/ppermute | solution.py:1009
  (135 other events, 2127.2 us)
Sparse Core Ops, SparseCore 0:
  355.7 34.6 reduce-scatter.4
  393.2 25.9 reduce-scatter.2
  421.1 32.9 all-gather.2

commit v5 on v4

--- a/solution.py
+++ b/solution.py
@@ -318,7 +318,7 @@
         ),
         out_shape=jax.ShapeDtypeStruct((tokens, width), jnp.bfloat16),
         cost_estimate=cost(2 * tokens * width * wide, 2 * width * wide),
-        compiler_params=params(32),
+        compiler_params=params(60),
     )(where, residual, active, bias, own, *flat(pieces))
 
 
@@ -373,7 +373,7 @@
             jax.ShapeDtypeStruct((1, wide), jnp.float32),
         ],
         cost_estimate=cost(2 * tokens * width * wide, 2 * width * wide),
-        compiler_params=params(34),
+        compiler_params=params(60),
     )(where, grad_block, slope, own, *flat(pieces))
 
 
@@ -520,7 +520,7 @@
             jax.ShapeDtypeStruct((1, width), jnp.float32),
         ],
         cost_estimate=cost(2 * tokens * width * wide, 2 * width * wide),
-        compiler_params=params(46),
+        compiler_params=params(60),
     )(where, grad_proj, image, grad_res, gain, own, *flat(pieces))
 
 
@@ -602,7 +602,7 @@
         out_shape=[jax.ShapeDtypeStruct((3, tokens, width), jnp.bfloat16)]
         + [jax.ShapeDtypeStruct((1, width), jnp.float32)] * 2,
         cost_estimate=cost(40 * tokens * tokens * width, 16 * tokens * width),
-        compiler_params=params(28),
+        compiler_params=params(60),
     )(projected, projected, projected, grad_mixed, totals)
 
 

time: 488 us -> 491 us (level)
    unnamed x230 -> x168, local copies, waits for them, and re-layouts: 25.5 us -> 21.4 us
  transfers between devices with their start and end apart: 84 -> 84, of which waited for: 31 -> 32; matrix products, arithmetic and copies ran while one was open for 2% -> 2% of each run, Pallas kernels for 24% -> 24%
where the time goes in v5:
time: 491 us; the launch traced here: 487 us
  waiting for transfers between devices  182 us (37%)
  Pallas kernels  171 us (35%)
  starting transfers between devices  82.6 us (17%)
  local copies, waits for them, and re-layouts  25.8 us (5%)
  between operations  15.2 us (3%)
  other arithmetic  10.5 us (2%)
    ppermute x81, waiting for transfers between devices, exchange(): return lax.ppermute(tensor, axis, [(at, at ^ mask) for at in range(size)])  155 us
    ppermute x81, starting transfers between devices, exchange(): return lax.ppermute(tensor, axis, [(at, at ^ mask) for at in range(size)])  82.4 us
    reduce_scatter x2, waiting for transfers between devices, scatter(): return lax.psum_scatter(total, GRP, scatter_dimension=0, tiled=True)  26.1 us
    pallas_call x1, Pallas kernels, attention_backward(): pl.pallas_call(body, grid=(count,), in_specs=[spec(0), spec(1), spec(2),...  24.9 us
    pallas_call x2, Pallas kernels, weight_grads(): pl.pallas_call(body, grid_spec=pltpu.PrefetchScalarGridSpec(num_scalar_pr...  22.3 us
    unnamed x168, local copies, waits for them, and re-layouts  21.4 us
    pallas_call x1, Pallas kernels, middle_backward(): pl.pallas_call(body, grid_spec=pltpu.PrefetchScalarGridSpec(num_scalar_pr...  18.8 us
    pallas_call x1, Pallas kernels, up_forward(): pl.pallas_call(body, grid_spec=pltpu.PrefetchScalarGridSpec(num_scalar_pr...  14.4 us
  transfers between devices with their start and end apart: 84, of which 32 were waited for; matrix products, arithmetic and copies ran while one was open for 2% of the time, Pallas kernels for 24%

profile of v5, /device:TPU:0, one launch (start us, length us, event | category | flops | bytes accessed | tf_op | source)
XLA Modules:
  0.0 487.1 jit_solution(2099928660475131205)
XLA Ops:
  10.4 3.1 collective-permute-start.3
  13.5 2.6 collective-permute-start.4
  16.1 8.6 %collective-permute-done.3.refs_0_ = bf16[256,512]{1,0:T(8,128)(2,1)S(1)} collective-permute-done((bf16[256,512]{1,0:T(8,128)(2,1)S(1)}, bf16[256,512]{1,0:T(8,128)(2,1)S(1)}, u32[]{:S(2)}, u32[]{:S(2)}) %collective-permute-start.3) | collective-permute-done | bytes 262176 | tf_op jit(solution)/shard_map/ppermute | solution.py:1009
  24.7 10.1 %collective-permute-done.4.refs_1_ = bf16[256,512]{1,0:T(8,128)(2,1)S(1)} collective-permute-done((bf16[256,512]{1,0:T(8,128)(2,1)S(1)}, bf16[256,512]{1,0:T(8,128)(2,1)S(1)}, u32[]{:S(2)}, u32[]{:S(2)}) %collective-permute-start.4) | collective-permute-done | bytes 262176 | tf_op jit(solution)/shard_map/ppermute | solution.py:1009
  34.9 1.6 collective-permute-start.7
  36.5 1.5 collective-permute-start.9
  39.4 4.8 collective-permute-start.15
  45.2 1.5 collective-permute-start.17
  46.6 5.2 %collective-permute-done.7.rest_2_.rest_12_ = bf16[768,512]{1,0:T(8,128)(2,1)S(1)} collective-permute-done((bf16[768,512]{1,0:T(8,128)(2,1)S(1)}, bf16[768,512]{1,0:T(8,128)(2,1)S(1)}, u32[]{:S(2)}, u32[]{:S(2)}) %collective-permute-start.7) | collective-permute-done | bytes 786464 | tf_op jit(solution)/shard_map/ppermute | solution.py:1009
  54.8 10.5 %collective-permute-done.16.refs_1_ = bf16[256,512]{1,0:T(8,128)(2,1)S(1)} collective-permute-done((bf16[256,512]{1,0:T(8,128)(2,1)S(1)}, bf16[256,512]{1,0:T(8,128)(2,1)S(1)}, u32[]{:S(2)}, u32[]{:S(2)}) %collective-permute-start.16) | collective-permute-done | bytes 262176 | tf_op jit(solution)/shard_map/ppermute | solution.py:1009
  67.2 1.5 collective-permute-start.11
  68.8 1.5 collective-permute-start.12
  71.6 3.4 collective-permute-start
  75.1 1.7 collective-permute-done.refs_1_
  76.7 3.0 collective-permute-start.1
  79.7 1.6 collective-permute-done.1.refs_2_
  81.4 2.4 collective-permute-start.2
  83.7 3.1 collective-permute-done.2.refs_3_
  86.8 2.1 collective-permute-done.11.rest_6_.rest_16_
  93.1 1.5 collective-permute-start.24
  95.9 1.5 copy-done.11
  97.4 8.7 %shard_map.248 = (bf16[577,1024]{1,0:T(8,128)(2,1)S(1)}, bf16[577,3072]{1,0:T(8,128)(2,1)S(1)}) custom-call(s32[2]{0:T(128)S(1)} %pad_add_fusion.1.where_ref, bf16[577,1024]{1,0:T(8,128)(2,1)S(1)} %bitcast.41, f32[1,1024]{1,0:T(1,128)S(1)} %get-tuple-element.111.gain_ref, f32[1,1024]{1,0:T(1,128)S(1)} %get-tuple-element.112.shift_ref, ...), custom_call_target="tpu_custom_call" | custom-call | flops 3630170112 | bytes 6291456 | tf_op jit(solution)/shard_map/pallas_call | solution.py:148
  107.7 13.9 %shard_map.249 = (bf16[577,1024]{1,0:T(8,128)(2,1)S(1)}, f32[8,2,577]{2,1,0:T(2,128)S(1)}) custom-call(bf16[577,3072]{1,0:T(8,128)(2,1)S(1)} %get-tuple-element.114.query_ref.key_ref.value_ref, bf16[577,3072]{1,0:T(8,128)(2,1)S(1)} %get-tuple-element.114.query_ref.key_ref.value_ref, bf16[577,3072]{1,0:T(8,128)(2,1)S(1)} %get-tuple-element.114.query_ref.key_ref.value_ref), custom_call_target="tpu_custom_call" | custom-call | flops 5454708736 | bytes 4726784 | tf_op jit(solution)/shard_map/pallas_call | solution.py:548
  121.8 5.7 %shard_map.250 = (f32[577,1024]{1,0:T(8,128)S(1)}, bf16[577,1024]{1,0:T(8,128)(2,1)}) custom-call(s32[2]{0:T(128)S(1)} %pad_add_fusion.1.where_ref, bf16[577,1024]{1,0:T(8,128)(2,1)S(1)} %bitcast.42, bf16[577,1024]{1,0:T(8,128)(2,1)S(1)} %get-tuple-element.115.attended_ref.refs_4_, f32[1,1024]{1,0:T(1,128)S(1)} %get-tuple-element.116.bias_ref, ...), custom_call_target="tpu_custom_call" | custom-call | flops 1210056704 | bytes 2097152 | tf_op jit(solution)/shard_map/pallas_call | solution.py:204
  129.0 14.4 %shard_map.253 = (bf16[577,4096]{1,0:T(8,128)(2,1)S(1)}, bf16[577,4096]{1,0:T(8,128)(2,1)}) custom-call(s32[2]{0:T(128)S(1)} %pad_add_fusion.1.where_ref, bf16[577,1024]{1,0:T(8,128)(2,1)} %get-tuple-element.119.normed_ref.refs_0_, f32[1,4096]{1,0:T(1,128)S(1)} %get-tuple-element.120.bias_ref, bf16[256,4096]{1,0:T(8,128)(2,1)S(1)} %copy-done.7, ...), custom_call_target="tpu_custom_call" | custom-call | flops 4840226816 | bytes 8388608 | tf_op jit(solution)/shard_map/pallas_call | solution.py:256
  143.8 6.0 %collective-permute-start.29 = (bf16[1024,128]{1,0:T(8,128)(2,1)S(1)}, bf16[1024,128]{1,0:T(8,128)(2,1)S(1)}, u32[]{:S(2)}, u32[]{:S(2)}) collective-permute-start(bf16[1024,128]{1,0:T(8,128)(2,1)S(1)} %copy-done.61), channel_id=1, source_target_pairs={{0,1},{1,0},{2,3},{3,2},{4,5},{5,4},{6,7},{7,6},{8,9},{9,8},{10,11... | collective-permute-start | bytes 786440 | tf_op jit(solution)/shard_map/ppermute | solution.py:1009
  149.8 1.9 collective-permute-start.30
  151.7 1.5 collective-permute-start.31
  153.2 8.9 %collective-permute-done.29.refs_0_ = bf16[1024,128]{1,0:T(8,128)(2,1)S(1)} collective-permute-done((bf16[1024,128]{1,0:T(8,128)(2,1)S(1)}, bf16[1024,128]{1,0:T(8,128)(2,1)S(1)}, u32[]{:S(2)}, u32[]{:S(2)}) %collective-permute-start.29) | collective-permute-done | bytes 262176 | tf_op jit(solution)/shard_map/ppermute | solution.py:1009
  162.1 9.1 %collective-permute-done.30.refs_1_ = bf16[1024,128]{1,0:T(8,128)(2,1)S(1)} collective-permute-done((bf16[1024,128]{1,0:T(8,128)(2,1)S(1)}, bf16[1024,128]{1,0:T(8,128)(2,1)S(1)}, u32[]{:S(2)}, u32[]{:S(2)}) %collective-permute-start.30) | collective-permute-done | bytes 262176 | tf_op jit(solution)/shard_map/ppermute | solution.py:1009
  172.9 17.0 %collective-permute-done.33.rest_2_ = bf16[3072,128]{1,0:T(8,128)(2,1)S(1)} collective-permute-done((bf16[3072,128]{1,0:T(8,128)(2,1)S(1)}, bf16[3072,128]{1,0:T(8,128)(2,1)S(1)}, u32[]{:S(2)}, u32[]{:S(2)}) %collective-permute-start.33) | collective-permute-done | bytes 786464 | tf_op jit(solution)/shard_map/ppermute | solution.py:1009
  192.5 6.7 %collective-permute-done.37.rest_6_ = bf16[1536,128]{1,0:T(8,128)(2,1)S(1)} collective-permute-done((bf16[1536,128]{1,0:T(8,128)(2,1)S(1)}, bf16[1536,128]{1,0:T(8,128)(2,1)S(1)}, u32[]{:S(2)}, u32[]{:S(2)}) %collective-permute-start.37) | collective-permute-done | bytes 393248 | tf_op jit(solution)/shard_map/ppermute | solution.py:1009
  200.6 11.9 %shard_map.254 = (bf16[2,2,128,1024]{3,2,1,0:T(8,128)(2,1)}, bf16[2,2,128,1024]{3,2,1,0:T(8,128)(2,1)S(1)}, bf16[2,2,128,1024]{3,2,1,0:T(8,128)(2,1)}, bf16[2,2,128,1024]{3,2,1,0:T(8,128)(2,1)S(1)}) custom-call(s32[2]{0:T(128)S(1)} %copy-done.40, bf16[577,4096]{1,0:T(8,128)(2,1)S(1)} %get-tuple-element.125.left_ref.active_ref, ...), custom_call_target="tpu_custom_call" | custom-call | flops 4840226816 | bytes 13647872 | tf_op jit(solution)/shard_map/pallas_call | solution.py:747
  214.6 2.1 copy-done.52
  218.9 11.9 %shard_map.256 = (bf16[577,4096]{1,0:T(8,128)(2,1)}, f32[1,4096]{1,0:T(1,128)}) custom-call(s32[2]{0:T(128)} %copy-done.39, bf16[577,1024]{1,0:T(8,128)(2,1)} %bitcast.44, bf16[577,4096]{1,0:T(8,128)(2,1)} %get-tuple-element.131.slope_ref, bf16[1024,1024]{1,0:T(8,128)(2,1)} %own_ref.13, bf16[3072,128]{1,0:T(8,128)(2,1)} %copy-done.33, ...), custom_call_target="tpu_custom_call" | custom-call | flops 4840226816 | bytes 8388608 | tf_op jit(solution)/shard_map/pallas_call | solution.py:355
  233.2 18.8 %shard_map.257 = (f32[577,1024]{1,0:T(8,128)}, bf16[577,1024]{1,0:T(8,128)(2,1)}, bf16[577,1024]{1,0:T(8,128)(2,1)}, f32[1,1024]{1,0:T(1,128)}, f32[1,1024]{1,0:...) custom-call(s32[2]{0:T(128)} %copy-done.39, bf16[577,4096]{1,0:T(8,128)(2,1)} %get-tuple-element.136.pre_ref.refs_2_, ...), custom_call_target="tpu_custom_call" | custom-call | flops 6050283520 | bytes 10485760 | tf_op jit(solution)/shard_map/pallas_call | solution.py:438
  252.0 4.9 collective-permute-done.41
  257.7 1.8 fusion.7
  259.5 1.7 fusion.6
  261.2 1.5 collective-permute-start.50
  265.0 13.9 %shard_map.258 = (bf16[2,512,640]{2,1,0:T(8,128)(2,1)S(1)}, bf16[2,512,640]{2,1,0:T(8,128)(2,1)S(1)}, bf16[2,512,640]{2,1,0:T(8,128)(2,1)S(1)}, bf16[2,512,640]{2,1,0:T(8,128)(2,1)S(1)}) custom-call(s32[2]{0:T(128)S(1)} %copy-done.41, bf16[577,1024]{1,0:T(8,128)(2,1)} %get-tuple-element.119.normed_ref.refs_0_, ...), custom_call_target="tpu_custom_call" | custom-call | flops 6050283520 | bytes 7606272 | tf_op jit(solution)/shard_map/pallas_call | solution.py:678
  282.6 24.9 %shard_map.259 = (bf16[3,577,1024]{2,1,0:T(8,128)(2,1)}, f32[1,1024]{1,0:T(1,128)}, f32[1,1024]{1,0:T(1,128)}) custom-call(bf16[577,3072]{1,0:T(8,128)(2,1)} %copy-done.63, bf16[577,3072]{1,0:T(8,128)(2,1)} %copy-done.63, bf16[577,3072]{1,0:T(8,128)(2,1)} %copy-done.63, bf16[577,1024]{1,0:T(8,128)(2,1)} %get-tuple-element.150.grad_ref, f32[8,2,577]{2,1,0:T(2,128)} %copy-done.64), custom_call_target="tpu_custom_call" | custom-call | flops 13636771840 | bytes 9453568 | tf_op jit(solution)/shard_map/pallas_call | solution.py:596
  309.2 29.7 %collective-permute-done.47 = bf16[2,512,640]{2,1,0:T(8,128)(2,1)S(1)} collective-permute-done((bf16[2,512,640]{2,1,0:T(8,128)(2,1)}, bf16[2,512,640]{2,1,0:T(8,128)(2,1)S(1)}, u32[]{:S(2)}, u32[]{:S(2)}) %collective-permute-start.47) | collective-permute-done | bytes 1310752 | tf_op jit(solution)/shard_map/ppermute | solution.py:1009
  342.5 8.3 %shard_map.260 = (bf16[2,512,384]{2,1,0:T(8,128)(2,1)S(1)}, bf16[2,512,384]{2,1,0:T(8,128)(2,1)S(1)}, bf16[2,512,384]{2,1,0:T(8,128)(2,1)S(1)}, bf16[2,512,384]{2,1,0:T(8,128)(2,1)S(1)}) custom-call(s32[2]{0:T(128)S(1)} %copy-done.41, bf16[577,1024]{1,0:T(8,128)(2,1)S(1)} %copy-done.56, bf16[577,1024]{1,0:T(8,128)(2,1)S(1)} %collective-permute-done.51.refs_1_, ...), custom_call_target="tpu_custom_call" | custom-call | flops 3630170112 | bytes 5509120 | tf_op jit(solution)/shard_map/pallas_call | solution.py:678
  350.8 4.8 collective-permute-done.54
  355.6 1.5 collective-permute-done.53
  361.4 13.3 %shard_map.261 = (bf16[577,1024]{1,0:T(8,128)(2,1)}, f32[1,1024]{1,0:T(1,128)}, f32[1,1024]{1,0:T(1,128)}) custom-call(s32[2]{0:T(128)} %copy-done.39, bf16[3,577,1024]{2,1,0:T(8,128)(2,1)} %get-tuple-element.152.refs_2_.proj_ref, bf16[577,1024]{1,0:T(8,128)(2,1)} %bitcast.40, f32[577,1024]{1,0:T(8,128)} %get-tuple-element.138.res_ref, ...), custom_call_target="tpu_custom_call" | custom-call | flops 3630170112 | bytes 6291456 | tf_op jit(solution)/shard_map/pallas_call | solution.py:502
  383.5 11.8 %shard_map.263 = bf16[577,1024]{1,0:T(8,128)(2,1)} custom-call(s32[2]{0:T(128)} %copy-done.39, f32[577,1024]{1,0:T(8,128)} %copy-done.21, bf16[577,4096]{1,0:T(8,128)(2,1)} %copy-done.52, f32[1,1024]{1,0:T(1,128)} %copy-done.62, bf16[1024,1024]{1,0:T(8,128)(2,1)} %own_ref.13, bf16[3072,128]{1,0:T(8,128)(2,1)} %copy-done.33, bf16[3072,128]{1,0:T(8,128)(2,1)} %copy-done.77, ...), custom_call_target="tpu_custom_call" | custom-call | flops 4840226816 | bytes 8388608 | tf_op jit(solution)/shard_map/pallas_call | solution.py:302
  396.4 26.1 %reduce-scatter.3.cloned.1.call-done = bf16[1,128,1024]{2,1,0:T(8,128)(2,1)} async-done(((bf16[4,128,1024]{2,1,0:T(8,128)(2,1)}), bf16[1,128,1024]{2,1,0:T(8,128)(2,1)}) %reduce-scatter.3.cloned.1.call-update) | async-done | bytes 262160 | tf_op jit(solution)/shard_map/reduce_scatter | solution.py:1062
  423.9 1.5 collective-permute-start.66
  425.9 1.5 collective-permute-start.63
  427.4 5.2 %collective-permute-done.61 = f32[4,3072]{1,0:T(4,128)S(1)} collective-permute-done((f32[4,3072]{1,0:T(4,128)S(1)}, f32[4,3072]{1,0:T(4,128)S(1)}, u32[]{:S(2)}, u32[]{:S(2)}) %collective-permute-start.61) | collective-permute-done | bytes 49184 | tf_op jit(solution)/shard_map/ppermute | solution.py:1009
  433.3 1.8 collective-permute-done.62
  435.1 6.3 %collective-permute-done.63 = bf16[256,384]{1,0:T(8,128)(2,1)S(1)} collective-permute-done((bf16[256,384]{1,0:T(8,128)(2,1)S(1)}, bf16[256,384]{1,0:T(8,128)(2,1)S(1)}, u32[]{:S(2)}, u32[]{:S(2)}) %collective-permute-start.63) | collective-permute-done | bytes 196640 | tf_op jit(solution)/shard_map/ppermute | solution.py:1009
  443.6 4.1 collective-permute-start.67
  447.7 2.1 collective-permute-done.67
  449.8 1.5 collective-permute-done.68.refs_2_
  454.7 4.7 collective-permute-done.72.refs_4_
  459.4 6.1 %collective-permute-start.69 = (f32[4,3072]{1,0:T(4,128)S(1)}, f32[4,3072]{1,0:T(4,128)S(1)}, u32[]{:S(2)}, u32[]{:S(2)}) collective-permute-start(f32[4,3072]{1,0:T(4,128)S(1)} %add.151.first_ref), channel_id=1, source_target_pairs={{0,2},{1,3},{2,0},{3,1},{4,6},{5,7},{6,4},{7,5},{8,10},{9,11},{10,... | collective-permute-start | bytes 147464 | tf_op jit(solution)/shard_map/ppermute | solution.py:1009
  465.5 2.1 collective-permute-done.69.second_ref
  469.8 3.6 shard_map.267
  473.4 2.4 shard_map.266
  475.9 1.7 copy-done.20
  477.6 2.7 shard_map.268
  (325 shorter events, 69.3 us)
Async XLA Ops:
  7.2 389.2 %reduce-scatter.5.cloned.1.call-start = ((), (), s32[]{:S(2)}) async-start(), calls=%async_computation.3 | async-start | bytes 1638400 | tf_op jit(solution)/shard_map/reduce_scatter | solution.py:1062
  10.4 14.3 %collective-permute-start.3 = (bf16[256,512]{1,0:T(8,128)(2,1)S(1)}, bf16[256,512]{1,0:T(8,128)(2,1)S(1)}, u32[]{:S(2)}, u32[]{:S(2)}) collective-permute-start(bf16[256,512]{1,0:T(8,128)(2,1)S(1)} %shard_map.246), channel_id=1, source_target_pairs={{0,1},{1,0},{2,3},{3,2},{4,5},{5,4},{6,7},{7,6},{8,9},{9,8},{10,11... | collective-permute-start | bytes 786440 | tf_op jit(solution)/shard_map/ppermute | solution.py:1009
  13.5 21.3 %collective-permute-start.4 = (bf16[256,512]{1,0:T(8,128)(2,1)S(1)}, bf16[256,512]{1,0:T(8,128)(2,1)S(1)}, u32[]{:S(2)}, u32[]{:S(2)}) collective-permute-start(bf16[256,512]{1,0:T(8,128)(2,1)S(1)} %shard_map.246), channel_id=1, source_target_pairs={{0,2},{1,3},{2,0},{3,1},{4,6},{5,7},{6,4},{7,5},{8,10},{9,11},{10,... | collective-permute-start | bytes 786440 | tf_op jit(solution)/shard_map/ppermute | solution.py:1009
  16.1 18.7 %collective-permute-start.5 = (bf16[256,512]{1,0:T(8,128)(2,1)S(1)}, bf16[256,512]{1,0:T(8,128)(2,1)S(1)}, u32[]{:S(2)}, u32[]{:S(2)}) collective-permute-start(bf16[256,512]{1,0:T(8,128)(2,1)S(1)} %shard_map.246), channel_id=1, source_target_pairs={{0,3},{1,2},{2,1},{3,0},{4,7},{5,6},{6,5},{7,4},{8,11},{9,10},{10,... | collective-permute-start | bytes 786440 | tf_op jit(solution)/shard_map/ppermute | solution.py:1009
  34.9 17.0 %collective-permute-start.7 = (bf16[768,512]{1,0:T(8,128)(2,1)S(1)}, bf16[768,512]{1,0:T(8,128)(2,1)S(1)}, u32[]{:S(2)}, u32[]{:S(2)}) collective-permute-start(bf16[768,512]{1,0:T(8,128)(2,1)S(1)} %shard_map.247.rest_0_.rest_10_), channel_id=1, source_target_pairs={{0,8},{4,12},{8,0},{12,4},{16,24},{20,28},{24,16},{28,20},{1,9},{5... | collective-permute-start | bytes 2359304 | tf_op jit(solution)/shard_map/ppermute | solution.py:1009
  36.5 16.6 %collective-permute-start.9 = (bf16[768,512]{1,0:T(8,128)(2,1)S(1)}, bf16[768,512]{1,0:T(8,128)(2,1)S(1)}, u32[]{:S(2)}, u32[]{:S(2)}) collective-permute-start(bf16[768,512]{1,0:T(8,128)(2,1)S(1)} %shard_map.247.rest_0_.rest_10_), channel_id=1, source_target_pairs={{0,16},{4,20},{8,24},{12,28},{16,0},{20,4},{24,8},{28,12},{1,17},{... | collective-permute-start | bytes 2359304 | tf_op jit(solution)/shard_map/ppermute | solution.py:1009
  39.4 15.4 %collective-permute-start.15 = (bf16[256,512]{1,0:T(8,128)(2,1)S(1)}, bf16[256,512]{1,0:T(8,128)(2,1)S(1)}, u32[]{:S(2)}, u32[]{:S(2)}) collective-permute-start(bf16[256,512]{1,0:T(8,128)(2,1)S(1)} %get-tuple-element.121), channel_id=1, source_target_pairs={{0,1},{1,0},{2,3},{3,2},{4,5},{5,4},{6,7},{7,6},{8,9},{9,8},{10,11... | collective-permute-start | bytes 786440 | tf_op jit(solution)/shard_map/ppermute | solution.py:1009
  44.2 21.1 %collective-permute-start.16 = (bf16[256,512]{1,0:T(8,128)(2,1)S(1)}, bf16[256,512]{1,0:T(8,128)(2,1)S(1)}, u32[]{:S(2)}, u32[]{:S(2)}) collective-permute-start(bf16[256,512]{1,0:T(8,128)(2,1)S(1)} %get-tuple-element.121), channel_id=1, source_target_pairs={{0,2},{1,3},{2,0},{3,1},{4,6},{5,7},{6,4},{7,5},{8,10},{9,11},{10,... | collective-permute-start | bytes 786440 | tf_op jit(solution)/shard_map/ppermute | solution.py:1009
  45.2 20.1 %collective-permute-start.17 = (bf16[256,512]{1,0:T(8,128)(2,1)S(1)}, bf16[256,512]{1,0:T(8,128)(2,1)S(1)}, u32[]{:S(2)}, u32[]{:S(2)}) collective-permute-start(bf16[256,512]{1,0:T(8,128)(2,1)S(1)} %get-tuple-element.121), channel_id=1, source_target_pairs={{0,3},{1,2},{2,1},{3,0},{4,7},{5,6},{6,5},{7,4},{8,11},{9,10},{10,... | collective-permute-start | bytes 786440 | tf_op jit(solution)/shard_map/ppermute | solution.py:1009
  66.2 23.2 %collective-permute-start.19 = (bf16[768,512]{1,0:T(8,128)(2,1)}, bf16[768,512]{1,0:T(8,128)(2,1)}, u32[]{:S(2)}, u32[]{:S(2)}) collective-permute-start(bf16[768,512]{1,0:T(8,128)(2,1)} %shard_map.252.rest_0_), channel_id=1, source_target_pairs={{0,8},{4,12},{8,0},{12,4},{16,24},{20,28},{24,16},{28,20},{1,9},{5... | collective-permute-start | bytes 2359304 | tf_op jit(solution)/shard_map/ppermute | solution.py:1009
  66.7 22.7 %collective-permute-start.21 = (bf16[768,512]{1,0:T(8,128)(2,1)}, bf16[768,512]{1,0:T(8,128)(2,1)}, u32[]{:S(2)}, u32[]{:S(2)}) collective-permute-start(bf16[768,512]{1,0:T(8,128)(2,1)} %shard_map.252.rest_0_), channel_id=1, source_target_pairs={{0,16},{4,20},{8,24},{12,28},{16,0},{20,4},{24,8},{28,12},{1,17},{... | collective-permute-start | bytes 2359304 | tf_op jit(solution)/shard_map/ppermute | solution.py:1009
  67.2 21.6 %collective-permute-start.11 = (bf16[384,512]{1,0:T(8,128)(2,1)}, bf16[384,512]{1,0:T(8,128)(2,1)S(1)}, u32[]{:S(2)}, u32[]{:S(2)}) collective-permute-start(bf16[384,512]{1,0:T(8,128)(2,1)} %slice.120), channel_id=1, source_target_pairs={{0,16},{4,20},{8,24},{12,28},{16,0},{20,4},{24,8},{28,12},{1,17},{... | collective-permute-start | bytes 1179656 | tf_op jit(solution)/shard_map/ppermute | solution.py:1009
  68.8 20.1 %collective-permute-start.12 = (bf16[384,512]{1,0:T(8,128)(2,1)}, bf16[384,512]{1,0:T(8,128)(2,1)}, u32[]{:S(2)}, u32[]{:S(2)}) collective-permute-start(bf16[384,512]{1,0:T(8,128)(2,1)} %slice.121), channel_id=1, source_target_pairs={{0,8},{4,12},{8,0},{12,4},{16,24},{20,28},{24,16},{28,20},{1,9},{5... | collective-permute-start | bytes 1179656 | tf_op jit(solution)/shard_map/ppermute | solution.py:1009
  92.0 15.2 %collective-permute-start.23 = (bf16[384,512]{1,0:T(8,128)(2,1)S(1)}, bf16[384,512]{1,0:T(8,128)(2,1)S(1)}, u32[]{:S(2)}, u32[]{:S(2)}) collective-permute-start(bf16[384,512]{1,0:T(8,128)(2,1)S(1)} %slice.122), channel_id=1, source_target_pairs={{0,16},{4,20},{8,24},{12,28},{16,0},{20,4},{24,8},{28,12},{1,17},{... | collective-permute-start | bytes 1179656 | tf_op jit(solution)/shard_map/ppermute | solution.py:1009
  93.1 14.4 %collective-permute-start.24 = (bf16[384,512]{1,0:T(8,128)(2,1)S(1)}, bf16[384,512]{1,0:T(8,128)(2,1)S(1)}, u32[]{:S(2)}, u32[]{:S(2)}) collective-permute-start(bf16[384,512]{1,0:T(8,128)(2,1)S(1)} %slice.123), channel_id=1, source_target_pairs={{0,8},{4,12},{8,0},{12,4},{16,24},{20,28},{24,16},{28,20},{1,9},{5... | collective-permute-start | bytes 1179656 | tf_op jit(solution)/shard_map/ppermute | solution.py:1009
  95.2 33.6 %collective-permute-start.18 = (bf16[768,512]{1,0:T(8,128)(2,1)}, bf16[768,512]{1,0:T(8,128)(2,1)S(1)}, u32[]{:S(2)}, u32[]{:S(2)}) collective-permute-start(bf16[768,512]{1,0:T(8,128)(2,1)} %shard_map.252.rest_0_), channel_id=1, source_target_pairs={{0,4},{4,0},{8,12},{12,8},{16,20},{20,16},{24,28},{28,24},{1,5},{5... | collective-permute-start | bytes 2359304 | tf_op jit(solution)/shard_map/ppermute | solution.py:1009
  95.3 33.6 %collective-permute-start.20 = (bf16[768,512]{1,0:T(8,128)(2,1)}, bf16[768,512]{1,0:T(8,128)(2,1)S(1)}, u32[]{:S(2)}, u32[]{:S(2)}) collective-permute-start(bf16[768,512]{1,0:T(8,128)(2,1)} %collective-permute-done.19.rest_2_), channel_id=1, source_target_pairs={{0,4},{4,0},{8,12},{12,8},{16,20},{20,16},{24,28},{28,24},{1,5},{5... | collective-permute-start | bytes 2359304 | tf_op jit(solution)/shard_map/ppermute | solution.py:1009
  95.8 33.1 %collective-permute-start.22 = (bf16[768,512]{1,0:T(8,128)(2,1)}, bf16[768,512]{1,0:T(8,128)(2,1)S(1)}, u32[]{:S(2)}, u32[]{:S(2)}) collective-permute-start(bf16[768,512]{1,0:T(8,128)(2,1)} %collective-permute-done.21.rest_4_), channel_id=1, source_target_pairs={{0,4},{4,0},{8,12},{12,8},{16,20},{20,16},{24,28},{28,24},{1,5},{5... | collective-permute-start | bytes 2359304 | tf_op jit(solution)/shard_map/ppermute | solution.py:1009
  107.2 21.7 %collective-permute-start.25 = (bf16[384,512]{1,0:T(8,128)(2,1)S(1)}, bf16[384,512]{1,0:T(8,128)(2,1)S(1)}, u32[]{:S(2)}, u32[]{:S(2)}) collective-permute-start(bf16[384,512]{1,0:T(8,128)(2,1)S(1)} %collective-permute-done.23.rest_6_), channel_id=1, source_target_pairs={{0,4},{4,0},{8,12},{12,8},{16,20},{20,16},{24,28},{28,24},{1,5},{5... | collective-permute-start | bytes 1179656 | tf_op jit(solution)/shard_map/ppermute | solution.py:1009
  107.4 21.4 %collective-permute-start.26 = (bf16[384,512]{1,0:T(8,128)(2,1)S(1)}, bf16[384,512]{1,0:T(8,128)(2,1)S(1)}, u32[]{:S(2)}, u32[]{:S(2)}) collective-permute-start(bf16[384,512]{1,0:T(8,128)(2,1)S(1)} %collective-permute-done.24.rest_7_), channel_id=1, source_target_pairs={{0,4},{4,0},{8,12},{12,8},{16,20},{20,16},{24,28},{28,24},{1,5},{5... | collective-permute-start | bytes 1179656 | tf_op jit(solution)/shard_map/ppermute | solution.py:1009
  143.5 56.6 %collective-permute-start.27 = (bf16[577,4096]{1,0:T(8,128)(2,1)S(1)}, bf16[577,4096]{1,0:T(8,128)(2,1)S(1)}, u32[]{:S(2)}, u32[]{:S(2)}) collective-permute-start(bf16[577,4096]{1,0:T(8,128)(2,1)S(1)} %get-tuple-element.125.left_ref.active_ref), channel_id=1, source_target_pairs={{0,4},{4,0},{8,12},{12,8},{16,20},{20,16},{24,28},{28,24},{1,5},{5... | collective-permute-start | bytes 14180360 | tf_op jit(solution)/shard_map/ppermute | solution.py:1009
  143.8 18.3 %collective-permute-start.29 = (bf16[1024,128]{1,0:T(8,128)(2,1)S(1)}, bf16[1024,128]{1,0:T(8,128)(2,1)S(1)}, u32[]{:S(2)}, u32[]{:S(2)}) collective-permute-start(bf16[1024,128]{1,0:T(8,128)(2,1)S(1)} %copy-done.61), channel_id=1, source_target_pairs={{0,1},{1,0},{2,3},{3,2},{4,5},{5,4},{6,7},{7,6},{8,9},{9,8},{10,11... | collective-permute-start | bytes 786440 | tf_op jit(solution)/shard_map/ppermute | solution.py:1009
  149.8 21.3 %collective-permute-start.30 = (bf16[1024,128]{1,0:T(8,128)(2,1)S(1)}, bf16[1024,128]{1,0:T(8,128)(2,1)S(1)}, u32[]{:S(2)}, u32[]{:S(2)}) collective-permute-start(bf16[1024,128]{1,0:T(8,128)(2,1)S(1)} %copy-done.61), channel_id=1, source_target_pairs={{0,2},{1,3},{2,0},{3,1},{4,6},{5,7},{6,4},{7,5},{8,10},{9,11},{10,... | collective-permute-start | bytes 786440 | tf_op jit(solution)/shard_map/ppermute | solution.py:1009
  151.7 19.5 %collective-permute-start.31 = (bf16[1024,128]{1,0:T(8,128)(2,1)S(1)}, bf16[1024,128]{1,0:T(8,128)(2,1)S(1)}, u32[]{:S(2)}, u32[]{:S(2)}) collective-permute-start(bf16[1024,128]{1,0:T(8,128)(2,1)S(1)} %copy-done.61), channel_id=1, source_target_pairs={{0,3},{1,2},{2,1},{3,0},{4,7},{5,6},{6,5},{7,4},{8,11},{9,10},{10,... | collective-permute-start | bytes 786440 | tf_op jit(solution)/shard_map/ppermute | solution.py:1009
  153.2 38.8 %collective-permute-start.28 = (bf16[577,1024]{1,0:T(8,128)(2,1)S(1)}, bf16[577,1024]{1,0:T(8,128)(2,1)S(1)}, u32[]{:S(2)}, u32[]{:S(2)}) collective-permute-start(bf16[577,1024]{1,0:T(8,128)(2,1)S(1)} %bitcast.46), channel_id=1, source_target_pairs={{0,4},{4,0},{8,12},{12,8},{16,20},{20,16},{24,28},{28,24},{1,5},{5... | collective-permute-start | bytes 3545096 | tf_op jit(solution)/shard_map/ppermute | solution.py:1009
  171.2 18.6 %collective-permute-start.33 = (bf16[3072,128]{1,0:T(8,128)(2,1)S(1)}, bf16[3072,128]{1,0:T(8,128)(2,1)S(1)}, u32[]{:S(2)}, u32[]{:S(2)}) collective-permute-start(bf16[3072,128]{1,0:T(8,128)(2,1)S(1)} %shard_map.255.rest_0_), channel_id=1, source_target_pairs={{0,8},{4,12},{8,0},{12,4},{16,24},{20,28},{24,16},{28,20},{1,9},{5... | collective-permute-start | bytes 2359304 | tf_op jit(solution)/shard_map/ppermute | solution.py:1009
  171.8 19.2 %collective-permute-start.35 = (bf16[3072,128]{1,0:T(8,128)(2,1)S(1)}, bf16[3072,128]{1,0:T(8,128)(2,1)S(1)}, u32[]{:S(2)}, u32[]{:S(2)}) collective-permute-start(bf16[3072,128]{1,0:T(8,128)(2,1)S(1)} %shard_map.255.rest_0_), channel_id=1, source_target_pairs={{0,16},{4,20},{8,24},{12,28},{16,0},{20,4},{24,8},{28,12},{1,17},{... | collective-permute-start | bytes 2359304 | tf_op jit(solution)/shard_map/ppermute | solution.py:1009
  189.9 9.3 %collective-permute-start.37 = (bf16[1536,128]{1,0:T(8,128)(2,1)S(1)}, bf16[1536,128]{1,0:T(8,128)(2,1)S(1)}, u32[]{:S(2)}, u32[]{:S(2)}) collective-permute-start(bf16[1536,128]{1,0:T(8,128)(2,1)S(1)} %slice.124), channel_id=1, source_target_pairs={{0,16},{4,20},{8,24},{12,28},{16,0},{20,4},{24,8},{28,12},{1,17},{... | collective-permute-start | bytes 1179656 | tf_op jit(solution)/shard_map/ppermute | solution.py:1009
  192.0 24.8 %collective-permute-start.32 = (bf16[3072,128]{1,0:T(8,128)(2,1)S(1)}, bf16[3072,128]{1,0:T(8,128)(2,1)S(1)}, u32[]{:S(2)}, u32[]{:S(2)}) collective-permute-start(bf16[3072,128]{1,0:T(8,128)(2,1)S(1)} %shard_map.255.rest_0_), channel_id=1, source_target_pairs={{0,4},{4,0},{8,12},{12,8},{16,20},{20,16},{24,28},{28,24},{1,5},{5... | collective-permute-start | bytes 2359304 | tf_op jit(solution)/shard_map/ppermute | solution.py:1009
  192.0 24.8 %collective-permute-start.34 = (bf16[3072,128]{1,0:T(8,128)(2,1)S(1)}, bf16[3072,128]{1,0:T(8,128)(2,1)S(1)}, u32[]{:S(2)}, u32[]{:S(2)}) collective-permute-start(bf16[3072,128]{1,0:T(8,128)(2,1)S(1)} %collective-permute-done.33.rest_2_), channel_id=1, source_target_pairs={{0,4},{4,0},{8,12},{12,8},{16,20},{20,16},{24,28},{28,24},{1,5},{5... | collective-permute-start | bytes 2359304 | tf_op jit(solution)/shard_map/ppermute | solution.py:1009
  199.3 17.6 %collective-permute-start.36 = (bf16[3072,128]{1,0:T(8,128)(2,1)S(1)}, bf16[3072,128]{1,0:T(8,128)(2,1)S(1)}, u32[]{:S(2)}, u32[]{:S(2)}) collective-permute-start(bf16[3072,128]{1,0:T(8,128)(2,1)S(1)} %collective-permute-done.35.rest_4_), channel_id=1, source_target_pairs={{0,4},{4,0},{8,12},{12,8},{16,20},{20,16},{24,28},{28,24},{1,5},{5... | collective-permute-start | bytes 2359304 | tf_op jit(solution)/shard_map/ppermute | solution.py:1009
  200.1 16.7 %collective-permute-start.39 = (bf16[1536,128]{1,0:T(8,128)(2,1)S(1)}, bf16[1536,128]{1,0:T(8,128)(2,1)S(1)}, u32[]{:S(2)}, u32[]{:S(2)}) collective-permute-start(bf16[1536,128]{1,0:T(8,128)(2,1)S(1)} %collective-permute-done.37.rest_6_), channel_id=1, source_target_pairs={{0,4},{4,0},{8,12},{12,8},{16,20},{20,16},{24,28},{28,24},{1,5},{5... | collective-permute-start | bytes 1179656 | tf_op jit(solution)/shard_map/ppermute | solution.py:1009
  200.1 16.7 %collective-permute-start.40 = (bf16[1536,128]{1,0:T(8,128)(2,1)S(1)}, bf16[1536,128]{1,0:T(8,128)(2,1)S(1)}, u32[]{:S(2)}, u32[]{:S(2)}) collective-permute-start(bf16[1536,128]{1,0:T(8,128)(2,1)S(1)} %collective-permute-done.38.rest_7_), channel_id=1, source_target_pairs={{0,4},{4,0},{8,12},{12,8},{16,20},{20,16},{24,28},{28,24},{1,5},{5... | collective-permute-start | bytes 1179656 | tf_op jit(solution)/shard_map/ppermute | solution.py:1009
  230.9 32.8 %collective-permute-start.44 = (bf16[577,4096]{1,0:T(8,128)(2,1)}, bf16[577,4096]{1,0:T(8,128)(2,1)}, u32[]{:S(2)}, u32[]{:S(2)}) collective-permute-start(bf16[577,4096]{1,0:T(8,128)(2,1)} %get-tuple-element.136.pre_ref.refs_2_), channel_id=1, source_target_pairs={{0,4},{4,0},{8,12},{12,8},{16,20},{20,16},{24,28},{28,24},{1,5},{5... | collective-permute-start | bytes 14180360 | tf_op jit(solution)/shard_map/ppermute | solution.py:1009
  231.0 25.8 %collective-permute-start.41 = (bf16[2,2,128,1024]{3,2,1,0:T(8,128)(2,1)}, bf16[2,2,128,1024]{3,2,1,0:T(8,128)(2,1)}, u32[]{:S(2)}, u32[]{:S(2)}) collective-permute-start(bf16[2,2,128,1024]{3,2,1,0:T(8,128)(2,1)} %get-tuple-element.126), channel_id=1, source_target_pairs={{0,8},{4,12},{8,0},{12,4},{16,24},{20,28},{24,16},{28,20},{1,9},{5... | collective-permute-start | bytes 3145736 | tf_op jit(solution)/shard_map/ppermute | solution.py:1009
  231.6 31.0 %collective-permute-start.43 = (bf16[577,1024]{1,0:T(8,128)(2,1)}, bf16[577,1024]{1,0:T(8,128)(2,1)}, u32[]{:S(2)}, u32[]{:S(2)}) collective-permute-start(bf16[577,1024]{1,0:T(8,128)(2,1)} %get-tuple-element.119.normed_ref.refs_0_), channel_id=1, source_target_pairs={{0,4},{4,0},{8,12},{12,8},{16,20},{20,16},{24,28},{28,24},{1,5},{5... | collective-permute-start | bytes 3545096 | tf_op jit(solution)/shard_map/ppermute | solution.py:1009
  231.8 31.9 %collective-permute-start.45 = (bf16[577,1024]{1,0:T(8,128)(2,1)S(1)}, bf16[577,1024]{1,0:T(8,128)(2,1)}, u32[]{:S(2)}, u32[]{:S(2)}) collective-permute-start(bf16[577,1024]{1,0:T(8,128)(2,1)S(1)} %get-tuple-element.115.attended_ref.refs_4_), channel_id=1, source_target_pairs={{0,4},{4,0},{8,12},{12,8},{16,20},{20,16},{24,28},{28,24},{1,5},{5... | collective-permute-start | bytes 3545096 | tf_op jit(solution)/shard_map/ppermute | solution.py:1009
  232.1 25.5 %collective-permute-start.42 = (bf16[2,2,128,1024]{3,2,1,0:T(8,128)(2,1)}, bf16[2,2,128,1024]{3,2,1,0:T(8,128)(2,1)}, u32[]{:S(2)}, u32[]{:S(2)}) collective-permute-start(bf16[2,2,128,1024]{3,2,1,0:T(8,128)(2,1)} %get-tuple-element.128), channel_id=1, source_target_pairs={{0,16},{4,20},{8,24},{12,28},{16,0},{20,4},{24,8},{28,12},{1,17},{... | collective-permute-start | bytes 3145736 | tf_op jit(solution)/shard_map/ppermute | solution.py:1009
  261.2 18.9 %collective-permute-start.50 = (bf16[2,128,1024]{2,1,0:T(8,128)(2,1)S(1)}, bf16[2,128,1024]{2,1,0:T(8,128)(2,1)S(1)}, u32[]{:S(2)}, u32[]{:S(2)}) collective-permute-start(bf16[2,128,1024]{2,1,0:T(8,128)(2,1)S(1)} %get-tuple-element.212), channel_id=1, source_target_pairs={{0,8},{4,12},{8,0},{12,4},{16,24},{20,28},{24,16},{28,20},{1,9},{5... | collective-permute-start | bytes 1572872 | tf_op jit(solution)/shard_map/ppermute | solution.py:1009
  262.7 18.5 %collective-permute-start.49 = (bf16[2,128,1024]{2,1,0:T(8,128)(2,1)S(1)}, bf16[2,128,1024]{2,1,0:T(8,128)(2,1)S(1)}, u32[]{:S(2)}, u32[]{:S(2)}) collective-permute-start(bf16[2,128,1024]{2,1,0:T(8,128)(2,1)S(1)} %get-tuple-element.214), channel_id=1, source_target_pairs={{0,16},{4,20},{8,24},{12,28},{16,0},{20,4},{24,8},{28,12},{1,17},{... | collective-permute-start | bytes 1572872 | tf_op jit(solution)/shard_map/ppermute | solution.py:1009
  307.5 35.0 %collective-permute-start.52 = (bf16[3,577,1024]{2,1,0:T(8,128)(2,1)}, bf16[3,577,1024]{2,1,0:T(8,128)(2,1)S(1)}, u32[]{:S(2)}, u32[]{:S(2)}) collective-permute-start(bf16[3,577,1024]{2,1,0:T(8,128)(2,1)} %get-tuple-element.152.refs_2_.proj_ref), channel_id=1, source_target_pairs={{0,4},{4,0},{8,12},{12,8},{16,20},{20,16},{24,28},{28,24},{1,5},{5... | collective-permute-start | bytes 10635272 | tf_op jit(solution)/shard_map/ppermute | solution.py:1009
  307.5 31.4 %collective-permute-start.47 = (bf16[2,512,640]{2,1,0:T(8,128)(2,1)}, bf16[2,512,640]{2,1,0:T(8,128)(2,1)S(1)}, u32[]{:S(2)}, u32[]{:S(2)}) collective-permute-start(bf16[2,512,640]{2,1,0:T(8,128)(2,1)} %copy-done.54), channel_id=1, source_target_pairs={{0,8},{4,12},{8,0},{12,4},{16,24},{20,28},{24,16},{28,20},{1,9},{5... | collective-permute-start | bytes 3932168 | tf_op jit(solution)/shard_map/ppermute | solution.py:1009
  308.2 31.0 %collective-permute-start.48 = (bf16[2,512,640]{2,1,0:T(8,128)(2,1)}, bf16[2,512,640]{2,1,0:T(8,128)(2,1)S(1)}, u32[]{:S(2)}, u32[]{:S(2)}) collective-permute-start(bf16[2,512,640]{2,1,0:T(8,128)(2,1)} %copy-done.53), channel_id=1, source_target_pairs={{0,16},{4,20},{8,24},{12,28},{16,0},{20,4},{24,8},{28,12},{1,17},{... | collective-permute-start | bytes 3932168 | tf_op jit(solution)/shard_map/ppermute | solution.py:1009
  309.2 33.2 %collective-permute-start.51 = (bf16[577,1024]{1,0:T(8,128)(2,1)}, bf16[577,1024]{1,0:T(8,128)(2,1)S(1)}, u32[]{:S(2)}, u32[]{:S(2)}) collective-permute-start(bf16[577,1024]{1,0:T(8,128)(2,1)} %copy-done.55), channel_id=1, source_target_pairs={{0,4},{4,0},{8,12},{12,8},{16,20},{20,16},{24,28},{28,24},{1,5},{5... | collective-permute-start | bytes 3545096 | tf_op jit(solution)/shard_map/ppermute | solution.py:1009
  339.6 16.0 %collective-permute-start.54 = (bf16[512,640]{1,0:T(8,128)(2,1)S(1)}, bf16[512,640]{1,0:T(8,128)(2,1)S(1)}, u32[]{:S(2)}, u32[]{:S(2)}) collective-permute-start(bf16[512,640]{1,0:T(8,128)(2,1)S(1)} %get-tuple-element.208), channel_id=1, source_target_pairs={{0,8},{4,12},{8,0},{12,4},{16,24},{20,28},{24,16},{28,20},{1,9},{5... | collective-permute-start | bytes 1966088 | tf_op jit(solution)/shard_map/ppermute | solution.py:1009
  341.3 15.7 %collective-permute-start.53 = (bf16[512,640]{1,0:T(8,128)(2,1)S(1)}, bf16[512,640]{1,0:T(8,128)(2,1)S(1)}, u32[]{:S(2)}, u32[]{:S(2)}) collective-permute-start(bf16[512,640]{1,0:T(8,128)(2,1)S(1)} %get-tuple-element.210), channel_id=1, source_target_pairs={{0,16},{4,20},{8,24},{12,28},{16,0},{20,4},{24,8},{28,12},{1,17},{... | collective-permute-start | bytes 1966088 | tf_op jit(solution)/shard_map/ppermute | solution.py:1009
  358.6 63.9 %reduce-scatter.3.cloned.1.call-start = ((), (), s32[]{:S(2)}) async-start(), calls=%async_computation.2 | async-start | bytes 1310720 | tf_op jit(solution)/shard_map/reduce_scatter | solution.py:1062
  359.3 116.5 %all-gather.3.cloned.1.call-start = ((), (), s32[]{:S(2)}) async-start(), calls=%async_computation.4 | async-start | bytes 2949120 | tf_op jit(solution)/shard_map/all_gather | solution.py:1066
  359.7 17.7 %collective-permute-start.56 = (bf16[2,512,384]{2,1,0:T(8,128)(2,1)S(1)}, bf16[2,512,384]{2,1,0:T(8,128)(2,1)}, u32[]{:S(2)}, u32[]{:S(2)}) collective-permute-start(bf16[2,512,384]{2,1,0:T(8,128)(2,1)S(1)} %copy-done.59), channel_id=1, source_target_pairs={{0,8},{4,12},{8,0},{12,4},{16,24},{20,28},{24,16},{28,20},{1,9},{5... | collective-permute-start | bytes 2359304 | tf_op jit(solution)/shard_map/ppermute | solution.py:1009
  360.3 17.4 %collective-permute-start.57 = (bf16[2,512,384]{2,1,0:T(8,128)(2,1)S(1)}, bf16[2,512,384]{2,1,0:T(8,128)(2,1)}, u32[]{:S(2)}, u32[]{:S(2)}) collective-permute-start(bf16[2,512,384]{2,1,0:T(8,128)(2,1)S(1)} %get-tuple-element.159), channel_id=1, source_target_pairs={{0,16},{4,20},{8,24},{12,28},{16,0},{20,4},{24,8},{28,12},{1,17},{... | collective-permute-start | bytes 2359304 | tf_op jit(solution)/shard_map/ppermute | solution.py:1009
  380.4 14.9 %collective-permute-start.58 = (f32[4,3072]{1,0:T(4,128)S(1)}, f32[4,3072]{1,0:T(4,128)S(1)}, u32[]{:S(2)}, u32[]{:S(2)}) collective-permute-start(f32[4,3072]{1,0:T(4,128)S(1)} %add.143), channel_id=1, source_target_pairs={{0,8},{4,12},{8,0},{12,4},{16,24},{20,28},{24,16},{28,20},{1,9},{5... | collective-permute-start | bytes 147464 | tf_op jit(solution)/shard_map/ppermute | solution.py:1009
  381.9 13.5 %collective-permute-start.60 = (bf16[512,384]{1,0:T(8,128)(2,1)S(1)}, bf16[512,384]{1,0:T(8,128)(2,1)S(1)}, u32[]{:S(2)}, u32[]{:S(2)}) collective-permute-start(bf16[512,384]{1,0:T(8,128)(2,1)S(1)} %get-tuple-element.216), channel_id=1, source_target_pairs={{0,8},{4,12},{8,0},{12,4},{16,24},{20,28},{24,16},{28,20},{1,9},{5... | collective-permute-start | bytes 1179656 | tf_op jit(solution)/shard_map/ppermute | solution.py:1009
  382.5 12.9 %collective-permute-start.59 = (bf16[512,384]{1,0:T(8,128)(2,1)S(1)}, bf16[512,384]{1,0:T(8,128)(2,1)S(1)}, u32[]{:S(2)}, u32[]{:S(2)}) collective-permute-start(bf16[512,384]{1,0:T(8,128)(2,1)S(1)} %get-tuple-element.218), channel_id=1, source_target_pairs={{0,16},{4,20},{8,24},{12,28},{16,0},{20,4},{24,8},{28,12},{1,17},{... | collective-permute-start | bytes 1179656 | tf_op jit(solution)/shard_map/ppermute | solution.py:1009
  422.4 19.0 %collective-permute-start.65 = (bf16[128,1024]{1,0:T(8,128)(2,1)}, bf16[128,1024]{1,0:T(8,128)(2,1)S(1)}, u32[]{:S(2)}, u32[]{:S(2)}) collective-permute-start(bf16[128,1024]{1,0:T(8,128)(2,1)} %bitcast.48), channel_id=1, source_target_pairs={{0,8},{4,12},{8,0},{12,4},{16,24},{20,28},{24,16},{28,20},{1,9},{5... | collective-permute-start | bytes 786440 | tf_op jit(solution)/shard_map/ppermute | solution.py:1009
  423.9 17.5 %collective-permute-start.66 = (bf16[128,1024]{1,0:T(8,128)(2,1)}, bf16[128,1024]{1,0:T(8,128)(2,1)S(1)}, u32[]{:S(2)}, u32[]{:S(2)}) collective-permute-start(bf16[128,1024]{1,0:T(8,128)(2,1)} %bitcast.49), channel_id=1, source_target_pairs={{0,16},{4,20},{8,24},{12,28},{16,0},{20,4},{24,8},{28,12},{1,17},{... | collective-permute-start | bytes 786440 | tf_op jit(solution)/shard_map/ppermute | solution.py:1009
  425.9 9.2 %collective-permute-start.62 = (bf16[256,384]{1,0:T(8,128)(2,1)S(1)}, bf16[256,384]{1,0:T(8,128)(2,1)S(1)}, u32[]{:S(2)}, u32[]{:S(2)}) collective-permute-start(bf16[256,384]{1,0:T(8,128)(2,1)S(1)} %get-tuple-element.184), channel_id=1, source_target_pairs={{0,1},{1,0},{2,3},{3,2},{4,5},{5,4},{6,7},{7,6},{8,9},{9,8},{10,11... | collective-permute-start | bytes 589832 | tf_op jit(solution)/shard_map/ppermute | solution.py:1009
  425.9 15.5 %collective-permute-start.63 = (bf16[256,384]{1,0:T(8,128)(2,1)S(1)}, bf16[256,384]{1,0:T(8,128)(2,1)S(1)}, u32[]{:S(2)}, u32[]{:S(2)}) collective-permute-start(bf16[256,384]{1,0:T(8,128)(2,1)S(1)} %get-tuple-element.185), channel_id=1, source_target_pairs={{0,2},{1,3},{2,0},{3,1},{4,6},{5,7},{6,4},{7,5},{8,10},{9,11},{10,... | collective-permute-start | bytes 589832 | tf_op jit(solution)/shard_map/ppermute | solution.py:1009
  435.1 17.7 %collective-permute-start.76 = (bf16[128,1024]{1,0:T(8,128)(2,1)}, bf16[128,1024]{1,0:T(8,128)(2,1)S(1)}, u32[]{:S(2)}, u32[]{:S(2)}) collective-permute-start(bf16[128,1024]{1,0:T(8,128)(2,1)} %bitcast.50), channel_id=1, source_target_pairs={{0,4},{4,0},{8,12},{12,8},{16,20},{20,16},{24,28},{28,24},{1,5},{5... | collective-permute-start | bytes 786440 | tf_op jit(solution)/shard_map/ppermute | solution.py:1009
  441.5 9.8 %collective-permute-start.68 = (bf16[256,384]{1,0:T(8,128)(2,1)S(1)}, bf16[256,384]{1,0:T(8,128)(2,1)S(1)}, u32[]{:S(2)}, u32[]{:S(2)}) collective-permute-start(bf16[256,384]{1,0:T(8,128)(2,1)S(1)} %add_convert_fusion.16.refs_0_), channel_id=1, source_target_pairs={{0,8},{4,12},{8,0},{12,4},{16,24},{20,28},{24,16},{28,20},{1,9},{5... | collective-permute-start | bytes 589832 | tf_op jit(solution)/shard_map/ppermute | solution.py:1009
  442.2 12.6 %collective-permute-start.79 = (bf16[128,1024]{1,0:T(8,128)(2,1)S(1)}, bf16[128,1024]{1,0:T(8,128)(2,1)S(1)}, u32[]{:S(2)}, u32[]{:S(2)}) collective-permute-start(bf16[128,1024]{1,0:T(8,128)(2,1)S(1)} %collective-permute-done.65.refs_2_), channel_id=1, source_target_pairs={{0,16},{4,20},{8,24},{12,28},{16,0},{20,4},{24,8},{28,12},{1,17},{... | collective-permute-start | bytes 786440 | tf_op jit(solution)/shard_map/ppermute | solution.py:1009
  447.7 19.8 %collective-permute-start.77 = (bf16[128,1024]{1,0:T(8,128)(2,1)S(1)}, bf16[128,1024]{1,0:T(8,128)(2,1)S(1)}, u32[]{:S(2)}, u32[]{:S(2)}) collective-permute-start(bf16[128,1024]{1,0:T(8,128)(2,1)S(1)} %collective-permute-done.65.refs_2_), channel_id=1, source_target_pairs={{0,4},{4,0},{8,12},{12,8},{16,20},{20,16},{24,28},{28,24},{1,5},{5... | collective-permute-start | bytes 786440 | tf_op jit(solution)/shard_map/ppermute | solution.py:1009
  449.8 18.3 %collective-permute-start.78 = (bf16[128,1024]{1,0:T(8,128)(2,1)S(1)}, bf16[128,1024]{1,0:T(8,128)(2,1)S(1)}, u32[]{:S(2)}, u32[]{:S(2)}) collective-permute-start(bf16[128,1024]{1,0:T(8,128)(2,1)S(1)} %collective-permute-done.66.refs_4_), channel_id=1, source_target_pairs={{0,4},{4,0},{8,12},{12,8},{16,20},{20,16},{24,28},{28,24},{1,5},{5... | collective-permute-start | bytes 786440 | tf_op jit(solution)/shard_map/ppermute | solution.py:1009
  452.8 15.3 %collective-permute-start.74 = (bf16[256,384]{1,0:T(8,128)(2,1)S(1)}, bf16[256,384]{1,0:T(8,128)(2,1)S(1)}, u32[]{:S(2)}, u32[]{:S(2)}) collective-permute-start(bf16[256,384]{1,0:T(8,128)(2,1)S(1)} %collective-permute-done.68.refs_2_), channel_id=1, source_target_pairs={{0,16},{4,20},{8,24},{12,28},{16,0},{20,4},{24,8},{28,12},{1,17},{... | collective-permute-start | bytes 589832 | tf_op jit(solution)/shard_map/ppermute | solution.py:1009
  454.7 15.0 %collective-permute-start.80 = (bf16[128,1024]{1,0:T(8,128)(2,1)S(1)}, bf16[128,1024]{1,0:T(8,128)(2,1)S(1)}, u32[]{:S(2)}, u32[]{:S(2)}) collective-permute-start(bf16[128,1024]{1,0:T(8,128)(2,1)S(1)} %collective-permute-done.79.refs_6_), channel_id=1, source_target_pairs={{0,4},{4,0},{8,12},{12,8},{16,20},{20,16},{24,28},{28,24},{1,5},{5... | collective-permute-start | bytes 786440 | tf_op jit(solution)/shard_map/ppermute | solution.py:1009
  (104 other events, 1596.5 us)
Sparse Core Ops, SparseCore 0:
  358.7 34.8 reduce-scatter.4
  396.4 25.9 reduce-scatter.2
  424.3 32.8 all-gather.2
